TPU v7x, 32 devices: a whole 2x2x4 slice. The times are simulated.
32 devices in a mesh: sub: 8 (over y, x, core), pole: 4 (over z).
Axes of the slice: x: 2, y: 2, z: 4, core: 2. Of those that a mesh axis runs over, the one named last changes fastest.
Arguments:
- state: float32 [6144, 512], P('sub'), may hold values from -6 to 6
- conductivity: float32 [6144], P('sub'), may hold values from 0.2 to 2
- pole_shift: float32 [4, 2], P('pole'), may hold values from 0.2 to 1
- pole_weight: float32 [4, 2], P('pole'), may hold values from -1.5 to 1.5
- order_list: int32 [8, 1024], P('sub'), may hold values from 0 to 1023, as said below
- inverse: bfloat16 [4, 6144, 2048], P('pole', 'sub'), may hold values from -0.1 to 0.4
Outputs:
- final_state: float32 [6144, 512], P(('sub', 'pole'))
Inputs may be any that keep to these rules, and one draw needn't show every extreme that they name: `order_list`: row s holds each of 0 to 1023 exactly once.
All inputs are finite; a program needn't handle non-finite values.
Results may differ from a plain program's by a relative error of at most 0.0052.
Values may be sent and summed in bfloat16 or wider, within the bound.
No kernel may reach another device: no remote copies, remote signals or barrier semaphores. Data moves between devices by JAX's collectives and lax.ppermute only.
A program may use at most 64 MiB of HBM per device.

v0:
```python
import jax
import jax.numpy as jnp
from jax import lax
from jax.sharding import PartitionSpec as P

H = 128
STEPS = 2


def with_halo(x, sides, width):
    for axis, dim in sides:
        devices, length = (lax.axis_size(axis), x.shape[dim])
        up = [(i, (i + 1) % devices) for i in range(devices - 1)]
        down = [(j, i) for i, j in up]
        last = lax.slice_in_dim(x, length - width, length, axis=dim)
        initial = lax.slice_in_dim(x, 0, width, axis=dim)
        before = lax.ppermute(last, axis, up)
        after = lax.ppermute(initial, axis, down)
        x = jnp.concatenate([before, x, after], axis=dim)
    return x


def laplace(padded, rim_width):
    inner_count = padded.shape[0] - 2 * rim_width
    middle = padded[rim_width : rim_width + inner_count]
    return (
        4.0 * middle
        - padded[rim_width - 1 : rim_width - 1 + inner_count]
        - padded[rim_width + 1 : rim_width + 1 + inner_count]
        - padded[:inner_count]
        - padded[2 * rim_width : 2 * rim_width + inner_count]
    )


def shifted(padded, sigma_mid, shift_re, shift_im, rim_width):
    laplace_part = laplace(padded, rim_width)
    inner_count = laplace_part.shape[0]
    middle = padded[rim_width : rim_width + inner_count]
    column_half = middle.shape[1] // 2
    real_part = middle[:, :column_half]
    imag_part = middle[:, column_half:]
    sigma_col = sigma_mid[:, None]
    return laplace_part + jnp.concatenate(
        [
            sigma_col * (shift_re * real_part - shift_im * imag_part),
            sigma_col * (shift_im * real_part + shift_re * imag_part),
        ],
        axis=1,
    )


def correct(residual_ext, ordering, inverse_block):
    permuted = jnp.take(residual_ext, ordering, axis=0)
    column_half = permuted.shape[1] // 2
    real_part = permuted[:, :column_half]
    imag_part = permuted[:, column_half:]
    stacked = jnp.concatenate(
        [
            jnp.concatenate([real_part, imag_part], axis=1),
            jnp.concatenate([-imag_part, real_part], axis=1),
        ],
        axis=0,
    )
    return jnp.dot(inverse_block, stacked, preferred_element_type=jnp.float32)


def shards(state, conductivity, pole_shift, pole_weight, order_list, inverse):
    row_count = conductivity.shape[0]
    column_half = state.shape[1]
    pole_count = lax.axis_size("pole")
    share_rows = row_count // pole_count
    ordering = order_list[0]
    inverse_block = inverse[0]
    shift_re = pole_shift[0, 0]
    shift_im = pole_shift[0, 1]
    weight_re = pole_weight[0, 0]
    weight_im = pole_weight[0, 1]
    pole_start = lax.axis_index("pole") * share_rows
    right_side = conductivity[:, None] * state
    result = state[:share_rows]
    for time_step in range(STEPS):
        rhs_ext = with_halo(right_side, (("sub", 0),), H)
        source_ext = jnp.concatenate([rhs_ext, jnp.zeros_like(rhs_ext)], axis=1)
        iterate = correct(source_ext.astype(jnp.bfloat16), ordering, inverse_block)
        padded = with_halo(iterate, (("sub", 0),), H)
        applied = shifted(padded, conductivity, shift_re, shift_im, H)
        own_rows = (source_ext[H : H + row_count] - applied).astype(jnp.bfloat16)
        residual = with_halo(own_rows, (("sub", 0),), H)
        iterate = iterate + correct(residual, ordering, inverse_block)
        partial_value = 2.0 * (
            weight_re * iterate[:, :column_half] - weight_im * iterate[:, column_half:]
        )
        result = lax.psum_scatter(partial_value, "pole", scatter_dimension=0, tiled=True)
        if time_step + 1 < STEPS:
            sigma_share = lax.dynamic_slice_in_dim(conductivity, pole_start, share_rows, 0)
            right_side = lax.all_gather(sigma_share[:, None] * result, "pole", axis=0, tiled=True)
    return result


def solution(mesh):
    placed = (
        P("sub", None),
        P("sub"),
        P("pole", None),
        P("pole", None),
        P("sub", None),
        P("pole", "sub", None),
    )
    return jax.shard_map(
        shards, mesh=mesh, in_specs=placed, out_specs=P(("sub", "pole"), None), check_vma=False
    )
```

profile of v0, /device:TPU:18, one launch (start us, length us, event | category | flops | bytes accessed | tf_op | source)
XLA Modules:
  0.0 278.1 jit_solution(13963762971498977683)
XLA Ops:
  6.5 1.7 broadcast_multiply_fusion
  8.3 1.9 collective-permute-start.1
  10.3 2.4 collective-permute-start
  12.7 0.6 fusion.87
  13.3 0.8 collective-permute-done.1
  14.1 3.8 %collective-permute-done = f32[128,512]{1,0:T(8,128)S(1)} collective-permute-done((f32[128,512]{1,0:T(8,128)S(1)}, f32[128,512]{1,0:T(8,128)S(1)}, u32[]{:S(2)}, u32[]{:S(2)}) %collective-permute-start) | collective-permute-done | bytes 262176 | tf_op jit(solution)/shard_map/ppermute | solution.py:17
  18.0 0.7 copy-done.8
  18.7 1.6 fusion.79
  20.3 7.9 %gather_fusion = bf16[1024,1024]{1,0:T(8,128)(2,1)} fusion(bf16[1024,1024]{1,0:T(8,128)(2,1)} %fusion.79, s32[1024]{0:T(1024)S(1)} %fusion.73), kind=kCustom, calls=%fused_computation.clone | custom fusion | bytes 4198400 | tf_op jit(solution)/shard_map/jit(_take)/gather | solution.py:53
  28.2 1.9 broadcast_select_fusion.2
  30.0 0.1 slice_negate_fusion.3
  30.2 3.5 %fusion.56 = f32[768,1024]{1,0:T(8,128)S(1)} fusion(bf16[1024,512]{1,0:T(8,128)(2,1)S(1)} %get-tuple-element.21, bf16[1024,512]{1,0:T(8,128)(2,1)S(1)} %get-tuple-element.20, bf16[1024,1024]{1,0:T(8,128)(2,1)S(1)} %broadcast_select_fusion.2, bf16[1,768,2048]{2,1,0:T(8,128)(2,1)S(1)} %copy-done), kind=kOutput, calls=%fused_computation.79 | convolution fusion | flops 3233808384 | bytes 10485760 | tf_op jit(solution)/shard_map/dot_general | solution.py:64
  33.7 0.1 fusion.81
  33.8 2.2 collective-permute-start.3
  36.0 2.4 collective-permute-start.2
  38.4 0.5 fusion.4
  39.0 1.6 subtract_multiply_fusion.1
  40.6 3.1 %collective-permute-done.3 = f32[128,1024]{1,0:T(8,128)S(1)} collective-permute-done((f32[128,1024]{1,0:T(8,128)S(1)}, f32[128,1024]{1,0:T(8,128)S(1)}, u32[]{:S(2)}, u32[]{:S(2)}) %collective-permute-start.3) | collective-permute-done | bytes 524320 | tf_op jit(solution)/shard_map/ppermute | solution.py:18
  43.7 2.8 %collective-permute-done.2 = f32[128,1024]{1,0:T(8,128)S(1)} collective-permute-done((f32[128,1024]{1,0:T(8,128)S(1)}, f32[128,1024]{1,0:T(8,128)S(1)}, u32[]{:S(2)}, u32[]{:S(2)}) %collective-permute-start.2) | collective-permute-done | bytes 524320 | tf_op jit(solution)/shard_map/ppermute | solution.py:17
  46.5 4.5 %fusion.44 = bf16[768,1024]{1,0:T(8,128)(2,1)S(1)} fusion(f32[768,1024]{1,0:T(8,128)S(1)} %fusion.56, f32[128,1024]{1,0:T(8,128)S(1)} %collective-permute-done.3, f32[128,1024]{1,0:T(8,128)S(1)} %collective-permute-done.2, f32[1024,1024]{1,0:T(8,128)S(1)} %fusion.4, f32[768,512]{1,0:T(8,128)S(1)} %get-tuple-element.9, f32[768,512]{1,0:T(8,128)S(1)} %get-tuple-element.8), kind=kLoop, calls=%fused_computation.59 | loop fusion | flops 10223616 | bytes 12058624 | tf_op jit(solution)/shard_map/convert_element_type | solution.py:87
  51.1 1.9 collective-permute-start.5
  53.0 5.5 %collective-permute-start.4 = (bf16[128,1024]{1,0:T(8,128)(2,1)S(1)}, bf16[128,1024]{1,0:T(8,128)(2,1)S(1)}, u32[]{:S(2)}, u32[]{:S(2)}) collective-permute-start(bf16[128,1024]{1,0:T(8,128)(2,1)S(1)} %get-tuple-element.26), channel_id=1, source_target_pairs={{0,4},{4,8},{8,12},{12,16},{16,20},{20,24},{24,28},{1,5},{5,9},{9,... | collective-permute-start | bytes 786440 | tf_op jit(solution)/shard_map/ppermute | solution.py:17
  58.5 0.6 fusion.86
  59.1 1.6 collective-permute-done.4
  60.7 1.5 pad_maximum_fusion.4
  62.2 7.9 %gather_fusion.1 = bf16[1024,1024]{1,0:T(8,128)(2,1)} fusion(bf16[1024,1024]{1,0:T(8,128)(2,1)} %pad_maximum_fusion.4, s32[1024]{0:T(1024)S(1)} %fusion.73), kind=kCustom, calls=%fused_computation.1.clone | custom fusion | bytes 4198400 | tf_op jit(solution)/shard_map/jit(_take)/gather | solution.py:53
  70.1 1.9 broadcast_select_fusion.1
  72.0 0.1 slice_negate_fusion.2
  72.1 1.7 copy-done.4
  73.9 3.4 %bitcast_add_fusion.1 = f32[768,1024]{1,0:T(8,128)S(1)} fusion(f32[768,1024]{1,0:T(8,128)S(1)} %copy-done.4, bf16[1024,512]{1,0:T(8,128)(2,1)S(1)} %get-tuple-element.19, bf16[1024,512]{1,0:T(8,128)(2,1)S(1)} %get-tuple-element.18, bf16[1024,1024]{1,0:T(8,128)(2,1)S(1)} %broadcast_select_fusion.1, bf16[1,768,2048]{2,1,0:T(8,128)(2,1)S(1)} %copy-done), kind=kOutput, calls=%fused_computation.67 | convolution fusion | flops 3234594816 | bytes 13631488 | tf_op jit(solution)/shard_map/dot_general | solution.py:64
  77.3 2.8 fusion.72
  80.2 39.9 %reduce-scatter.3.cloned.1.call-done = f32[192,512]{1,0:T(8,128)} async-done(((f32[768,512]{1,0:T(8,128)}), f32[192,512]{1,0:T(8,128)}) %reduce-scatter.3.cloned.1.call-update) | async-done | bytes 393232 | tf_op jit(solution)/shard_map/reduce_scatter | solution.py:93
  120.1 1.8 broadcast_multiply_fusion.1
  122.0 36.0 %all-gather.2.cloned.1.call-done = f32[768,512]{1,0:T(8,128)} async-done(((f32[192,512]{1,0:T(8,128)}), f32[768,512]{1,0:T(8,128)}) %all-gather.2.cloned.1.call-update) | async-done | bytes 1572880 | tf_op jit(solution)/shard_map/all_gather | solution.py:96
  158.0 1.1 fusion.83
  159.1 1.9 collective-permute-start.7
  161.0 2.4 collective-permute-start.6
  163.4 1.5 collective-permute-done.7
  164.9 3.8 %collective-permute-done.6 = f32[128,512]{1,0:T(8,128)S(1)} collective-permute-done((f32[128,512]{1,0:T(8,128)S(1)}, f32[128,512]{1,0:T(8,128)S(1)}, u32[]{:S(2)}, u32[]{:S(2)}) %collective-permute-start.6) | collective-permute-done | bytes 262176 | tf_op jit(solution)/shard_map/ppermute | solution.py:17
  168.7 0.7 copy-done.10
  169.4 3.0 %fusion.78 = bf16[1024,1024]{1,0:T(8,128)(2,1)} fusion(f32[128,512]{1,0:T(8,128)S(1)} %collective-permute-done.7, f32[768,512]{1,0:T(8,128)} %all-gather.2.cloned.1.call-done, f32[128,512]{1,0:T(8,128)S(1)} %collective-permute-done.6), kind=kLoop, calls=%fused_computation.105 | loop fusion | flops 10485760 | bytes 4194304 | tf_op jit(solution)/shard_map/convert_element_type | solution.py:84
  172.5 7.9 %gather_fusion.2 = bf16[1024,1024]{1,0:T(8,128)(2,1)} fusion(bf16[1024,1024]{1,0:T(8,128)(2,1)} %fusion.78, s32[1024]{0:T(1024)S(1)} %fusion.73), kind=kCustom, calls=%fused_computation.2.clone | custom fusion | bytes 4198400 | tf_op jit(solution)/shard_map/jit(_take)/gather | solution.py:53
  180.3 1.9 broadcast_select_fusion.3
  182.2 0.1 slice_negate_fusion.1
  182.4 3.5 %fusion.51 = f32[768,1024]{1,0:T(8,128)S(1)} fusion(bf16[1024,512]{1,0:T(8,128)(2,1)S(1)} %get-tuple-element.17, bf16[1024,512]{1,0:T(8,128)(2,1)S(1)} %get-tuple-element.16, bf16[1024,1024]{1,0:T(8,128)(2,1)S(1)} %broadcast_select_fusion.3, bf16[1,768,2048]{2,1,0:T(8,128)(2,1)S(1)} %copy-done), kind=kOutput, calls=%fused_computation.78 | convolution fusion | flops 3233808384 | bytes 10485760 | tf_op jit(solution)/shard_map/dot_general | solution.py:64
  185.8 0.1 fusion.80
  186.0 2.2 collective-permute-start.9
  188.2 2.4 collective-permute-start.8
  190.6 0.5 select_maximum_fusion
  191.1 1.6 subtract_multiply_fusion
  192.8 3.2 %collective-permute-done.9 = f32[128,1024]{1,0:T(8,128)S(1)} collective-permute-done((f32[128,1024]{1,0:T(8,128)S(1)}, f32[128,1024]{1,0:T(8,128)S(1)}, u32[]{:S(2)}, u32[]{:S(2)}) %collective-permute-start.9) | collective-permute-done | bytes 524320 | tf_op jit(solution)/shard_map/ppermute | solution.py:18
  196.0 2.6 collective-permute-done.8
  198.7 4.5 %fusion.35 = bf16[768,1024]{1,0:T(8,128)(2,1)S(1)} fusion(f32[768,1024]{1,0:T(8,128)S(1)} %fusion.51, f32[128,1024]{1,0:T(8,128)S(1)} %collective-permute-done.9, f32[128,1024]{1,0:T(8,128)S(1)} %collective-permute-done.8, f32[1024,1024]{1,0:T(8,128)S(1)} %select_maximum_fusion, f32[768,512]{1,0:T(8,128)S(1)} %get-tuple-element.7, ...), kind=kLoop, calls=%fused_computation.50 | loop fusion | flops 10223616 | bytes 12058624 | tf_op jit(solution)/shard_map/convert_element_type | solution.py:87
  203.2 2.1 collective-permute-start.11
  205.4 5.2 %collective-permute-start.10 = (bf16[128,1024]{1,0:T(8,128)(2,1)S(1)}, bf16[128,1024]{1,0:T(8,128)(2,1)S(1)}, u32[]{:S(2)}, u32[]{:S(2)}) collective-permute-start(bf16[128,1024]{1,0:T(8,128)(2,1)S(1)} %get-tuple-element.22), channel_id=1, source_target_pairs={{0,4},{4,8},{8,12},{12,16},{16,20},{20,24},{24,28},{1,5},{5,9},{9,... | collective-permute-start | bytes 786440 | tf_op jit(solution)/shard_map/ppermute | solution.py:17
  210.5 2.5 collective-permute-done.10
  213.0 1.5 pad_maximum_fusion.5
  214.6 7.9 %gather_fusion.3 = bf16[1024,1024]{1,0:T(8,128)(2,1)} fusion(bf16[1024,1024]{1,0:T(8,128)(2,1)} %pad_maximum_fusion.5, s32[1024]{0:T(1024)S(1)} %fusion.73), kind=kCustom, calls=%fused_computation.3.clone | custom fusion | bytes 4198400 | tf_op jit(solution)/shard_map/jit(_take)/gather | solution.py:53
  222.5 1.9 broadcast_select_fusion
  224.3 0.1 slice_negate_fusion
  224.5 1.7 copy-done.6
  226.2 3.4 %bitcast_add_fusion = f32[768,1024]{1,0:T(8,128)S(1)} fusion(f32[768,1024]{1,0:T(8,128)S(1)} %copy-done.6, bf16[1024,512]{1,0:T(8,128)(2,1)S(1)} %get-tuple-element.15, bf16[1024,512]{1,0:T(8,128)(2,1)S(1)} %get-tuple-element.14, bf16[1024,1024]{1,0:T(8,128)(2,1)S(1)} %broadcast_select_fusion, bf16[1,768,2048]{2,1,0:T(8,128)(2,1)S(1)} %copy-done), kind=kOutput, calls=%fused_computation.66 | convolution fusion | flops 3234594816 | bytes 13631488 | tf_op jit(solution)/shard_map/dot_general | solution.py:64
  229.7 2.8 fusion.70
  232.5 39.1 %reduce-scatter.5.cloned.1.call-done = f32[192,512]{1,0:T(8,128)} async-done(((f32[768,512]{1,0:T(8,128)}), f32[192,512]{1,0:T(8,128)}) %reduce-scatter.5.cloned.1.call-update) | async-done | bytes 393232 | tf_op jit(solution)/shard_map/reduce_scatter | solution.py:93
  (42 shorter events, 0.4 us)
Async XLA Ops:
  6.5 23.6 %copy-start = (bf16[1,768,2048]{2,1,0:T(8,128)(2,1)S(1)}, bf16[1,768,2048]{2,1,0:T(8,128)(2,1)}, u32[]{:S(2)}) copy-start(bf16[1,768,2048]{2,1,0:T(8,128)(2,1)} %param.13) | copy-start | bytes 9437188
  6.5 6.1 %copy-start.13 = (s32[1,1024]{1,0:T(1,128)S(1)}, s32[1,1024]{1,0:T(1,128)}, u32[]{:S(2)}) copy-start(s32[1,1024]{1,0:T(1,128)} %param.12) | copy-start | bytes 12292
  6.5 6.2 %copy-start.14 = (f32[1,2]{1,0:T(1,128)S(1)}, f32[1,2]{1,0:T(1,128)}, u32[]{:S(2)}) copy-start(f32[1,2]{1,0:T(1,128)} %param.10) | copy-start | bytes 28
  6.5 113.6 %reduce-scatter.3.cloned.1.call-start = ((), (), s32[]{:S(2)}) async-start(), calls=%async_computation.2 | async-start | bytes 1966080 | tf_op jit(solution)/shard_map/reduce_scatter | solution.py:93
  8.3 9.7 %copy-start.1 = (f32[768,512]{1,0:T(8,128)}, f32[768,512]{1,0:T(8,128)S(1)}, u32[]{:S(2)}) copy-start(f32[768,512]{1,0:T(8,128)S(1)} %broadcast_multiply_fusion) | copy-start | bytes 4718596
  8.3 5.8 %collective-permute-start.1 = (f32[128,512]{1,0:T(8,128)S(1)}, f32[128,512]{1,0:T(8,128)S(1)}, u32[]{:S(2)}, u32[]{:S(2)}) collective-permute-start(f32[128,512]{1,0:T(8,128)S(1)} %get-tuple-element.29), channel_id=1, source_target_pairs={{4,0},{8,4},{12,8},{16,12},{20,16},{24,20},{28,24},{5,1},{9,5},{13... | collective-permute-start | bytes 786440 | tf_op jit(solution)/shard_map/ppermute | solution.py:18
  10.3 7.7 %collective-permute-start = (f32[128,512]{1,0:T(8,128)S(1)}, f32[128,512]{1,0:T(8,128)S(1)}, u32[]{:S(2)}, u32[]{:S(2)}) collective-permute-start(f32[128,512]{1,0:T(8,128)S(1)} %get-tuple-element.28), channel_id=1, source_target_pairs={{0,4},{4,8},{8,12},{12,16},{16,20},{20,24},{24,28},{1,5},{5,9},{9,... | collective-permute-start | bytes 786440 | tf_op jit(solution)/shard_map/ppermute | solution.py:17
  18.0 0.7 copy-start.8
  30.2 8.2 %copy-start.9 = (f32[128,512]{1,0:T(8,128)S(1)}, f32[128,512]{1,0:T(8,128)}, u32[]{:S(2)}) copy-start(f32[128,512]{1,0:T(8,128)} %copy-done.8) | copy-start | bytes 786436
  33.7 12.8 %copy-start.3 = (f32[768,1024]{1,0:T(8,128)}, f32[768,1024]{1,0:T(8,128)S(1)}, u32[]{:S(2)}) copy-start(f32[768,1024]{1,0:T(8,128)S(1)} %fusion.56) | copy-start | bytes 9437188
  33.7 4.8 %copy-start.2 = (f32[768,512]{1,0:T(8,128)S(1)}, f32[768,512]{1,0:T(8,128)}, u32[]{:S(2)}) copy-start(f32[768,512]{1,0:T(8,128)} %copy-done.1) | copy-start | bytes 4718596
  33.8 9.9 %collective-permute-start.3 = (f32[128,1024]{1,0:T(8,128)S(1)}, f32[128,1024]{1,0:T(8,128)S(1)}, u32[]{:S(2)}, u32[]{:S(2)}) collective-permute-start(f32[128,1024]{1,0:T(8,128)S(1)} %get-tuple-element.13), channel_id=1, source_target_pairs={{4,0},{8,4},{12,8},{16,12},{20,16},{24,20},{28,24},{5,1},{9,5},{13... | collective-permute-start | bytes 1572872 | tf_op jit(solution)/shard_map/ppermute | solution.py:18
  36.0 3.0 %copy-start.12 = (f32[768]{0:T(1024)S(1)}, f32[768]{0:T(1024)}, u32[]{:S(2)}) copy-start(f32[768]{0:T(1024)} %param.9) | copy-start | bytes 9220
  36.0 10.5 %collective-permute-start.2 = (f32[128,1024]{1,0:T(8,128)S(1)}, f32[128,1024]{1,0:T(8,128)S(1)}, u32[]{:S(2)}, u32[]{:S(2)}) collective-permute-start(f32[128,1024]{1,0:T(8,128)S(1)} %get-tuple-element.12), channel_id=1, source_target_pairs={{0,4},{4,8},{8,12},{12,16},{16,20},{20,24},{24,28},{1,5},{5,9},{9,... | collective-permute-start | bytes 1572872 | tf_op jit(solution)/shard_map/ppermute | solution.py:17
  46.5 12.0 %copy-start.15 = (f32[1,2]{1,0:T(1,128)S(1)}, f32[1,2]{1,0:T(1,128)}, u32[]{:S(2)}) copy-start(f32[1,2]{1,0:T(1,128)} %param.11) | copy-start | bytes 28
  51.1 8.0 %collective-permute-start.5 = (bf16[128,1024]{1,0:T(8,128)(2,1)S(1)}, bf16[128,1024]{1,0:T(8,128)(2,1)S(1)}, u32[]{:S(2)}, u32[]{:S(2)}) collective-permute-start(bf16[128,1024]{1,0:T(8,128)(2,1)S(1)} %get-tuple-element.27), channel_id=1, source_target_pairs={{4,0},{8,4},{12,8},{16,12},{20,16},{24,20},{28,24},{5,1},{9,5},{13... | collective-permute-start | bytes 786440 | tf_op jit(solution)/shard_map/ppermute | solution.py:18
  53.0 7.7 %collective-permute-start.4 = (bf16[128,1024]{1,0:T(8,128)(2,1)S(1)}, bf16[128,1024]{1,0:T(8,128)(2,1)S(1)}, u32[]{:S(2)}, u32[]{:S(2)}) collective-permute-start(bf16[128,1024]{1,0:T(8,128)(2,1)S(1)} %get-tuple-element.26), channel_id=1, source_target_pairs={{0,4},{4,8},{8,12},{12,16},{16,20},{20,24},{24,28},{1,5},{5,9},{9,... | collective-permute-start | bytes 786440 | tf_op jit(solution)/shard_map/ppermute | solution.py:17
  72.0 1.9 copy-start.4
  80.1 77.9 %all-gather.2.cloned.1.call-start = ((), (), s32[]{:S(2)}) async-start(), calls=%async_computation.3 | async-start | bytes 1966080 | tf_op jit(solution)/shard_map/all_gather | solution.py:96
  122.0 149.6 %reduce-scatter.5.cloned.1.call-start = ((), (), s32[]{:S(2)}) async-start(), calls=%async_computation.4 | async-start | bytes 1966080 | tf_op jit(solution)/shard_map/reduce_scatter | solution.py:93
  159.1 5.8 %collective-permute-start.7 = (f32[128,512]{1,0:T(8,128)S(1)}, f32[128,512]{1,0:T(8,128)S(1)}, u32[]{:S(2)}, u32[]{:S(2)}) collective-permute-start(f32[128,512]{1,0:T(8,128)S(1)} %get-tuple-element.25), channel_id=1, source_target_pairs={{4,0},{8,4},{12,8},{16,12},{20,16},{24,20},{28,24},{5,1},{9,5},{13... | collective-permute-start | bytes 786440 | tf_op jit(solution)/shard_map/ppermute | solution.py:18
  161.0 7.7 %collective-permute-start.6 = (f32[128,512]{1,0:T(8,128)S(1)}, f32[128,512]{1,0:T(8,128)S(1)}, u32[]{:S(2)}, u32[]{:S(2)}) collective-permute-start(f32[128,512]{1,0:T(8,128)S(1)} %get-tuple-element.24), channel_id=1, source_target_pairs={{0,4},{4,8},{8,12},{12,16},{16,20},{20,24},{24,28},{1,5},{5,9},{9,... | collective-permute-start | bytes 786440 | tf_op jit(solution)/shard_map/ppermute | solution.py:17
  168.7 0.7 copy-start.10
  182.3 8.2 %copy-start.11 = (f32[128,512]{1,0:T(8,128)S(1)}, f32[128,512]{1,0:T(8,128)}, u32[]{:S(2)}) copy-start(f32[128,512]{1,0:T(8,128)} %copy-done.10) | copy-start | bytes 786436
  185.8 12.8 %copy-start.5 = (f32[768,1024]{1,0:T(8,128)}, f32[768,1024]{1,0:T(8,128)S(1)}, u32[]{:S(2)}) copy-start(f32[768,1024]{1,0:T(8,128)S(1)} %fusion.51) | copy-start | bytes 9437188
  185.8 4.7 %copy-start.7 = (f32[768,512]{1,0:T(8,128)S(1)}, f32[768,512]{1,0:T(8,128)}, u32[]{:S(2)}) copy-start(f32[768,512]{1,0:T(8,128)} %all-gather.2.cloned.1.call-done) | copy-start | bytes 4718596
  186.0 10.1 %collective-permute-start.9 = (f32[128,1024]{1,0:T(8,128)S(1)}, f32[128,1024]{1,0:T(8,128)S(1)}, u32[]{:S(2)}, u32[]{:S(2)}) collective-permute-start(f32[128,1024]{1,0:T(8,128)S(1)} %get-tuple-element.11), channel_id=1, source_target_pairs={{4,0},{8,4},{12,8},{16,12},{20,16},{24,20},{28,24},{5,1},{9,5},{13... | collective-permute-start | bytes 1572872 | tf_op jit(solution)/shard_map/ppermute | solution.py:18
  188.2 10.5 %collective-permute-start.8 = (f32[128,1024]{1,0:T(8,128)S(1)}, f32[128,1024]{1,0:T(8,128)S(1)}, u32[]{:S(2)}, u32[]{:S(2)}) collective-permute-start(f32[128,1024]{1,0:T(8,128)S(1)} %get-tuple-element.10), channel_id=1, source_target_pairs={{0,4},{4,8},{8,12},{12,16},{16,20},{20,24},{24,28},{1,5},{5,9},{9,... | collective-permute-start | bytes 1572872 | tf_op jit(solution)/shard_map/ppermute | solution.py:17
  203.2 7.3 %collective-permute-start.11 = (bf16[128,1024]{1,0:T(8,128)(2,1)S(1)}, bf16[128,1024]{1,0:T(8,128)(2,1)S(1)}, u32[]{:S(2)}, u32[]{:S(2)}) collective-permute-start(bf16[128,1024]{1,0:T(8,128)(2,1)S(1)} %get-tuple-element.23), channel_id=1, source_target_pairs={{4,0},{8,4},{12,8},{16,12},{20,16},{24,20},{28,24},{5,1},{9,5},{13... | collective-permute-start | bytes 786440 | tf_op jit(solution)/shard_map/ppermute | solution.py:18
  205.4 7.7 %collective-permute-start.10 = (bf16[128,1024]{1,0:T(8,128)(2,1)S(1)}, bf16[128,1024]{1,0:T(8,128)(2,1)S(1)}, u32[]{:S(2)}, u32[]{:S(2)}) collective-permute-start(bf16[128,1024]{1,0:T(8,128)(2,1)S(1)} %get-tuple-element.22), channel_id=1, source_target_pairs={{0,4},{4,8},{8,12},{12,16},{16,20},{20,24},{24,28},{1,5},{5,9},{9,... | collective-permute-start | bytes 786440 | tf_op jit(solution)/shard_map/ppermute | solution.py:17
  224.3 1.9 copy-start.6
Sparse Core Ops, SparseCore 0:
  80.2 39.8 reduce-scatter.2
  122.1 35.8 all-gather.1
  232.6 38.9 reduce-scatter.4
where the time goes:
time: 282 us; the launch traced here: 278 us
  waiting for transfers between devices  141 us (50%)
  local copies, waits for them, and re-layouts  39.1 us (14%)
  other arithmetic  38.1 us (14%)
  starting transfers between devices  32.7 us (12%)
  matrix products  13.8 us (5%)
  between operations  13.6 us (5%)
    reduce_scatter x2, waiting for transfers between devices, shards(): lax.psum_scatter(partial_value, 'pole', scatter_dimension=0, tiled=True)  79 us
    all_gather x1, waiting for transfers between devices, shards(): lax.all_gather(sigma_share[:, None] * result, 'pole', axis=0, tiled=True)  36 us
    gather x4, local copies, waits for them, and re-layouts, correct(): permuted = jnp.take(residual_ext, ordering, axis=0)  31.5 us
    ppermute x6, starting transfers between devices, with_halo(): before = lax.ppermute(last, axis, up)  20.3 us
    ppermute x6, waiting for transfers between devices, with_halo(): before = lax.ppermute(last, axis, up)  17.2 us
    dot_general x4, matrix products, correct(): return jnp.dot(inverse_block, stacked, preferred_element_type=jnp.float32)  13.8 us
    ppermute x6, starting transfers between devices, with_halo(): after = lax.ppermute(initial, axis, down)  12.3 us
    convert_element_type x2, other arithmetic, shards(): own_rows = (source_ext[H:H + row_count] - applied).astype(jnp.bfloat16)  9 us
  transfers between devices with their start and end apart: 15, of which 13 were waited for; matrix products, arithmetic and copies ran while one was open for 2% of the time, Pallas kernels for 0%

commit v1 on v0

v1 whole, which is shorter than its diff:
```python
import jax
import jax.numpy as jnp
from jax import lax
from jax.sharding import PartitionSpec as P

STEPS = 2
CHUNKS = 1
BF16 = jnp.bfloat16
F16 = jnp.float16
F32 = jnp.float32


def neighbours(axis):
    count = lax.axis_size(axis)
    up = [(i, i + 1) for i in range(count - 1)]
    return up, [(j, i) for i, j in up]


def partner_of(index, hop, count):
    if count & (count - 1) == 0:
        return index ^ hop, index ^ hop, [(i, i ^ hop) for i in range(count)]
    to = lax.rem(index + hop, count)
    source = lax.rem(index + count - hop, count)
    return to, source, [(i, (i + hop) % count) for i in range(count)]


def natural_order(inverse, ordering):
    width = ordering.shape[0]
    ids = lax.broadcasted_iota(jnp.int32, (width, width), 1)
    place = (ordering[:, None] == ids).astype(BF16)
    real = jnp.dot(inverse[:, :width], place, preferred_element_type=F32).astype(BF16)
    imag = jnp.dot(inverse[:, width:], place, preferred_element_type=F32).astype(BF16)
    return real, imag


def reduce_poles(partial, share):
    count = lax.axis_size("pole")
    index = lax.axis_index("pole")
    columns = partial.shape[1]
    blocks = partial.reshape(count, share, columns)
    top = jnp.max(jnp.abs(blocks), axis=1)
    power = jnp.ceil(jnp.log2(jnp.maximum(top, 1e-30)))
    coded = (blocks * jnp.exp2(12.0 - power)[:, None]).astype(F16)
    tail = jnp.broadcast_to(power.astype(F16)[:, None], (count, 16, columns))
    coded = jnp.concatenate([coded, tail], axis=1)
    total = lax.dynamic_index_in_dim(blocks, index, 0, keepdims=False)
    for hop in range(1, count):
        to, _, pairs = partner_of(index, hop, count)
        sent = lax.dynamic_index_in_dim(coded, to, 0, keepdims=False)
        got = lax.ppermute(sent, "pole", pairs).astype(F32)
        total = total + got[:share] * jnp.exp2(got[share : share + 1] - 12.0)
    return total


def gather_poles(own):
    count = lax.axis_size("pole")
    index = lax.axis_index("pole")
    share = own.shape[0]
    whole = jnp.zeros((count * share, own.shape[1]), own.dtype)
    whole = lax.dynamic_update_slice_in_dim(whole, own, index * share, 0)
    for hop in range(1, count):
        _, source, pairs = partner_of(index, hop, count)
        got = lax.ppermute(own, "pole", pairs)
        whole = lax.dynamic_update_slice_in_dim(whole, got, source * share, 0)
    return whole


def shards(state, conductivity, pole_shift, pole_weight, order_list, inverse):
    rows, columns = state.shape
    rim = (order_list.shape[1] - rows) // 2
    share = rows // lax.axis_size("pole")
    up, down = neighbours("sub")
    g_real, g_imag = natural_order(inverse[0], order_list[0])
    both = jnp.concatenate([g_real, g_imag], axis=0)
    shift_re, shift_im = pole_shift[0, 0], pole_shift[0, 1]
    weight_re, weight_im = pole_weight[0, 0], pole_weight[0, 1]
    sigma = conductivity[:, None]
    sigma_share = lax.dynamic_slice_in_dim(conductivity, lax.axis_index("pole") * share, share, 0)[:, None]

    def sweep(source):
        rounded = source.astype(BF16)
        before = lax.ppermute(rounded[rows - rim :], "sub", up)
        after = lax.ppermute(rounded[:rim], "sub", down)
        first = jnp.dot(both[:, rim : rim + rows], rounded, preferred_element_type=F32)
        first = first + jnp.dot(both[:, :rim], before, preferred_element_type=F32)
        first = first + jnp.dot(both[:, rim + rows :], after, preferred_element_type=F32)
        real, imag = first[:rows], first[rows:]
        source = source.astype(F32)

        def local(x):
            zero = jnp.zeros((rim, x.shape[1]), F32)
            far = jnp.concatenate([zero, x, zero], axis=0)
            near = jnp.pad(x, ((1, 1), (0, 0)))
            return 4.0 * x - near[:rows] - near[2:] - far[:rows] - far[2 * rim :]

        r_real = source - local(real) - sigma * (shift_re * real - shift_im * imag)
        r_imag = -local(imag) - sigma * (shift_im * real + shift_re * imag)
        x = jnp.stack([real, imag])
        r = jnp.stack([r_real, r_imag])
        low = jnp.concatenate([x[:, :rim], r[:, :rim]], axis=0).astype(BF16)
        high = jnp.concatenate([x[:, rows - rim :], r[:, rows - rim :]], axis=0).astype(BF16)
        got_before = lax.ppermute(high, "sub", up).astype(F32)
        got_after = lax.ppermute(low, "sub", down).astype(F32)

        def joined(half):
            mine = x[half]
            xb, qb = got_before[half], got_before[2 + half]
            xa, qa = got_after[half], got_after[2 + half]
            one = lax.broadcasted_iota(jnp.int32, (rim, 1), 0)
            head = r[half, :rim] + xb + jnp.where(one == 0, xb[rim - 1 :], 0.0)
            foot = r[half, rows - rim :] + xa + jnp.where(one == rim - 1, xa[:1], 0.0)
            above = qb + mine[:rim] + jnp.where(one == rim - 1, mine[:1], 0.0)
            below = qa + mine[rows - rim :] + jnp.where(one == 0, mine[rows - 1 :], 0.0)
            return head.astype(BF16), foot.astype(BF16), above, below

        edge = []
        index = lax.axis_index("sub")
        last = lax.axis_size("sub") - 1
        for half in range(2):
            head, foot, above, below = joined(half)
            above = jnp.where(index == 0, 0.0, above).astype(BF16)
            below = jnp.where(index == last, 0.0, below).astype(BF16)
            middle = r[half, rim : rows - rim].astype(BF16)
            edge.append(jnp.concatenate([above, head, middle, foot, below], axis=0))
        e = jnp.concatenate(edge, axis=1)
        n = real.shape[1]
        y = jnp.dot(both, e, preferred_element_type=F32)
        real = real + y[:rows, :n] - y[rows:, n:]
        imag = imag + y[:rows, n:] + y[rows:, :n]
        return 2.0 * (weight_re * real - weight_im * imag)

    results = []
    width = columns // CHUNKS
    for chunk in range(CHUNKS):
        source = sigma * state[:, chunk * width : (chunk + 1) * width]
        for step in range(STEPS):
            total = reduce_poles(sweep(source), share)
            if step + 1 < STEPS:
                source = gather_poles((sigma_share * total).astype(BF16))
        results.append(total)
    return jnp.concatenate(results, axis=1) if CHUNKS > 1 else results[0]


def solution(mesh):
    placed = (
        P("sub", None),
        P("sub"),
        P("pole", None),
        P("pole", None),
        P("sub", None),
        P("pole", "sub", None),
    )
    return jax.shard_map(
        shards, mesh=mesh, in_specs=placed, out_specs=P(("sub", "pole"), None), check_vma=False
    )
```

time: 282 us -> 162 us (0.57); the launches traced: 278 us -> 162 us
  waiting for transfers between devices: 141 us -> 70.2 us
  local copies, waits for them, and re-layouts: 39.1 us -> 12.1 us
  other arithmetic: 38.1 us -> 22.9 us
  between operations: 13.6 us -> 0.7 us
  matrix products: 13.8 us -> 22.5 us
    reduce_scatter x2 -> x0, waiting for transfers between devices: 79 us -> none  [shards(): lax.psum_scatter(partial_value, 'pole', scatter_dimension=0, tiled=True)]
    ppermute x12 -> x17, waiting for transfers between devices: 25.8 us -> 70.2 us  [the longest x6 36.9 us: reduce_poles(): got = lax.ppermute(sent, 'pole', pairs).astype(F32)]
    all_gather x1 -> x0, waiting for transfers between devices: 36 us -> none  [shards(): lax.all_gather(sigma_share[:, None] * result, 'pole', axis=0, tiled=True)]
    gather x4 -> x0, local copies, waits for them, and re-layouts: 31.5 us -> none  [correct(): permuted = jnp.take(residual_ext, ordering, axis=0)]
    convert_element_type x4 -> x13, other arithmetic: 13.7 us -> 3.66 us  [the longest x1 1.59 us: sweep(): rounded = source.astype(BF16)]
    another operation x0 -> x6, other arithmetic: none -> 8.83 us  [the longest x2 8.62 us: sweep(): r = jnp.stack([r_real, r_imag])]
    dot_general x4 -> x10, matrix products: 13.8 us -> 22.5 us  [the longest x2 7 us: sweep(): y = jnp.dot(both, e, preferred_element_type=F32)]
    mul x6 -> x2, other arithmetic: 12.4 us -> 4.78 us  [sweep(): return 2.0 * (weight_re * real - weight_im * imag)]
  transfers between devices with their start and end apart: 15 -> 17, of which waited for: 13 -> 15; matrix products, arithmetic and copies ran while one was open for 2% -> 10% of each run, Pallas kernels for 0% -> 0%
where the time goes in v1:
time: 162 us
  waiting for transfers between devices  70.2 us (43%)
  starting transfers between devices  33.6 us (21%)
  other arithmetic  22.9 us (14%)
  matrix products  22.5 us (14%)
  local copies, waits for them, and re-layouts  12.1 us (7%)
    ppermute x6, waiting for transfers between devices, reduce_poles(): got = lax.ppermute(sent, 'pole', pairs).astype(F32)  36.9 us
    ppermute x3, waiting for transfers between devices, gather_poles(): got = lax.ppermute(own, 'pole', pairs)  15.7 us
    ppermute x2, waiting for transfers between devices, sweep(): got_before = lax.ppermute(high, 'sub', up).astype(F32)  8.62 us
    another operation x2, other arithmetic, sweep(): r = jnp.stack([r_real, r_imag])  8.62 us
    ppermute x2, starting transfers between devices, sweep(): got_after = lax.ppermute(low, 'sub', down).astype(F32)  7.82 us
    ppermute x2, starting transfers between devices, sweep(): after = lax.ppermute(rounded[:rim], 'sub', down)  7.28 us
    ppermute x6, starting transfers between devices, reduce_poles(): got = lax.ppermute(sent, 'pole', pairs).astype(F32)  7.03 us
    dot_general x2, matrix products, sweep(): y = jnp.dot(both, e, preferred_element_type=F32)  7 us
  transfers between devices with their start and end apart: 17, of which 15 were waited for; matrix products, arithmetic and copies ran while one was open for 10% of the time, Pallas kernels for 0%

profile of v1, /device:TPU:18, one launch (start us, length us, event | category | flops | bytes accessed | tf_op | source)
XLA Modules:
  0.0 161.9 jit_solution(13663204087050739851)
XLA Ops:
  0.0 1.6 multiply_convert_fusion.2
  1.6 0.7 fusion.181
  2.3 1.9 %collective-permute-start = (bf16[128,512]{1,0:T(8,128)(2,1)}, bf16[128,512]{1,0:T(8,128)(2,1)S(1)}, u32[]{:S(2)}, u32[]{:S(2)}) collective-permute-start(bf16[128,512]{1,0:T(8,128)(2,1)} %get-tuple-element.60), channel_id=1, source_target_pairs={{0,4},{4,8},{8,12},{12,16},{16,20},{20,24},{24,28},{1,5},{5,9},{9,... | collective-permute-start | bytes 393224 | tf_op jit(solution)/shard_map/ppermute | solution.py:82
  4.2 3.6 %collective-permute-start.1 = (bf16[128,512]{1,0:T(8,128)(2,1)S(1)}, bf16[128,512]{1,0:T(8,128)(2,1)S(1)}, u32[]{:S(2)}, u32[]{:S(2)}) collective-permute-start(bf16[128,512]{1,0:T(8,128)(2,1)S(1)} %get-tuple-element.59), channel_id=1, source_target_pairs={{4,0},{8,4},{12,8},{16,12},{20,16},{24,20},{28,24},{5,1},{9,5},{13... | collective-permute-start | bytes 393224 | tf_op jit(solution)/shard_map/ppermute | solution.py:83
  7.9 3.6 %fusion.46 = bf16[768,1024]{1,0:T(8,128)(2,1)S(1)} fusion(bf16[768,2048]{1,0:T(8,128)(2,1)} %bitcast.229, s32[1024]{0:T(1024)S(1)} %bitcast.231), kind=kOutput, calls=%fused_computation.83 | convolution fusion | flops 1612447744 | bytes 3149824 | tf_op jit(solution)/shard_map/dot_general | solution.py:32
  11.5 2.1 %fusion.49 = bf16[768,1024]{1,0:T(8,128)(2,1)S(1)} fusion(bf16[768,2048]{1,0:T(8,128)(2,1)S(1)} %bitcast.230, s32[1024]{0:T(1024)S(1)} %bitcast.232), kind=kOutput, calls=%fused_computation.84 | convolution fusion | flops 1612447744 | bytes 3149824 | tf_op jit(solution)/shard_map/dot_general | solution.py:31
  13.6 3.0 %fusion.167 = f32[1536,512]{1,0:T(8,128)} fusion(bf16[768,512]{1,0:T(8,128)(2,1)S(1)} %multiply_convert_fusion.2, bf16[768,1024]{1,0:T(8,128)(2,1)S(1)} %fusion.49, bf16[768,1024]{1,0:T(8,128)(2,1)S(1)} %fusion.46), kind=kOutput, calls=%fused_computation.272 | convolution fusion | flops 1212678144 | bytes 7077888 | tf_op jit(solution)/shard_map/dot_general | solution.py:84
  16.7 0.7 fusion.187
  17.4 2.4 %convolution_add_fusion.1 = f32[1536,512]{1,0:T(8,128)S(1)} fusion(f32[1536,512]{1,0:T(8,128)} %fusion.167, bf16[128,512]{1,0:T(8,128)(2,1)S(1)} %collective-permute-done, bf16[768,1024]{1,0:T(8,128)(2,1)S(1)} %fusion.49, bf16[768,1024]{1,0:T(8,128)(2,1)S(1)} %fusion.46), kind=kOutput, calls=%fused_computation.11 | convolution fusion | flops 202899456 | bytes 9568256 | tf_op jit(solution)/shard_map/dot_general | solution.py:85
  19.8 0.6 convolution_add_fusion
  20.4 0.3 fusion.179
  21.1 1.2 copy-done.3
  22.3 3.7 %fusion.20 = (f32[1,768,512]{2,1,0:T(8,128)S(1)}, f32[1,768,512]{2,1,0:T(8,128)S(1)}) fusion(f32[768,512]{1,0:T(8,128)S(1)} %get-tuple-element.37, f32[896,512]{1,0:T(8,128)S(1)} %slice.527, f32[768,512]{1,0:T(8,128)S(1)} %copy-done.3, f32[]{:T(128)} %bitcast.8, f32[]{:T(128)} %bitcast.7, f32[768]{0:T(1024)S(1)} %copy-done.4, pred[768]{0:T(1024)(128)(4,1)S(1)} %slice.528, ...), kind=kLoop, calls=%fused_computation.37 | loop fusion | flops 9437184 | bytes 12586760 | tf_op jit(solution)/shard_map/stack | solution.py:99
  26.1 1.9 %collective-permute-start.2 = (bf16[4,128,512]{2,1,0:T(8,128)(2,1)S(1)}, bf16[4,128,512]{2,1,0:T(8,128)(2,1)S(1)}, u32[]{:S(2)}, u32[]{:S(2)}) collective-permute-start(bf16[4,128,512]{2,1,0:T(8,128)(2,1)S(1)} %pad_maximum_fusion.7), channel_id=1, source_target_pairs={{0,4},{4,8},{8,12},{12,16},{16,20},{20,24},{24,28},{1,5},{5,9},{9,... | collective-permute-start | bytes 1572872 | tf_op jit(solution)/shard_map/ppermute | solution.py:102
  28.1 0.6 fusion.186
  28.8 3.8 %collective-permute-start.3 = (bf16[4,128,512]{2,1,0:T(8,128)(2,1)S(1)}, bf16[4,128,512]{2,1,0:T(8,128)(2,1)S(1)}, u32[]{:S(2)}, u32[]{:S(2)}) collective-permute-start(bf16[4,128,512]{2,1,0:T(8,128)(2,1)S(1)} %pad_maximum_fusion.8), channel_id=1, source_target_pairs={{4,0},{8,4},{12,8},{16,12},{20,16},{24,20},{28,24},{5,1},{9,5},{13... | collective-permute-start | bytes 1572872 | tf_op jit(solution)/shard_map/ppermute | solution.py:103
  32.6 4.0 %collective-permute-done.2 = bf16[4,128,512]{2,1,0:T(8,128)(2,1)S(1)} collective-permute-done((bf16[4,128,512]{2,1,0:T(8,128)(2,1)S(1)}, bf16[4,128,512]{2,1,0:T(8,128)(2,1)S(1)}, u32[]{:S(2)}, u32[]{:S(2)}) %collective-permute-start.2) | collective-permute-done | bytes 524320 | tf_op jit(solution)/shard_map/ppermute | solution.py:102
  37.2 5.0 %collective-permute-done.3 = bf16[4,128,512]{2,1,0:T(8,128)(2,1)S(1)} collective-permute-done((bf16[4,128,512]{2,1,0:T(8,128)(2,1)S(1)}, bf16[4,128,512]{2,1,0:T(8,128)(2,1)S(1)}, u32[]{:S(2)}, u32[]{:S(2)}) %collective-permute-start.3) | collective-permute-done | bytes 524320 | tf_op jit(solution)/shard_map/ppermute | solution.py:103
  42.6 3.5 %fusion.4 = f32[1536,1024]{1,0:T(8,128)S(1)} fusion(bf16[1024,512]{1,0:T(8,128)(2,1)S(1)} %get-tuple-element.12, bf16[1024,512]{1,0:T(8,128)(2,1)S(1)} %get-tuple-element.11, bf16[768,1024]{1,0:T(8,128)(2,1)S(1)} %fusion.46, bf16[768,1024]{1,0:T(8,128)(2,1)S(1)} %fusion.49), kind=kOutput, calls=%fused_computation.15 | convolution fusion | flops 3231711232 | bytes 11534336 | tf_op jit(solution)/shard_map/dot_general | solution.py:127
  46.1 2.4 %fusion.42 = f32[768,512]{1,0:T(8,128)S(1)} fusion(f32[1536,1024]{1,0:T(8,128)S(1)} %fusion.4, f32[]{:T(128)} %bitcast.29, f32[]{:T(128)} %bitcast, f32[1536,512]{1,0:T(8,128)S(1)} %convolution_add_fusion), kind=kLoop, calls=%fused_computation.65 | loop fusion | flops 3145728 | bytes 11010056 | tf_op jit(solution)/shard_map/mul | solution.py:130
  48.7 0.2 multiply_convert_fusion.1
  48.9 0.7 copy-done.2
  49.7 0.9 fusion.129
  50.6 1.6 collective-permute-start.4
  52.3 0.3 collective-permute-start.5
  52.6 1.6 collective-permute-start.6
  54.2 7.1 %collective-permute-done.4 = f16[208,512]{1,0:T(8,128)(2,1)} collective-permute-done((f16[208,512]{1,0:T(8,128)(2,1)}, f16[208,512]{1,0:T(8,128)(2,1)}, u32[]{:S(2)}, u32[]{:S(2)}) %collective-permute-start.4) | collective-permute-done | bytes 213024 | tf_op jit(solution)/shard_map/ppermute | solution.py:50
  61.3 1.0 convert_element_type.164
  62.3 5.3 %collective-permute-done.5 = f16[208,512]{1,0:T(8,128)(2,1)S(1)} collective-permute-done((f16[208,512]{1,0:T(8,128)(2,1)}, f16[208,512]{1,0:T(8,128)(2,1)S(1)}, u32[]{:S(2)}, u32[]{:S(2)}) %collective-permute-start.5) | collective-permute-done | bytes 213024 | tf_op jit(solution)/shard_map/ppermute | solution.py:50
  67.6 6.2 %collective-permute-done.6 = f16[208,512]{1,0:T(8,128)(2,1)S(1)} collective-permute-done((f16[208,512]{1,0:T(8,128)(2,1)S(1)}, f16[208,512]{1,0:T(8,128)(2,1)S(1)}, u32[]{:S(2)}, u32[]{:S(2)}) %collective-permute-start.6) | collective-permute-done | bytes 213024 | tf_op jit(solution)/shard_map/ppermute | solution.py:50
  73.9 0.9 broadcast_in_dim.245
  74.8 1.8 %constant_dynamic-update-slice_fusion.3 = (bf16[768,512]{1,0:T(8,128)(2,1)}, bf16[192,512]{1,0:T(8,128)(2,1)}) fusion(bf16[768,512]{1,0:T(8,128)(2,1)} %broadcast_in_dim.245, s32[]{:T(128)S(6)} %select_n.118, f32[512]{0:T(512)S(1)} %bitcast.228, f32[208,512]{1,0:T(8,128)S(1)} %convert_element_type.166, f32[512]{0:T(512)S(1)} %bitcast.227, ...), kind=kLoop, calls=%fused_computation.243 | loop fusion | flops 786432 | bytes 1973000 | tf_op jit(solution)/shard_map/dynamic_update_slice | solution.py:60
  76.7 1.9 %collective-permute-start.8 = (bf16[192,512]{1,0:T(8,128)(2,1)}, bf16[192,512]{1,0:T(8,128)(2,1)S(1)}, u32[]{:S(2)}, u32[]{:S(2)}) collective-permute-start(bf16[192,512]{1,0:T(8,128)(2,1)} %get-tuple-element.6), channel_id=1, source_target_pairs={{0,2},{1,3},{2,0},{3,1},{4,6},{5,7},{6,4},{7,5},{8,10},{9,11},{10,... | collective-permute-start | bytes 589832 | tf_op jit(solution)/shard_map/ppermute | solution.py:63
  78.6 1.6 collective-permute-start.9
  80.2 4.5 %collective-permute-done.7 = bf16[192,512]{1,0:T(8,128)(2,1)S(1)} collective-permute-done((bf16[192,512]{1,0:T(8,128)(2,1)}, bf16[192,512]{1,0:T(8,128)(2,1)S(1)}, u32[]{:S(2)}, u32[]{:S(2)}) %collective-permute-start.7) | collective-permute-done | bytes 196640 | tf_op jit(solution)/shard_map/ppermute | solution.py:63
  84.7 0.7 constant_dynamic-update-slice_fusion.2
  85.4 7.3 %collective-permute-done.8 = bf16[192,512]{1,0:T(8,128)(2,1)S(1)} collective-permute-done((bf16[192,512]{1,0:T(8,128)(2,1)}, bf16[192,512]{1,0:T(8,128)(2,1)S(1)}, u32[]{:S(2)}, u32[]{:S(2)}) %collective-permute-start.8) | collective-permute-done | bytes 196640 | tf_op jit(solution)/shard_map/ppermute | solution.py:63
  92.6 0.7 constant_dynamic-update-slice_fusion.1
  93.3 4.0 %collective-permute-done.9 = bf16[192,512]{1,0:T(8,128)(2,1)S(1)} collective-permute-done((bf16[192,512]{1,0:T(8,128)(2,1)}, bf16[192,512]{1,0:T(8,128)(2,1)S(1)}, u32[]{:S(2)}, u32[]{:S(2)}) %collective-permute-start.9) | collective-permute-done | bytes 196640 | tf_op jit(solution)/shard_map/ppermute | solution.py:63
  97.3 0.7 constant_dynamic-update-slice_fusion
  98.0 1.0 fusion.180
  99.0 1.9 %collective-permute-start.10 = (bf16[128,512]{1,0:T(8,128)(2,1)S(1)}, bf16[128,512]{1,0:T(8,128)(2,1)S(1)}, u32[]{:S(2)}, u32[]{:S(2)}) collective-permute-start(bf16[128,512]{1,0:T(8,128)(2,1)S(1)} %get-tuple-element.57), channel_id=1, source_target_pairs={{0,4},{4,8},{8,12},{12,16},{16,20},{20,24},{24,28},{1,5},{5,9},{9,... | collective-permute-start | bytes 393224 | tf_op jit(solution)/shard_map/ppermute | solution.py:82
  100.9 3.6 %collective-permute-start.11 = (bf16[128,512]{1,0:T(8,128)(2,1)S(1)}, bf16[128,512]{1,0:T(8,128)(2,1)S(1)}, u32[]{:S(2)}, u32[]{:S(2)}) collective-permute-start(bf16[128,512]{1,0:T(8,128)(2,1)S(1)} %get-tuple-element.58), channel_id=1, source_target_pairs={{4,0},{8,4},{12,8},{16,12},{20,16},{24,20},{28,24},{5,1},{9,5},{13... | collective-permute-start | bytes 393224 | tf_op jit(solution)/shard_map/ppermute | solution.py:83
  104.6 0.7 collective-permute-done.10
  105.3 0.5 fusion.172
  105.8 1.2 collective-permute-done.11
  107.1 0.6 fusion.169
  107.6 2.7 %fusion.2 = f32[1536,512]{1,0:T(8,128)S(1)} fusion(f32[1536,512]{1,0:T(8,128)S(1)} %fusion.169, f32[1536,512]{1,0:T(8,128)S(1)} %fusion.172, bf16[768,512]{1,0:T(8,128)(2,1)} %constant_dynamic-update-slice_fusion, bf16[768,1024]{1,0:T(8,128)(2,1)S(1)} %fusion.49, bf16[768,1024]{1,0:T(8,128)(2,1)S(1)} %fusion.46), kind=kOutput, calls=%fused_computation.13 | convolution fusion | flops 1214251008 | bytes 13369344 | tf_op jit(solution)/shard_map/dot_general | solution.py:84
  110.5 0.3 fusion.177
  110.8 1.1 copy-done
  112.0 1.5 slice-done
  113.4 5.0 %fusion.30 = (f32[1,768,512]{2,1,0:T(8,128)S(1)}, f32[1,768,512]{2,1,0:T(8,128)S(1)}) fusion(f32[768,512]{1,0:T(8,128)S(1)} %get-tuple-element.27, f32[896,512]{1,0:T(8,128)S(1)} %slice-done, bf16[768,512]{1,0:T(8,128)(2,1)} %constant_dynamic-update-slice_fusion, f32[]{:T(128)} %bitcast.8, f32[]{:T(128)} %bitcast.7, f32[768]{0:T(1024)S(1)} %copy-done.4, ...), kind=kLoop, calls=%fused_computation.47 | loop fusion | flops 9437184 | bytes 11800328 | tf_op jit(solution)/shard_map/stack | solution.py:99
  118.5 2.2 %collective-permute-start.12 = (bf16[4,128,512]{2,1,0:T(8,128)(2,1)S(1)}, bf16[4,128,512]{2,1,0:T(8,128)(2,1)S(1)}, u32[]{:S(2)}, u32[]{:S(2)}) collective-permute-start(bf16[4,128,512]{2,1,0:T(8,128)(2,1)S(1)} %pad_maximum_fusion.9), channel_id=1, source_target_pairs={{0,4},{4,8},{8,12},{12,16},{16,20},{20,24},{24,28},{1,5},{5,9},{9,... | collective-permute-start | bytes 1572872 | tf_op jit(solution)/shard_map/ppermute | solution.py:102
  120.8 4.0 %collective-permute-start.13 = (bf16[4,128,512]{2,1,0:T(8,128)(2,1)S(1)}, bf16[4,128,512]{2,1,0:T(8,128)(2,1)S(1)}, u32[]{:S(2)}, u32[]{:S(2)}) collective-permute-start(bf16[4,128,512]{2,1,0:T(8,128)(2,1)S(1)} %pad_maximum_fusion.10), channel_id=1, source_target_pairs={{4,0},{8,4},{12,8},{16,12},{20,16},{24,20},{28,24},{5,1},{9,5},{13... | collective-permute-start | bytes 1572872 | tf_op jit(solution)/shard_map/ppermute | solution.py:103
  124.8 4.6 %collective-permute-done.12 = bf16[4,128,512]{2,1,0:T(8,128)(2,1)S(1)} collective-permute-done((bf16[4,128,512]{2,1,0:T(8,128)(2,1)S(1)}, bf16[4,128,512]{2,1,0:T(8,128)(2,1)S(1)}, u32[]{:S(2)}, u32[]{:S(2)}) %collective-permute-start.12) | collective-permute-done | bytes 524320 | tf_op jit(solution)/shard_map/ppermute | solution.py:102
  130.0 2.0 %collective-permute-done.13 = bf16[4,128,512]{2,1,0:T(8,128)(2,1)S(1)} collective-permute-done((bf16[4,128,512]{2,1,0:T(8,128)(2,1)S(1)}, bf16[4,128,512]{2,1,0:T(8,128)(2,1)S(1)}, u32[]{:S(2)}, u32[]{:S(2)}) %collective-permute-start.13) | collective-permute-done | bytes 524320 | tf_op jit(solution)/shard_map/ppermute | solution.py:103
  132.4 3.5 %fusion.8 = f32[1536,1024]{1,0:T(8,128)S(1)} fusion(bf16[1024,512]{1,0:T(8,128)(2,1)S(1)} %get-tuple-element.8, bf16[1024,512]{1,0:T(8,128)(2,1)S(1)} %get-tuple-element.7, bf16[768,1024]{1,0:T(8,128)(2,1)S(1)} %fusion.46, bf16[768,1024]{1,0:T(8,128)(2,1)S(1)} %fusion.49), kind=kOutput, calls=%fused_computation.19 | convolution fusion | flops 3231711232 | bytes 11534336 | tf_op jit(solution)/shard_map/dot_general | solution.py:127
  135.9 2.4 %fusion.38 = f32[768,512]{1,0:T(8,128)S(1)} fusion(f32[1536,1024]{1,0:T(8,128)S(1)} %fusion.8, f32[]{:T(128)} %bitcast.29, f32[]{:T(128)} %bitcast, f32[1536,512]{1,0:T(8,128)S(1)} %copy-done.1), kind=kLoop, calls=%fused_computation.56 | loop fusion | flops 3145728 | bytes 11010056 | tf_op jit(solution)/shard_map/mul | solution.py:130
  139.0 1.9 %collective-permute-start.15 = (f16[208,512]{1,0:T(8,128)(2,1)S(1)}, f16[208,512]{1,0:T(8,128)(2,1)S(1)}, u32[]{:S(2)}, u32[]{:S(2)}) collective-permute-start(f16[208,512]{1,0:T(8,128)(2,1)S(1)} %get-tuple-element.52), channel_id=1, source_target_pairs={{0,2},{1,3},{2,0},{3,1},{4,6},{5,7},{6,4},{7,5},{8,10},{9,11},{10,... | collective-permute-start | bytes 638984 | tf_op jit(solution)/shard_map/ppermute | solution.py:50
  140.9 1.6 collective-permute-start.16
  142.5 4.6 %collective-permute-done.14 = f16[208,512]{1,0:T(8,128)(2,1)S(1)} collective-permute-done((f16[208,512]{1,0:T(8,128)(2,1)S(1)}, f16[208,512]{1,0:T(8,128)(2,1)S(1)}, u32[]{:S(2)}, u32[]{:S(2)}) %collective-permute-start.14) | collective-permute-done | bytes 213024 | tf_op jit(solution)/shard_map/ppermute | solution.py:50
  147.2 8.5 %collective-permute-done.15 = f16[208,512]{1,0:T(8,128)(2,1)S(1)} collective-permute-done((f16[208,512]{1,0:T(8,128)(2,1)S(1)}, f16[208,512]{1,0:T(8,128)(2,1)S(1)}, u32[]{:S(2)}, u32[]{:S(2)}) %collective-permute-start.15) | collective-permute-done | bytes 213024 | tf_op jit(solution)/shard_map/ppermute | solution.py:50
  155.7 5.2 %collective-permute-done.16 = f16[208,512]{1,0:T(8,128)(2,1)S(1)} collective-permute-done((f16[208,512]{1,0:T(8,128)(2,1)S(1)}, f16[208,512]{1,0:T(8,128)(2,1)S(1)}, u32[]{:S(2)}, u32[]{:S(2)}) %collective-permute-start.16) | collective-permute-done | bytes 213024 | tf_op jit(solution)/shard_map/ppermute | solution.py:50
  161.0 0.9 fusion.66
  (77 shorter events, 4.1 us)
Async XLA Ops:
  0.0 7.8 %copy-start.9 = (s32[1,1024]{1,0:T(1,128)S(1)}, s32[1,1024]{1,0:T(1,128)}, u32[]{:S(2)}) copy-start(s32[1,1024]{1,0:T(1,128)} %param.10) | copy-start | bytes 12292
  2.3 15.1 %collective-permute-start = (bf16[128,512]{1,0:T(8,128)(2,1)}, bf16[128,512]{1,0:T(8,128)(2,1)S(1)}, u32[]{:S(2)}, u32[]{:S(2)}) collective-permute-start(bf16[128,512]{1,0:T(8,128)(2,1)} %get-tuple-element.60), channel_id=1, source_target_pairs={{0,4},{4,8},{8,12},{12,16},{16,20},{20,24},{24,28},{1,5},{5,9},{9,... | collective-permute-start | bytes 393224 | tf_op jit(solution)/shard_map/ppermute | solution.py:82
  4.2 15.6 %collective-permute-start.1 = (bf16[128,512]{1,0:T(8,128)(2,1)S(1)}, bf16[128,512]{1,0:T(8,128)(2,1)S(1)}, u32[]{:S(2)}, u32[]{:S(2)}) collective-permute-start(bf16[128,512]{1,0:T(8,128)(2,1)S(1)} %get-tuple-element.59), channel_id=1, source_target_pairs={{4,0},{8,4},{12,8},{16,12},{20,16},{24,20},{28,24},{5,1},{9,5},{13... | collective-permute-start | bytes 393224 | tf_op jit(solution)/shard_map/ppermute | solution.py:83
  7.8 3.6 %copy-start.8 = (bf16[1,768,2048]{2,1,0:T(8,128)(2,1)S(1)}, bf16[1,768,2048]{2,1,0:T(8,128)(2,1)}, u32[]{:S(2)}) copy-start(bf16[1,768,2048]{2,1,0:T(8,128)(2,1)} %param.11) | copy-start | bytes 9437188
  13.6 3.0 %copy-start.7 = (pred[896]{0:T(1024)(128)(4,1)S(1)}, pred[896]{0:T(1024)(128)(4,1)}, u32[]{:S(2)}) copy-start(pred[896]{0:T(1024)(128)(4,1)} %constant.65.clone.1) | copy-start | bytes 2692
  13.6 3.1 %copy-start.5 = (f32[1,2]{1,0:T(1,128)S(1)}, f32[1,2]{1,0:T(1,128)}, u32[]{:S(2)}) copy-start(f32[1,2]{1,0:T(1,128)} %param.8) | copy-start | bytes 28
  20.8 1.4 copy-start.3
  20.9 1.4 copy-start.4
  26.0 2.1 %copy-start.6 = (f32[1,2]{1,0:T(1,128)S(1)}, f32[1,2]{1,0:T(1,128)}, u32[]{:S(2)}) copy-start(f32[1,2]{1,0:T(1,128)} %param.9) | copy-start | bytes 28
  26.1 10.5 %collective-permute-start.2 = (bf16[4,128,512]{2,1,0:T(8,128)(2,1)S(1)}, bf16[4,128,512]{2,1,0:T(8,128)(2,1)S(1)}, u32[]{:S(2)}, u32[]{:S(2)}) collective-permute-start(bf16[4,128,512]{2,1,0:T(8,128)(2,1)S(1)} %pad_maximum_fusion.7), channel_id=1, source_target_pairs={{0,4},{4,8},{8,12},{12,16},{16,20},{20,24},{24,28},{1,5},{5,9},{9,... | collective-permute-start | bytes 1572872 | tf_op jit(solution)/shard_map/ppermute | solution.py:102
  28.8 13.4 %collective-permute-start.3 = (bf16[4,128,512]{2,1,0:T(8,128)(2,1)S(1)}, bf16[4,128,512]{2,1,0:T(8,128)(2,1)S(1)}, u32[]{:S(2)}, u32[]{:S(2)}) collective-permute-start(bf16[4,128,512]{2,1,0:T(8,128)(2,1)S(1)} %pad_maximum_fusion.8), channel_id=1, source_target_pairs={{4,0},{8,4},{12,8},{16,12},{20,16},{24,20},{28,24},{5,1},{9,5},{13... | collective-permute-start | bytes 1572872 | tf_op jit(solution)/shard_map/ppermute | solution.py:103
  48.5 1.2 copy-start.2
  50.6 10.7 %collective-permute-start.4 = (f16[208,512]{1,0:T(8,128)(2,1)}, f16[208,512]{1,0:T(8,128)(2,1)}, u32[]{:S(2)}, u32[]{:S(2)}) collective-permute-start(f16[208,512]{1,0:T(8,128)(2,1)} %get-tuple-element.54), channel_id=1, source_target_pairs={{0,1},{1,0},{2,3},{3,2},{4,5},{5,4},{6,7},{7,6},{8,9},{9,8},{10,11... | collective-permute-start | bytes 638984 | tf_op jit(solution)/shard_map/ppermute | solution.py:50
  52.3 15.3 %collective-permute-start.5 = (f16[208,512]{1,0:T(8,128)(2,1)}, f16[208,512]{1,0:T(8,128)(2,1)S(1)}, u32[]{:S(2)}, u32[]{:S(2)}) collective-permute-start(f16[208,512]{1,0:T(8,128)(2,1)} %get-tuple-element.55), channel_id=1, source_target_pairs={{0,2},{1,3},{2,0},{3,1},{4,6},{5,7},{6,4},{7,5},{8,10},{9,11},{10,... | collective-permute-start | bytes 638984 | tf_op jit(solution)/shard_map/ppermute | solution.py:50
  52.6 21.2 %collective-permute-start.6 = (f16[208,512]{1,0:T(8,128)(2,1)S(1)}, f16[208,512]{1,0:T(8,128)(2,1)S(1)}, u32[]{:S(2)}, u32[]{:S(2)}) collective-permute-start(f16[208,512]{1,0:T(8,128)(2,1)S(1)} %get-tuple-element.56), channel_id=1, source_target_pairs={{0,3},{1,2},{2,1},{3,0},{4,7},{5,6},{6,5},{7,4},{8,11},{9,10},{10,... | collective-permute-start | bytes 638984 | tf_op jit(solution)/shard_map/ppermute | solution.py:50
  76.7 8.0 %collective-permute-start.7 = (bf16[192,512]{1,0:T(8,128)(2,1)}, bf16[192,512]{1,0:T(8,128)(2,1)S(1)}, u32[]{:S(2)}, u32[]{:S(2)}) collective-permute-start(bf16[192,512]{1,0:T(8,128)(2,1)} %get-tuple-element.6), channel_id=1, source_target_pairs={{0,1},{1,0},{2,3},{3,2},{4,5},{5,4},{6,7},{7,6},{8,9},{9,8},{10,11... | collective-permute-start | bytes 589832 | tf_op jit(solution)/shard_map/ppermute | solution.py:63
  76.7 15.9 %collective-permute-start.8 = (bf16[192,512]{1,0:T(8,128)(2,1)}, bf16[192,512]{1,0:T(8,128)(2,1)S(1)}, u32[]{:S(2)}, u32[]{:S(2)}) collective-permute-start(bf16[192,512]{1,0:T(8,128)(2,1)} %get-tuple-element.6), channel_id=1, source_target_pairs={{0,2},{1,3},{2,0},{3,1},{4,6},{5,7},{6,4},{7,5},{8,10},{9,11},{10,... | collective-permute-start | bytes 589832 | tf_op jit(solution)/shard_map/ppermute | solution.py:63
  78.6 18.7 %collective-permute-start.9 = (bf16[192,512]{1,0:T(8,128)(2,1)}, bf16[192,512]{1,0:T(8,128)(2,1)S(1)}, u32[]{:S(2)}, u32[]{:S(2)}) collective-permute-start(bf16[192,512]{1,0:T(8,128)(2,1)} %get-tuple-element.6), channel_id=1, source_target_pairs={{0,3},{1,2},{2,1},{3,0},{4,7},{5,6},{6,5},{7,4},{8,11},{9,10},{10,... | collective-permute-start | bytes 589832 | tf_op jit(solution)/shard_map/ppermute | solution.py:63
  99.0 6.3 %collective-permute-start.10 = (bf16[128,512]{1,0:T(8,128)(2,1)S(1)}, bf16[128,512]{1,0:T(8,128)(2,1)S(1)}, u32[]{:S(2)}, u32[]{:S(2)}) collective-permute-start(bf16[128,512]{1,0:T(8,128)(2,1)S(1)} %get-tuple-element.57), channel_id=1, source_target_pairs={{0,4},{4,8},{8,12},{12,16},{16,20},{20,24},{24,28},{1,5},{5,9},{9,... | collective-permute-start | bytes 393224 | tf_op jit(solution)/shard_map/ppermute | solution.py:82
  100.9 6.1 %collective-permute-start.11 = (bf16[128,512]{1,0:T(8,128)(2,1)S(1)}, bf16[128,512]{1,0:T(8,128)(2,1)S(1)}, u32[]{:S(2)}, u32[]{:S(2)}) collective-permute-start(bf16[128,512]{1,0:T(8,128)(2,1)S(1)} %get-tuple-element.58), channel_id=1, source_target_pairs={{4,0},{8,4},{12,8},{16,12},{20,16},{24,20},{28,24},{5,1},{9,5},{13... | collective-permute-start | bytes 393224 | tf_op jit(solution)/shard_map/ppermute | solution.py:83
  110.3 1.6 %copy-start = (f32[1536,512]{1,0:T(8,128)}, f32[1536,512]{1,0:T(8,128)S(1)}, u32[]{:S(2)}) copy-start(f32[1536,512]{1,0:T(8,128)S(1)} %fusion.2) | copy-start | bytes 9437188
  111.9 1.5 slice-start
  118.4 6.4 %copy-start.1 = (f32[1536,512]{1,0:T(8,128)S(1)}, f32[1536,512]{1,0:T(8,128)}, u32[]{:S(2)}) copy-start(f32[1536,512]{1,0:T(8,128)} %copy-done) | copy-start | bytes 9437188
  118.5 10.9 %collective-permute-start.12 = (bf16[4,128,512]{2,1,0:T(8,128)(2,1)S(1)}, bf16[4,128,512]{2,1,0:T(8,128)(2,1)S(1)}, u32[]{:S(2)}, u32[]{:S(2)}) collective-permute-start(bf16[4,128,512]{2,1,0:T(8,128)(2,1)S(1)} %pad_maximum_fusion.9), channel_id=1, source_target_pairs={{0,4},{4,8},{8,12},{12,16},{16,20},{20,24},{24,28},{1,5},{5,9},{9,... | collective-permute-start | bytes 1572872 | tf_op jit(solution)/shard_map/ppermute | solution.py:102
  120.8 11.2 %collective-permute-start.13 = (bf16[4,128,512]{2,1,0:T(8,128)(2,1)S(1)}, bf16[4,128,512]{2,1,0:T(8,128)(2,1)S(1)}, u32[]{:S(2)}, u32[]{:S(2)}) collective-permute-start(bf16[4,128,512]{2,1,0:T(8,128)(2,1)S(1)} %pad_maximum_fusion.10), channel_id=1, source_target_pairs={{4,0},{8,4},{12,8},{16,12},{20,16},{24,20},{28,24},{5,1},{9,5},{13... | collective-permute-start | bytes 1572872 | tf_op jit(solution)/shard_map/ppermute | solution.py:103
  138.9 8.2 %collective-permute-start.14 = (f16[208,512]{1,0:T(8,128)(2,1)S(1)}, f16[208,512]{1,0:T(8,128)(2,1)S(1)}, u32[]{:S(2)}, u32[]{:S(2)}) collective-permute-start(f16[208,512]{1,0:T(8,128)(2,1)S(1)} %get-tuple-element.51), channel_id=1, source_target_pairs={{0,1},{1,0},{2,3},{3,2},{4,5},{5,4},{6,7},{7,6},{8,9},{9,8},{10,11... | collective-permute-start | bytes 638984 | tf_op jit(solution)/shard_map/ppermute | solution.py:50
  139.0 16.7 %collective-permute-start.15 = (f16[208,512]{1,0:T(8,128)(2,1)S(1)}, f16[208,512]{1,0:T(8,128)(2,1)S(1)}, u32[]{:S(2)}, u32[]{:S(2)}) collective-permute-start(f16[208,512]{1,0:T(8,128)(2,1)S(1)} %get-tuple-element.52), channel_id=1, source_target_pairs={{0,2},{1,3},{2,0},{3,1},{4,6},{5,7},{6,4},{7,5},{8,10},{9,11},{10,... | collective-permute-start | bytes 638984 | tf_op jit(solution)/shard_map/ppermute | solution.py:50
  140.9 20.0 %collective-permute-start.16 = (f16[208,512]{1,0:T(8,128)(2,1)S(1)}, f16[208,512]{1,0:T(8,128)(2,1)S(1)}, u32[]{:S(2)}, u32[]{:S(2)}) collective-permute-start(f16[208,512]{1,0:T(8,128)(2,1)S(1)} %get-tuple-element.53), channel_id=1, source_target_pairs={{0,3},{1,2},{2,1},{3,0},{4,7},{5,6},{6,5},{7,4},{8,11},{9,10},{10,... | collective-permute-start | bytes 638984 | tf_op jit(solution)/shard_map/ppermute | solution.py:50

commit v2 on v0

v2 whole, which is shorter than its diff:
```python
import functools

import jax
import jax.numpy as jnp
from jax import lax
from jax.experimental import pallas as pl
from jax.experimental.pallas import tpu as pltpu
from jax.sharding import PartitionSpec as P

STEPS = 2
CHUNKS = 1
TAIL = 16
TOP = 12.0
BF16 = jnp.bfloat16
F16 = jnp.float16
F32 = jnp.float32
VMEM = pl.BlockSpec(memory_space=pltpu.VMEM)
SMEM = pl.BlockSpec(memory_space=pltpu.SMEM)


def call(kernel, outs, ins, scratch=(), flops=0, moved=0):
    return pl.pallas_call(
        kernel,
        out_shape=[jax.ShapeDtypeStruct(s, d) for s, d in outs],
        in_specs=[SMEM if s else VMEM for s, _ in ins],
        out_specs=[VMEM] * len(outs),
        scratch_shapes=list(scratch),
        compiler_params=pltpu.CompilerParams(vmem_limit_bytes=30 * 2**20),
        cost_estimate=pl.CostEstimate(flops=flops, bytes_accessed=moved, transcendentals=0),
    )(*[a for _, a in ins])


def dot(a, b):
    return jnp.dot(a, b, preferred_element_type=F32)


def coded(block):
    top = jnp.max(jnp.abs(block), axis=0, keepdims=True)
    power = jnp.ceil(jnp.log2(jnp.maximum(top, 1e-30)))
    return block * jnp.exp2(TOP - power), jnp.broadcast_to(power, (TAIL, block.shape[1]))


def pick(flag, a, b):
    return jnp.where(flag == 0, a, b)


def order_kernel(order_ref, inv_ref, g_ref):
    rows, width = inv_ref.shape[0], inv_ref.shape[1] // 2
    ids = lax.broadcasted_iota(jnp.int32, (width, width), 1)
    place = (order_ref[...] == ids).astype(BF16)
    g_ref[:rows] = dot(inv_ref[:, :width], place).astype(BF16)
    g_ref[rows:] = dot(inv_ref[:, width:], place).astype(BF16)


def first_kernel(rim, scaled, shift_ref, weight_ref, ids_ref, g_ref, src_ref, one_ref, two_ref, sigma_ref,
                 base_ref, mid_ref, edge_ref, msg1_ref, msg2_ref, e_ref, xr_ref, xi_ref):
    rows, n = src_ref.shape
    parity = ids_ref[0, 0]
    e_ref[:rim] = pick(parity, two_ref[...], one_ref[...])
    e_ref[rim + rows:] = pick(parity, one_ref[...], two_ref[...])
    if scaled:
        e_ref[rim:rim + rows] = (src_ref[...] * sigma_ref[...]).astype(BF16)
    else:
        e_ref[rim:rim + rows] = src_ref[...]
    for ref, lo in ((xr_ref, 0), (xi_ref, rows)):
        ref[:8] = jnp.zeros((8, n), F32)
        ref[8 + rows:] = jnp.zeros((8, n), F32)
        ref[8:8 + rows] = dot(g_ref[lo:lo + rows], e_ref[...])
    a, b = shift_ref[0, 0], shift_ref[0, 1]
    wr, wi = 2.0 * weight_ref[0, 0], 2.0 * weight_ref[0, 1]
    step = 32

    def local(ref, lo):
        mid = 4.0 * ref[8 + lo:8 + lo + step] - ref[7 + lo:7 + lo + step] - ref[9 + lo:9 + lo + step]
        if lo >= rim:
            mid = mid - ref[8 + lo - rim:8 + lo - rim + step]
        if lo + rim < rows:
            mid = mid - ref[8 + lo + rim:8 + lo + rim + step]
        return mid

    for lo in range(0, rows, step):
        at = slice(lo, lo + step)
        xr, xi = xr_ref[8 + lo:8 + lo + step], xi_ref[8 + lo:8 + lo + step]
        sigma = sigma_ref[at]
        source = src_ref[at] * sigma if scaled else src_ref[at].astype(F32)
        rr = source - local(xr_ref, lo) - sigma * (a * xr - b * xi)
        ri = -local(xi_ref, lo) - sigma * (b * xr + a * xi)
        base_ref[at] = wr * xr - wi * xi
        if lo < rim or lo >= rows - rim:
            side, row = (0, lo) if lo < rim else (1, lo - rows + rim)
            for k, v in enumerate((xr, xi, rr, ri)):
                edge_ref[side, k * rim + row:k * rim + row + step] = v
        else:
            mid_ref[0, lo - rim:lo - rim + step] = rr.astype(BF16)
            mid_ref[1, lo - rim:lo - rim + step] = ri.astype(BF16)
    low, low_tail = coded(edge_ref[0])
    high, high_tail = coded(edge_ref[1])
    msg1_ref[:4 * rim] = pick(parity, high, low)
    msg2_ref[:4 * rim] = pick(parity, low, high)
    msg1_ref[4 * rim:] = pick(parity, high_tail, low_tail)
    msg2_ref[4 * rim:] = pick(parity, low_tail, high_tail)


def product(g_ref, rows, cols, er, ei, wr, wi):
    gr, gi = g_ref[:rows, cols], g_ref[rows:, cols]
    return wr * (dot(gr, er) - dot(gi, ei)) - wi * (dot(gr, ei) + dot(gi, er))


def middle_kernel(rim, weight_ref, g_ref, base_ref, mid_ref, out_ref):
    rows = base_ref.shape[0]
    wr, wi = 2.0 * weight_ref[0, 0], 2.0 * weight_ref[0, 1]
    out_ref[...] = base_ref[...] + product(g_ref, rows, slice(2 * rim, rows), mid_ref[0], mid_ref[1], wr, wi)


def last_kernel(rim, hops, weight_ref, ids_ref, g_ref, part_ref, edge_ref, one_ref, two_ref, *rest):
    own_ref, msgs, u_ref, e_ref = rest[0], rest[1:1 + hops], rest[1 + hops], rest[2 + hops]
    rows, n = part_ref.shape
    share = own_ref.shape[0]
    parity, first, final = ids_ref[0, 0], ids_ref[0, 1], ids_ref[0, 2]
    wr, wi = 2.0 * weight_ref[0, 0], 2.0 * weight_ref[0, 1]
    before = pick(parity, two_ref[...], one_ref[...])
    after = pick(parity, one_ref[...], two_ref[...])
    before = before[:4 * rim] * jnp.exp2(before[4 * rim:4 * rim + 1] - TOP)
    after = after[:4 * rim] * jnp.exp2(after[4 * rim:4 * rim + 1] - TOP)
    at = lax.broadcasted_iota(jnp.int32, (rim, 1), 0)
    for half in range(2):
        x, r = slice(half * rim, (half + 1) * rim), slice((2 + half) * rim, (3 + half) * rim)
        xb, qb, xa, qa = before[x], before[r], after[x], after[r]
        low, high = edge_ref[0, x], edge_ref[1, x]
        above = qb + low + jnp.where(at == rim - 1, low[:1], 0.0)
        below = qa + high + jnp.where(at == 0, high[rim - 1:], 0.0)
        head = edge_ref[0, r] + xb + jnp.where(at == 0, xb[rim - 1:], 0.0)
        foot = edge_ref[1, r] + xa + jnp.where(at == rim - 1, xa[:1], 0.0)
        e_ref[half, :rim] = jnp.where(first == 1, 0.0, above).astype(BF16)
        e_ref[half, rim:2 * rim] = head.astype(BF16)
        e_ref[half, 2 * rim:3 * rim] = foot.astype(BF16)
        e_ref[half, 3 * rim:] = jnp.where(final == 1, 0.0, below).astype(BF16)
    u_ref[...] = part_ref[...] + product(
        g_ref, rows, slice(0, 2 * rim), e_ref[0, :2 * rim], e_ref[1, :2 * rim], wr, wi
    ) + product(
        g_ref, rows, slice(rows, rows + 2 * rim), e_ref[0, 2 * rim:], e_ref[1, 2 * rim:], wr, wi
    )
    own_ref[...] = u_ref[pl.ds(pl.multiple_of(ids_ref[0, 3] * share, share), share)]
    for hop, ref in enumerate(msgs):
        block = u_ref[pl.ds(pl.multiple_of(ids_ref[0, 4 + hop] * share, share), share)]
        ref[:share], ref[share:] = coded(block)


def join_kernel(rim, ids_ref, own_ref, *rest):
    got, (src_ref, msg1_ref, msg2_ref) = rest[:-3], rest[-3:]
    share = own_ref.shape[0]
    rows = src_ref.shape[0]
    parity = ids_ref[0, 0]
    for k, ref in enumerate((own_ref,) + tuple(got)):
        src_ref[pl.ds(pl.multiple_of(ids_ref[0, 3 + k] * share, share), share)] = ref[...]
    low, high = src_ref[:rim], src_ref[rows - rim:]
    msg1_ref[...] = pick(parity, high, low)
    msg2_ref[...] = pick(parity, low, high)


def shards(state, conductivity, pole_shift, pole_weight, order_list, inverse):
    rows, columns = state.shape
    order = order_list.shape[1]
    rim = (order - rows) // 2
    subs, poles = lax.axis_size("sub"), lax.axis_size("pole")
    sub, pole = lax.axis_index("sub"), lax.axis_index("pole")
    share, hops = rows // poles, poles - 1
    n = columns // CHUNKS
    pairs1 = [(i ^ 1, i) for i in range(subs) if i ^ 1 < subs]
    pairs2 = [(j, i) for i in range(subs) for j in [((i + 1) ^ 1) - 1] if 0 <= j < subs]
    if poles & hops == 0:
        target = [pole ^ k for k in range(1, poles)]
        source_of = target
        hop_pairs = [[(i, i ^ k) for i in range(poles)] for k in range(1, poles)]
    else:
        target = [lax.rem(pole + k, poles) for k in range(1, poles)]
        source_of = [lax.rem(pole + poles - k, poles) for k in range(1, poles)]
        hop_pairs = [[(i, (i + k) % poles) for i in range(poles)] for k in range(1, poles)]
    flags = [sub % 2, (sub == 0).astype(jnp.int32), (sub == subs - 1).astype(jnp.int32), pole]
    to_ids = jnp.stack([f.astype(jnp.int32) for f in flags + target])[None]
    from_ids = to_ids if source_of is target else jnp.stack([f.astype(jnp.int32) for f in flags + source_of])[None]
    parity = sub % 2
    sigma = conductivity[:, None]
    sigma_share = lax.dynamic_slice_in_dim(conductivity, pole * share, share, 0)[:, None]

    (g,) = call(
        order_kernel, [((2 * rows, order), BF16)], [(0, order_list.reshape(order, 1)), (0, inverse[0])],
        flops=4 * rows * order * order, moved=6 * rows * order,
    )

    def exchange(one, two):
        return lax.ppermute(one, "sub", pairs1), lax.ppermute(two, "sub", pairs2)

    def sweep(source, got, scaled):
        base, mid, edge, msg1, msg2 = call(
            functools.partial(first_kernel, rim, scaled),
            [((rows, n), F32), ((2, rows - 2 * rim, n), BF16), ((2, 4 * rim, n), F32),
             ((4 * rim + TAIL, n), F32), ((4 * rim + TAIL, n), F32)],
            [(1, pole_shift), (1, pole_weight), (1, to_ids), (0, g), (0, source), (0, got[0]), (0, got[1]), (0, sigma)],
            [pltpu.VMEM((order, n), BF16), pltpu.VMEM((rows + 16, n), F32), pltpu.VMEM((rows + 16, n), F32)],
            flops=4 * rows * order * n, moved=4 * rows * order,
        )
        got = exchange(msg1.astype(F16), msg2.astype(F16))
        (part,) = call(
            functools.partial(middle_kernel, rim), [((rows, n), F32)],
            [(1, pole_weight), (0, g), (0, base), (0, mid)],
            flops=8 * rows * (rows - 2 * rim) * n, moved=4 * rows * order,
        )
        return call(
            functools.partial(last_kernel, rim, hops), [((share, n), F32)] + [((share + TAIL, n), F32)] * hops,
            [(1, pole_weight), (1, to_ids), (0, g), (0, part), (0, edge), (0, got[0].astype(F32)), (0, got[1].astype(F32))],
            [pltpu.VMEM((rows, n), F32), pltpu.VMEM((2, 4 * rim, n), BF16)],
            flops=8 * rows * 4 * rim * n, moved=4 * rows * order,
        )

    def reduced(own, *sent):
        for block, pairs in zip(sent, hop_pairs):
            got = lax.ppermute(block.astype(F16), "pole", pairs).astype(F32)
            own = own + got[:share] * jnp.exp2(got[share:share + 1] - TOP)
        return own

    def gathered(own):
        got = [lax.ppermute(own, "pole", pairs) for pairs in hop_pairs]
        return call(
            functools.partial(join_kernel, rim), [((rows, n), BF16), ((rim, n), BF16), ((rim, n), BF16)],
            [(1, from_ids), (0, own)] + [(0, x) for x in got], moved=4 * rows * n,
        )

    results = []
    for chunk in range(CHUNKS):
        source = state[:, chunk * n:(chunk + 1) * n]
        low = (sigma[:rim] * source[:rim]).astype(BF16)
        high = (sigma[rows - rim:] * source[rows - rim:]).astype(BF16)
        one, two = pick(parity, high, low), pick(parity, low, high)
        for step in range(STEPS):
            total = reduced(*sweep(source, exchange(one, two), step == 0))
            if step + 1 < STEPS:
                source, one, two = gathered((sigma_share * total).astype(BF16))
        results.append(total)
    return jnp.concatenate(results, axis=1) if CHUNKS > 1 else results[0]


def solution(mesh):
    placed = (
        P("sub", None),
        P("sub"),
        P("pole", None),
        P("pole", None),
        P("sub", None),
        P("pole", "sub", None),
    )
    return jax.shard_map(
        shards, mesh=mesh, in_specs=placed, out_specs=P(("sub", "pole"), None), check_vma=False
    )
```

time: 282 us -> 142 us (0.50)
  waiting for transfers between devices: 141 us -> 76.7 us
  local copies, waits for them, and re-layouts: 39.1 us -> 8.66 us
  other arithmetic: 38.1 us -> 8.04 us
  Pallas kernels: 0 us -> 24.9 us
  matrix products: 13.8 us -> 0 us
  between operations: 13.6 us -> 0.42 us
  starting transfers between devices: 32.7 us -> 22.2 us
    reduce_scatter x2 -> x0, waiting for transfers between devices: 79 us -> none  [shards(): lax.psum_scatter(partial_value, 'pole', scatter_dimension=0, tiled=True)]
    ppermute x12 -> x17, waiting for transfers between devices: 25.8 us -> 76.7 us  [the longest x6 35.7 us: reduced(): got = lax.ppermute(block.astype(F16), 'pole', pairs).astype(F32)]
    all_gather x1 -> x0, waiting for transfers between devices: 36 us -> none  [shards(): lax.all_gather(sigma_share[:, None] * result, 'pole', axis=0, tiled=True)]
    gather x4 -> x0, local copies, waits for them, and re-layouts: 31.5 us -> none  [correct(): permuted = jnp.take(residual_ext, ordering, axis=0)]
    pallas_call x0 -> x8, Pallas kernels: none -> 24.9 us  [call(): pl.pallas_call(kernel, out_shape=[jax.ShapeDtypeStruct(s, d) for s, d in...]
    dot_general x4 -> x0, matrix products: 13.8 us -> none  [correct(): return jnp.dot(inverse_block, stacked, preferred_element_type=jnp.float32)]
    mul x6 -> x0, other arithmetic: 12.4 us -> none  [the longest x2 5.55 us: shards(): 2.0 * (weight_re * iterate[:, :column_half] - weight_im * iterate[:, colu...]
    ppermute x12 -> x17, starting transfers between devices: 32.6 us -> 22.2 us  [the longest x8 11.4 us: exchange(): return (lax.ppermute(one, 'sub', pairs1), lax.ppermute(two, 'sub', pairs2))]
  transfers between devices with their start and end apart: 15 -> 17, of which waited for: 13 -> 12; matrix products, arithmetic and copies ran while one was open for 2% -> 4% of each run, Pallas kernels for 0% -> 6%
where the time goes in v2:
time: 142 us; the launch traced here: 141 us
  waiting for transfers between devices  76.7 us (54%)
  Pallas kernels  24.9 us (18%)
  starting transfers between devices  22.2 us (16%)
  local copies, waits for them, and re-layouts  8.66 us (6%)
  other arithmetic  8.04 us (6%)
    ppermute x6, waiting for transfers between devices, reduced(): got = lax.ppermute(block.astype(F16), 'pole', pairs).astype(F32)  35.7 us
    pallas_call x8, Pallas kernels, call(): pl.pallas_call(kernel, out_shape=[jax.ShapeDtypeStruct(s, d) for s, d in...  24.9 us
    ppermute x8, waiting for transfers between devices, exchange(): return (lax.ppermute(one, 'sub', pairs1), lax.ppermute(two, 'sub', pairs2))  22.9 us
    ppermute x3, waiting for transfers between devices, gathered(): got = [lax.ppermute(own, 'pole', pairs) for pairs in hop_pairs]  18 us
    ppermute x8, starting transfers between devices, exchange(): return (lax.ppermute(one, 'sub', pairs1), lax.ppermute(two, 'sub', pairs2))  11.4 us
    ppermute x6, starting transfers between devices, reduced(): got = lax.ppermute(block.astype(F16), 'pole', pairs).astype(F32)  7.29 us
    unnamed x20, local copies, waits for them, and re-layouts  5.88 us
    convert_element_type x12, other arithmetic, reduced(): got = lax.ppermute(block.astype(F16), 'pole', pairs).astype(F32)  4.18 us
  transfers between devices with their start and end apart: 17, of which 12 were waited for; matrix products, arithmetic and copies ran while one was open for 4% of the time, Pallas kernels for 6%

profile of v2, /device:TPU:18, one launch (start us, length us, event | category | flops | bytes accessed | tf_op | source)
XLA Modules:
  0.0 140.9 jit_solution(13497104363332157232)
XLA Ops:
  0.0 0.8 fusion.20
  0.8 1.8 %broadcast_select_fusion = (bf16[128,512]{1,0:T(8,128)(2,1)}, bf16[128,512]{1,0:T(8,128)(2,1)}) fusion(pred[]{:T(512)S(6)} %eq.15, f32[768,512]{1,0:T(8,128)} %src_ref.1, f32[128]{0:T(128)S(1)} %get-tuple-element.50, f32[128]{0:T(128)S(1)} %get-tuple-element.49), kind=kLoop, calls=%fused_computation.16 | loop fusion | flops 393216 | bytes 787457 | tf_op jit(solution)/shard_map/jit(_where)/select_n | solution.py:44
  2.6 2.5 %collective-permute-start.1 = (bf16[128,512]{1,0:T(8,128)(2,1)}, bf16[128,512]{1,0:T(8,128)(2,1)}, u32[]{:S(2)}, u32[]{:S(2)}) collective-permute-start(bf16[128,512]{1,0:T(8,128)(2,1)} %get-tuple-element.47), channel_id=1, source_target_pairs={{8,4},{4,8},{16,12},{12,16},{24,20},{20,24},{9,5},{5,9},{17,13},{1... | collective-permute-start | bytes 393224 | tf_op jit(solution)/shard_map/ppermute | solution.py:192
  5.2 1.7 %copy.7.order_ref = s32[1024,1]{1,0:T(8,128)} copy(s32[1024,1]{0,1:T(1,128)} %bitcast.28) | data formatting | bytes 8192 | tf_op jit(solution)/shard_map/reshape | solution.py:187
  6.9 1.0 copy-done
  7.9 1.9 %copy-done.7 = bf16[1,768,2048]{2,1,0:T(8,128)(2,1)S(1)} copy-done((bf16[1,768,2048]{2,1,0:T(8,128)(2,1)S(1)}, bf16[1,768,2048]{2,1,0:T(8,128)(2,1)}, u32[]{:S(2)}) %copy-start.7) | copy-done | bytes 3145752
  9.8 3.7 %shard_map.64.g_ref = bf16[1536,1024]{1,0:T(8,128)(2,1)S(1)} custom-call(s32[1024,1]{1,0:T(8,128)S(1)} %copy-done, bf16[768,2048]{1,0:T(8,128)(2,1)S(1)} %bitcast.21), custom_call_target="tpu_custom_call" | custom-call | flops 3221225472 | bytes 4718592 | tf_op jit(solution)/shard_map/pallas_call | solution.py:22
  13.6 0.2 broadcast_in_dim.9.sigma_ref
  13.7 0.1 stack.39
  13.8 0.0 collective-permute-done.one_ref
  13.8 0.0 copy-start.5
  13.9 1.4 copy-done.5
  15.3 5.2 %shard_map.65 = (f32[768,512]{1,0:T(8,128)S(1)}, bf16[2,512,512]{2,1,0:T(8,128)(2,1)S(1)}, f32[2,512,512]{2,1,0:T(8,128)S(1)}, f32[528,512]{1,0:T(8,128)S(1)}, f32[528,512]{1,0:T(8,128)S(1)}) custom-call(f32[1,2]{1,0:T(1,128)S(1)} %copy-done.8, f32[1,2]{1,0:T(1,128)S(1)} %copy-done.6, s32[1,7]{1,0:T(1,128)S(1)} %bitcast.16, ...), custom_call_target="tpu_custom_call" | custom-call | flops 1610612736 | bytes 3145728 | tf_op jit(solution)/shard_map/pallas_call | solution.py:22
  20.5 0.1 convert_element_type.73
  20.6 1.0 collective-permute-start.2
  21.6 0.1 convert_element_type.75
  21.7 2.3 %collective-permute-start.3 = (f16[528,512]{1,0:T(8,128)(2,1)S(1)}, f16[528,512]{1,0:T(8,128)(2,1)S(1)}, u32[]{:S(2)}, u32[]{:S(2)}) collective-permute-start(f16[528,512]{1,0:T(8,128)(2,1)S(1)} %convert_element_type.75), channel_id=1, source_target_pairs={{8,4},{4,8},{16,12},{12,16},{24,20},{20,24},{9,5},{5,9},{17,13},{1... | collective-permute-start | bytes 1622024 | tf_op jit(solution)/shard_map/ppermute | solution.py:192
  23.9 2.4 %shard_map.66.part_ref = f32[768,512]{1,0:T(8,128)S(1)} custom-call(f32[1,2]{1,0:T(1,128)S(1)} %copy-done.6, bf16[1536,1024]{1,0:T(8,128)(2,1)S(1)} %shard_map.64.g_ref, f32[768,512]{1,0:T(8,128)S(1)} %get-tuple-element.26.base_ref, bf16[2,512,512]{2,1,0:T(8,128)(2,1)S(1)} %get-tuple-element.27.mid_ref), custom_call_target="tpu_custom_call" | custom-call | flops 1610612736 | bytes 3145728 | tf_op jit(solution)/shard_map/pallas_call | solution.py:22
  26.4 0.1 convert_element_type.74.one_ref
  26.5 9.2 %collective-permute-done.3 = f16[528,512]{1,0:T(8,128)(2,1)S(1)} collective-permute-done((f16[528,512]{1,0:T(8,128)(2,1)S(1)}, f16[528,512]{1,0:T(8,128)(2,1)S(1)}, u32[]{:S(2)}, u32[]{:S(2)}) %collective-permute-start.3) | collective-permute-done | bytes 540704 | tf_op jit(solution)/shard_map/ppermute | solution.py:192
  35.7 0.1 convert_element_type.76.two_ref
  35.8 3.0 %shard_map.67 = (f32[192,512]{1,0:T(8,128)S(1)}, f32[208,512]{1,0:T(8,128)S(1)}, f32[208,512]{1,0:T(8,128)S(1)}, f32[208,512]{1,0:T(8,128)S(1)}) custom-call(f32[1,2]{1,0:T(1,128)S(1)} %copy-done.6, s32[1,7]{1,0:T(1,128)S(1)} %bitcast.17, bf16[1536,1024]{1,0:T(8,128)(2,1)S(1)} %shard_map.64.g_ref, f32[768,512]{1,0:T(8,128)S(1)} %shard_map.66.part_ref, ...), custom_call_target="tpu_custom_call" | custom-call | flops 1610612736 | bytes 3145728 | tf_op jit(solution)/shard_map/pallas_call | solution.py:22
  38.8 0.8 copy-done.1
  39.6 0.8 copy-done.2
  40.4 0.8 convert_element_type.77
  41.1 0.0 copy-done.3
  41.2 1.5 %collective-permute-start.4 = (f16[208,512]{1,0:T(8,128)(2,1)}, f16[208,512]{1,0:T(8,128)(2,1)}, u32[]{:S(2)}, u32[]{:S(2)}) collective-permute-start(f16[208,512]{1,0:T(8,128)(2,1)} %convert_element_type.77), channel_id=1, source_target_pairs={{0,1},{1,0},{2,3},{3,2},{4,5},{5,4},{6,7},{7,6},{8,9},{9,8},{10,11... | collective-permute-start | bytes 638984 | tf_op jit(solution)/shard_map/ppermute | solution.py:218
  42.7 0.1 dynamic_slice.3
  42.8 1.1 convert_element_type.79
  43.9 0.4 collective-permute-start.5
  44.3 1.0 convert_element_type.81
  45.3 1.7 %collective-permute-start.6 = (f16[208,512]{1,0:T(8,128)(2,1)S(1)}, f16[208,512]{1,0:T(8,128)(2,1)S(1)}, u32[]{:S(2)}, u32[]{:S(2)}) collective-permute-start(f16[208,512]{1,0:T(8,128)(2,1)S(1)} %convert_element_type.81), channel_id=1, source_target_pairs={{0,3},{1,2},{2,1},{3,0},{4,7},{5,6},{6,5},{7,4},{8,11},{9,10},{10,... | collective-permute-start | bytes 638984 | tf_op jit(solution)/shard_map/ppermute | solution.py:218
  47.0 1.4 %collective-permute-done.4 = f16[208,512]{1,0:T(8,128)(2,1)} collective-permute-done((f16[208,512]{1,0:T(8,128)(2,1)}, f16[208,512]{1,0:T(8,128)(2,1)}, u32[]{:S(2)}, u32[]{:S(2)}) %collective-permute-start.4) | collective-permute-done | bytes 213024 | tf_op jit(solution)/shard_map/ppermute | solution.py:218
  48.4 1.0 convert_element_type.78
  49.4 8.5 %collective-permute-done.5 = f16[208,512]{1,0:T(8,128)(2,1)S(1)} collective-permute-done((f16[208,512]{1,0:T(8,128)(2,1)S(1)}, f16[208,512]{1,0:T(8,128)(2,1)S(1)}, u32[]{:S(2)}, u32[]{:S(2)}) %collective-permute-start.5) | collective-permute-done | bytes 213024 | tf_op jit(solution)/shard_map/ppermute | solution.py:218
  58.0 6.6 %collective-permute-done.6 = f16[208,512]{1,0:T(8,128)(2,1)S(1)} collective-permute-done((f16[208,512]{1,0:T(8,128)(2,1)S(1)}, f16[208,512]{1,0:T(8,128)(2,1)S(1)}, u32[]{:S(2)}, u32[]{:S(2)}) %collective-permute-start.6) | collective-permute-done | bytes 213024 | tf_op jit(solution)/shard_map/ppermute | solution.py:218
  64.7 0.1 fusion.5.own_ref
  64.9 0.1 collective-permute-start.7
  64.9 1.9 %collective-permute-start.8 = (bf16[192,512]{1,0:T(8,128)(2,1)S(1)}, bf16[192,512]{1,0:T(8,128)(2,1)S(1)}, u32[]{:S(2)}, u32[]{:S(2)}) collective-permute-start(bf16[192,512]{1,0:T(8,128)(2,1)S(1)} %fusion.5.own_ref), channel_id=1, source_target_pairs={{0,2},{1,3},{2,0},{3,1},{4,6},{5,7},{6,4},{7,5},{8,10},{9,11},{10,... | collective-permute-start | bytes 589832 | tf_op jit(solution)/shard_map/ppermute | solution.py:223
  66.9 1.6 %collective-permute-start.9 = (bf16[192,512]{1,0:T(8,128)(2,1)S(1)}, bf16[192,512]{1,0:T(8,128)(2,1)S(1)}, u32[]{:S(2)}, u32[]{:S(2)}) collective-permute-start(bf16[192,512]{1,0:T(8,128)(2,1)S(1)} %fusion.5.own_ref), channel_id=1, source_target_pairs={{0,3},{1,2},{2,1},{3,0},{4,7},{5,6},{6,5},{7,4},{8,11},{9,10},{10,... | collective-permute-start | bytes 589832 | tf_op jit(solution)/shard_map/ppermute | solution.py:223
  68.4 4.6 %collective-permute-done.7.rest_0_ = bf16[192,512]{1,0:T(8,128)(2,1)S(1)} collective-permute-done((bf16[192,512]{1,0:T(8,128)(2,1)S(1)}, bf16[192,512]{1,0:T(8,128)(2,1)S(1)}, u32[]{:S(2)}, u32[]{:S(2)}) %collective-permute-start.7) | collective-permute-done | bytes 196640 | tf_op jit(solution)/shard_map/ppermute | solution.py:223
  73.0 7.4 %collective-permute-done.8.rest_1_ = bf16[192,512]{1,0:T(8,128)(2,1)S(1)} collective-permute-done((bf16[192,512]{1,0:T(8,128)(2,1)S(1)}, bf16[192,512]{1,0:T(8,128)(2,1)S(1)}, u32[]{:S(2)}, u32[]{:S(2)}) %collective-permute-start.8) | collective-permute-done | bytes 196640 | tf_op jit(solution)/shard_map/ppermute | solution.py:223
  80.5 6.0 %collective-permute-done.9.rest_2_ = bf16[192,512]{1,0:T(8,128)(2,1)S(1)} collective-permute-done((bf16[192,512]{1,0:T(8,128)(2,1)S(1)}, bf16[192,512]{1,0:T(8,128)(2,1)S(1)}, u32[]{:S(2)}, u32[]{:S(2)}) %collective-permute-start.9) | collective-permute-done | bytes 196640 | tf_op jit(solution)/shard_map/ppermute | solution.py:223
  86.5 0.6 shard_map.68
  87.1 0.1 collective-permute-start.10
  87.2 1.9 %collective-permute-start.11 = (bf16[128,512]{1,0:T(8,128)(2,1)S(1)}, bf16[128,512]{1,0:T(8,128)(2,1)S(1)}, u32[]{:S(2)}, u32[]{:S(2)}) collective-permute-start(bf16[128,512]{1,0:T(8,128)(2,1)S(1)} %get-tuple-element.37), channel_id=1, source_target_pairs={{8,4},{4,8},{16,12},{12,16},{24,20},{20,24},{9,5},{5,9},{17,13},{1... | collective-permute-start | bytes 393224 | tf_op jit(solution)/shard_map/ppermute | solution.py:192
  89.1 4.3 %collective-permute-done.11.two_ref = bf16[128,512]{1,0:T(8,128)(2,1)S(1)} collective-permute-done((bf16[128,512]{1,0:T(8,128)(2,1)S(1)}, bf16[128,512]{1,0:T(8,128)(2,1)S(1)}, u32[]{:S(2)}, u32[]{:S(2)}) %collective-permute-start.11) | collective-permute-done | bytes 131104 | tf_op jit(solution)/shard_map/ppermute | solution.py:192
  93.5 4.5 %shard_map.69 = (f32[768,512]{1,0:T(8,128)S(1)}, bf16[2,512,512]{2,1,0:T(8,128)(2,1)S(1)}, f32[2,512,512]{2,1,0:T(8,128)S(1)}, f32[528,512]{1,0:T(8,128)S(1)}, f32[528,512]{1,0:T(8,128)S(1)}) custom-call(f32[1,2]{1,0:T(1,128)S(1)} %copy-done.8, f32[1,2]{1,0:T(1,128)S(1)} %copy-done.6, s32[1,7]{1,0:T(1,128)S(1)} %bitcast.19, ...), custom_call_target="tpu_custom_call" | custom-call | flops 1610612736 | bytes 3145728 | tf_op jit(solution)/shard_map/pallas_call | solution.py:22
  98.0 0.1 convert_element_type.84
  98.1 1.5 %collective-permute-start.12 = (f16[528,512]{1,0:T(8,128)(2,1)S(1)}, f16[528,512]{1,0:T(8,128)(2,1)S(1)}, u32[]{:S(2)}, u32[]{:S(2)}) collective-permute-start(f16[528,512]{1,0:T(8,128)(2,1)S(1)} %convert_element_type.84), channel_id=1, source_target_pairs={{4,0},{0,4},{12,8},{8,12},{20,16},{16,20},{28,24},{24,28},{5,1},{1... | collective-permute-start | bytes 1622024 | tf_op jit(solution)/shard_map/ppermute | solution.py:192
  99.6 0.1 convert_element_type.86
  99.7 2.1 %collective-permute-start.13 = (f16[528,512]{1,0:T(8,128)(2,1)S(1)}, f16[528,512]{1,0:T(8,128)(2,1)S(1)}, u32[]{:S(2)}, u32[]{:S(2)}) collective-permute-start(f16[528,512]{1,0:T(8,128)(2,1)S(1)} %convert_element_type.86), channel_id=1, source_target_pairs={{8,4},{4,8},{16,12},{12,16},{24,20},{20,24},{9,5},{5,9},{17,13},{1... | collective-permute-start | bytes 1622024 | tf_op jit(solution)/shard_map/ppermute | solution.py:192
  101.8 2.4 %shard_map.70.part_ref = f32[768,512]{1,0:T(8,128)S(1)} custom-call(f32[1,2]{1,0:T(1,128)S(1)} %copy-done.6, bf16[1536,1024]{1,0:T(8,128)(2,1)S(1)} %shard_map.64.g_ref, f32[768,512]{1,0:T(8,128)S(1)} %get-tuple-element.38.base_ref, bf16[2,512,512]{2,1,0:T(8,128)(2,1)S(1)} %get-tuple-element.39.mid_ref), custom_call_target="tpu_custom_call" | custom-call | flops 1610612736 | bytes 3145728 | tf_op jit(solution)/shard_map/pallas_call | solution.py:22
  104.2 0.1 convert_element_type.85.one_ref
  104.4 9.4 %collective-permute-done.13 = f16[528,512]{1,0:T(8,128)(2,1)S(1)} collective-permute-done((f16[528,512]{1,0:T(8,128)(2,1)S(1)}, f16[528,512]{1,0:T(8,128)(2,1)S(1)}, u32[]{:S(2)}, u32[]{:S(2)}) %collective-permute-start.13) | collective-permute-done | bytes 540704 | tf_op jit(solution)/shard_map/ppermute | solution.py:192
  113.7 0.1 convert_element_type.87.two_ref
  113.8 3.0 %shard_map.71 = (f32[192,512]{1,0:T(8,128)S(1)}, f32[208,512]{1,0:T(8,128)S(1)}, f32[208,512]{1,0:T(8,128)S(1)}, f32[208,512]{1,0:T(8,128)S(1)}) custom-call(f32[1,2]{1,0:T(1,128)S(1)} %copy-done.6, s32[1,7]{1,0:T(1,128)S(1)} %bitcast.20, bf16[1536,1024]{1,0:T(8,128)(2,1)S(1)} %shard_map.64.g_ref, f32[768,512]{1,0:T(8,128)S(1)} %shard_map.70.part_ref, ...), custom_call_target="tpu_custom_call" | custom-call | flops 1610612736 | bytes 3145728 | tf_op jit(solution)/shard_map/pallas_call | solution.py:22
  116.9 0.1 collective-permute-start.14
  117.0 2.0 %collective-permute-start.15 = (f16[208,512]{1,0:T(8,128)(2,1)S(1)}, f16[208,512]{1,0:T(8,128)(2,1)S(1)}, u32[]{:S(2)}, u32[]{:S(2)}) collective-permute-start(f16[208,512]{1,0:T(8,128)(2,1)S(1)} %convert_element_type.90), channel_id=1, source_target_pairs={{0,2},{1,3},{2,0},{3,1},{4,6},{5,7},{6,4},{7,5},{8,10},{9,11},{10,... | collective-permute-start | bytes 638984 | tf_op jit(solution)/shard_map/ppermute | solution.py:218
  119.1 1.6 %collective-permute-start.16 = (f16[208,512]{1,0:T(8,128)(2,1)S(1)}, f16[208,512]{1,0:T(8,128)(2,1)S(1)}, u32[]{:S(2)}, u32[]{:S(2)}) collective-permute-start(f16[208,512]{1,0:T(8,128)(2,1)S(1)} %convert_element_type.92), channel_id=1, source_target_pairs={{0,3},{1,2},{2,1},{3,0},{4,7},{5,6},{6,5},{7,4},{8,11},{9,10},{10,... | collective-permute-start | bytes 638984 | tf_op jit(solution)/shard_map/ppermute | solution.py:218
  120.7 3.7 %collective-permute-done.14 = f16[208,512]{1,0:T(8,128)(2,1)S(1)} collective-permute-done((f16[208,512]{1,0:T(8,128)(2,1)S(1)}, f16[208,512]{1,0:T(8,128)(2,1)S(1)}, u32[]{:S(2)}, u32[]{:S(2)}) %collective-permute-start.14) | collective-permute-done | bytes 213024 | tf_op jit(solution)/shard_map/ppermute | solution.py:218
  124.4 4.5 %collective-permute-done.15 = f16[208,512]{1,0:T(8,128)(2,1)S(1)} collective-permute-done((f16[208,512]{1,0:T(8,128)(2,1)S(1)}, f16[208,512]{1,0:T(8,128)(2,1)S(1)}, u32[]{:S(2)}, u32[]{:S(2)}) %collective-permute-start.15) | collective-permute-done | bytes 213024 | tf_op jit(solution)/shard_map/ppermute | solution.py:218
  129.0 10.9 %collective-permute-done.16 = f16[208,512]{1,0:T(8,128)(2,1)S(1)} collective-permute-done((f16[208,512]{1,0:T(8,128)(2,1)S(1)}, f16[208,512]{1,0:T(8,128)(2,1)S(1)}, u32[]{:S(2)}, u32[]{:S(2)}) %collective-permute-start.16) | collective-permute-done | bytes 213024 | tf_op jit(solution)/shard_map/ppermute | solution.py:218
  140.0 0.9 fusion
  (32 shorter events, 0.4 us)
Async XLA Ops:
  2.6 11.2 %collective-permute-start = (bf16[128,512]{1,0:T(8,128)(2,1)}, bf16[128,512]{1,0:T(8,128)(2,1)}, u32[]{:S(2)}, u32[]{:S(2)}) collective-permute-start(bf16[128,512]{1,0:T(8,128)(2,1)} %get-tuple-element.48), channel_id=1, source_target_pairs={{4,0},{0,4},{12,8},{8,12},{20,16},{16,20},{28,24},{24,28},{5,1},{1... | collective-permute-start | bytes 393224 | tf_op jit(solution)/shard_map/ppermute | solution.py:192
  2.6 11.2 %collective-permute-start.1 = (bf16[128,512]{1,0:T(8,128)(2,1)}, bf16[128,512]{1,0:T(8,128)(2,1)}, u32[]{:S(2)}, u32[]{:S(2)}) collective-permute-start(bf16[128,512]{1,0:T(8,128)(2,1)} %get-tuple-element.47), channel_id=1, source_target_pairs={{8,4},{4,8},{16,12},{12,16},{24,20},{20,24},{9,5},{5,9},{17,13},{1... | collective-permute-start | bytes 393224 | tf_op jit(solution)/shard_map/ppermute | solution.py:192
  6.9 1.0 copy-start
  7.9 1.9 %copy-start.7 = (bf16[1,768,2048]{2,1,0:T(8,128)(2,1)S(1)}, bf16[1,768,2048]{2,1,0:T(8,128)(2,1)}, u32[]{:S(2)}) copy-start(bf16[1,768,2048]{2,1,0:T(8,128)(2,1)} %param.11) | copy-start | bytes 9437188
  9.8 3.8 %copy-start.9 = (f32[768]{0:T(1024)S(1)}, f32[768]{0:T(1024)}, u32[]{:S(2)}) copy-start(f32[768]{0:T(1024)} %param.7) | copy-start | bytes 9220
  9.8 4.0 %copy-start.6 = (f32[1,2]{1,0:T(1,128)S(1)}, f32[1,2]{1,0:T(1,128)}, u32[]{:S(2)}) copy-start(f32[1,2]{1,0:T(1,128)} %weight_ref.11) | copy-start | bytes 28
  9.8 4.0 %copy-start.8 = (f32[1,2]{1,0:T(1,128)S(1)}, f32[1,2]{1,0:T(1,128)}, u32[]{:S(2)}) copy-start(f32[1,2]{1,0:T(1,128)} %shift_ref.3) | copy-start | bytes 28
  13.8 1.4 %copy-start.5 = (f32[768,512]{1,0:T(8,128)S(1)}, f32[768,512]{1,0:T(8,128)}, u32[]{:S(2)}) copy-start(f32[768,512]{1,0:T(8,128)} %src_ref.1) | copy-start | bytes 4718596
  20.6 5.8 %collective-permute-start.2 = (f16[528,512]{1,0:T(8,128)(2,1)S(1)}, f16[528,512]{1,0:T(8,128)(2,1)S(1)}, u32[]{:S(2)}, u32[]{:S(2)}) collective-permute-start(f16[528,512]{1,0:T(8,128)(2,1)S(1)} %convert_element_type.73), channel_id=1, source_target_pairs={{4,0},{0,4},{12,8},{8,12},{20,16},{16,20},{28,24},{24,28},{5,1},{1... | collective-permute-start | bytes 1622024 | tf_op jit(solution)/shard_map/ppermute | solution.py:192
  21.7 14.0 %collective-permute-start.3 = (f16[528,512]{1,0:T(8,128)(2,1)S(1)}, f16[528,512]{1,0:T(8,128)(2,1)S(1)}, u32[]{:S(2)}, u32[]{:S(2)}) collective-permute-start(f16[528,512]{1,0:T(8,128)(2,1)S(1)} %convert_element_type.75), channel_id=1, source_target_pairs={{8,4},{4,8},{16,12},{12,16},{24,20},{20,24},{9,5},{5,9},{17,13},{1... | collective-permute-start | bytes 1622024 | tf_op jit(solution)/shard_map/ppermute | solution.py:192
  38.8 0.8 copy-start.1
  39.6 0.8 copy-start.2
  40.4 0.8 copy-start.3
  41.2 7.3 %collective-permute-start.4 = (f16[208,512]{1,0:T(8,128)(2,1)}, f16[208,512]{1,0:T(8,128)(2,1)}, u32[]{:S(2)}, u32[]{:S(2)}) collective-permute-start(f16[208,512]{1,0:T(8,128)(2,1)} %convert_element_type.77), channel_id=1, source_target_pairs={{0,1},{1,0},{2,3},{3,2},{4,5},{5,4},{6,7},{7,6},{8,9},{9,8},{10,11... | collective-permute-start | bytes 638984 | tf_op jit(solution)/shard_map/ppermute | solution.py:218
  42.8 22.0 %copy-start.4 = (f32[192,512]{1,0:T(8,128)S(1)}, f32[192,512]{1,0:T(8,128)}, u32[]{:S(2)}) copy-start(f32[192,512]{1,0:T(8,128)} %copy-done.3) | copy-start | bytes 1179652
  43.9 14.1 %collective-permute-start.5 = (f16[208,512]{1,0:T(8,128)(2,1)S(1)}, f16[208,512]{1,0:T(8,128)(2,1)S(1)}, u32[]{:S(2)}, u32[]{:S(2)}) collective-permute-start(f16[208,512]{1,0:T(8,128)(2,1)S(1)} %convert_element_type.79), channel_id=1, source_target_pairs={{0,2},{1,3},{2,0},{3,1},{4,6},{5,7},{6,4},{7,5},{8,10},{9,11},{10,... | collective-permute-start | bytes 638984 | tf_op jit(solution)/shard_map/ppermute | solution.py:218
  45.3 19.3 %collective-permute-start.6 = (f16[208,512]{1,0:T(8,128)(2,1)S(1)}, f16[208,512]{1,0:T(8,128)(2,1)S(1)}, u32[]{:S(2)}, u32[]{:S(2)}) collective-permute-start(f16[208,512]{1,0:T(8,128)(2,1)S(1)} %convert_element_type.81), channel_id=1, source_target_pairs={{0,3},{1,2},{2,1},{3,0},{4,7},{5,6},{6,5},{7,4},{8,11},{9,10},{10,... | collective-permute-start | bytes 638984 | tf_op jit(solution)/shard_map/ppermute | solution.py:218
  64.9 8.2 %collective-permute-start.7 = (bf16[192,512]{1,0:T(8,128)(2,1)S(1)}, bf16[192,512]{1,0:T(8,128)(2,1)S(1)}, u32[]{:S(2)}, u32[]{:S(2)}) collective-permute-start(bf16[192,512]{1,0:T(8,128)(2,1)S(1)} %fusion.5.own_ref), channel_id=1, source_target_pairs={{0,1},{1,0},{2,3},{3,2},{4,5},{5,4},{6,7},{7,6},{8,9},{9,8},{10,11... | collective-permute-start | bytes 589832 | tf_op jit(solution)/shard_map/ppermute | solution.py:223
  64.9 15.5 %collective-permute-start.8 = (bf16[192,512]{1,0:T(8,128)(2,1)S(1)}, bf16[192,512]{1,0:T(8,128)(2,1)S(1)}, u32[]{:S(2)}, u32[]{:S(2)}) collective-permute-start(bf16[192,512]{1,0:T(8,128)(2,1)S(1)} %fusion.5.own_ref), channel_id=1, source_target_pairs={{0,2},{1,3},{2,0},{3,1},{4,6},{5,7},{6,4},{7,5},{8,10},{9,11},{10,... | collective-permute-start | bytes 589832 | tf_op jit(solution)/shard_map/ppermute | solution.py:223
  66.9 19.6 %collective-permute-start.9 = (bf16[192,512]{1,0:T(8,128)(2,1)S(1)}, bf16[192,512]{1,0:T(8,128)(2,1)S(1)}, u32[]{:S(2)}, u32[]{:S(2)}) collective-permute-start(bf16[192,512]{1,0:T(8,128)(2,1)S(1)} %fusion.5.own_ref), channel_id=1, source_target_pairs={{0,3},{1,2},{2,1},{3,0},{4,7},{5,6},{6,5},{7,4},{8,11},{9,10},{10,... | collective-permute-start | bytes 589832 | tf_op jit(solution)/shard_map/ppermute | solution.py:223
  87.1 2.0 %collective-permute-start.10 = (bf16[128,512]{1,0:T(8,128)(2,1)S(1)}, bf16[128,512]{1,0:T(8,128)(2,1)S(1)}, u32[]{:S(2)}, u32[]{:S(2)}) collective-permute-start(bf16[128,512]{1,0:T(8,128)(2,1)S(1)} %get-tuple-element.36), channel_id=1, source_target_pairs={{4,0},{0,4},{12,8},{8,12},{20,16},{16,20},{28,24},{24,28},{5,1},{1... | collective-permute-start | bytes 393224 | tf_op jit(solution)/shard_map/ppermute | solution.py:192
  87.2 6.3 %collective-permute-start.11 = (bf16[128,512]{1,0:T(8,128)(2,1)S(1)}, bf16[128,512]{1,0:T(8,128)(2,1)S(1)}, u32[]{:S(2)}, u32[]{:S(2)}) collective-permute-start(bf16[128,512]{1,0:T(8,128)(2,1)S(1)} %get-tuple-element.37), channel_id=1, source_target_pairs={{8,4},{4,8},{16,12},{12,16},{24,20},{20,24},{9,5},{5,9},{17,13},{1... | collective-permute-start | bytes 393224 | tf_op jit(solution)/shard_map/ppermute | solution.py:192
  98.1 6.1 %collective-permute-start.12 = (f16[528,512]{1,0:T(8,128)(2,1)S(1)}, f16[528,512]{1,0:T(8,128)(2,1)S(1)}, u32[]{:S(2)}, u32[]{:S(2)}) collective-permute-start(f16[528,512]{1,0:T(8,128)(2,1)S(1)} %convert_element_type.84), channel_id=1, source_target_pairs={{4,0},{0,4},{12,8},{8,12},{20,16},{16,20},{28,24},{24,28},{5,1},{1... | collective-permute-start | bytes 1622024 | tf_op jit(solution)/shard_map/ppermute | solution.py:192
  99.7 14.0 %collective-permute-start.13 = (f16[528,512]{1,0:T(8,128)(2,1)S(1)}, f16[528,512]{1,0:T(8,128)(2,1)S(1)}, u32[]{:S(2)}, u32[]{:S(2)}) collective-permute-start(f16[528,512]{1,0:T(8,128)(2,1)S(1)} %convert_element_type.86), channel_id=1, source_target_pairs={{8,4},{4,8},{16,12},{12,16},{24,20},{20,24},{9,5},{5,9},{17,13},{1... | collective-permute-start | bytes 1622024 | tf_op jit(solution)/shard_map/ppermute | solution.py:192
  116.9 7.4 %collective-permute-start.14 = (f16[208,512]{1,0:T(8,128)(2,1)S(1)}, f16[208,512]{1,0:T(8,128)(2,1)S(1)}, u32[]{:S(2)}, u32[]{:S(2)}) collective-permute-start(f16[208,512]{1,0:T(8,128)(2,1)S(1)} %convert_element_type.88), channel_id=1, source_target_pairs={{0,1},{1,0},{2,3},{3,2},{4,5},{5,4},{6,7},{7,6},{8,9},{9,8},{10,11... | collective-permute-start | bytes 638984 | tf_op jit(solution)/shard_map/ppermute | solution.py:218
  117.0 11.9 %collective-permute-start.15 = (f16[208,512]{1,0:T(8,128)(2,1)S(1)}, f16[208,512]{1,0:T(8,128)(2,1)S(1)}, u32[]{:S(2)}, u32[]{:S(2)}) collective-permute-start(f16[208,512]{1,0:T(8,128)(2,1)S(1)} %convert_element_type.90), channel_id=1, source_target_pairs={{0,2},{1,3},{2,0},{3,1},{4,6},{5,7},{6,4},{7,5},{8,10},{9,11},{10,... | collective-permute-start | bytes 638984 | tf_op jit(solution)/shard_map/ppermute | solution.py:218
  119.1 20.9 %collective-permute-start.16 = (f16[208,512]{1,0:T(8,128)(2,1)S(1)}, f16[208,512]{1,0:T(8,128)(2,1)S(1)}, u32[]{:S(2)}, u32[]{:S(2)}) collective-permute-start(f16[208,512]{1,0:T(8,128)(2,1)S(1)} %convert_element_type.92), channel_id=1, source_target_pairs={{0,3},{1,2},{2,1},{3,0},{4,7},{5,6},{6,5},{7,4},{8,11},{9,10},{10,... | collective-permute-start | bytes 638984 | tf_op jit(solution)/shard_map/ppermute | solution.py:218

commit v3 on v2

v3 whole, which is shorter than its diff:
```python
import functools

import jax
import jax.numpy as jnp
from jax import lax
from jax.experimental import pallas as pl
from jax.experimental.pallas import tpu as pltpu
from jax.sharding import PartitionSpec as P

STEPS = 2
CHUNKS = 2
TAIL = 8
TOP = 12.0
BF16 = jnp.bfloat16
F16 = jnp.float16
F32 = jnp.float32
VMEM = pl.BlockSpec(memory_space=pltpu.VMEM)
SMEM = pl.BlockSpec(memory_space=pltpu.SMEM)
HBM = pl.BlockSpec(memory_space=pltpu.HBM)


def call(kernel, outs, ins, scratch=(), flops=0, moved=0):
    return pl.pallas_call(
        kernel,
        out_shape=[jax.ShapeDtypeStruct(s, d) for s, d in outs],
        in_specs=[s for s, _ in ins],
        out_specs=[VMEM] * len(outs),
        scratch_shapes=list(scratch),
        compiler_params=pltpu.CompilerParams(vmem_limit_bytes=16 * 2**20),
        cost_estimate=pl.CostEstimate(flops=flops, bytes_accessed=moved, transcendentals=0),
    )(*[a for _, a in ins])


def dot(a, b):
    return jnp.dot(a, b, preferred_element_type=F32)


def coded(block):
    top = jnp.max(jnp.abs(block), axis=0, keepdims=True)
    power = jnp.ceil(jnp.log2(jnp.maximum(top, 1e-30)))
    return block * jnp.exp2(TOP - power), jnp.broadcast_to(power, (TAIL, block.shape[1]))


def pick(flag, a, b):
    return jnp.where(flag == 0, a, b)


def hop_target(pole, hop, poles):
    return pole ^ hop if poles & (poles - 1) == 0 else lax.rem(pole + hop, poles)


def hop_source(pole, hop, poles):
    return pole ^ hop if poles & (poles - 1) == 0 else lax.rem(pole + poles - hop, poles)


def hop_pairs(hop, poles):
    return [(i, i ^ hop if poles & (poles - 1) == 0 else (i + hop) % poles) for i in range(poles)]


def rows_of(index, share):
    return pl.ds(pl.multiple_of(index * share, share), share)


def column(row, count):
    return jnp.transpose(jnp.broadcast_to(row, (8, count)))[:, :1]


def start_kernel(sigma_ref, state_hbm, msg1_ref, msg2_ref, wide_ref, low_ref, high_ref, low_sem, high_sem):
    rows, rim = state_hbm.shape[0], low_ref.shape[0]
    low_copy = pltpu.make_async_copy(state_hbm.at[pl.ds(0, rim)], low_ref, low_sem)
    high_copy = pltpu.make_async_copy(state_hbm.at[pl.ds(rows - rim, rim)], high_ref, high_sem)
    low_copy.start()
    high_copy.start()
    sigma = column(sigma_ref[...], rows)
    wide_ref[...] = jnp.broadcast_to(sigma, wide_ref.shape)
    parity = lax.rem(lax.axis_index("sub"), 2)
    low_copy.wait()
    high_copy.wait()
    low = (low_ref[...] * sigma[:rim]).astype(BF16)
    high = (high_ref[...] * sigma[rows - rim:]).astype(BF16)
    msg1_ref[...] = pick(parity, high, low)
    msg2_ref[...] = pick(parity, low, high)


def setup_kernel(order_ref, wide_ref, inv_hbm, state_hbm, g_ref, share_ref, *rest):
    chunks, (inv_ref, state_ref, inv_sem, state_sem) = rest[:-4], rest[-4:]
    rows, width = inv_ref.shape[0], inv_ref.shape[1] // 2
    n, share = share_ref.shape[1], share_ref.shape[0]
    inv_copy = pltpu.make_async_copy(inv_hbm.at[0], inv_ref, inv_sem)
    state_copy = pltpu.make_async_copy(state_hbm, state_ref, state_sem)
    inv_copy.start()
    state_copy.start()
    share_ref[...] = wide_ref[rows_of(lax.axis_index("pole"), share)]
    order = column(order_ref[...].astype(F32), width).astype(jnp.int32)
    ids = lax.broadcasted_iota(jnp.int32, (width, width), 1)
    place = (order == ids).astype(BF16)
    inv_copy.wait()
    g_ref[:rows] = dot(inv_ref[:, :width], place).astype(BF16)
    g_ref[rows:] = dot(inv_ref[:, width:], place).astype(BF16)
    state_copy.wait()
    for k, ref in enumerate(chunks):
        ref[...] = state_ref[:, k * n:(k + 1) * n] * wide_ref[...]


def stencil(ref, lo, count, rim, far_up, far_down):
    mid = 4.0 * ref[8 + lo:8 + lo + count] - ref[7 + lo:7 + lo + count] - ref[9 + lo:9 + lo + count]
    if far_up:
        mid = mid - ref[8 + lo - rim:8 + lo - rim + count]
    if far_down:
        mid = mid - ref[8 + lo + rim:8 + lo + rim + count]
    return mid


def residual(xr_ref, xi_ref, at, lo, count, rim, far_up, far_down, src_ref, sigma_ref, a, b):
    xr, xi = xr_ref[8 + lo:8 + lo + count], xi_ref[8 + lo:8 + lo + count]
    sigma = sigma_ref[at]
    rr = src_ref[at].astype(F32) - stencil(xr_ref, lo, count, rim, far_up, far_down) - sigma * (a * xr - b * xi)
    ri = -stencil(xi_ref, lo, count, rim, far_up, far_down) - sigma * (b * xr + a * xi)
    return xr, xi, rr, ri


def edge_kernel(rim, lane, shift_ref, g_ref, src_ref, one_ref, two_ref, sigma_ref,
                ext_ref, x_ref, edge_ref, msg1_ref, msg2_ref, xr_ref, xi_ref):
    rows, n = src_ref.shape
    parity = lax.rem(lax.axis_index("sub"), 2)
    one, two = one_ref[:, lane:lane + n], two_ref[:, lane:lane + n]
    ext_ref[:rim] = pick(parity, two, one)
    ext_ref[rim:rim + rows] = src_ref[...].astype(BF16)
    ext_ref[rim + rows:] = pick(parity, one, two)
    a, b = shift_ref[0, 0], shift_ref[0, 1]
    span, step = 2 * rim, 32
    for side in range(2):
        lo = side * (rows - span)
        for half, ref in ((0, xr_ref), (1, xi_ref)):
            ref[:8] = jnp.zeros((8, n), F32)
            ref[8 + span:] = jnp.zeros((8, n), F32)
            block = dot(g_ref[half * rows + lo:half * rows + lo + span], ext_ref[...])
            ref[8:8 + span] = block
            x_ref[side, half] = block
        for k in range(0, rim, step):
            at = side * rim + k
            out = residual(xr_ref, xi_ref, slice(lo + at, lo + at + step), at, step, rim, side == 1, side == 0,
                           src_ref, sigma_ref, a, b)
            for j, v in enumerate(out):
                edge_ref[side, j * rim + k:j * rim + k + step] = v
    low, low_tail = coded(edge_ref[0])
    high, high_tail = coded(edge_ref[1])
    msg1_ref[:4 * rim] = pick(parity, high, low)
    msg2_ref[:4 * rim] = pick(parity, low, high)
    msg1_ref[4 * rim:] = pick(parity, high_tail, low_tail)
    msg2_ref[4 * rim:] = pick(parity, low_tail, high_tail)


def product(g_ref, rows, cols, er, ei, wr, wi):
    gr, gi = g_ref[:rows, cols], g_ref[rows:, cols]
    return wr * (dot(gr, er) - dot(gi, ei)) - wi * (dot(gr, ei) + dot(gi, er))


def middle_kernel(rim, shift_ref, weight_ref, g_ref, src_ref, ext_ref, x_ref, sigma_ref, out_ref, xr_ref, xi_ref, e_ref):
    rows, n = src_ref.shape
    span = 2 * rim
    a, b = shift_ref[0, 0], shift_ref[0, 1]
    wr, wi = 2.0 * weight_ref[0, 0], 2.0 * weight_ref[0, 1]
    for half, ref in ((0, xr_ref), (1, xi_ref)):
        ref[8:8 + span] = x_ref[0, half]
        ref[8 + rows - span:8 + rows] = x_ref[1, half]
        if rows > 2 * span:
            ref[8 + span:8 + rows - span] = dot(g_ref[half * rows + span:half * rows + rows - span], ext_ref[...])
    step = 32
    for lo in range(0, rows, step):
        at = slice(lo, lo + step)
        if rim <= lo < rows - rim:
            xr, xi, rr, ri = residual(xr_ref, xi_ref, at, lo, step, rim, True, True, src_ref, sigma_ref, a, b)
            e_ref[0, lo - rim:lo - rim + step] = rr.astype(BF16)
            e_ref[1, lo - rim:lo - rim + step] = ri.astype(BF16)
    base = wr * xr_ref[8:8 + rows] - wi * xi_ref[8:8 + rows]
    out_ref[...] = base + product(g_ref, rows, slice(span, rows), e_ref[0], e_ref[1], wr, wi)


def last_kernel(rim, hops, weight_ref, g_ref, part_ref, edge_ref, one_ref, two_ref, *rest):
    own_ref, msgs, u_ref, e_ref = rest[0], rest[1:1 + hops], rest[1 + hops], rest[2 + hops]
    rows, n = part_ref.shape
    share = own_ref.shape[0]
    sub, pole = lax.axis_index("sub"), lax.axis_index("pole")
    parity, first, final = lax.rem(sub, 2), sub == 0, sub == lax.axis_size("sub") - 1
    wr, wi = 2.0 * weight_ref[0, 0], 2.0 * weight_ref[0, 1]
    before = pick(parity, two_ref[...], one_ref[...])
    after = pick(parity, one_ref[...], two_ref[...])
    before = before[:4 * rim] * jnp.exp2(before[4 * rim:4 * rim + 1] - TOP)
    after = after[:4 * rim] * jnp.exp2(after[4 * rim:4 * rim + 1] - TOP)
    at = lax.broadcasted_iota(jnp.int32, (rim, 1), 0)
    for half in range(2):
        x, r = slice(half * rim, (half + 1) * rim), slice((2 + half) * rim, (3 + half) * rim)
        xb, qb, xa, qa = before[x], before[r], after[x], after[r]
        low, high = edge_ref[0, x], edge_ref[1, x]
        above = qb + low + jnp.where(at == rim - 1, low[:1], 0.0)
        below = qa + high + jnp.where(at == 0, high[rim - 1:], 0.0)
        head = edge_ref[0, r] + xb + jnp.where(at == 0, xb[rim - 1:], 0.0)
        foot = edge_ref[1, r] + xa + jnp.where(at == rim - 1, xa[:1], 0.0)
        e_ref[half, :rim] = jnp.where(first, 0.0, above).astype(BF16)
        e_ref[half, rim:2 * rim] = head.astype(BF16)
        e_ref[half, 2 * rim:3 * rim] = foot.astype(BF16)
        e_ref[half, 3 * rim:] = jnp.where(final, 0.0, below).astype(BF16)
    u_ref[...] = part_ref[...] + product(
        g_ref, rows, slice(0, 2 * rim), e_ref[0, :2 * rim], e_ref[1, :2 * rim], wr, wi
    ) + product(
        g_ref, rows, slice(rows, rows + 2 * rim), e_ref[0, 2 * rim:], e_ref[1, 2 * rim:], wr, wi
    )
    own_ref[...] = u_ref[rows_of(pole, share)]
    for hop, ref in enumerate(msgs):
        ref[:share], ref[share:] = coded(u_ref[rows_of(hop_target(pole, hop + 1, hops + 1), share)])


def join_kernel(rim, own_ref, *rest):
    got, (src_ref, msg1_ref, msg2_ref) = rest[:-3], rest[-3:]
    share, rows, poles = own_ref.shape[0], src_ref.shape[0], len(got) + 1
    parity, pole = lax.rem(lax.axis_index("sub"), 2), lax.axis_index("pole")
    src_ref[rows_of(pole, share)] = own_ref[...]
    for hop, ref in enumerate(got):
        src_ref[rows_of(hop_source(pole, hop + 1, poles), share)] = ref[...]
    low, high = src_ref[:rim], src_ref[rows - rim:]
    msg1_ref[...] = pick(parity, high, low)
    msg2_ref[...] = pick(parity, low, high)


def shards(state, conductivity, pole_shift, pole_weight, order_list, inverse):
    rows, columns = state.shape
    order = order_list.shape[1]
    rim = (order - rows) // 2
    subs, poles = lax.axis_size("sub"), lax.axis_size("pole")
    share, hops = rows // poles, poles - 1
    n = columns // CHUNKS
    pairs1 = [(i ^ 1, i) for i in range(subs) if i ^ 1 < subs]
    pairs2 = [(j, i) for i in range(subs) for j in [((i + 1) ^ 1) - 1] if 0 <= j < subs]
    def exchange(one, two):
        return lax.ppermute(one, "sub", pairs1), lax.ppermute(two, "sub", pairs2)

    one, two, sigma = call(
        start_kernel, [((rim, columns), BF16), ((rim, columns), BF16), ((rows, n), F32)],
        [(VMEM, conductivity.reshape(1, rows)), (HBM, state)],
        [pltpu.VMEM((rim, columns), F32), pltpu.VMEM((rim, columns), F32),
         pltpu.SemaphoreType.DMA, pltpu.SemaphoreType.DMA],
        moved=8 * rim * columns,
    )
    first_halo = exchange(one, two)
    g, sigma_share, *sources = call(
        setup_kernel, [((2 * rows, order), BF16), ((share, n), F32)] + [((rows, n), F32)] * CHUNKS,
        [(VMEM, order_list), (VMEM, sigma), (HBM, inverse), (HBM, state)],
        [pltpu.VMEM((rows, 2 * order), BF16), pltpu.VMEM((rows, columns), F32),
         pltpu.SemaphoreType.DMA, pltpu.SemaphoreType.DMA],
        flops=4 * rows * order * order, moved=6 * rows * order,
    )

    def sweep(source, got, lane):
        ext, x, edge, msg1, msg2 = call(
            functools.partial(edge_kernel, rim, lane),
            [((order, n), BF16), ((2, 2, 2 * rim, n), F32), ((2, 4 * rim, n), F32),
             ((4 * rim + TAIL, n), F32), ((4 * rim + TAIL, n), F32)],
            [(SMEM, pole_shift), (VMEM, g), (VMEM, source), (VMEM, got[0]), (VMEM, got[1]), (VMEM, sigma)],
            [pltpu.VMEM((2 * rim + 16, n), F32), pltpu.VMEM((2 * rim + 16, n), F32)],
            flops=16 * rim * order * n, moved=4 * rows * order,
        )
        got = exchange(msg1.astype(F16), msg2.astype(F16))
        (part,) = call(
            functools.partial(middle_kernel, rim), [((rows, n), F32)],
            [(SMEM, pole_shift), (SMEM, pole_weight), (VMEM, g), (VMEM, source), (VMEM, ext), (VMEM, x), (VMEM, sigma)],
            [pltpu.VMEM((rows + 16, n), F32), pltpu.VMEM((rows + 16, n), F32), pltpu.VMEM((2, rows - 2 * rim, n), BF16)],
            flops=8 * rows * rows * n, moved=4 * rows * order,
        )
        return call(
            functools.partial(last_kernel, rim, hops), [((share, n), F32)] + [((share + TAIL, n), F32)] * hops,
            [(SMEM, pole_weight), (VMEM, g), (VMEM, part), (VMEM, edge), (VMEM, got[0].astype(F32)), (VMEM, got[1].astype(F32))],
            [pltpu.VMEM((rows, n), F32), pltpu.VMEM((2, 4 * rim, n), BF16)],
            flops=8 * rows * 4 * rim * n, moved=4 * rows * order,
        )

    def reduced(own, *sent):
        for hop, block in enumerate(sent):
            got = lax.ppermute(block.astype(F16), "pole", hop_pairs(hop + 1, poles)).astype(F32)
            own = own + got[:share] * jnp.exp2(got[share:share + 1] - TOP)
        return own

    def gathered(own):
        got = [lax.ppermute(own, "pole", hop_pairs(hop, poles)) for hop in range(1, poles)]
        return call(
            functools.partial(join_kernel, rim), [((rows, n), BF16), ((rim, n), BF16), ((rim, n), BF16)],
            [(VMEM, own)] + [(VMEM, x) for x in got], moved=4 * rows * n,
        )

    results = []
    for chunk in range(CHUNKS):
        source, halo = sources[chunk], first_halo
        for step in range(STEPS):
            total = reduced(*sweep(source, halo, 0 if step else chunk * n))
            if step + 1 < STEPS:
                source, one, two = gathered((sigma_share * total).astype(BF16))
                halo = exchange(one, two)
        results.append(total)
    return jnp.concatenate(results, axis=1) if CHUNKS > 1 else results[0]


def solution(mesh):
    placed = (
        P("sub", None),
        P("sub"),
        P("pole", None),
        P("pole", None),
        P("sub", None),
        P("pole", "sub", None),
    )
    return jax.shard_map(
        shards, mesh=mesh, in_specs=placed, out_specs=P(("sub", "pole"), None), check_vma=False
    )
```

time: 142 us -> 116 us (0.82)
  the two profiles are of different devices: /device:TPU:18 before, /device:TPU:5 now
where the time goes in v3:
time: 116 us; the launch traced here: 115 us
  starting transfers between devices  47.7 us (41%)
  waiting for transfers between devices  30.3 us (26%)
  Pallas kernels  28.3 us (24%)
  local copies, waits for them, and re-layouts  6.08 us (5%)
  other arithmetic  2.15 us (2%)
    pallas_call x16, Pallas kernels, call(): pl.pallas_call(kernel, out_shape=[jax.ShapeDtypeStruct(s, d) for s, d in...  28.3 us
    ppermute x14, starting transfers between devices, exchange(): return (lax.ppermute(one, 'sub', pairs1), lax.ppermute(two, 'sub', pairs2))  25.7 us
    ppermute x12, waiting for transfers between devices, reduced(): lax.ppermute(block.astype(F16), 'pole', hop_pairs(hop + 1, poles))  18 us
    ppermute x12, starting transfers between devices, reduced(): lax.ppermute(block.astype(F16), 'pole', hop_pairs(hop + 1, poles))  14.7 us
    ppermute x6, waiting for transfers between devices, gathered(): lax.ppermute(own, 'pole', hop_pairs(hop, poles))  8.23 us
    ppermute x6, starting transfers between devices, gathered(): lax.ppermute(own, 'pole', hop_pairs(hop, poles))  7.23 us
    unnamed x12, local copies, waits for them, and re-layouts  5.39 us
    ppermute x14, waiting for transfers between devices, exchange(): return (lax.ppermute(one, 'sub', pairs1), lax.ppermute(two, 'sub', pairs2))  4.07 us
  transfers between devices with their start and end apart: 32, of which 10 were waited for; matrix products, arithmetic and copies ran while one was open for 1% of the time, Pallas kernels for 23%

profile of v3, /device:TPU:5, one launch (start us, length us, event | category | flops | bytes accessed | tf_op | source)
XLA Modules:
  0.0 115.1 jit_solution(14783233300438164643)
XLA Ops:
  0.0 0.7 reshape.3.sigma_ref
  0.7 1.4 %copy-done = f32[768,512]{1,0:T(8,128)S(1)} copy-done((f32[768,512]{1,0:T(8,128)S(1)}, f32[768,512]{1,0:T(8,128)}, u32[]{:S(2)}) %copy-start) | copy-done | bytes 1572888
  2.1 0.4 shard_map.64
  2.5 0.7 collective-permute-start
  3.3 3.0 %collective-permute-start.1 = (bf16[128,512]{1,0:T(8,128)(2,1)S(1)}, bf16[128,512]{1,0:T(8,128)(2,1)S(1)}, u32[]{:S(2)}, u32[]{:S(2)}) collective-permute-start(bf16[128,512]{1,0:T(8,128)(2,1)S(1)} %get-tuple-element.59), channel_id=1, source_target_pairs={{8,4},{4,8},{16,12},{12,16},{24,20},{20,24},{9,5},{5,9},{17,13},{1... | collective-permute-start | bytes 393224 | tf_op jit(solution)/shard_map/ppermute | solution.py:236
  6.3 0.0 copy-start.1
  6.3 1.4 %copy-done.1 = f32[768,512]{1,0:T(8,128)S(1)} copy-done((f32[768,512]{1,0:T(8,128)S(1)}, f32[768,512]{1,0:T(8,128)}, u32[]{:S(2)}) %copy-start.1) | copy-done | bytes 1572888
  7.7 1.9 %copy-done.4 = bf16[1,768,2048]{2,1,0:T(8,128)(2,1)S(1)} copy-done((bf16[1,768,2048]{2,1,0:T(8,128)(2,1)S(1)}, bf16[1,768,2048]{2,1,0:T(8,128)(2,1)}, u32[]{:S(2)}) %copy-start.4) | copy-done | bytes 3145752
  9.6 0.7 copy-done.5
  10.3 4.7 %shard_map.65 = (bf16[1536,1024]{1,0:T(8,128)(2,1)S(1)}, f32[192,256]{1,0:T(8,128)S(1)}, f32[768,256]{1,0:T(8,128)S(1)}, f32[768,256]{1,0:T(8,128)S(1)}) custom-call(s32[1,1024]{1,0:T(1,128)S(1)} %copy-done.5, f32[768,256]{1,0:T(8,128)S(1)} %get-tuple-element.54.wide_ref.sigma_ref, bf16[1,768,2048]{2,1,0:T(8,128)(2,1)S(1)} %copy-done.4, f32[768,512]{1,0:T(8,128)S(1)} %copy-done.1), custom_call_target="tpu_custom_call" | custom-call | flops 3221225472 | bytes 4718592 | tf_op jit(solution)/shard_map/pallas_call | solution.py:23
  15.0 0.0 collective-permute-done.1.two_ref
  15.0 1.8 %shard_map.66 = (bf16[1024,256]{1,0:T(8,128)(2,1)S(1)}, f32[2,2,256,256]{3,2,1,0:T(8,128)S(1)}, f32[2,512,256]{2,1,0:T(8,128)S(1)}, f32[520,256]{1,0:T(8,128)S(1)}, f32[520,256]{1,0:T(8,128)S(1)}) custom-call(f32[1,2]{1,0:T(1,128)S(1)} %copy-done.2, bf16[1536,1024]{1,0:T(8,128)(2,1)S(1)} %get-tuple-element.55.g_ref, ...), custom_call_target="tpu_custom_call" | custom-call | flops 536870912 | bytes 3145728 | tf_op jit(solution)/shard_map/pallas_call | solution.py:23
  16.9 2.5 %collective-permute-start.3 = (f16[520,256]{1,0:T(8,128)(2,1)S(1)}, f16[520,256]{1,0:T(8,128)(2,1)S(1)}, u32[]{:S(2)}, u32[]{:S(2)}) collective-permute-start(f16[520,256]{1,0:T(8,128)(2,1)S(1)} %convert_element_type.128), channel_id=1, source_target_pairs={{8,4},{4,8},{16,12},{12,16},{24,20},{20,24},{9,5},{5,9},{17,13},{1... | collective-permute-start | bytes 798728 | tf_op jit(solution)/shard_map/ppermute | solution.py:236
  19.5 1.0 collective-permute-start.2
  20.5 1.8 %shard_map.73 = (bf16[1024,256]{1,0:T(8,128)(2,1)S(1)}, f32[2,2,256,256]{3,2,1,0:T(8,128)S(1)}, f32[2,512,256]{2,1,0:T(8,128)S(1)}, f32[520,256]{1,0:T(8,128)S(1)}, f32[520,256]{1,0:T(8,128)S(1)}) custom-call(f32[1,2]{1,0:T(1,128)S(1)} %copy-done.2, bf16[1536,1024]{1,0:T(8,128)(2,1)S(1)} %get-tuple-element.55.g_ref, ...), custom_call_target="tpu_custom_call" | custom-call | flops 536870912 | bytes 3145728 | tf_op jit(solution)/shard_map/pallas_call | solution.py:23
  22.4 2.3 %collective-permute-start.18 = (f16[520,256]{1,0:T(8,128)(2,1)S(1)}, f16[520,256]{1,0:T(8,128)(2,1)S(1)}, u32[]{:S(2)}, u32[]{:S(2)}) collective-permute-start(f16[520,256]{1,0:T(8,128)(2,1)S(1)} %convert_element_type.149), channel_id=1, source_target_pairs={{8,4},{4,8},{16,12},{12,16},{24,20},{20,24},{9,5},{5,9},{17,13},{1... | collective-permute-start | bytes 798728 | tf_op jit(solution)/shard_map/ppermute | solution.py:236
  24.7 1.4 %collective-permute-start.17 = (f16[520,256]{1,0:T(8,128)(2,1)S(1)}, f16[520,256]{1,0:T(8,128)(2,1)S(1)}, u32[]{:S(2)}, u32[]{:S(2)}) collective-permute-start(f16[520,256]{1,0:T(8,128)(2,1)S(1)} %convert_element_type.147), channel_id=1, source_target_pairs={{4,0},{0,4},{12,8},{8,12},{20,16},{16,20},{28,24},{24,28},{5,1},{1... | collective-permute-start | bytes 798728 | tf_op jit(solution)/shard_map/ppermute | solution.py:236
  26.1 2.2 %shard_map.67.part_ref = f32[768,256]{1,0:T(8,128)S(1)} custom-call(f32[1,2]{1,0:T(1,128)S(1)} %copy-done.2, f32[1,2]{1,0:T(1,128)S(1)} %copy-done.3, bf16[1536,1024]{1,0:T(8,128)(2,1)S(1)} %get-tuple-element.55.g_ref, f32[768,256]{1,0:T(8,128)S(1)} %get-tuple-element.57.src_ref, bf16[1024,256]{1,0:T(8,128)(2,1)S(1)} %get-tuple-element.60.ext_ref, ...), custom_call_target="tpu_custom_call" | custom-call | flops 1207959552 | bytes 3145728 | tf_op jit(solution)/shard_map/pallas_call | solution.py:23
  28.3 0.0 collective-permute-done.3
  28.4 1.8 %shard_map.68 = (f32[192,256]{1,0:T(8,128)S(1)}, f32[200,256]{1,0:T(8,128)S(1)}, f32[200,256]{1,0:T(8,128)S(1)}, f32[200,256]{1,0:T(8,128)S(1)}) custom-call(f32[1,2]{1,0:T(1,128)S(1)} %copy-done.3, bf16[1536,1024]{1,0:T(8,128)(2,1)S(1)} %get-tuple-element.55.g_ref, f32[768,256]{1,0:T(8,128)S(1)} %shard_map.67.part_ref, ...), custom_call_target="tpu_custom_call" | custom-call | flops 805306368 | bytes 3145728 | tf_op jit(solution)/shard_map/pallas_call | solution.py:23
  30.2 3.4 %collective-permute-start.6 = (f16[200,256]{1,0:T(8,128)(2,1)S(1)}, f16[200,256]{1,0:T(8,128)(2,1)S(1)}, u32[]{:S(2)}, u32[]{:S(2)}) collective-permute-start(f16[200,256]{1,0:T(8,128)(2,1)S(1)} %convert_element_type.134), channel_id=1, source_target_pairs={{0,3},{1,2},{2,1},{3,0},{4,7},{5,6},{6,5},{7,4},{8,11},{9,10},{10,... | collective-permute-start | bytes 307208 | tf_op jit(solution)/shard_map/ppermute | solution.py:279
  33.6 2.2 %shard_map.74.part_ref = f32[768,256]{1,0:T(8,128)S(1)} custom-call(f32[1,2]{1,0:T(1,128)S(1)} %copy-done.2, f32[1,2]{1,0:T(1,128)S(1)} %copy-done.3, bf16[1536,1024]{1,0:T(8,128)(2,1)S(1)} %get-tuple-element.55.g_ref, f32[768,256]{1,0:T(8,128)S(1)} %get-tuple-element.81.src_ref, bf16[1024,256]{1,0:T(8,128)(2,1)S(1)} %get-tuple-element.82.ext_ref, ...), custom_call_target="tpu_custom_call" | custom-call | flops 1207959552 | bytes 3145728 | tf_op jit(solution)/shard_map/pallas_call | solution.py:23
  35.9 0.1 collective-permute-start.5
  35.9 0.3 collective-permute-start.4
  36.3 1.8 %shard_map.75 = (f32[192,256]{1,0:T(8,128)S(1)}, f32[200,256]{1,0:T(8,128)S(1)}, f32[200,256]{1,0:T(8,128)S(1)}, f32[200,256]{1,0:T(8,128)S(1)}) custom-call(f32[1,2]{1,0:T(1,128)S(1)} %copy-done.3, bf16[1536,1024]{1,0:T(8,128)(2,1)S(1)} %get-tuple-element.55.g_ref, f32[768,256]{1,0:T(8,128)S(1)} %shard_map.74.part_ref, ...), custom_call_target="tpu_custom_call" | custom-call | flops 805306368 | bytes 3145728 | tf_op jit(solution)/shard_map/pallas_call | solution.py:23
  38.2 3.3 %collective-permute-start.21 = (f16[200,256]{1,0:T(8,128)(2,1)S(1)}, f16[200,256]{1,0:T(8,128)(2,1)S(1)}, u32[]{:S(2)}, u32[]{:S(2)}) collective-permute-start(f16[200,256]{1,0:T(8,128)(2,1)S(1)} %convert_element_type.155), channel_id=1, source_target_pairs={{0,3},{1,2},{2,1},{3,0},{4,7},{5,6},{6,5},{7,4},{8,11},{9,10},{10,... | collective-permute-start | bytes 307208 | tf_op jit(solution)/shard_map/ppermute | solution.py:279
  41.5 0.4 collective-permute-start.19
  41.9 1.1 collective-permute-done.5
  43.0 0.8 collective-permute-done.21
  43.9 7.7 %collective-permute-done.20 = f16[200,256]{1,0:T(8,128)(2,1)S(1)} collective-permute-done((f16[200,256]{1,0:T(8,128)(2,1)S(1)}, f16[200,256]{1,0:T(8,128)(2,1)S(1)}, u32[]{:S(2)}, u32[]{:S(2)}) %collective-permute-start.20) | collective-permute-done | bytes 102432 | tf_op jit(solution)/shard_map/ppermute | solution.py:279
  51.7 0.1 fusion.13
  51.9 2.1 %collective-permute-start.9 = (bf16[192,256]{1,0:T(8,128)(2,1)S(1)}, bf16[192,256]{1,0:T(8,128)(2,1)S(1)}, u32[]{:S(2)}, u32[]{:S(2)}) collective-permute-start(bf16[192,256]{1,0:T(8,128)(2,1)S(1)} %get-tuple-element.103.own_ref), channel_id=1, source_target_pairs={{0,3},{1,2},{2,1},{3,0},{4,7},{5,6},{6,5},{7,4},{8,11},{9,10},{10,... | collective-permute-start | bytes 294920 | tf_op jit(solution)/shard_map/ppermute | solution.py:284
  53.9 1.6 %collective-permute-start.7 = (bf16[192,256]{1,0:T(8,128)(2,1)S(1)}, bf16[192,256]{1,0:T(8,128)(2,1)S(1)}, u32[]{:S(2)}, u32[]{:S(2)}) collective-permute-start(bf16[192,256]{1,0:T(8,128)(2,1)S(1)} %get-tuple-element.103.own_ref), channel_id=1, source_target_pairs={{0,1},{1,0},{2,3},{3,2},{4,5},{5,4},{6,7},{7,6},{8,9},{9,8},{10,11... | collective-permute-start | bytes 294920 | tf_op jit(solution)/shard_map/ppermute | solution.py:284
  55.5 2.1 %collective-permute-done.9.rest_2_ = bf16[192,256]{1,0:T(8,128)(2,1)S(1)} collective-permute-done((bf16[192,256]{1,0:T(8,128)(2,1)S(1)}, bf16[192,256]{1,0:T(8,128)(2,1)S(1)}, u32[]{:S(2)}, u32[]{:S(2)}) %collective-permute-start.9) | collective-permute-done | bytes 98336 | tf_op jit(solution)/shard_map/ppermute | solution.py:284
  57.6 5.1 %collective-permute-done.8.rest_1_ = bf16[192,256]{1,0:T(8,128)(2,1)S(1)} collective-permute-done((bf16[192,256]{1,0:T(8,128)(2,1)S(1)}, bf16[192,256]{1,0:T(8,128)(2,1)S(1)}, u32[]{:S(2)}, u32[]{:S(2)}) %collective-permute-start.8) | collective-permute-done | bytes 98336 | tf_op jit(solution)/shard_map/ppermute | solution.py:284
  62.7 0.6 collective-permute-start.10
  63.3 2.1 %collective-permute-start.11 = (bf16[128,256]{1,0:T(8,128)(2,1)S(1)}, bf16[128,256]{1,0:T(8,128)(2,1)S(1)}, u32[]{:S(2)}, u32[]{:S(2)}) collective-permute-start(bf16[128,256]{1,0:T(8,128)(2,1)S(1)} %get-tuple-element.71), channel_id=1, source_target_pairs={{8,4},{4,8},{16,12},{12,16},{24,20},{20,24},{9,5},{5,9},{17,13},{1... | collective-permute-start | bytes 196616 | tf_op jit(solution)/shard_map/ppermute | solution.py:236
  65.4 2.0 %collective-permute-start.24 = (bf16[192,256]{1,0:T(8,128)(2,1)S(1)}, bf16[192,256]{1,0:T(8,128)(2,1)S(1)}, u32[]{:S(2)}, u32[]{:S(2)}) collective-permute-start(bf16[192,256]{1,0:T(8,128)(2,1)S(1)} %get-tuple-element.104.own_ref), channel_id=1, source_target_pairs={{0,3},{1,2},{2,1},{3,0},{4,7},{5,6},{6,5},{7,4},{8,11},{9,10},{10,... | collective-permute-start | bytes 294920 | tf_op jit(solution)/shard_map/ppermute | solution.py:284
  67.5 1.6 %collective-permute-start.22 = (bf16[192,256]{1,0:T(8,128)(2,1)S(1)}, bf16[192,256]{1,0:T(8,128)(2,1)S(1)}, u32[]{:S(2)}, u32[]{:S(2)}) collective-permute-start(bf16[192,256]{1,0:T(8,128)(2,1)S(1)} %get-tuple-element.104.own_ref), channel_id=1, source_target_pairs={{0,1},{1,0},{2,3},{3,2},{4,5},{5,4},{6,7},{7,6},{8,9},{9,8},{10,11... | collective-permute-start | bytes 294920 | tf_op jit(solution)/shard_map/ppermute | solution.py:284
  69.0 0.1 collective-permute-done.11.two_ref
  69.1 1.8 %shard_map.70 = (bf16[1024,256]{1,0:T(8,128)(2,1)S(1)}, f32[2,2,256,256]{3,2,1,0:T(8,128)S(1)}, f32[2,512,256]{2,1,0:T(8,128)S(1)}, f32[520,256]{1,0:T(8,128)S(1)}, f32[520,256]{1,0:T(8,128)S(1)}) custom-call(f32[1,2]{1,0:T(1,128)S(1)} %copy-done.2, bf16[1536,1024]{1,0:T(8,128)(2,1)S(1)} %get-tuple-element.55.g_ref, ...), custom_call_target="tpu_custom_call" | custom-call | flops 536870912 | bytes 3145728 | tf_op jit(solution)/shard_map/pallas_call | solution.py:23
  71.0 4.2 %collective-permute-start.13 = (f16[520,256]{1,0:T(8,128)(2,1)S(1)}, f16[520,256]{1,0:T(8,128)(2,1)S(1)}, u32[]{:S(2)}, u32[]{:S(2)}) collective-permute-start(f16[520,256]{1,0:T(8,128)(2,1)S(1)} %convert_element_type.139), channel_id=1, source_target_pairs={{8,4},{4,8},{16,12},{12,16},{24,20},{20,24},{9,5},{5,9},{17,13},{1... | collective-permute-start | bytes 798728 | tf_op jit(solution)/shard_map/ppermute | solution.py:236
  75.2 0.2 collective-permute-start.12
  75.4 1.0 collective-permute-done.23.rest_1_
  76.5 0.7 collective-permute-start.25
  77.2 1.9 %collective-permute-start.26 = (bf16[128,256]{1,0:T(8,128)(2,1)S(1)}, bf16[128,256]{1,0:T(8,128)(2,1)S(1)}, u32[]{:S(2)}, u32[]{:S(2)}) collective-permute-start(bf16[128,256]{1,0:T(8,128)(2,1)S(1)} %get-tuple-element.93), channel_id=1, source_target_pairs={{8,4},{4,8},{16,12},{12,16},{24,20},{20,24},{9,5},{5,9},{17,13},{1... | collective-permute-start | bytes 196616 | tf_op jit(solution)/shard_map/ppermute | solution.py:236
  79.1 3.9 %collective-permute-done.26.two_ref = bf16[128,256]{1,0:T(8,128)(2,1)S(1)} collective-permute-done((bf16[128,256]{1,0:T(8,128)(2,1)S(1)}, bf16[128,256]{1,0:T(8,128)(2,1)S(1)}, u32[]{:S(2)}, u32[]{:S(2)}) %collective-permute-start.26) | collective-permute-done | bytes 65568 | tf_op jit(solution)/shard_map/ppermute | solution.py:236
  83.1 1.8 %shard_map.77 = (bf16[1024,256]{1,0:T(8,128)(2,1)S(1)}, f32[2,2,256,256]{3,2,1,0:T(8,128)S(1)}, f32[2,512,256]{2,1,0:T(8,128)S(1)}, f32[520,256]{1,0:T(8,128)S(1)}, f32[520,256]{1,0:T(8,128)S(1)}) custom-call(f32[1,2]{1,0:T(1,128)S(1)} %copy-done.2, bf16[1536,1024]{1,0:T(8,128)(2,1)S(1)} %get-tuple-element.55.g_ref, ...), custom_call_target="tpu_custom_call" | custom-call | flops 536870912 | bytes 3145728 | tf_op jit(solution)/shard_map/pallas_call | solution.py:23
  85.0 3.7 %collective-permute-start.28 = (f16[520,256]{1,0:T(8,128)(2,1)S(1)}, f16[520,256]{1,0:T(8,128)(2,1)S(1)}, u32[]{:S(2)}, u32[]{:S(2)}) collective-permute-start(f16[520,256]{1,0:T(8,128)(2,1)S(1)} %convert_element_type.160), channel_id=1, source_target_pairs={{8,4},{4,8},{16,12},{12,16},{24,20},{20,24},{9,5},{5,9},{17,13},{1... | collective-permute-start | bytes 798728 | tf_op jit(solution)/shard_map/ppermute | solution.py:236
  88.7 1.4 %collective-permute-start.27 = (f16[520,256]{1,0:T(8,128)(2,1)S(1)}, f16[520,256]{1,0:T(8,128)(2,1)S(1)}, u32[]{:S(2)}, u32[]{:S(2)}) collective-permute-start(f16[520,256]{1,0:T(8,128)(2,1)S(1)} %convert_element_type.158), channel_id=1, source_target_pairs={{4,0},{0,4},{12,8},{8,12},{20,16},{16,20},{28,24},{24,28},{5,1},{1... | collective-permute-start | bytes 798728 | tf_op jit(solution)/shard_map/ppermute | solution.py:236
  90.0 2.2 %shard_map.71.part_ref = f32[768,256]{1,0:T(8,128)S(1)} custom-call(f32[1,2]{1,0:T(1,128)S(1)} %copy-done.2, f32[1,2]{1,0:T(1,128)S(1)} %copy-done.3, bf16[1536,1024]{1,0:T(8,128)(2,1)S(1)} %get-tuple-element.55.g_ref, bf16[768,256]{1,0:T(8,128)(2,1)S(1)} %get-tuple-element.69.src_ref, bf16[1024,256]{1,0:T(8,128)(2,1)S(1)} %get-tuple-element.72.ext_ref, ...), custom_call_target="tpu_custom_call" | custom-call | flops 1207959552 | bytes 3145728 | tf_op jit(solution)/shard_map/pallas_call | solution.py:23
  92.4 1.8 %shard_map.72 = (f32[192,256]{1,0:T(8,128)S(1)}, f32[200,256]{1,0:T(8,128)S(1)}, f32[200,256]{1,0:T(8,128)S(1)}, f32[200,256]{1,0:T(8,128)S(1)}) custom-call(f32[1,2]{1,0:T(1,128)S(1)} %copy-done.3, bf16[1536,1024]{1,0:T(8,128)(2,1)S(1)} %get-tuple-element.55.g_ref, f32[768,256]{1,0:T(8,128)S(1)} %shard_map.71.part_ref, ...), custom_call_target="tpu_custom_call" | custom-call | flops 805306368 | bytes 3145728 | tf_op jit(solution)/shard_map/pallas_call | solution.py:23
  94.2 2.1 %collective-permute-start.16 = (f16[200,256]{1,0:T(8,128)(2,1)S(1)}, f16[200,256]{1,0:T(8,128)(2,1)S(1)}, u32[]{:S(2)}, u32[]{:S(2)}) collective-permute-start(f16[200,256]{1,0:T(8,128)(2,1)S(1)} %convert_element_type.145), channel_id=1, source_target_pairs={{0,3},{1,2},{2,1},{3,0},{4,7},{5,6},{6,5},{7,4},{8,11},{9,10},{10,... | collective-permute-start | bytes 307208 | tf_op jit(solution)/shard_map/ppermute | solution.py:279
  96.2 2.2 %shard_map.78.part_ref = f32[768,256]{1,0:T(8,128)S(1)} custom-call(f32[1,2]{1,0:T(1,128)S(1)} %copy-done.2, f32[1,2]{1,0:T(1,128)S(1)} %copy-done.3, bf16[1536,1024]{1,0:T(8,128)(2,1)S(1)} %get-tuple-element.55.g_ref, bf16[768,256]{1,0:T(8,128)(2,1)S(1)} %get-tuple-element.91.src_ref, bf16[1024,256]{1,0:T(8,128)(2,1)S(1)} %get-tuple-element.94.ext_ref, ...), custom_call_target="tpu_custom_call" | custom-call | flops 1207959552 | bytes 3145728 | tf_op jit(solution)/shard_map/pallas_call | solution.py:23
  98.4 0.1 collective-permute-start.15
  98.5 1.5 %collective-permute-start.14 = (f16[200,256]{1,0:T(8,128)(2,1)S(1)}, f16[200,256]{1,0:T(8,128)(2,1)S(1)}, u32[]{:S(2)}, u32[]{:S(2)}) collective-permute-start(f16[200,256]{1,0:T(8,128)(2,1)S(1)} %convert_element_type.141), channel_id=1, source_target_pairs={{0,1},{1,0},{2,3},{3,2},{4,5},{5,4},{6,7},{7,6},{8,9},{9,8},{10,11... | collective-permute-start | bytes 307208 | tf_op jit(solution)/shard_map/ppermute | solution.py:279
  100.2 1.8 %shard_map.79 = (f32[192,256]{1,0:T(8,128)S(1)}, f32[200,256]{1,0:T(8,128)S(1)}, f32[200,256]{1,0:T(8,128)S(1)}, f32[200,256]{1,0:T(8,128)S(1)}) custom-call(f32[1,2]{1,0:T(1,128)S(1)} %copy-done.3, bf16[1536,1024]{1,0:T(8,128)(2,1)S(1)} %get-tuple-element.55.g_ref, f32[768,256]{1,0:T(8,128)S(1)} %shard_map.78.part_ref, ...), custom_call_target="tpu_custom_call" | custom-call | flops 805306368 | bytes 3145728 | tf_op jit(solution)/shard_map/pallas_call | solution.py:23
  102.0 2.1 %collective-permute-start.31 = (f16[200,256]{1,0:T(8,128)(2,1)S(1)}, f16[200,256]{1,0:T(8,128)(2,1)S(1)}, u32[]{:S(2)}, u32[]{:S(2)}) collective-permute-start(f16[200,256]{1,0:T(8,128)(2,1)S(1)} %convert_element_type.166), channel_id=1, source_target_pairs={{0,3},{1,2},{2,1},{3,0},{4,7},{5,6},{6,5},{7,4},{8,11},{9,10},{10,... | collective-permute-start | bytes 307208 | tf_op jit(solution)/shard_map/ppermute | solution.py:279
  104.1 1.5 %collective-permute-start.29 = (f16[200,256]{1,0:T(8,128)(2,1)S(1)}, f16[200,256]{1,0:T(8,128)(2,1)S(1)}, u32[]{:S(2)}, u32[]{:S(2)}) collective-permute-start(f16[200,256]{1,0:T(8,128)(2,1)S(1)} %convert_element_type.162), channel_id=1, source_target_pairs={{0,1},{1,0},{2,3},{3,2},{4,5},{5,4},{6,7},{7,6},{8,9},{9,8},{10,11... | collective-permute-start | bytes 307208 | tf_op jit(solution)/shard_map/ppermute | solution.py:279
  105.8 1.8 %collective-permute-done.31 = f16[200,256]{1,0:T(8,128)(2,1)S(1)} collective-permute-done((f16[200,256]{1,0:T(8,128)(2,1)S(1)}, f16[200,256]{1,0:T(8,128)(2,1)S(1)}, u32[]{:S(2)}, u32[]{:S(2)}) %collective-permute-start.31) | collective-permute-done | bytes 102432 | tf_op jit(solution)/shard_map/ppermute | solution.py:279
  107.6 6.5 %collective-permute-done.30 = f16[200,256]{1,0:T(8,128)(2,1)S(1)} collective-permute-done((f16[200,256]{1,0:T(8,128)(2,1)S(1)}, f16[200,256]{1,0:T(8,128)(2,1)S(1)}, u32[]{:S(2)}, u32[]{:S(2)}) %collective-permute-start.30) | collective-permute-done | bytes 102432 | tf_op jit(solution)/shard_map/ppermute | solution.py:279
  114.2 0.1 fusion.8
  114.3 0.1 fusion
  114.4 0.8 pad_maximum_fusion
  (85 shorter events, 1.3 us)
Async XLA Ops:
  0.7 1.4 %copy-start = (f32[768,512]{1,0:T(8,128)S(1)}, f32[768,512]{1,0:T(8,128)}, u32[]{:S(2)}) copy-start(f32[768,512]{1,0:T(8,128)} %state_hbm.3) | copy-start | bytes 4718596
  2.5 12.5 %collective-permute-start = (bf16[128,512]{1,0:T(8,128)(2,1)S(1)}, bf16[128,512]{1,0:T(8,128)(2,1)S(1)}, u32[]{:S(2)}, u32[]{:S(2)}) collective-permute-start(bf16[128,512]{1,0:T(8,128)(2,1)S(1)} %get-tuple-element.58), channel_id=1, source_target_pairs={{4,0},{0,4},{12,8},{8,12},{20,16},{16,20},{28,24},{24,28},{5,1},{1... | collective-permute-start | bytes 393224 | tf_op jit(solution)/shard_map/ppermute | solution.py:236
  3.3 11.7 %collective-permute-start.1 = (bf16[128,512]{1,0:T(8,128)(2,1)S(1)}, bf16[128,512]{1,0:T(8,128)(2,1)S(1)}, u32[]{:S(2)}, u32[]{:S(2)}) collective-permute-start(bf16[128,512]{1,0:T(8,128)(2,1)S(1)} %get-tuple-element.59), channel_id=1, source_target_pairs={{8,4},{4,8},{16,12},{12,16},{24,20},{20,24},{9,5},{5,9},{17,13},{1... | collective-permute-start | bytes 393224 | tf_op jit(solution)/shard_map/ppermute | solution.py:236
  6.3 1.4 %copy-start.1 = (f32[768,512]{1,0:T(8,128)S(1)}, f32[768,512]{1,0:T(8,128)}, u32[]{:S(2)}) copy-start(f32[768,512]{1,0:T(8,128)} %state_hbm.3) | copy-start | bytes 4718596
  7.7 1.9 %copy-start.4 = (bf16[1,768,2048]{2,1,0:T(8,128)(2,1)S(1)}, bf16[1,768,2048]{2,1,0:T(8,128)(2,1)}, u32[]{:S(2)}) copy-start(bf16[1,768,2048]{2,1,0:T(8,128)(2,1)} %inv_hbm.1) | copy-start | bytes 9437188
  9.6 0.7 copy-start.5
  10.3 4.7 %copy-start.2 = (f32[1,2]{1,0:T(1,128)S(1)}, f32[1,2]{1,0:T(1,128)}, u32[]{:S(2)}) copy-start(f32[1,2]{1,0:T(1,128)} %shift_ref.15) | copy-start | bytes 28
  16.9 11.4 %collective-permute-start.3 = (f16[520,256]{1,0:T(8,128)(2,1)S(1)}, f16[520,256]{1,0:T(8,128)(2,1)S(1)}, u32[]{:S(2)}, u32[]{:S(2)}) collective-permute-start(f16[520,256]{1,0:T(8,128)(2,1)S(1)} %convert_element_type.128), channel_id=1, source_target_pairs={{8,4},{4,8},{16,12},{12,16},{24,20},{20,24},{9,5},{5,9},{17,13},{1... | collective-permute-start | bytes 798728 | tf_op jit(solution)/shard_map/ppermute | solution.py:236
  19.5 8.9 %collective-permute-start.2 = (f16[520,256]{1,0:T(8,128)(2,1)S(1)}, f16[520,256]{1,0:T(8,128)(2,1)S(1)}, u32[]{:S(2)}, u32[]{:S(2)}) collective-permute-start(f16[520,256]{1,0:T(8,128)(2,1)S(1)} %convert_element_type.126), channel_id=1, source_target_pairs={{4,0},{0,4},{12,8},{8,12},{20,16},{16,20},{28,24},{24,28},{5,1},{1... | collective-permute-start | bytes 798728 | tf_op jit(solution)/shard_map/ppermute | solution.py:236
  20.5 5.6 %copy-start.3 = (f32[1,2]{1,0:T(1,128)S(1)}, f32[1,2]{1,0:T(1,128)}, u32[]{:S(2)}) copy-start(f32[1,2]{1,0:T(1,128)} %weight_ref.15) | copy-start | bytes 28
  22.4 13.9 %collective-permute-start.18 = (f16[520,256]{1,0:T(8,128)(2,1)S(1)}, f16[520,256]{1,0:T(8,128)(2,1)S(1)}, u32[]{:S(2)}, u32[]{:S(2)}) collective-permute-start(f16[520,256]{1,0:T(8,128)(2,1)S(1)} %convert_element_type.149), channel_id=1, source_target_pairs={{8,4},{4,8},{16,12},{12,16},{24,20},{20,24},{9,5},{5,9},{17,13},{1... | collective-permute-start | bytes 798728 | tf_op jit(solution)/shard_map/ppermute | solution.py:236
  24.7 11.6 %collective-permute-start.17 = (f16[520,256]{1,0:T(8,128)(2,1)S(1)}, f16[520,256]{1,0:T(8,128)(2,1)S(1)}, u32[]{:S(2)}, u32[]{:S(2)}) collective-permute-start(f16[520,256]{1,0:T(8,128)(2,1)S(1)} %convert_element_type.147), channel_id=1, source_target_pairs={{4,0},{0,4},{12,8},{8,12},{20,16},{16,20},{28,24},{24,28},{5,1},{1... | collective-permute-start | bytes 798728 | tf_op jit(solution)/shard_map/ppermute | solution.py:236
  30.2 11.3 %collective-permute-start.6 = (f16[200,256]{1,0:T(8,128)(2,1)S(1)}, f16[200,256]{1,0:T(8,128)(2,1)S(1)}, u32[]{:S(2)}, u32[]{:S(2)}) collective-permute-start(f16[200,256]{1,0:T(8,128)(2,1)S(1)} %convert_element_type.134), channel_id=1, source_target_pairs={{0,3},{1,2},{2,1},{3,0},{4,7},{5,6},{6,5},{7,4},{8,11},{9,10},{10,... | collective-permute-start | bytes 307208 | tf_op jit(solution)/shard_map/ppermute | solution.py:279
  35.9 7.1 %collective-permute-start.5 = (f16[200,256]{1,0:T(8,128)(2,1)S(1)}, f16[200,256]{1,0:T(8,128)(2,1)S(1)}, u32[]{:S(2)}, u32[]{:S(2)}) collective-permute-start(f16[200,256]{1,0:T(8,128)(2,1)S(1)} %convert_element_type.132), channel_id=1, source_target_pairs={{0,2},{1,3},{2,0},{3,1},{4,6},{5,7},{6,4},{7,5},{8,10},{9,11},{10,... | collective-permute-start | bytes 307208 | tf_op jit(solution)/shard_map/ppermute | solution.py:279
  35.9 7.1 %collective-permute-start.4 = (f16[200,256]{1,0:T(8,128)(2,1)S(1)}, f16[200,256]{1,0:T(8,128)(2,1)S(1)}, u32[]{:S(2)}, u32[]{:S(2)}) collective-permute-start(f16[200,256]{1,0:T(8,128)(2,1)S(1)} %convert_element_type.130), channel_id=1, source_target_pairs={{0,1},{1,0},{2,3},{3,2},{4,5},{5,4},{6,7},{7,6},{8,9},{9,8},{10,11... | collective-permute-start | bytes 307208 | tf_op jit(solution)/shard_map/ppermute | solution.py:279
  38.2 5.7 %collective-permute-start.21 = (f16[200,256]{1,0:T(8,128)(2,1)S(1)}, f16[200,256]{1,0:T(8,128)(2,1)S(1)}, u32[]{:S(2)}, u32[]{:S(2)}) collective-permute-start(f16[200,256]{1,0:T(8,128)(2,1)S(1)} %convert_element_type.155), channel_id=1, source_target_pairs={{0,3},{1,2},{2,1},{3,0},{4,7},{5,6},{6,5},{7,4},{8,11},{9,10},{10,... | collective-permute-start | bytes 307208 | tf_op jit(solution)/shard_map/ppermute | solution.py:279
  41.5 10.1 %collective-permute-start.20 = (f16[200,256]{1,0:T(8,128)(2,1)S(1)}, f16[200,256]{1,0:T(8,128)(2,1)S(1)}, u32[]{:S(2)}, u32[]{:S(2)}) collective-permute-start(f16[200,256]{1,0:T(8,128)(2,1)S(1)} %convert_element_type.153), channel_id=1, source_target_pairs={{0,2},{1,3},{2,0},{3,1},{4,6},{5,7},{6,4},{7,5},{8,10},{9,11},{10,... | collective-permute-start | bytes 307208 | tf_op jit(solution)/shard_map/ppermute | solution.py:279
  41.5 10.2 %collective-permute-start.19 = (f16[200,256]{1,0:T(8,128)(2,1)S(1)}, f16[200,256]{1,0:T(8,128)(2,1)S(1)}, u32[]{:S(2)}, u32[]{:S(2)}) collective-permute-start(f16[200,256]{1,0:T(8,128)(2,1)S(1)} %convert_element_type.151), channel_id=1, source_target_pairs={{0,1},{1,0},{2,3},{3,2},{4,5},{5,4},{6,7},{7,6},{8,9},{9,8},{10,11... | collective-permute-start | bytes 307208 | tf_op jit(solution)/shard_map/ppermute | solution.py:279
  51.9 5.7 %collective-permute-start.9 = (bf16[192,256]{1,0:T(8,128)(2,1)S(1)}, bf16[192,256]{1,0:T(8,128)(2,1)S(1)}, u32[]{:S(2)}, u32[]{:S(2)}) collective-permute-start(bf16[192,256]{1,0:T(8,128)(2,1)S(1)} %get-tuple-element.103.own_ref), channel_id=1, source_target_pairs={{0,3},{1,2},{2,1},{3,0},{4,7},{5,6},{6,5},{7,4},{8,11},{9,10},{10,... | collective-permute-start | bytes 294920 | tf_op jit(solution)/shard_map/ppermute | solution.py:284
  53.9 8.7 %collective-permute-start.8 = (bf16[192,256]{1,0:T(8,128)(2,1)S(1)}, bf16[192,256]{1,0:T(8,128)(2,1)S(1)}, u32[]{:S(2)}, u32[]{:S(2)}) collective-permute-start(bf16[192,256]{1,0:T(8,128)(2,1)S(1)} %get-tuple-element.103.own_ref), channel_id=1, source_target_pairs={{0,2},{1,3},{2,0},{3,1},{4,6},{5,7},{6,4},{7,5},{8,10},{9,11},{10,... | collective-permute-start | bytes 294920 | tf_op jit(solution)/shard_map/ppermute | solution.py:284
  53.9 8.7 %collective-permute-start.7 = (bf16[192,256]{1,0:T(8,128)(2,1)S(1)}, bf16[192,256]{1,0:T(8,128)(2,1)S(1)}, u32[]{:S(2)}, u32[]{:S(2)}) collective-permute-start(bf16[192,256]{1,0:T(8,128)(2,1)S(1)} %get-tuple-element.103.own_ref), channel_id=1, source_target_pairs={{0,1},{1,0},{2,3},{3,2},{4,5},{5,4},{6,7},{7,6},{8,9},{9,8},{10,11... | collective-permute-start | bytes 294920 | tf_op jit(solution)/shard_map/ppermute | solution.py:284
  62.7 6.3 %collective-permute-start.10 = (bf16[128,256]{1,0:T(8,128)(2,1)S(1)}, bf16[128,256]{1,0:T(8,128)(2,1)S(1)}, u32[]{:S(2)}, u32[]{:S(2)}) collective-permute-start(bf16[128,256]{1,0:T(8,128)(2,1)S(1)} %get-tuple-element.70), channel_id=1, source_target_pairs={{4,0},{0,4},{12,8},{8,12},{20,16},{16,20},{28,24},{24,28},{5,1},{1... | collective-permute-start | bytes 196616 | tf_op jit(solution)/shard_map/ppermute | solution.py:236
  63.3 5.9 %collective-permute-start.11 = (bf16[128,256]{1,0:T(8,128)(2,1)S(1)}, bf16[128,256]{1,0:T(8,128)(2,1)S(1)}, u32[]{:S(2)}, u32[]{:S(2)}) collective-permute-start(bf16[128,256]{1,0:T(8,128)(2,1)S(1)} %get-tuple-element.71), channel_id=1, source_target_pairs={{8,4},{4,8},{16,12},{12,16},{24,20},{20,24},{9,5},{5,9},{17,13},{1... | collective-permute-start | bytes 196616 | tf_op jit(solution)/shard_map/ppermute | solution.py:236
  65.4 9.9 %collective-permute-start.24 = (bf16[192,256]{1,0:T(8,128)(2,1)S(1)}, bf16[192,256]{1,0:T(8,128)(2,1)S(1)}, u32[]{:S(2)}, u32[]{:S(2)}) collective-permute-start(bf16[192,256]{1,0:T(8,128)(2,1)S(1)} %get-tuple-element.104.own_ref), channel_id=1, source_target_pairs={{0,3},{1,2},{2,1},{3,0},{4,7},{5,6},{6,5},{7,4},{8,11},{9,10},{10,... | collective-permute-start | bytes 294920 | tf_op jit(solution)/shard_map/ppermute | solution.py:284
  67.5 9.0 %collective-permute-start.23 = (bf16[192,256]{1,0:T(8,128)(2,1)S(1)}, bf16[192,256]{1,0:T(8,128)(2,1)S(1)}, u32[]{:S(2)}, u32[]{:S(2)}) collective-permute-start(bf16[192,256]{1,0:T(8,128)(2,1)S(1)} %get-tuple-element.104.own_ref), channel_id=1, source_target_pairs={{0,2},{1,3},{2,0},{3,1},{4,6},{5,7},{6,4},{7,5},{8,10},{9,11},{10,... | collective-permute-start | bytes 294920 | tf_op jit(solution)/shard_map/ppermute | solution.py:284
  67.5 9.0 %collective-permute-start.22 = (bf16[192,256]{1,0:T(8,128)(2,1)S(1)}, bf16[192,256]{1,0:T(8,128)(2,1)S(1)}, u32[]{:S(2)}, u32[]{:S(2)}) collective-permute-start(bf16[192,256]{1,0:T(8,128)(2,1)S(1)} %get-tuple-element.104.own_ref), channel_id=1, source_target_pairs={{0,1},{1,0},{2,3},{3,2},{4,5},{5,4},{6,7},{7,6},{8,9},{9,8},{10,11... | collective-permute-start | bytes 294920 | tf_op jit(solution)/shard_map/ppermute | solution.py:284
  71.0 21.2 %collective-permute-start.13 = (f16[520,256]{1,0:T(8,128)(2,1)S(1)}, f16[520,256]{1,0:T(8,128)(2,1)S(1)}, u32[]{:S(2)}, u32[]{:S(2)}) collective-permute-start(f16[520,256]{1,0:T(8,128)(2,1)S(1)} %convert_element_type.139), channel_id=1, source_target_pairs={{8,4},{4,8},{16,12},{12,16},{24,20},{20,24},{9,5},{5,9},{17,13},{1... | collective-permute-start | bytes 798728 | tf_op jit(solution)/shard_map/ppermute | solution.py:236
  75.2 17.1 %collective-permute-start.12 = (f16[520,256]{1,0:T(8,128)(2,1)S(1)}, f16[520,256]{1,0:T(8,128)(2,1)S(1)}, u32[]{:S(2)}, u32[]{:S(2)}) collective-permute-start(f16[520,256]{1,0:T(8,128)(2,1)S(1)} %convert_element_type.137), channel_id=1, source_target_pairs={{4,0},{0,4},{12,8},{8,12},{20,16},{16,20},{28,24},{24,28},{5,1},{1... | collective-permute-start | bytes 798728 | tf_op jit(solution)/shard_map/ppermute | solution.py:236
  76.5 2.6 %collective-permute-start.25 = (bf16[128,256]{1,0:T(8,128)(2,1)S(1)}, bf16[128,256]{1,0:T(8,128)(2,1)S(1)}, u32[]{:S(2)}, u32[]{:S(2)}) collective-permute-start(bf16[128,256]{1,0:T(8,128)(2,1)S(1)} %get-tuple-element.92), channel_id=1, source_target_pairs={{4,0},{0,4},{12,8},{8,12},{20,16},{16,20},{28,24},{24,28},{5,1},{1... | collective-permute-start | bytes 196616 | tf_op jit(solution)/shard_map/ppermute | solution.py:236
  77.2 5.9 %collective-permute-start.26 = (bf16[128,256]{1,0:T(8,128)(2,1)S(1)}, bf16[128,256]{1,0:T(8,128)(2,1)S(1)}, u32[]{:S(2)}, u32[]{:S(2)}) collective-permute-start(bf16[128,256]{1,0:T(8,128)(2,1)S(1)} %get-tuple-element.93), channel_id=1, source_target_pairs={{8,4},{4,8},{16,12},{12,16},{24,20},{20,24},{9,5},{5,9},{17,13},{1... | collective-permute-start | bytes 196616 | tf_op jit(solution)/shard_map/ppermute | solution.py:236
  85.0 15.1 %collective-permute-start.28 = (f16[520,256]{1,0:T(8,128)(2,1)S(1)}, f16[520,256]{1,0:T(8,128)(2,1)S(1)}, u32[]{:S(2)}, u32[]{:S(2)}) collective-permute-start(f16[520,256]{1,0:T(8,128)(2,1)S(1)} %convert_element_type.160), channel_id=1, source_target_pairs={{8,4},{4,8},{16,12},{12,16},{24,20},{20,24},{9,5},{5,9},{17,13},{1... | collective-permute-start | bytes 798728 | tf_op jit(solution)/shard_map/ppermute | solution.py:236
  88.7 11.4 %collective-permute-start.27 = (f16[520,256]{1,0:T(8,128)(2,1)S(1)}, f16[520,256]{1,0:T(8,128)(2,1)S(1)}, u32[]{:S(2)}, u32[]{:S(2)}) collective-permute-start(f16[520,256]{1,0:T(8,128)(2,1)S(1)} %convert_element_type.158), channel_id=1, source_target_pairs={{4,0},{0,4},{12,8},{8,12},{20,16},{16,20},{28,24},{24,28},{5,1},{1... | collective-permute-start | bytes 798728 | tf_op jit(solution)/shard_map/ppermute | solution.py:236
  94.2 9.9 %collective-permute-start.16 = (f16[200,256]{1,0:T(8,128)(2,1)S(1)}, f16[200,256]{1,0:T(8,128)(2,1)S(1)}, u32[]{:S(2)}, u32[]{:S(2)}) collective-permute-start(f16[200,256]{1,0:T(8,128)(2,1)S(1)} %convert_element_type.145), channel_id=1, source_target_pairs={{0,3},{1,2},{2,1},{3,0},{4,7},{5,6},{6,5},{7,4},{8,11},{9,10},{10,... | collective-permute-start | bytes 307208 | tf_op jit(solution)/shard_map/ppermute | solution.py:279
  98.4 7.2 %collective-permute-start.15 = (f16[200,256]{1,0:T(8,128)(2,1)S(1)}, f16[200,256]{1,0:T(8,128)(2,1)S(1)}, u32[]{:S(2)}, u32[]{:S(2)}) collective-permute-start(f16[200,256]{1,0:T(8,128)(2,1)S(1)} %convert_element_type.143), channel_id=1, source_target_pairs={{0,2},{1,3},{2,0},{3,1},{4,6},{5,7},{6,4},{7,5},{8,10},{9,11},{10,... | collective-permute-start | bytes 307208 | tf_op jit(solution)/shard_map/ppermute | solution.py:279
  98.5 7.2 %collective-permute-start.14 = (f16[200,256]{1,0:T(8,128)(2,1)S(1)}, f16[200,256]{1,0:T(8,128)(2,1)S(1)}, u32[]{:S(2)}, u32[]{:S(2)}) collective-permute-start(f16[200,256]{1,0:T(8,128)(2,1)S(1)} %convert_element_type.141), channel_id=1, source_target_pairs={{0,1},{1,0},{2,3},{3,2},{4,5},{5,4},{6,7},{7,6},{8,9},{9,8},{10,11... | collective-permute-start | bytes 307208 | tf_op jit(solution)/shard_map/ppermute | solution.py:279
  102.0 5.6 %collective-permute-start.31 = (f16[200,256]{1,0:T(8,128)(2,1)S(1)}, f16[200,256]{1,0:T(8,128)(2,1)S(1)}, u32[]{:S(2)}, u32[]{:S(2)}) collective-permute-start(f16[200,256]{1,0:T(8,128)(2,1)S(1)} %convert_element_type.166), channel_id=1, source_target_pairs={{0,3},{1,2},{2,1},{3,0},{4,7},{5,6},{6,5},{7,4},{8,11},{9,10},{10,... | collective-permute-start | bytes 307208 | tf_op jit(solution)/shard_map/ppermute | solution.py:279
  104.1 10.0 %collective-permute-start.30 = (f16[200,256]{1,0:T(8,128)(2,1)S(1)}, f16[200,256]{1,0:T(8,128)(2,1)S(1)}, u32[]{:S(2)}, u32[]{:S(2)}) collective-permute-start(f16[200,256]{1,0:T(8,128)(2,1)S(1)} %convert_element_type.164), channel_id=1, source_target_pairs={{0,2},{1,3},{2,0},{3,1},{4,6},{5,7},{6,4},{7,5},{8,10},{9,11},{10,... | collective-permute-start | bytes 307208 | tf_op jit(solution)/shard_map/ppermute | solution.py:279
  104.1 10.1 %collective-permute-start.29 = (f16[200,256]{1,0:T(8,128)(2,1)S(1)}, f16[200,256]{1,0:T(8,128)(2,1)S(1)}, u32[]{:S(2)}, u32[]{:S(2)}) collective-permute-start(f16[200,256]{1,0:T(8,128)(2,1)S(1)} %convert_element_type.162), channel_id=1, source_target_pairs={{0,1},{1,0},{2,3},{3,2},{4,5},{5,4},{6,7},{7,6},{8,9},{9,8},{10,11... | collective-permute-start | bytes 307208 | tf_op jit(solution)/shard_map/ppermute | solution.py:279

commit v4 on v3

v4 whole, which is shorter than its diff:
```python
import functools

import jax
import jax.numpy as jnp
from jax import lax
from jax.experimental import pallas as pl
from jax.experimental.pallas import tpu as pltpu
from jax.sharding import PartitionSpec as P


STEPS = 2
CHUNKS = 2
TAIL = 8
TOP = 12.0
BF16 = jnp.bfloat16
F16 = jnp.float16
F32 = jnp.float32
VMEM = pl.BlockSpec(memory_space=pltpu.VMEM)
SMEM = pl.BlockSpec(memory_space=pltpu.SMEM)


def call(kernel, outs, ins, scratch=(), flops=0, moved=0, alias=()):
    return pl.pallas_call(
        kernel,
        out_shape=[jax.ShapeDtypeStruct(s, d) for s, d in outs],
        in_specs=[s for s, _ in ins],
        out_specs=[VMEM] * len(outs),
        scratch_shapes=list(scratch),
        input_output_aliases=dict(alias),
        compiler_params=pltpu.CompilerParams(vmem_limit_bytes=16 * 2**20),
        cost_estimate=pl.CostEstimate(flops=flops, bytes_accessed=moved, transcendentals=0),
    )(*[a for _, a in ins])


def dot(a, b):
    return jnp.dot(a, b, preferred_element_type=F32)


def store_coded(ref, blocks):
    top = functools.reduce(jnp.maximum, [jnp.max(jnp.abs(b), axis=0, keepdims=True) for b in blocks])
    power = jnp.ceil(jnp.log2(jnp.maximum(top, 1e-30)))
    scale, at = jnp.exp2(TOP - power), 0
    for block in blocks:
        ref[at:at + block.shape[0]] = block * scale
        at += block.shape[0]
    ref[at:] = jnp.broadcast_to(power, (TAIL, top.shape[1]))


def pick(flag, a, b):
    return jnp.where(flag == 0, a, b)


def hop_target(pole, hop, poles):
    return pole ^ hop if poles & (poles - 1) == 0 else lax.rem(pole + hop, poles)


def hop_source(pole, hop, poles):
    return pole ^ hop if poles & (poles - 1) == 0 else lax.rem(pole + poles - hop, poles)


def hop_pairs(hop, poles):
    return [(i, i ^ hop if poles & (poles - 1) == 0 else (i + hop) % poles) for i in range(poles)]


def rows_of(index, share):
    return pl.ds(pl.multiple_of(index * share, share), share)


def column(row, count):
    return jnp.transpose(jnp.broadcast_to(row, (8, count)))[:, :1]


def start_kernel(rim, sigma_ref, order_ref, state_ref, msg1_ref, msg2_ref, wide_ref, share_ref, row_ref, *chunks):
    rows, n, share = state_ref.shape[0], wide_ref.shape[1], share_ref.shape[0]
    parity = lax.rem(lax.axis_index("sub"), 2)
    sigma = column(sigma_ref[...].reshape(1, rows), rows)
    low = (state_ref[:rim] * sigma[:rim]).astype(BF16)
    high = (state_ref[rows - rim:] * sigma[rows - rim:]).astype(BF16)
    msg1_ref[...] = pick(parity, high, low)
    msg2_ref[...] = pick(parity, low, high)
    wide_ref[...] = jnp.broadcast_to(sigma, wide_ref.shape)
    share_ref[...] = wide_ref[rows_of(lax.axis_index("pole"), share)]
    row_ref[...] = order_ref[...].astype(F32)
    for k, ref in enumerate(chunks):
        ref[...] = state_ref[:, k * n:(k + 1) * n] * sigma


def setup_kernel(row_ref, inv_ref, g_ref):
    rows, width = inv_ref.shape[1], inv_ref.shape[2] // 2
    ids = lax.broadcasted_iota(jnp.int32, (width, width), 1)
    place = (column(row_ref[...], width).astype(jnp.int32) == ids).astype(BF16)
    g_ref[:rows] = dot(inv_ref[0, :, :width], place).astype(BF16)
    g_ref[rows:] = dot(inv_ref[0, :, width:], place).astype(BF16)


def stencil(x_ref, half, lo, count, rim, far_up, far_down):
    def row(shift):
        return x_ref[half, 8 + lo + shift:8 + lo + shift + count]

    mid = 4.0 * row(0) - row(-1) - row(1)
    if far_up:
        mid = mid - row(-rim)
    if far_down:
        mid = mid - row(rim)
    return mid


def residual(x_ref, lo, count, rim, far_up, far_down, src_ref, sigma_ref, a, b):
    at = slice(lo, lo + count)
    xr, xi, sigma = x_ref[0, 8 + lo:8 + lo + count], x_ref[1, 8 + lo:8 + lo + count], sigma_ref[at]
    real = src_ref[at].astype(F32) - stencil(x_ref, 0, lo, count, rim, far_up, far_down) - sigma * (a * xr - b * xi)
    imag = -stencil(x_ref, 1, lo, count, rim, far_up, far_down) - sigma * (b * xr + a * xi)
    return real, imag


def edge_kernel(rim, lane, shift_ref, g_ref, src_ref, one_ref, two_ref, sigma_ref, ext_ref, x_ref, r_ref, msgs_ref):
    rows, n = src_ref.shape
    parity = lax.rem(lax.axis_index("sub"), 2)
    one, two = one_ref[:, lane:lane + n], two_ref[:, lane:lane + n]
    ext_ref[:rim] = pick(parity, two, one)
    ext_ref[rim:rim + rows] = src_ref[...].astype(BF16)
    ext_ref[rim + rows:] = pick(parity, one, two)
    a, b = shift_ref[0, 0], shift_ref[0, 1]
    span, step = 2 * rim, 32
    x_ref[:, :8] = jnp.zeros((2, 8, n), F32)
    x_ref[:, 8 + rows:] = jnp.zeros((2, 8, n), F32)
    for lo in (0, rows - span):
        for half in range(2):
            x_ref[half, 8 + lo:8 + lo + span] = dot(g_ref[half * rows + lo:half * rows + lo + span], ext_ref[...])
    for side, lo in ((0, 0), (1, rows - rim)):
        for k in range(0, rim, step):
            out = residual(x_ref, lo + k, step, rim, side == 1, side == 0, src_ref, sigma_ref, a, b)
            for half in range(2):
                r_ref[side, half, k:k + step] = out[half]
        blocks = [x_ref[half, 8 + lo:8 + lo + rim] for half in range(2)] + [r_ref[side, half] for half in range(2)]
        store_coded(msgs_ref.at[parity if side else 1 - parity], blocks)


def add_product(rows, g_ref, cols, er, ei, wr, wi, base, out_ref):
    block = rows // 3 if rows % 384 == 0 else rows
    for lo in range(0, rows, block):
        gr, gi = [jnp.concatenate([g_ref[half + lo:half + lo + block, c] for c in cols], axis=1) for half in (0, rows)]
        real = dot(gr, er) - dot(gi, ei)
        imag = dot(gr, ei) + dot(gi, er)
        out_ref[lo:lo + block] = base(lo, block) + (wr * real - wi * imag)


def middle_kernel(rim, shift_ref, weight_ref, g_ref, src_ref, ext_ref, outer_ref, sigma_ref, out_ref, x_ref, e_ref):
    rows, _ = src_ref.shape
    span, step = 2 * rim, 32
    a, b = shift_ref[0, 0], shift_ref[0, 1]
    wr, wi = 2.0 * weight_ref[0, 0], 2.0 * weight_ref[0, 1]
    if rows > 2 * span:
        for half in range(2):
            x_ref[half, 8 + span:8 + rows - span] = dot(g_ref[half * rows + span:(half + 1) * rows - span], ext_ref[...])
    for lo in range(rim, rows - rim, step):
        out = residual(x_ref, lo, step, rim, True, True, src_ref, sigma_ref, a, b)
        for half in range(2):
            e_ref[half, lo - rim:lo - rim + step] = out[half].astype(BF16)

    def base(lo, count):
        return wr * x_ref[0, 8 + lo:8 + lo + count] - wi * x_ref[1, 8 + lo:8 + lo + count]

    add_product(rows, g_ref, [slice(span, rows)], e_ref[0], e_ref[1], wr, wi, base, out_ref)


def last_kernel(rim, hops, weight_ref, g_ref, part_ref, x_ref, r_ref, got_ref, *rest):
    own_ref, msgs, u_ref, e_ref = rest[0], rest[1:1 + hops], rest[1 + hops], rest[2 + hops]
    rows, _ = part_ref.shape
    share = own_ref.shape[0]
    sub, pole = lax.axis_index("sub"), lax.axis_index("pole")
    parity = lax.rem(sub, 2)
    wr, wi = 2.0 * weight_ref[0, 0], 2.0 * weight_ref[0, 1]
    before_ref, after_ref = got_ref.at[1 - parity], got_ref.at[parity]
    inner_up = jnp.where(sub == 0, 0.0, 1.0)
    inner_down = jnp.where(sub == lax.axis_size("sub") - 1, 0.0, 1.0)
    up_scale = jnp.exp2(before_ref[4 * rim:4 * rim + 1] - TOP)
    down_scale = jnp.exp2(after_ref[4 * rim:4 * rim + 1] - TOP)
    at = lax.broadcasted_iota(jnp.int32, (rim, 1), 0)
    for half in range(2):
        x, r = slice(half * rim, (half + 1) * rim), slice((2 + half) * rim, (3 + half) * rim)
        xb, qb = before_ref[x] * up_scale, before_ref[r] * up_scale
        xa, qa = after_ref[x] * down_scale, after_ref[r] * down_scale
        low, high = x_ref[half, 8:8 + rim], x_ref[half, 8 + rows - rim:8 + rows]
        above = qb + low + jnp.where(at == rim - 1, low[:1], 0.0)
        below = qa + high + jnp.where(at == 0, high[rim - 1:], 0.0)
        head = r_ref[0, half] + xb + jnp.where(at == 0, xb[rim - 1:], 0.0)
        foot = r_ref[1, half] + xa + jnp.where(at == rim - 1, xa[:1], 0.0)
        e_ref[half, :rim] = (inner_up * above).astype(BF16)
        e_ref[half, rim:2 * rim] = head.astype(BF16)
        e_ref[half, 2 * rim:3 * rim] = foot.astype(BF16)
        e_ref[half, 3 * rim:] = (inner_down * below).astype(BF16)
    add_product(
        rows, g_ref, [slice(0, 2 * rim), slice(rows, rows + 2 * rim)], e_ref[0], e_ref[1], wr, wi,
        lambda lo, count: part_ref[lo:lo + count], u_ref,
    )
    own_ref[...] = u_ref[rows_of(pole, share)]
    for hop, ref in enumerate(msgs):
        store_coded(ref, [u_ref[rows_of(hop_target(pole, hop + 1, hops + 1), share)]])


def sum_kernel(own_ref, *rest):
    got, total_ref = rest[:-1], rest[-1]
    share = own_ref.shape[0]
    total = own_ref[...]
    for ref in got:
        if ref.shape[0] == share:
            total = total * ref[...]
        else:
            total = total + ref[:share] * jnp.exp2(ref[share:share + 1] - TOP)
    total_ref[...] = total.astype(total_ref.dtype)


def join_kernel(rim, own_ref, *rest):
    got, (src_ref, msg1_ref, msg2_ref) = rest[:-3], rest[-3:]
    share, rows, poles = own_ref.shape[0], src_ref.shape[0], len(got) + 1
    parity, pole = lax.rem(lax.axis_index("sub"), 2), lax.axis_index("pole")
    src_ref[rows_of(pole, share)] = own_ref[...]
    for hop, ref in enumerate(got):
        src_ref[rows_of(hop_source(pole, hop + 1, poles), share)] = ref[...]
    low, high = src_ref[:rim], src_ref[rows - rim:]
    msg1_ref[...] = pick(parity, high, low)
    msg2_ref[...] = pick(parity, low, high)


def shards(state, conductivity, pole_shift, pole_weight, order_list, inverse):
    rows, columns = state.shape
    order = order_list.shape[1]
    rim = (order - rows) // 2
    subs, poles = lax.axis_size("sub"), lax.axis_size("pole")
    share, hops = rows // poles, poles - 1
    n = columns // CHUNKS
    pairs1 = [(i ^ 1, i) for i in range(subs) if i ^ 1 < subs]
    pairs2 = [(j, i) for i in range(subs) for j in [((i + 1) ^ 1) - 1] if 0 <= j < subs]

    def exchange(one, two):
        one = lax.ppermute(one, "sub", pairs1)
        two = lax.ppermute(two, "sub", pairs2)
        return one, two

    one, two, sigma, sigma_share, order_row, *sources = call(
        functools.partial(start_kernel, rim),
        [((rim, columns), BF16), ((rim, columns), BF16), ((rows, n), F32), ((share, n), F32), ((1, order), F32)]
        + [((rows, n), F32)] * CHUNKS,
        [(VMEM, conductivity), (VMEM, order_list), (VMEM, state)], moved=8 * rows * columns,
    )
    first_halo = exchange(one, two)
    (g,) = call(
        setup_kernel, [((2 * rows, order), BF16)], [(VMEM, order_row), (VMEM, inverse)],
        flops=4 * rows * order * order, moved=6 * rows * order,
    )

    def sweep(source, got, lane):
        ext, x, r, msgs = call(
            functools.partial(edge_kernel, rim, lane),
            [((order, n), BF16), ((2, rows + 16, n), F32), ((2, 2, rim, n), F32), ((2, 4 * rim + TAIL, n), F32)],
            [(SMEM, pole_shift), (VMEM, g), (VMEM, source), (VMEM, got[0]), (VMEM, got[1]), (VMEM, sigma)],
            flops=16 * rim * order * n, moved=4 * rows * order,
        )
        got = exchange(msgs[0].astype(F16), msgs[1].astype(F16))
        part, x = call(
            functools.partial(middle_kernel, rim), [((rows, n), F32), ((2, rows + 16, n), F32)],
            [(SMEM, pole_shift), (SMEM, pole_weight), (VMEM, g), (VMEM, source), (VMEM, ext), (VMEM, x), (VMEM, sigma)],
            [pltpu.VMEM((2, rows - 2 * rim, n), BF16)],
            flops=8 * rows * rows * n, moved=4 * rows * order, alias={5: 1},
        )
        return call(
            functools.partial(last_kernel, rim, hops),
            [((share, n), F32)] + [((share + TAIL, n), F32)] * hops,
            [(SMEM, pole_weight), (VMEM, g), (VMEM, part), (VMEM, x), (VMEM, r), (VMEM, jnp.stack(got).astype(F32))],
            [pltpu.VMEM((rows, n), F32), pltpu.VMEM((2, 4 * rim, n), BF16)],
            flops=8 * rows * 4 * rim * n, moved=4 * rows * order,
        )

    def reduced(sent, factor):
        own, *sent = sent
        got = []
        for hop, block in enumerate(sent):
            got.append(lax.ppermute(block.astype(F16), "pole", hop_pairs(hop + 1, poles)))
        ins = [own] + [x.astype(F32) for x in got] + factor
        return call(
            sum_kernel, [((share, n), BF16 if factor else F32)], [(VMEM, x) for x in ins],
            moved=4 * rows * n,
        )[0]

    def gathered(own):
        got = []
        for hop in range(hops):
            got.append(lax.ppermute(own, "pole", hop_pairs(hop + 1, poles)))
        return call(
            functools.partial(join_kernel, rim),
            [((rows, n), BF16), ((rim, n), BF16), ((rim, n), BF16)],
            [(VMEM, own)] + [(VMEM, x) for x in got], moved=4 * rows * n,
        )

    results = []
    for chunk in range(CHUNKS):
        source, halo = sources[chunk], first_halo
        for step in range(STEPS):
            factor = [sigma_share] if step + 1 < STEPS else []
            total = reduced(sweep(source, halo, 0 if step else chunk * n), factor)
            if step + 1 < STEPS:
                source, one, two = gathered(total)
                halo = exchange(one, two)
        results.append(total)
    return jnp.concatenate(results, axis=1) if CHUNKS > 1 else results[0]


def solution(mesh):
    placed = (
        P("sub", None),
        P("sub"),
        P("pole", None),
        P("pole", None),
        P("sub", None),
        P("pole", "sub", None),
    )
    return jax.shard_map(
        shards, mesh=mesh, in_specs=placed, out_specs=P(("sub", "pole"), None), check_vma=False
    )
```

time: 116 us -> 110 us (0.948)
  waiting for transfers between devices: 30.3 us -> 23.9 us
  starting transfers between devices: 47.7 us -> 50.2 us
    ppermute x20, waiting for transfers between devices: 12.3 us -> 4.1 us  [the longest x6 3.94 us: gathered(): got.append(lax.ppermute(own, 'pole', hop_pairs(hop + 1, poles)))]
    ppermute x20, starting transfers between devices: 32.9 us -> 35.5 us  [the longest x7 17.4 us: exchange(): two = lax.ppermute(two, 'sub', pairs2)]
    ppermute x12, waiting for transfers between devices: 18 us -> 19.8 us  [reduced(): lax.ppermute(block.astype(F16), 'pole', hop_pairs(hop + 1, poles))]
    pallas_call x16 -> x20, Pallas kernels: 28.3 us -> 28.4 us  [call(): pl.pallas_call(kernel, out_shape=[jax.ShapeDtypeStruct(s, d) for s, d in...]
  transfers between devices with their start and end apart: 32 -> 32, of which waited for: 10 -> 6; matrix products, arithmetic and copies ran while one was open for 1% -> 1% of each run, Pallas kernels for 23% -> 22%
where the time goes in v4:
time: 110 us
  starting transfers between devices  50.2 us (46%)
  Pallas kernels  28.4 us (26%)
  waiting for transfers between devices  23.9 us (22%)
  local copies, waits for them, and re-layouts  5.12 us (5%)
  other arithmetic  1.86 us (2%)
    pallas_call x20, Pallas kernels, call(): pl.pallas_call(kernel, out_shape=[jax.ShapeDtypeStruct(s, d) for s, d in...  28.4 us
    ppermute x12, waiting for transfers between devices, reduced(): lax.ppermute(block.astype(F16), 'pole', hop_pairs(hop + 1, poles))  19.8 us
    ppermute x7, starting transfers between devices, exchange(): two = lax.ppermute(two, 'sub', pairs2)  17.4 us
    ppermute x12, starting transfers between devices, reduced(): lax.ppermute(block.astype(F16), 'pole', hop_pairs(hop + 1, poles))  14.7 us
    ppermute x7, starting transfers between devices, exchange(): one = lax.ppermute(one, 'sub', pairs1)  10.1 us
    ppermute x6, starting transfers between devices, gathered(): got.append(lax.ppermute(own, 'pole', hop_pairs(hop + 1, poles)))  7.95 us
    unnamed x12, local copies, waits for them, and re-layouts  4.67 us
    ppermute x6, waiting for transfers between devices, gathered(): got.append(lax.ppermute(own, 'pole', hop_pairs(hop + 1, poles)))  3.94 us
  transfers between devices with their start and end apart: 32, of which 6 were waited for; matrix products, arithmetic and copies ran while one was open for 1% of the time, Pallas kernels for 22%

profile of v4, /device:TPU:5, one launch (start us, length us, event | category | flops | bytes accessed | tf_op | source)
XLA Modules:
  0.0 110.0 jit_solution(11737156636179470605)
XLA Ops:
  0.0 1.4 %copy-done = f32[768,512]{1,0:T(8,128)S(1)} copy-done((f32[768,512]{1,0:T(8,128)S(1)}, f32[768,512]{1,0:T(8,128)}, u32[]{:S(2)}) %copy-start) | copy-done | bytes 1572888
  1.4 0.7 copy-done.3
  2.1 0.7 copy-done.4
  2.8 0.4 shard_map.64
  3.2 0.7 collective-permute-start
  3.9 3.0 %collective-permute-start.1 = (bf16[128,512]{1,0:T(8,128)(2,1)S(1)}, bf16[128,512]{1,0:T(8,128)(2,1)S(1)}, u32[]{:S(2)}, u32[]{:S(2)}) collective-permute-start(bf16[128,512]{1,0:T(8,128)(2,1)S(1)} %get-tuple-element.61), channel_id=1, source_target_pairs={{8,4},{4,8},{16,12},{12,16},{24,20},{20,24},{9,5},{5,9},{17,13},{1... | collective-permute-start | bytes 393224 | tf_op jit(solution)/shard_map/ppermute | solution.py:238
  7.0 1.9 %copy-done.5 = bf16[1,768,2048]{2,1,0:T(8,128)(2,1)S(1)} copy-done((bf16[1,768,2048]{2,1,0:T(8,128)(2,1)S(1)}, bf16[1,768,2048]{2,1,0:T(8,128)(2,1)}, u32[]{:S(2)}) %copy-start.5) | copy-done | bytes 3145752
  8.9 3.9 %shard_map.65.g_ref = bf16[1536,1024]{1,0:T(8,128)(2,1)S(1)} custom-call(f32[1,1024]{1,0:T(1,128)S(1)} %get-tuple-element.58.row_ref, bf16[1,768,2048]{2,1,0:T(8,128)(2,1)S(1)} %copy-done.5), custom_call_target="tpu_custom_call" | custom-call | flops 3221225472 | bytes 4718592 | tf_op jit(solution)/shard_map/pallas_call | solution.py:23
  12.8 1.7 %shard_map.75 = (bf16[1024,256]{1,0:T(8,128)(2,1)S(1)}, f32[2,784,256]{2,1,0:T(8,128)S(1)}, f32[2,2,128,256]{3,2,1,0:T(8,128)S(1)}, f32[2,520,256]{2,1,0:T(8,128)S(1)}) custom-call(f32[1,2]{1,0:T(1,128)S(1)} %copy-done.1, bf16[1536,1024]{1,0:T(8,128)(2,1)S(1)} %shard_map.65.g_ref, f32[768,256]{1,0:T(8,128)S(1)} %get-tuple-element.87.src_ref, ...), custom_call_target="tpu_custom_call" | custom-call | flops 536870912 | bytes 3145728 | tf_op jit(solution)/shard_map/pallas_call | solution.py:23
  14.5 0.1 convert.18
  14.6 1.7 %shard_map.66 = (bf16[1024,256]{1,0:T(8,128)(2,1)S(1)}, f32[2,784,256]{2,1,0:T(8,128)S(1)}, f32[2,2,128,256]{3,2,1,0:T(8,128)S(1)}, f32[2,520,256]{2,1,0:T(8,128)S(1)}) custom-call(f32[1,2]{1,0:T(1,128)S(1)} %copy-done.1, bf16[1536,1024]{1,0:T(8,128)(2,1)S(1)} %shard_map.65.g_ref, f32[768,256]{1,0:T(8,128)S(1)} %get-tuple-element.59.src_ref, ...), custom_call_target="tpu_custom_call" | custom-call | flops 536870912 | bytes 3145728 | tf_op jit(solution)/shard_map/pallas_call | solution.py:23
  16.3 0.1 convert.16
  16.4 0.1 slice_bitcast_fusion.7
  16.5 0.5 collective-permute-start.2
  17.0 2.1 %collective-permute-start.3 = (f16[520,256]{1,0:T(8,128)(2,1)S(1)}, f16[520,256]{1,0:T(8,128)(2,1)S(1)}, u32[]{:S(2)}, u32[]{:S(2)}) collective-permute-start(f16[520,256]{1,0:T(8,128)(2,1)S(1)} %get-tuple-element.114), channel_id=1, source_target_pairs={{8,4},{4,8},{16,12},{12,16},{24,20},{20,24},{9,5},{5,9},{17,13},{1... | collective-permute-start | bytes 798728 | tf_op jit(solution)/shard_map/ppermute | solution.py:238
  19.1 0.1 slice_bitcast_fusion.3
  19.2 1.0 collective-permute-start.17
  20.2 2.7 %collective-permute-start.18 = (f16[520,256]{1,0:T(8,128)(2,1)S(1)}, f16[520,256]{1,0:T(8,128)(2,1)S(1)}, u32[]{:S(2)}, u32[]{:S(2)}) collective-permute-start(f16[520,256]{1,0:T(8,128)(2,1)S(1)} %get-tuple-element.118), channel_id=1, source_target_pairs={{8,4},{4,8},{16,12},{12,16},{24,20},{20,24},{9,5},{5,9},{17,13},{1... | collective-permute-start | bytes 798728 | tf_op jit(solution)/shard_map/ppermute | solution.py:238
  23.0 2.4 %shard_map.76 = (f32[768,256]{1,0:T(8,128)S(1)}, f32[2,784,256]{2,1,0:T(8,128)S(1)}) custom-call(f32[1,2]{1,0:T(1,128)S(1)} %copy-done.1, f32[1,2]{1,0:T(1,128)S(1)} %copy-done.2, bf16[1536,1024]{1,0:T(8,128)(2,1)S(1)} %shard_map.65.g_ref, f32[768,256]{1,0:T(8,128)S(1)} %get-tuple-element.87.src_ref, ...), custom_call_target="tpu_custom_call", output_to_operand_aliasing={{1}: (5, {})} | custom-call | flops 1207959552 | bytes 3145728 | tf_op jit(solution)/shard_map/pallas_call | solution.py:23
  25.4 2.4 %shard_map.67 = (f32[768,256]{1,0:T(8,128)S(1)}, f32[2,784,256]{2,1,0:T(8,128)S(1)}) custom-call(f32[1,2]{1,0:T(1,128)S(1)} %copy-done.1, f32[1,2]{1,0:T(1,128)S(1)} %copy-done.2, bf16[1536,1024]{1,0:T(8,128)(2,1)S(1)} %shard_map.65.g_ref, f32[768,256]{1,0:T(8,128)S(1)} %get-tuple-element.59.src_ref, ...), custom_call_target="tpu_custom_call", output_to_operand_aliasing={{1}: (5, {})} | custom-call | flops 1207959552 | bytes 3145728 | tf_op jit(solution)/shard_map/pallas_call | solution.py:23
  27.9 0.1 maximum_convert_fusion.got_ref
  28.0 1.8 %shard_map.68 = (f32[192,256]{1,0:T(8,128)S(1)}, f32[200,256]{1,0:T(8,128)S(1)}, f32[200,256]{1,0:T(8,128)S(1)}, f32[200,256]{1,0:T(8,128)S(1)}) custom-call(f32[1,2]{1,0:T(1,128)S(1)} %copy-done.2, bf16[1536,1024]{1,0:T(8,128)(2,1)S(1)} %shard_map.65.g_ref, f32[768,256]{1,0:T(8,128)S(1)} %get-tuple-element.65.part_ref, ...), custom_call_target="tpu_custom_call" | custom-call | flops 805306368 | bytes 3145728 | tf_op jit(solution)/shard_map/pallas_call | solution.py:23
  29.8 3.4 %collective-permute-start.6 = (f16[200,256]{1,0:T(8,128)(2,1)S(1)}, f16[200,256]{1,0:T(8,128)(2,1)S(1)}, u32[]{:S(2)}, u32[]{:S(2)}) collective-permute-start(f16[200,256]{1,0:T(8,128)(2,1)S(1)} %convert_element_type.123), channel_id=1, source_target_pairs={{0,3},{1,2},{2,1},{3,0},{4,7},{5,6},{6,5},{7,4},{8,11},{9,10},{10,... | collective-permute-start | bytes 307208 | tf_op jit(solution)/shard_map/ppermute | solution.py:279
  33.2 0.4 collective-permute-start.4
  33.6 0.1 maximum_convert_fusion.2.got_ref
  33.7 1.8 %shard_map.77 = (f32[192,256]{1,0:T(8,128)S(1)}, f32[200,256]{1,0:T(8,128)S(1)}, f32[200,256]{1,0:T(8,128)S(1)}, f32[200,256]{1,0:T(8,128)S(1)}) custom-call(f32[1,2]{1,0:T(1,128)S(1)} %copy-done.2, bf16[1536,1024]{1,0:T(8,128)(2,1)S(1)} %shard_map.65.g_ref, f32[768,256]{1,0:T(8,128)S(1)} %get-tuple-element.90.part_ref, ...), custom_call_target="tpu_custom_call" | custom-call | flops 805306368 | bytes 3145728 | tf_op jit(solution)/shard_map/pallas_call | solution.py:23
  35.5 3.3 %collective-permute-start.21 = (f16[200,256]{1,0:T(8,128)(2,1)S(1)}, f16[200,256]{1,0:T(8,128)(2,1)S(1)}, u32[]{:S(2)}, u32[]{:S(2)}) collective-permute-start(f16[200,256]{1,0:T(8,128)(2,1)S(1)} %convert_element_type.141), channel_id=1, source_target_pairs={{0,3},{1,2},{2,1},{3,0},{4,7},{5,6},{6,5},{7,4},{8,11},{9,10},{10,... | collective-permute-start | bytes 307208 | tf_op jit(solution)/shard_map/ppermute | solution.py:279
  38.9 0.3 collective-permute-start.19
  39.2 5.7 %collective-permute-done.5 = f16[200,256]{1,0:T(8,128)(2,1)S(1)} collective-permute-done((f16[200,256]{1,0:T(8,128)(2,1)S(1)}, f16[200,256]{1,0:T(8,128)(2,1)S(1)}, u32[]{:S(2)}, u32[]{:S(2)}) %collective-permute-start.5) | collective-permute-done | bytes 102432 | tf_op jit(solution)/shard_map/ppermute | solution.py:279
  44.9 0.1 shard_map.69.own_ref
  45.2 3.4 %collective-permute-start.7 = (bf16[192,256]{1,0:T(8,128)(2,1)S(1)}, bf16[192,256]{1,0:T(8,128)(2,1)S(1)}, u32[]{:S(2)}, u32[]{:S(2)}) collective-permute-start(bf16[192,256]{1,0:T(8,128)(2,1)S(1)} %shard_map.69.own_ref), channel_id=1, source_target_pairs={{0,1},{1,0},{2,3},{3,2},{4,5},{5,4},{6,7},{7,6},{8,9},{9,8},{10,11... | collective-permute-start | bytes 294920 | tf_op jit(solution)/shard_map/ppermute | solution.py:289
  48.7 3.7 %collective-permute-done.20 = f16[200,256]{1,0:T(8,128)(2,1)S(1)} collective-permute-done((f16[200,256]{1,0:T(8,128)(2,1)S(1)}, f16[200,256]{1,0:T(8,128)(2,1)S(1)}, u32[]{:S(2)}, u32[]{:S(2)}) %collective-permute-start.20) | collective-permute-done | bytes 102432 | tf_op jit(solution)/shard_map/ppermute | solution.py:279
  52.4 0.1 shard_map.78.own_ref
  52.5 1.5 %collective-permute-start.24 = (bf16[192,256]{1,0:T(8,128)(2,1)S(1)}, bf16[192,256]{1,0:T(8,128)(2,1)S(1)}, u32[]{:S(2)}, u32[]{:S(2)}) collective-permute-start(bf16[192,256]{1,0:T(8,128)(2,1)S(1)} %shard_map.78.own_ref), channel_id=1, source_target_pairs={{0,3},{1,2},{2,1},{3,0},{4,7},{5,6},{6,5},{7,4},{8,11},{9,10},{10,... | collective-permute-start | bytes 294920 | tf_op jit(solution)/shard_map/ppermute | solution.py:289
  53.9 2.9 %collective-permute-start.22 = (bf16[192,256]{1,0:T(8,128)(2,1)S(1)}, bf16[192,256]{1,0:T(8,128)(2,1)S(1)}, u32[]{:S(2)}, u32[]{:S(2)}) collective-permute-start(bf16[192,256]{1,0:T(8,128)(2,1)S(1)} %shard_map.78.own_ref), channel_id=1, source_target_pairs={{0,1},{1,0},{2,3},{3,2},{4,5},{5,4},{6,7},{7,6},{8,9},{9,8},{10,11... | collective-permute-start | bytes 294920 | tf_op jit(solution)/shard_map/ppermute | solution.py:289
  56.8 3.9 %collective-permute-done.8.rest_1_ = bf16[192,256]{1,0:T(8,128)(2,1)S(1)} collective-permute-done((bf16[192,256]{1,0:T(8,128)(2,1)S(1)}, bf16[192,256]{1,0:T(8,128)(2,1)S(1)}, u32[]{:S(2)}, u32[]{:S(2)}) %collective-permute-start.8) | collective-permute-done | bytes 98336 | tf_op jit(solution)/shard_map/ppermute | solution.py:289
  60.8 4.5 %collective-permute-start.10 = (bf16[128,256]{1,0:T(8,128)(2,1)S(1)}, bf16[128,256]{1,0:T(8,128)(2,1)S(1)}, u32[]{:S(2)}, u32[]{:S(2)}) collective-permute-start(bf16[128,256]{1,0:T(8,128)(2,1)S(1)} %get-tuple-element.75), channel_id=1, source_target_pairs={{4,0},{0,4},{12,8},{8,12},{20,16},{16,20},{28,24},{24,28},{5,1},{1... | collective-permute-start | bytes 196616 | tf_op jit(solution)/shard_map/ppermute | solution.py:237
  65.3 1.9 %collective-permute-start.11 = (bf16[128,256]{1,0:T(8,128)(2,1)S(1)}, bf16[128,256]{1,0:T(8,128)(2,1)S(1)}, u32[]{:S(2)}, u32[]{:S(2)}) collective-permute-start(bf16[128,256]{1,0:T(8,128)(2,1)S(1)} %get-tuple-element.76), channel_id=1, source_target_pairs={{8,4},{4,8},{16,12},{12,16},{24,20},{20,24},{9,5},{5,9},{17,13},{1... | collective-permute-start | bytes 196616 | tf_op jit(solution)/shard_map/ppermute | solution.py:238
  67.3 1.3 %collective-permute-start.25 = (bf16[128,256]{1,0:T(8,128)(2,1)S(1)}, bf16[128,256]{1,0:T(8,128)(2,1)S(1)}, u32[]{:S(2)}, u32[]{:S(2)}) collective-permute-start(bf16[128,256]{1,0:T(8,128)(2,1)S(1)} %get-tuple-element.99), channel_id=1, source_target_pairs={{4,0},{0,4},{12,8},{8,12},{20,16},{16,20},{28,24},{24,28},{5,1},{1... | collective-permute-start | bytes 196616 | tf_op jit(solution)/shard_map/ppermute | solution.py:237
  68.6 2.4 %collective-permute-start.26 = (bf16[128,256]{1,0:T(8,128)(2,1)S(1)}, bf16[128,256]{1,0:T(8,128)(2,1)S(1)}, u32[]{:S(2)}, u32[]{:S(2)}) collective-permute-start(bf16[128,256]{1,0:T(8,128)(2,1)S(1)} %get-tuple-element.100), channel_id=1, source_target_pairs={{8,4},{4,8},{16,12},{12,16},{24,20},{20,24},{9,5},{5,9},{17,13},{1... | collective-permute-start | bytes 196616 | tf_op jit(solution)/shard_map/ppermute | solution.py:238
  71.0 0.1 collective-permute-done.11.two_ref
  71.1 1.7 %shard_map.71 = (bf16[1024,256]{1,0:T(8,128)(2,1)S(1)}, f32[2,784,256]{2,1,0:T(8,128)S(1)}, f32[2,2,128,256]{3,2,1,0:T(8,128)S(1)}, f32[2,520,256]{2,1,0:T(8,128)S(1)}) custom-call(f32[1,2]{1,0:T(1,128)S(1)} %copy-done.1, bf16[1536,1024]{1,0:T(8,128)(2,1)S(1)} %shard_map.65.g_ref, bf16[768,256]{1,0:T(8,128)(2,1)S(1)} %get-tuple-element.74.src_ref, ...), custom_call_target="tpu_custom_call" | custom-call | flops 536870912 | bytes 3145728 | tf_op jit(solution)/shard_map/pallas_call | solution.py:23
  72.8 0.1 convert.17
  72.9 0.1 slice_bitcast_fusion.5
  73.0 1.5 %collective-permute-start.12 = (f16[520,256]{1,0:T(8,128)(2,1)S(1)}, f16[520,256]{1,0:T(8,128)(2,1)S(1)}, u32[]{:S(2)}, u32[]{:S(2)}) collective-permute-start(f16[520,256]{1,0:T(8,128)(2,1)S(1)} %get-tuple-element.111), channel_id=1, source_target_pairs={{4,0},{0,4},{12,8},{8,12},{20,16},{16,20},{28,24},{24,28},{5,1},{1... | collective-permute-start | bytes 798728 | tf_op jit(solution)/shard_map/ppermute | solution.py:237
  74.5 1.9 %collective-permute-start.13 = (f16[520,256]{1,0:T(8,128)(2,1)S(1)}, f16[520,256]{1,0:T(8,128)(2,1)S(1)}, u32[]{:S(2)}, u32[]{:S(2)}) collective-permute-start(f16[520,256]{1,0:T(8,128)(2,1)S(1)} %get-tuple-element.112), channel_id=1, source_target_pairs={{8,4},{4,8},{16,12},{12,16},{24,20},{20,24},{9,5},{5,9},{17,13},{1... | collective-permute-start | bytes 798728 | tf_op jit(solution)/shard_map/ppermute | solution.py:238
  76.5 1.7 %shard_map.80 = (bf16[1024,256]{1,0:T(8,128)(2,1)S(1)}, f32[2,784,256]{2,1,0:T(8,128)S(1)}, f32[2,2,128,256]{3,2,1,0:T(8,128)S(1)}, f32[2,520,256]{2,1,0:T(8,128)S(1)}) custom-call(f32[1,2]{1,0:T(1,128)S(1)} %copy-done.1, bf16[1536,1024]{1,0:T(8,128)(2,1)S(1)} %shard_map.65.g_ref, bf16[768,256]{1,0:T(8,128)(2,1)S(1)} %get-tuple-element.98.src_ref, ...), custom_call_target="tpu_custom_call" | custom-call | flops 536870912 | bytes 3145728 | tf_op jit(solution)/shard_map/pallas_call | solution.py:23
  78.2 0.1 convert.19
  78.3 0.1 slice_bitcast_fusion.1
  78.4 0.7 collective-permute-start.27
  79.0 3.3 %collective-permute-start.28 = (f16[520,256]{1,0:T(8,128)(2,1)S(1)}, f16[520,256]{1,0:T(8,128)(2,1)S(1)}, u32[]{:S(2)}, u32[]{:S(2)}) collective-permute-start(f16[520,256]{1,0:T(8,128)(2,1)S(1)} %get-tuple-element.116), channel_id=1, source_target_pairs={{8,4},{4,8},{16,12},{12,16},{24,20},{20,24},{9,5},{5,9},{17,13},{1... | collective-permute-start | bytes 798728 | tf_op jit(solution)/shard_map/ppermute | solution.py:238
  82.3 2.5 %shard_map.72 = (f32[768,256]{1,0:T(8,128)S(1)}, f32[2,784,256]{2,1,0:T(8,128)S(1)}) custom-call(f32[1,2]{1,0:T(1,128)S(1)} %copy-done.1, f32[1,2]{1,0:T(1,128)S(1)} %copy-done.2, bf16[1536,1024]{1,0:T(8,128)(2,1)S(1)} %shard_map.65.g_ref, bf16[768,256]{1,0:T(8,128)(2,1)S(1)} %get-tuple-element.74.src_ref, ...), custom_call_target="tpu_custom_call", output_to_operand_aliasing={{1}: (5, {})} | custom-call | flops 1207959552 | bytes 3145728 | tf_op jit(solution)/shard_map/pallas_call | solution.py:23
  84.8 2.5 %shard_map.81 = (f32[768,256]{1,0:T(8,128)S(1)}, f32[2,784,256]{2,1,0:T(8,128)S(1)}) custom-call(f32[1,2]{1,0:T(1,128)S(1)} %copy-done.1, f32[1,2]{1,0:T(1,128)S(1)} %copy-done.2, bf16[1536,1024]{1,0:T(8,128)(2,1)S(1)} %shard_map.65.g_ref, bf16[768,256]{1,0:T(8,128)(2,1)S(1)} %get-tuple-element.98.src_ref, ...), custom_call_target="tpu_custom_call", output_to_operand_aliasing={{1}: (5, {})} | custom-call | flops 1207959552 | bytes 3145728 | tf_op jit(solution)/shard_map/pallas_call | solution.py:23
  87.3 0.1 maximum_convert_fusion.1.got_ref
  87.4 1.8 %shard_map.73 = (f32[192,256]{1,0:T(8,128)S(1)}, f32[200,256]{1,0:T(8,128)S(1)}, f32[200,256]{1,0:T(8,128)S(1)}, f32[200,256]{1,0:T(8,128)S(1)}) custom-call(f32[1,2]{1,0:T(1,128)S(1)} %copy-done.2, bf16[1536,1024]{1,0:T(8,128)(2,1)S(1)} %shard_map.65.g_ref, f32[768,256]{1,0:T(8,128)S(1)} %get-tuple-element.79.part_ref, ...), custom_call_target="tpu_custom_call" | custom-call | flops 805306368 | bytes 3145728 | tf_op jit(solution)/shard_map/pallas_call | solution.py:23
  89.2 2.2 %collective-permute-start.16 = (f16[200,256]{1,0:T(8,128)(2,1)S(1)}, f16[200,256]{1,0:T(8,128)(2,1)S(1)}, u32[]{:S(2)}, u32[]{:S(2)}) collective-permute-start(f16[200,256]{1,0:T(8,128)(2,1)S(1)} %convert_element_type.132), channel_id=1, source_target_pairs={{0,3},{1,2},{2,1},{3,0},{4,7},{5,6},{6,5},{7,4},{8,11},{9,10},{10,... | collective-permute-start | bytes 307208 | tf_op jit(solution)/shard_map/ppermute | solution.py:279
  91.5 1.4 %collective-permute-start.14 = (f16[200,256]{1,0:T(8,128)(2,1)S(1)}, f16[200,256]{1,0:T(8,128)(2,1)S(1)}, u32[]{:S(2)}, u32[]{:S(2)}) collective-permute-start(f16[200,256]{1,0:T(8,128)(2,1)S(1)} %convert_element_type.128), channel_id=1, source_target_pairs={{0,1},{1,0},{2,3},{3,2},{4,5},{5,4},{6,7},{7,6},{8,9},{9,8},{10,11... | collective-permute-start | bytes 307208 | tf_op jit(solution)/shard_map/ppermute | solution.py:279
  92.9 0.1 maximum_convert_fusion.3.got_ref
  92.9 1.8 %shard_map.82 = (f32[192,256]{1,0:T(8,128)S(1)}, f32[200,256]{1,0:T(8,128)S(1)}, f32[200,256]{1,0:T(8,128)S(1)}, f32[200,256]{1,0:T(8,128)S(1)}) custom-call(f32[1,2]{1,0:T(1,128)S(1)} %copy-done.2, bf16[1536,1024]{1,0:T(8,128)(2,1)S(1)} %shard_map.65.g_ref, f32[768,256]{1,0:T(8,128)S(1)} %get-tuple-element.103.part_ref, ...), custom_call_target="tpu_custom_call" | custom-call | flops 805306368 | bytes 3145728 | tf_op jit(solution)/shard_map/pallas_call | solution.py:23
  94.8 2.3 %collective-permute-start.31 = (f16[200,256]{1,0:T(8,128)(2,1)S(1)}, f16[200,256]{1,0:T(8,128)(2,1)S(1)}, u32[]{:S(2)}, u32[]{:S(2)}) collective-permute-start(f16[200,256]{1,0:T(8,128)(2,1)S(1)} %convert_element_type.150), channel_id=1, source_target_pairs={{0,3},{1,2},{2,1},{3,0},{4,7},{5,6},{6,5},{7,4},{8,11},{9,10},{10,... | collective-permute-start | bytes 307208 | tf_op jit(solution)/shard_map/ppermute | solution.py:279
  97.1 1.3 %collective-permute-start.29 = (f16[200,256]{1,0:T(8,128)(2,1)S(1)}, f16[200,256]{1,0:T(8,128)(2,1)S(1)}, u32[]{:S(2)}, u32[]{:S(2)}) collective-permute-start(f16[200,256]{1,0:T(8,128)(2,1)S(1)} %convert_element_type.146), channel_id=1, source_target_pairs={{0,1},{1,0},{2,3},{3,2},{4,5},{5,4},{6,7},{7,6},{8,9},{9,8},{10,11... | collective-permute-start | bytes 307208 | tf_op jit(solution)/shard_map/ppermute | solution.py:279
  98.5 2.8 %collective-permute-done.15 = f16[200,256]{1,0:T(8,128)(2,1)S(1)} collective-permute-done((f16[200,256]{1,0:T(8,128)(2,1)S(1)}, f16[200,256]{1,0:T(8,128)(2,1)S(1)}, u32[]{:S(2)}, u32[]{:S(2)}) %collective-permute-start.15) | collective-permute-done | bytes 102432 | tf_op jit(solution)/shard_map/ppermute | solution.py:279
  101.4 7.7 %collective-permute-done.30 = f16[200,256]{1,0:T(8,128)(2,1)S(1)} collective-permute-done((f16[200,256]{1,0:T(8,128)(2,1)S(1)}, f16[200,256]{1,0:T(8,128)(2,1)S(1)}, u32[]{:S(2)}, u32[]{:S(2)}) %collective-permute-start.30) | collective-permute-done | bytes 102432 | tf_op jit(solution)/shard_map/ppermute | solution.py:279
  109.2 0.8 pad_maximum_fusion
  (69 shorter events, 1.0 us)
Async XLA Ops:
  0.0 1.4 %copy-start = (f32[768,512]{1,0:T(8,128)S(1)}, f32[768,512]{1,0:T(8,128)}, u32[]{:S(2)}) copy-start(f32[768,512]{1,0:T(8,128)} %state_ref.1) | copy-start | bytes 4718596
  1.4 0.7 copy-start.3
  2.1 0.7 copy-start.4
  3.2 9.6 %collective-permute-start = (bf16[128,512]{1,0:T(8,128)(2,1)S(1)}, bf16[128,512]{1,0:T(8,128)(2,1)S(1)}, u32[]{:S(2)}, u32[]{:S(2)}) collective-permute-start(bf16[128,512]{1,0:T(8,128)(2,1)S(1)} %get-tuple-element.60), channel_id=1, source_target_pairs={{4,0},{0,4},{12,8},{8,12},{20,16},{16,20},{28,24},{24,28},{5,1},{1... | collective-permute-start | bytes 393224 | tf_op jit(solution)/shard_map/ppermute | solution.py:237
  3.9 8.9 %collective-permute-start.1 = (bf16[128,512]{1,0:T(8,128)(2,1)S(1)}, bf16[128,512]{1,0:T(8,128)(2,1)S(1)}, u32[]{:S(2)}, u32[]{:S(2)}) collective-permute-start(bf16[128,512]{1,0:T(8,128)(2,1)S(1)} %get-tuple-element.61), channel_id=1, source_target_pairs={{8,4},{4,8},{16,12},{12,16},{24,20},{20,24},{9,5},{5,9},{17,13},{1... | collective-permute-start | bytes 393224 | tf_op jit(solution)/shard_map/ppermute | solution.py:238
  7.0 1.9 %copy-start.5 = (bf16[1,768,2048]{2,1,0:T(8,128)(2,1)S(1)}, bf16[1,768,2048]{2,1,0:T(8,128)(2,1)}, u32[]{:S(2)}) copy-start(bf16[1,768,2048]{2,1,0:T(8,128)(2,1)} %inv_ref.1) | copy-start | bytes 9437188
  8.9 3.9 %copy-start.1 = (f32[1,2]{1,0:T(1,128)S(1)}, f32[1,2]{1,0:T(1,128)}, u32[]{:S(2)}) copy-start(f32[1,2]{1,0:T(1,128)} %shift_ref.15) | copy-start | bytes 28
  16.4 6.6 %copy-start.2 = (f32[1,2]{1,0:T(1,128)S(1)}, f32[1,2]{1,0:T(1,128)}, u32[]{:S(2)}) copy-start(f32[1,2]{1,0:T(1,128)} %weight_ref.15) | copy-start | bytes 28
  16.5 11.4 %collective-permute-start.2 = (f16[520,256]{1,0:T(8,128)(2,1)S(1)}, f16[520,256]{1,0:T(8,128)(2,1)S(1)}, u32[]{:S(2)}, u32[]{:S(2)}) collective-permute-start(f16[520,256]{1,0:T(8,128)(2,1)S(1)} %get-tuple-element.113), channel_id=1, source_target_pairs={{4,0},{0,4},{12,8},{8,12},{20,16},{16,20},{28,24},{24,28},{5,1},{1... | collective-permute-start | bytes 798728 | tf_op jit(solution)/shard_map/ppermute | solution.py:237
  17.0 10.9 %collective-permute-start.3 = (f16[520,256]{1,0:T(8,128)(2,1)S(1)}, f16[520,256]{1,0:T(8,128)(2,1)S(1)}, u32[]{:S(2)}, u32[]{:S(2)}) collective-permute-start(f16[520,256]{1,0:T(8,128)(2,1)S(1)} %get-tuple-element.114), channel_id=1, source_target_pairs={{8,4},{4,8},{16,12},{12,16},{24,20},{20,24},{9,5},{5,9},{17,13},{1... | collective-permute-start | bytes 798728 | tf_op jit(solution)/shard_map/ppermute | solution.py:238
  19.2 14.3 %collective-permute-start.17 = (f16[520,256]{1,0:T(8,128)(2,1)S(1)}, f16[520,256]{1,0:T(8,128)(2,1)S(1)}, u32[]{:S(2)}, u32[]{:S(2)}) collective-permute-start(f16[520,256]{1,0:T(8,128)(2,1)S(1)} %get-tuple-element.117), channel_id=1, source_target_pairs={{4,0},{0,4},{12,8},{8,12},{20,16},{16,20},{28,24},{24,28},{5,1},{1... | collective-permute-start | bytes 798728 | tf_op jit(solution)/shard_map/ppermute | solution.py:237
  20.2 13.3 %collective-permute-start.18 = (f16[520,256]{1,0:T(8,128)(2,1)S(1)}, f16[520,256]{1,0:T(8,128)(2,1)S(1)}, u32[]{:S(2)}, u32[]{:S(2)}) collective-permute-start(f16[520,256]{1,0:T(8,128)(2,1)S(1)} %get-tuple-element.118), channel_id=1, source_target_pairs={{8,4},{4,8},{16,12},{12,16},{24,20},{20,24},{9,5},{5,9},{17,13},{1... | collective-permute-start | bytes 798728 | tf_op jit(solution)/shard_map/ppermute | solution.py:238
  29.8 9.0 %collective-permute-start.6 = (f16[200,256]{1,0:T(8,128)(2,1)S(1)}, f16[200,256]{1,0:T(8,128)(2,1)S(1)}, u32[]{:S(2)}, u32[]{:S(2)}) collective-permute-start(f16[200,256]{1,0:T(8,128)(2,1)S(1)} %convert_element_type.123), channel_id=1, source_target_pairs={{0,3},{1,2},{2,1},{3,0},{4,7},{5,6},{6,5},{7,4},{8,11},{9,10},{10,... | collective-permute-start | bytes 307208 | tf_op jit(solution)/shard_map/ppermute | solution.py:279
  33.2 11.7 %collective-permute-start.5 = (f16[200,256]{1,0:T(8,128)(2,1)S(1)}, f16[200,256]{1,0:T(8,128)(2,1)S(1)}, u32[]{:S(2)}, u32[]{:S(2)}) collective-permute-start(f16[200,256]{1,0:T(8,128)(2,1)S(1)} %convert_element_type.121), channel_id=1, source_target_pairs={{0,2},{1,3},{2,0},{3,1},{4,6},{5,7},{6,4},{7,5},{8,10},{9,11},{10,... | collective-permute-start | bytes 307208 | tf_op jit(solution)/shard_map/ppermute | solution.py:279
  33.2 11.7 %collective-permute-start.4 = (f16[200,256]{1,0:T(8,128)(2,1)S(1)}, f16[200,256]{1,0:T(8,128)(2,1)S(1)}, u32[]{:S(2)}, u32[]{:S(2)}) collective-permute-start(f16[200,256]{1,0:T(8,128)(2,1)S(1)} %convert_element_type.119), channel_id=1, source_target_pairs={{0,1},{1,0},{2,3},{3,2},{4,5},{5,4},{6,7},{7,6},{8,9},{9,8},{10,11... | collective-permute-start | bytes 307208 | tf_op jit(solution)/shard_map/ppermute | solution.py:279
  35.5 9.7 %collective-permute-start.21 = (f16[200,256]{1,0:T(8,128)(2,1)S(1)}, f16[200,256]{1,0:T(8,128)(2,1)S(1)}, u32[]{:S(2)}, u32[]{:S(2)}) collective-permute-start(f16[200,256]{1,0:T(8,128)(2,1)S(1)} %convert_element_type.141), channel_id=1, source_target_pairs={{0,3},{1,2},{2,1},{3,0},{4,7},{5,6},{6,5},{7,4},{8,11},{9,10},{10,... | collective-permute-start | bytes 307208 | tf_op jit(solution)/shard_map/ppermute | solution.py:279
  38.8 13.5 %collective-permute-start.20 = (f16[200,256]{1,0:T(8,128)(2,1)S(1)}, f16[200,256]{1,0:T(8,128)(2,1)S(1)}, u32[]{:S(2)}, u32[]{:S(2)}) collective-permute-start(f16[200,256]{1,0:T(8,128)(2,1)S(1)} %convert_element_type.139), channel_id=1, source_target_pairs={{0,2},{1,3},{2,0},{3,1},{4,6},{5,7},{6,4},{7,5},{8,10},{9,11},{10,... | collective-permute-start | bytes 307208 | tf_op jit(solution)/shard_map/ppermute | solution.py:279
  38.9 13.5 %collective-permute-start.19 = (f16[200,256]{1,0:T(8,128)(2,1)S(1)}, f16[200,256]{1,0:T(8,128)(2,1)S(1)}, u32[]{:S(2)}, u32[]{:S(2)}) collective-permute-start(f16[200,256]{1,0:T(8,128)(2,1)S(1)} %convert_element_type.137), channel_id=1, source_target_pairs={{0,1},{1,0},{2,3},{3,2},{4,5},{5,4},{6,7},{7,6},{8,9},{9,8},{10,11... | collective-permute-start | bytes 307208 | tf_op jit(solution)/shard_map/ppermute | solution.py:279
  45.0 8.9 %collective-permute-start.9 = (bf16[192,256]{1,0:T(8,128)(2,1)S(1)}, bf16[192,256]{1,0:T(8,128)(2,1)S(1)}, u32[]{:S(2)}, u32[]{:S(2)}) collective-permute-start(bf16[192,256]{1,0:T(8,128)(2,1)S(1)} %shard_map.69.own_ref), channel_id=1, source_target_pairs={{0,3},{1,2},{2,1},{3,0},{4,7},{5,6},{6,5},{7,4},{8,11},{9,10},{10,... | collective-permute-start | bytes 294920 | tf_op jit(solution)/shard_map/ppermute | solution.py:289
  45.1 15.6 %collective-permute-start.8 = (bf16[192,256]{1,0:T(8,128)(2,1)S(1)}, bf16[192,256]{1,0:T(8,128)(2,1)S(1)}, u32[]{:S(2)}, u32[]{:S(2)}) collective-permute-start(bf16[192,256]{1,0:T(8,128)(2,1)S(1)} %shard_map.69.own_ref), channel_id=1, source_target_pairs={{0,2},{1,3},{2,0},{3,1},{4,6},{5,7},{6,4},{7,5},{8,10},{9,11},{10,... | collective-permute-start | bytes 294920 | tf_op jit(solution)/shard_map/ppermute | solution.py:289
  45.2 15.6 %collective-permute-start.7 = (bf16[192,256]{1,0:T(8,128)(2,1)S(1)}, bf16[192,256]{1,0:T(8,128)(2,1)S(1)}, u32[]{:S(2)}, u32[]{:S(2)}) collective-permute-start(bf16[192,256]{1,0:T(8,128)(2,1)S(1)} %shard_map.69.own_ref), channel_id=1, source_target_pairs={{0,1},{1,0},{2,3},{3,2},{4,5},{5,4},{6,7},{7,6},{8,9},{9,8},{10,11... | collective-permute-start | bytes 294920 | tf_op jit(solution)/shard_map/ppermute | solution.py:289
  52.5 14.7 %collective-permute-start.24 = (bf16[192,256]{1,0:T(8,128)(2,1)S(1)}, bf16[192,256]{1,0:T(8,128)(2,1)S(1)}, u32[]{:S(2)}, u32[]{:S(2)}) collective-permute-start(bf16[192,256]{1,0:T(8,128)(2,1)S(1)} %shard_map.78.own_ref), channel_id=1, source_target_pairs={{0,3},{1,2},{2,1},{3,0},{4,7},{5,6},{6,5},{7,4},{8,11},{9,10},{10,... | collective-permute-start | bytes 294920 | tf_op jit(solution)/shard_map/ppermute | solution.py:289
  53.9 13.3 %collective-permute-start.23 = (bf16[192,256]{1,0:T(8,128)(2,1)S(1)}, bf16[192,256]{1,0:T(8,128)(2,1)S(1)}, u32[]{:S(2)}, u32[]{:S(2)}) collective-permute-start(bf16[192,256]{1,0:T(8,128)(2,1)S(1)} %shard_map.78.own_ref), channel_id=1, source_target_pairs={{0,2},{1,3},{2,0},{3,1},{4,6},{5,7},{6,4},{7,5},{8,10},{9,11},{10,... | collective-permute-start | bytes 294920 | tf_op jit(solution)/shard_map/ppermute | solution.py:289
  53.9 13.3 %collective-permute-start.22 = (bf16[192,256]{1,0:T(8,128)(2,1)S(1)}, bf16[192,256]{1,0:T(8,128)(2,1)S(1)}, u32[]{:S(2)}, u32[]{:S(2)}) collective-permute-start(bf16[192,256]{1,0:T(8,128)(2,1)S(1)} %shard_map.78.own_ref), channel_id=1, source_target_pairs={{0,1},{1,0},{2,3},{3,2},{4,5},{5,4},{6,7},{7,6},{8,9},{9,8},{10,11... | collective-permute-start | bytes 294920 | tf_op jit(solution)/shard_map/ppermute | solution.py:289
  60.8 10.2 %collective-permute-start.10 = (bf16[128,256]{1,0:T(8,128)(2,1)S(1)}, bf16[128,256]{1,0:T(8,128)(2,1)S(1)}, u32[]{:S(2)}, u32[]{:S(2)}) collective-permute-start(bf16[128,256]{1,0:T(8,128)(2,1)S(1)} %get-tuple-element.75), channel_id=1, source_target_pairs={{4,0},{0,4},{12,8},{8,12},{20,16},{16,20},{28,24},{24,28},{5,1},{1... | collective-permute-start | bytes 196616 | tf_op jit(solution)/shard_map/ppermute | solution.py:237
  65.3 5.9 %collective-permute-start.11 = (bf16[128,256]{1,0:T(8,128)(2,1)S(1)}, bf16[128,256]{1,0:T(8,128)(2,1)S(1)}, u32[]{:S(2)}, u32[]{:S(2)}) collective-permute-start(bf16[128,256]{1,0:T(8,128)(2,1)S(1)} %get-tuple-element.76), channel_id=1, source_target_pairs={{8,4},{4,8},{16,12},{12,16},{24,20},{20,24},{9,5},{5,9},{17,13},{1... | collective-permute-start | bytes 196616 | tf_op jit(solution)/shard_map/ppermute | solution.py:238
  67.3 9.2 %collective-permute-start.25 = (bf16[128,256]{1,0:T(8,128)(2,1)S(1)}, bf16[128,256]{1,0:T(8,128)(2,1)S(1)}, u32[]{:S(2)}, u32[]{:S(2)}) collective-permute-start(bf16[128,256]{1,0:T(8,128)(2,1)S(1)} %get-tuple-element.99), channel_id=1, source_target_pairs={{4,0},{0,4},{12,8},{8,12},{20,16},{16,20},{28,24},{24,28},{5,1},{1... | collective-permute-start | bytes 196616 | tf_op jit(solution)/shard_map/ppermute | solution.py:237
  68.6 7.9 %collective-permute-start.26 = (bf16[128,256]{1,0:T(8,128)(2,1)S(1)}, bf16[128,256]{1,0:T(8,128)(2,1)S(1)}, u32[]{:S(2)}, u32[]{:S(2)}) collective-permute-start(bf16[128,256]{1,0:T(8,128)(2,1)S(1)} %get-tuple-element.100), channel_id=1, source_target_pairs={{8,4},{4,8},{16,12},{12,16},{24,20},{20,24},{9,5},{5,9},{17,13},{1... | collective-permute-start | bytes 196616 | tf_op jit(solution)/shard_map/ppermute | solution.py:238
  73.0 14.3 %collective-permute-start.12 = (f16[520,256]{1,0:T(8,128)(2,1)S(1)}, f16[520,256]{1,0:T(8,128)(2,1)S(1)}, u32[]{:S(2)}, u32[]{:S(2)}) collective-permute-start(f16[520,256]{1,0:T(8,128)(2,1)S(1)} %get-tuple-element.111), channel_id=1, source_target_pairs={{4,0},{0,4},{12,8},{8,12},{20,16},{16,20},{28,24},{24,28},{5,1},{1... | collective-permute-start | bytes 798728 | tf_op jit(solution)/shard_map/ppermute | solution.py:237
  74.5 12.8 %collective-permute-start.13 = (f16[520,256]{1,0:T(8,128)(2,1)S(1)}, f16[520,256]{1,0:T(8,128)(2,1)S(1)}, u32[]{:S(2)}, u32[]{:S(2)}) collective-permute-start(f16[520,256]{1,0:T(8,128)(2,1)S(1)} %get-tuple-element.112), channel_id=1, source_target_pairs={{8,4},{4,8},{16,12},{12,16},{24,20},{20,24},{9,5},{5,9},{17,13},{1... | collective-permute-start | bytes 798728 | tf_op jit(solution)/shard_map/ppermute | solution.py:238
  78.4 14.5 %collective-permute-start.27 = (f16[520,256]{1,0:T(8,128)(2,1)S(1)}, f16[520,256]{1,0:T(8,128)(2,1)S(1)}, u32[]{:S(2)}, u32[]{:S(2)}) collective-permute-start(f16[520,256]{1,0:T(8,128)(2,1)S(1)} %get-tuple-element.115), channel_id=1, source_target_pairs={{4,0},{0,4},{12,8},{8,12},{20,16},{16,20},{28,24},{24,28},{5,1},{1... | collective-permute-start | bytes 798728 | tf_op jit(solution)/shard_map/ppermute | solution.py:237
  79.0 13.8 %collective-permute-start.28 = (f16[520,256]{1,0:T(8,128)(2,1)S(1)}, f16[520,256]{1,0:T(8,128)(2,1)S(1)}, u32[]{:S(2)}, u32[]{:S(2)}) collective-permute-start(f16[520,256]{1,0:T(8,128)(2,1)S(1)} %get-tuple-element.116), channel_id=1, source_target_pairs={{8,4},{4,8},{16,12},{12,16},{24,20},{20,24},{9,5},{5,9},{17,13},{1... | collective-permute-start | bytes 798728 | tf_op jit(solution)/shard_map/ppermute | solution.py:238
  89.2 7.9 %collective-permute-start.16 = (f16[200,256]{1,0:T(8,128)(2,1)S(1)}, f16[200,256]{1,0:T(8,128)(2,1)S(1)}, u32[]{:S(2)}, u32[]{:S(2)}) collective-permute-start(f16[200,256]{1,0:T(8,128)(2,1)S(1)} %convert_element_type.132), channel_id=1, source_target_pairs={{0,3},{1,2},{2,1},{3,0},{4,7},{5,6},{6,5},{7,4},{8,11},{9,10},{10,... | collective-permute-start | bytes 307208 | tf_op jit(solution)/shard_map/ppermute | solution.py:279
  91.5 9.8 %collective-permute-start.15 = (f16[200,256]{1,0:T(8,128)(2,1)S(1)}, f16[200,256]{1,0:T(8,128)(2,1)S(1)}, u32[]{:S(2)}, u32[]{:S(2)}) collective-permute-start(f16[200,256]{1,0:T(8,128)(2,1)S(1)} %convert_element_type.130), channel_id=1, source_target_pairs={{0,2},{1,3},{2,0},{3,1},{4,6},{5,7},{6,4},{7,5},{8,10},{9,11},{10,... | collective-permute-start | bytes 307208 | tf_op jit(solution)/shard_map/ppermute | solution.py:279
  91.5 9.8 %collective-permute-start.14 = (f16[200,256]{1,0:T(8,128)(2,1)S(1)}, f16[200,256]{1,0:T(8,128)(2,1)S(1)}, u32[]{:S(2)}, u32[]{:S(2)}) collective-permute-start(f16[200,256]{1,0:T(8,128)(2,1)S(1)} %convert_element_type.128), channel_id=1, source_target_pairs={{0,1},{1,0},{2,3},{3,2},{4,5},{5,4},{6,7},{7,6},{8,9},{9,8},{10,11... | collective-permute-start | bytes 307208 | tf_op jit(solution)/shard_map/ppermute | solution.py:279
  94.8 6.6 %collective-permute-start.31 = (f16[200,256]{1,0:T(8,128)(2,1)S(1)}, f16[200,256]{1,0:T(8,128)(2,1)S(1)}, u32[]{:S(2)}, u32[]{:S(2)}) collective-permute-start(f16[200,256]{1,0:T(8,128)(2,1)S(1)} %convert_element_type.150), channel_id=1, source_target_pairs={{0,3},{1,2},{2,1},{3,0},{4,7},{5,6},{6,5},{7,4},{8,11},{9,10},{10,... | collective-permute-start | bytes 307208 | tf_op jit(solution)/shard_map/ppermute | solution.py:279
  97.0 12.0 %collective-permute-start.30 = (f16[200,256]{1,0:T(8,128)(2,1)S(1)}, f16[200,256]{1,0:T(8,128)(2,1)S(1)}, u32[]{:S(2)}, u32[]{:S(2)}) collective-permute-start(f16[200,256]{1,0:T(8,128)(2,1)S(1)} %convert_element_type.148), channel_id=1, source_target_pairs={{0,2},{1,3},{2,0},{3,1},{4,6},{5,7},{6,4},{7,5},{8,10},{9,11},{10,... | collective-permute-start | bytes 307208 | tf_op jit(solution)/shard_map/ppermute | solution.py:279
  97.1 12.0 %collective-permute-start.29 = (f16[200,256]{1,0:T(8,128)(2,1)S(1)}, f16[200,256]{1,0:T(8,128)(2,1)S(1)}, u32[]{:S(2)}, u32[]{:S(2)}) collective-permute-start(f16[200,256]{1,0:T(8,128)(2,1)S(1)} %convert_element_type.146), channel_id=1, source_target_pairs={{0,1},{1,0},{2,3},{3,2},{4,5},{5,4},{6,7},{7,6},{8,9},{9,8},{10,11... | collective-permute-start | bytes 307208 | tf_op jit(solution)/shard_map/ppermute | solution.py:279

commit v5 on v4

--- a/solution.py
+++ b/solution.py
@@ -9,7 +9,7 @@
 
 
 STEPS = 2
-CHUNKS = 2
+PARTS = (1, 1)
 TAIL = 8
 TOP = 12.0
 BF16 = jnp.bfloat16
@@ -17,6 +17,10 @@
 F32 = jnp.float32
 VMEM = pl.BlockSpec(memory_space=pltpu.VMEM)
 SMEM = pl.BlockSpec(memory_space=pltpu.SMEM)
+
+
+def split_at(chunk):
+    return chunk == 0
 
 
 def call(kernel, outs, ins, scratch=(), flops=0, moved=0, alias=()):
@@ -71,7 +75,7 @@
 
 
 def start_kernel(rim, sigma_ref, order_ref, state_ref, msg1_ref, msg2_ref, wide_ref, share_ref, row_ref, *chunks):
-    rows, n, share = state_ref.shape[0], wide_ref.shape[1], share_ref.shape[0]
+    rows, share, lane = state_ref.shape[0], share_ref.shape[0], 0
     parity = lax.rem(lax.axis_index("sub"), 2)
     sigma = column(sigma_ref[...].reshape(1, rows), rows)
     low = (state_ref[:rim] * sigma[:rim]).astype(BF16)
@@ -81,8 +85,9 @@
     wide_ref[...] = jnp.broadcast_to(sigma, wide_ref.shape)
     share_ref[...] = wide_ref[rows_of(lax.axis_index("pole"), share)]
     row_ref[...] = order_ref[...].astype(F32)
-    for k, ref in enumerate(chunks):
-        ref[...] = state_ref[:, k * n:(k + 1) * n] * sigma
+    for ref in chunks:
+        ref[...] = state_ref[:, lane:lane + ref.shape[1]] * sigma
+        lane += ref.shape[1]
 
 
 def setup_kernel(row_ref, inv_ref, g_ref):
@@ -107,7 +112,8 @@
 
 def residual(x_ref, lo, count, rim, far_up, far_down, src_ref, sigma_ref, a, b):
     at = slice(lo, lo + count)
-    xr, xi, sigma = x_ref[0, 8 + lo:8 + lo + count], x_ref[1, 8 + lo:8 + lo + count], sigma_ref[at]
+    xr, xi = x_ref[0, 8 + lo:8 + lo + count], x_ref[1, 8 + lo:8 + lo + count]
+    sigma = sigma_ref[at, :src_ref.shape[1]]
     real = src_ref[at].astype(F32) - stencil(x_ref, 0, lo, count, rim, far_up, far_down) - sigma * (a * xr - b * xi)
     imag = -stencil(x_ref, 1, lo, count, rim, far_up, far_down) - sigma * (b * xr + a * xi)
     return real, imag
@@ -145,32 +151,23 @@
         out_ref[lo:lo + block] = base(lo, block) + (wr * real - wi * imag)
 
 
-def middle_kernel(rim, shift_ref, weight_ref, g_ref, src_ref, ext_ref, outer_ref, sigma_ref, out_ref, x_ref, e_ref):
-    rows, _ = src_ref.shape
+def inner_residual(rim, shift_ref, g_ref, src_ref, ext_ref, sigma_ref, x_ref, e_ref, at):
+    rows = src_ref.shape[0]
     span, step = 2 * rim, 32
     a, b = shift_ref[0, 0], shift_ref[0, 1]
-    wr, wi = 2.0 * weight_ref[0, 0], 2.0 * weight_ref[0, 1]
     if rows > 2 * span:
         for half in range(2):
             x_ref[half, 8 + span:8 + rows - span] = dot(g_ref[half * rows + span:(half + 1) * rows - span], ext_ref[...])
     for lo in range(rim, rows - rim, step):
         out = residual(x_ref, lo, step, rim, True, True, src_ref, sigma_ref, a, b)
         for half in range(2):
-            e_ref[half, lo - rim:lo - rim + step] = out[half].astype(BF16)
-
-    def base(lo, count):
-        return wr * x_ref[0, 8 + lo:8 + lo + count] - wi * x_ref[1, 8 + lo:8 + lo + count]
-
-    add_product(rows, g_ref, [slice(span, rows)], e_ref[0], e_ref[1], wr, wi, base, out_ref)
-
-
-def last_kernel(rim, hops, weight_ref, g_ref, part_ref, x_ref, r_ref, got_ref, *rest):
-    own_ref, msgs, u_ref, e_ref = rest[0], rest[1:1 + hops], rest[1 + hops], rest[2 + hops]
-    rows, _ = part_ref.shape
-    share = own_ref.shape[0]
-    sub, pole = lax.axis_index("sub"), lax.axis_index("pole")
+            e_ref[half, at + lo - rim:at + lo - rim + step] = out[half].astype(BF16)
+
+
+def outer_residual(rim, x_ref, r_ref, got_ref, e_ref, after_at):
+    rows = x_ref.shape[1] - 16
+    sub = lax.axis_index("sub")
     parity = lax.rem(sub, 2)
-    wr, wi = 2.0 * weight_ref[0, 0], 2.0 * weight_ref[0, 1]
     before_ref, after_ref = got_ref.at[1 - parity], got_ref.at[parity]
     inner_up = jnp.where(sub == 0, 0.0, 1.0)
     inner_down = jnp.where(sub == lax.axis_size("sub") - 1, 0.0, 1.0)
@@ -188,27 +185,75 @@
         foot = r_ref[1, half] + xa + jnp.where(at == rim - 1, xa[:1], 0.0)
         e_ref[half, :rim] = (inner_up * above).astype(BF16)
         e_ref[half, rim:2 * rim] = head.astype(BF16)
-        e_ref[half, 2 * rim:3 * rim] = foot.astype(BF16)
-        e_ref[half, 3 * rim:] = (inner_down * below).astype(BF16)
+        e_ref[half, after_at:after_at + rim] = foot.astype(BF16)
+        e_ref[half, after_at + rim:after_at + 2 * rim] = (inner_down * below).astype(BF16)
+
+
+def store_shares(u_ref, own_ref, msgs):
+    share, poles, pole = own_ref.shape[0], len(msgs) + 1, lax.axis_index("pole")
+    own_ref[...] = u_ref[rows_of(pole, share)]
+    for hop, ref in enumerate(msgs):
+        store_coded(ref, [u_ref[rows_of(hop_target(pole, hop + 1, poles), share)]])
+
+
+def middle_kernel(rim, shift_ref, weight_ref, g_ref, src_ref, ext_ref, outer_ref, sigma_ref, out_ref, x_ref, e_ref):
+    rows, _ = src_ref.shape
+    wr, wi = 2.0 * weight_ref[0, 0], 2.0 * weight_ref[0, 1]
+    inner_residual(rim, shift_ref, g_ref, src_ref, ext_ref, sigma_ref, x_ref, e_ref, 0)
+
+    def base(lo, count):
+        return wr * x_ref[0, 8 + lo:8 + lo + count] - wi * x_ref[1, 8 + lo:8 + lo + count]
+
+    add_product(rows, g_ref, [slice(2 * rim, rows)], e_ref[0], e_ref[1], wr, wi, base, out_ref)
+
+
+def last_kernel(rim, hops, weight_ref, g_ref, part_ref, x_ref, r_ref, got_ref, *rest):
+    own_ref, msgs, u_ref, e_ref = rest[0], rest[1:1 + hops], rest[1 + hops], rest[2 + hops]
+    rows, _ = part_ref.shape
+    wr, wi = 2.0 * weight_ref[0, 0], 2.0 * weight_ref[0, 1]
+    outer_residual(rim, x_ref, r_ref, got_ref, e_ref, rim * 2)
     add_product(
         rows, g_ref, [slice(0, 2 * rim), slice(rows, rows + 2 * rim)], e_ref[0], e_ref[1], wr, wi,
         lambda lo, count: part_ref[lo:lo + count], u_ref,
     )
-    own_ref[...] = u_ref[rows_of(pole, share)]
-    for hop, ref in enumerate(msgs):
-        store_coded(ref, [u_ref[rows_of(hop_target(pole, hop + 1, hops + 1), share)]])
-
-
-def sum_kernel(own_ref, *rest):
-    got, total_ref = rest[:-1], rest[-1]
+    store_shares(u_ref, own_ref, msgs)
+
+
+def tail_kernel(rim, hops, shift_ref, weight_ref, g_ref, src_ref, ext_ref, outer_ref, sigma_ref, r_ref, got_ref, *rest):
+    own_ref, msgs, x_ref, u_ref, e_ref = rest[0], rest[1:1 + hops], rest[1 + hops], rest[2 + hops], rest[3 + hops]
+    rows, _ = src_ref.shape
+    span = 2 * rim
+    wr, wi = 2.0 * weight_ref[0, 0], 2.0 * weight_ref[0, 1]
+    inner_residual(rim, shift_ref, g_ref, src_ref, ext_ref, sigma_ref, x_ref, e_ref, span)
+    outer_residual(rim, x_ref, r_ref, got_ref, e_ref, rows)
+
+    def base(lo, count):
+        return wr * x_ref[0, 8 + lo:8 + lo + count] - wi * x_ref[1, 8 + lo:8 + lo + count]
+
+    add_product(rows, g_ref, [slice(0, rows + span)], e_ref[0], e_ref[1], wr, wi, base, u_ref)
+    store_shares(u_ref, own_ref, msgs)
+
+
+def summed(own_ref, got):
     share = own_ref.shape[0]
     total = own_ref[...]
     for ref in got:
-        if ref.shape[0] == share:
-            total = total * ref[...]
-        else:
-            total = total + ref[:share] * jnp.exp2(ref[share:share + 1] - TOP)
-    total_ref[...] = total.astype(total_ref.dtype)
+        total = total + ref[:share] * jnp.exp2(ref[share:share + 1] - TOP)
+    return total
+
+
+def sum_kernel(factor_ref, own_ref, *rest):
+    got, total_ref = rest[:-1], rest[-1]
+    total_ref[...] = (summed(own_ref, got) * factor_ref[:, :total_ref.shape[1]]).astype(BF16)
+
+
+def final_kernel(*refs):
+    sets, out_ref, lane = refs[:-1], refs[-1], 0
+    each = len(sets) // len(PARTS)
+    for at in range(0, len(sets), each):
+        n = sets[at].shape[1]
+        out_ref[:, lane:lane + n] = summed(sets[at], sets[at + 1:at + each])
+        lane += n
 
 
 def join_kernel(rim, own_ref, *rest):
@@ -229,7 +274,8 @@
     rim = (order - rows) // 2
     subs, poles = lax.axis_size("sub"), lax.axis_size("pole")
     share, hops = rows // poles, poles - 1
-    n = columns // CHUNKS
+    widths = [columns * part // sum(PARTS) for part in PARTS]
+    widest = max(widths)
     pairs1 = [(i ^ 1, i) for i in range(subs) if i ^ 1 < subs]
     pairs2 = [(j, i) for i in range(subs) for j in [((i + 1) ^ 1) - 1] if 0 <= j < subs]
 
@@ -240,8 +286,8 @@
 
     one, two, sigma, sigma_share, order_row, *sources = call(
         functools.partial(start_kernel, rim),
-        [((rim, columns), BF16), ((rim, columns), BF16), ((rows, n), F32), ((share, n), F32), ((1, order), F32)]
-        + [((rows, n), F32)] * CHUNKS,
+        [((rim, columns), BF16), ((rim, columns), BF16), ((rows, widest), F32), ((share, widest), F32), ((1, order), F32)]
+        + [((rows, n), F32) for n in widths],
         [(VMEM, conductivity), (VMEM, order_list), (VMEM, state)], moved=8 * rows * columns,
     )
     first_halo = exchange(one, two)
@@ -250,7 +296,8 @@
         flops=4 * rows * order * order, moved=6 * rows * order,
     )
 
-    def sweep(source, got, lane):
+    def sweep(source, got, lane, split):
+        n = source.shape[1]
         ext, x, r, msgs = call(
             functools.partial(edge_kernel, rim, lane),
             [((order, n), BF16), ((2, rows + 16, n), F32), ((2, 2, rim, n), F32), ((2, 4 * rim + TAIL, n), F32)],
@@ -258,6 +305,15 @@
             flops=16 * rim * order * n, moved=4 * rows * order,
         )
         got = exchange(msgs[0].astype(F16), msgs[1].astype(F16))
+        shares = [((share, n), F32)] + [((share + TAIL, n), F32)] * hops
+        if not split:
+            return call(
+                functools.partial(tail_kernel, rim, hops), shares + [((2, rows + 16, n), F32)],
+                [(SMEM, pole_shift), (SMEM, pole_weight), (VMEM, g), (VMEM, source), (VMEM, ext), (VMEM, x),
+                 (VMEM, sigma), (VMEM, r), (VMEM, jnp.stack(got).astype(F32))],
+                [pltpu.VMEM((rows, n), F32), pltpu.VMEM((2, order, n), BF16)],
+                flops=8 * rows * order * n, moved=4 * rows * order, alias={5: 1 + hops},
+            )[:-1]
         part, x = call(
             functools.partial(middle_kernel, rim), [((rows, n), F32), ((2, rows + 16, n), F32)],
             [(SMEM, pole_shift), (SMEM, pole_weight), (VMEM, g), (VMEM, source), (VMEM, ext), (VMEM, x), (VMEM, sigma)],
@@ -265,26 +321,21 @@
             flops=8 * rows * rows * n, moved=4 * rows * order, alias={5: 1},
         )
         return call(
-            functools.partial(last_kernel, rim, hops),
-            [((share, n), F32)] + [((share + TAIL, n), F32)] * hops,
+            functools.partial(last_kernel, rim, hops), shares,
             [(SMEM, pole_weight), (VMEM, g), (VMEM, part), (VMEM, x), (VMEM, r), (VMEM, jnp.stack(got).astype(F32))],
             [pltpu.VMEM((rows, n), F32), pltpu.VMEM((2, 4 * rim, n), BF16)],
             flops=8 * rows * 4 * rim * n, moved=4 * rows * order,
         )
 
-    def reduced(sent, factor):
+    def moved(sent):
         own, *sent = sent
         got = []
         for hop, block in enumerate(sent):
             got.append(lax.ppermute(block.astype(F16), "pole", hop_pairs(hop + 1, poles)))
-        ins = [own] + [x.astype(F32) for x in got] + factor
-        return call(
-            sum_kernel, [((share, n), BF16 if factor else F32)], [(VMEM, x) for x in ins],
-            moved=4 * rows * n,
-        )[0]
+        return [own] + [x.astype(F32) for x in got]
 
     def gathered(own):
-        got = []
+        got, n = [], own.shape[1]
         for hop in range(hops):
             got.append(lax.ppermute(own, "pole", hop_pairs(hop + 1, poles)))
         return call(
@@ -293,17 +344,21 @@
             [(VMEM, own)] + [(VMEM, x) for x in got], moved=4 * rows * n,
         )
 
-    results = []
-    for chunk in range(CHUNKS):
+    results, lane = [], 0
+    for chunk, n in enumerate(widths):
         source, halo = sources[chunk], first_halo
         for step in range(STEPS):
-            factor = [sigma_share] if step + 1 < STEPS else []
-            total = reduced(sweep(source, halo, 0 if step else chunk * n), factor)
+            terms = moved(sweep(source, halo, 0 if step else lane, split_at(chunk)))
             if step + 1 < STEPS:
+                (total,) = call(
+                    sum_kernel, [((share, n), BF16)], [(VMEM, x) for x in [sigma_share] + terms],
+                    moved=4 * rows * n,
+                )
                 source, one, two = gathered(total)
                 halo = exchange(one, two)
-        results.append(total)
-    return jnp.concatenate(results, axis=1) if CHUNKS > 1 else results[0]
+        results.extend(terms)
+        lane += n
+    return call(final_kernel, [((share, columns), F32)], [(VMEM, x) for x in results], moved=4 * rows * columns)[0]
 
 
 def solution(mesh):

time: 110 us -> 110 us (level)
  the two profiles are of different devices: /device:TPU:5 before, /device:TPU:18 now
where the time goes in v5:
time: 110 us; the launch traced here: 108 us
  starting transfers between devices  46.6 us (42%)
  Pallas kernels  27.6 us (25%)
  waiting for transfers between devices  26.8 us (24%)
  local copies, waits for them, and re-layouts  5.12 us (5%)
    pallas_call x17, Pallas kernels, call(): pl.pallas_call(kernel, out_shape=[jax.ShapeDtypeStruct(s, d) for s, d in...  27.6 us
    ppermute x12, waiting for transfers between devices, moved(): lax.ppermute(block.astype(F16), 'pole', hop_pairs(hop + 1, poles))  19.5 us
    ppermute x7, starting transfers between devices, exchange(): two = lax.ppermute(two, 'sub', pairs2)  18.3 us
    ppermute x12, starting transfers between devices, moved(): lax.ppermute(block.astype(F16), 'pole', hop_pairs(hop + 1, poles))  15.2 us
    ppermute x6, waiting for transfers between devices, gathered(): got.append(lax.ppermute(own, 'pole', hop_pairs(hop + 1, poles)))  7.3 us
    ppermute x6, starting transfers between devices, gathered(): got.append(lax.ppermute(own, 'pole', hop_pairs(hop + 1, poles)))  7.09 us
    ppermute x7, starting transfers between devices, exchange(): one = lax.ppermute(one, 'sub', pairs1)  5.97 us
    unnamed x12, local copies, waits for them, and re-layouts  4.67 us
  transfers between devices with their start and end apart: 32, of which 5 were waited for; matrix products, arithmetic and copies ran while one was open for 1% of the time, Pallas kernels for 23%

profile of v5, /device:TPU:18, one launch (start us, length us, event | category | flops | bytes accessed | tf_op | source)
XLA Modules:
  0.0 107.8 jit_solution(1851845949375096859)
XLA Ops:
  0.0 1.4 %copy-done = f32[768,512]{1,0:T(8,128)S(1)} copy-done((f32[768,512]{1,0:T(8,128)S(1)}, f32[768,512]{1,0:T(8,128)}, u32[]{:S(2)}) %copy-start) | copy-done | bytes 1572888
  1.4 0.7 copy-done.3
  2.1 0.7 copy-done.4
  2.8 0.4 shard_map.64
  3.2 0.1 collective-permute-start
  3.3 2.5 %collective-permute-start.1 = (bf16[128,512]{1,0:T(8,128)(2,1)S(1)}, bf16[128,512]{1,0:T(8,128)(2,1)S(1)}, u32[]{:S(2)}, u32[]{:S(2)}) collective-permute-start(bf16[128,512]{1,0:T(8,128)(2,1)S(1)} %get-tuple-element.58), channel_id=1, source_target_pairs={{8,4},{4,8},{16,12},{12,16},{24,20},{20,24},{9,5},{5,9},{17,13},{1... | collective-permute-start | bytes 393224 | tf_op jit(solution)/shard_map/ppermute | solution.py:284
  5.8 1.9 %copy-done.5 = bf16[1,768,2048]{2,1,0:T(8,128)(2,1)S(1)} copy-done((bf16[1,768,2048]{2,1,0:T(8,128)(2,1)S(1)}, bf16[1,768,2048]{2,1,0:T(8,128)(2,1)}, u32[]{:S(2)}) %copy-start.5) | copy-done | bytes 3145752
  7.7 3.9 %shard_map.65.g_ref = bf16[1536,1024]{1,0:T(8,128)(2,1)S(1)} custom-call(f32[1,1024]{1,0:T(1,128)S(1)} %get-tuple-element.54.row_ref, bf16[1,768,2048]{2,1,0:T(8,128)(2,1)S(1)} %copy-done.5), custom_call_target="tpu_custom_call" | custom-call | flops 3221225472 | bytes 4718592 | tf_op jit(solution)/shard_map/pallas_call | solution.py:27
  11.7 1.7 %shard_map.66 = (bf16[1024,256]{1,0:T(8,128)(2,1)S(1)}, f32[2,784,256]{2,1,0:T(8,128)S(1)}, f32[2,2,128,256]{3,2,1,0:T(8,128)S(1)}, f32[2,520,256]{2,1,0:T(8,128)S(1)}) custom-call(f32[1,2]{1,0:T(1,128)S(1)} %copy-done.1, bf16[1536,1024]{1,0:T(8,128)(2,1)S(1)} %shard_map.65.g_ref, f32[768,256]{1,0:T(8,128)S(1)} %get-tuple-element.56.src_ref, ...), custom_call_target="tpu_custom_call" | custom-call | flops 536870912 | bytes 3145728 | tf_op jit(solution)/shard_map/pallas_call | solution.py:27
  13.3 0.1 convert.16
  13.4 0.1 slice_bitcast_fusion.7
  13.5 3.0 %collective-permute-start.3 = (f16[520,256]{1,0:T(8,128)(2,1)S(1)}, f16[520,256]{1,0:T(8,128)(2,1)S(1)}, u32[]{:S(2)}, u32[]{:S(2)}) collective-permute-start(f16[520,256]{1,0:T(8,128)(2,1)S(1)} %get-tuple-element.110), channel_id=1, source_target_pairs={{8,4},{4,8},{16,12},{12,16},{24,20},{20,24},{9,5},{5,9},{17,13},{1... | collective-permute-start | bytes 798728 | tf_op jit(solution)/shard_map/ppermute | solution.py:284
  16.6 1.4 %collective-permute-start.2 = (f16[520,256]{1,0:T(8,128)(2,1)S(1)}, f16[520,256]{1,0:T(8,128)(2,1)S(1)}, u32[]{:S(2)}, u32[]{:S(2)}) collective-permute-start(f16[520,256]{1,0:T(8,128)(2,1)S(1)} %get-tuple-element.109), channel_id=1, source_target_pairs={{4,0},{0,4},{12,8},{8,12},{20,16},{16,20},{28,24},{24,28},{5,1},{1... | collective-permute-start | bytes 798728 | tf_op jit(solution)/shard_map/ppermute | solution.py:283
  18.0 1.7 %shard_map.74 = (bf16[1024,256]{1,0:T(8,128)(2,1)S(1)}, f32[2,784,256]{2,1,0:T(8,128)S(1)}, f32[2,2,128,256]{3,2,1,0:T(8,128)S(1)}, f32[2,520,256]{2,1,0:T(8,128)S(1)}) custom-call(f32[1,2]{1,0:T(1,128)S(1)} %copy-done.1, bf16[1536,1024]{1,0:T(8,128)(2,1)S(1)} %shard_map.65.g_ref, f32[768,256]{1,0:T(8,128)S(1)} %get-tuple-element.83.src_ref, ...), custom_call_target="tpu_custom_call" | custom-call | flops 536870912 | bytes 3145728 | tf_op jit(solution)/shard_map/pallas_call | solution.py:27
  19.7 0.1 convert.18
  19.8 0.1 slice_bitcast_fusion.3
  19.9 2.1 %collective-permute-start.18 = (f16[520,256]{1,0:T(8,128)(2,1)S(1)}, f16[520,256]{1,0:T(8,128)(2,1)S(1)}, u32[]{:S(2)}, u32[]{:S(2)}) collective-permute-start(f16[520,256]{1,0:T(8,128)(2,1)S(1)} %get-tuple-element.106), channel_id=1, source_target_pairs={{8,4},{4,8},{16,12},{12,16},{24,20},{20,24},{9,5},{5,9},{17,13},{1... | collective-permute-start | bytes 798728 | tf_op jit(solution)/shard_map/ppermute | solution.py:284
  22.0 1.2 %collective-permute-start.17 = (f16[520,256]{1,0:T(8,128)(2,1)S(1)}, f16[520,256]{1,0:T(8,128)(2,1)S(1)}, u32[]{:S(2)}, u32[]{:S(2)}) collective-permute-start(f16[520,256]{1,0:T(8,128)(2,1)S(1)} %get-tuple-element.105), channel_id=1, source_target_pairs={{4,0},{0,4},{12,8},{8,12},{20,16},{16,20},{28,24},{24,28},{5,1},{1... | collective-permute-start | bytes 798728 | tf_op jit(solution)/shard_map/ppermute | solution.py:283
  23.3 2.4 %shard_map.67 = (f32[768,256]{1,0:T(8,128)S(1)}, f32[2,784,256]{2,1,0:T(8,128)S(1)}) custom-call(f32[1,2]{1,0:T(1,128)S(1)} %copy-done.1, f32[1,2]{1,0:T(1,128)S(1)} %copy-done.2, bf16[1536,1024]{1,0:T(8,128)(2,1)S(1)} %shard_map.65.g_ref, f32[768,256]{1,0:T(8,128)S(1)} %get-tuple-element.56.src_ref, ...), custom_call_target="tpu_custom_call", output_to_operand_aliasing={{1}: (5, {})} | custom-call | flops 1207959552 | bytes 3145728 | tf_op jit(solution)/shard_map/pallas_call | solution.py:27
  25.7 0.1 maximum_convert_fusion.got_ref
  25.7 1.8 %shard_map.68 = (f32[192,256]{1,0:T(8,128)S(1)}, f32[200,256]{1,0:T(8,128)S(1)}, f32[200,256]{1,0:T(8,128)S(1)}, f32[200,256]{1,0:T(8,128)S(1)}) custom-call(f32[1,2]{1,0:T(1,128)S(1)} %copy-done.2, bf16[1536,1024]{1,0:T(8,128)(2,1)S(1)} %shard_map.65.g_ref, f32[768,256]{1,0:T(8,128)S(1)} %get-tuple-element.62.part_ref, ...), custom_call_target="tpu_custom_call" | custom-call | flops 805306368 | bytes 3145728 | tf_op jit(solution)/shard_map/pallas_call | solution.py:27
  27.6 1.7 %collective-permute-start.4 = (f16[200,256]{1,0:T(8,128)(2,1)S(1)}, f16[200,256]{1,0:T(8,128)(2,1)S(1)}, u32[]{:S(2)}, u32[]{:S(2)}) collective-permute-start(f16[200,256]{1,0:T(8,128)(2,1)S(1)} %convert_element_type.119), channel_id=1, source_target_pairs={{0,1},{1,0},{2,3},{3,2},{4,5},{5,4},{6,7},{7,6},{8,9},{9,8},{10,11... | collective-permute-start | bytes 307208 | tf_op jit(solution)/shard_map/ppermute | solution.py:334
  29.2 0.4 collective-permute-start.5
  29.6 1.6 %collective-permute-start.6 = (f16[200,256]{1,0:T(8,128)(2,1)S(1)}, f16[200,256]{1,0:T(8,128)(2,1)S(1)}, u32[]{:S(2)}, u32[]{:S(2)}) collective-permute-start(f16[200,256]{1,0:T(8,128)(2,1)S(1)} %convert_element_type.123), channel_id=1, source_target_pairs={{0,3},{1,2},{2,1},{3,0},{4,7},{5,6},{6,5},{7,4},{8,11},{9,10},{10,... | collective-permute-start | bytes 307208 | tf_op jit(solution)/shard_map/ppermute | solution.py:334
  31.3 0.1 maximum_convert_fusion.2.got_ref
  31.4 3.6 %shard_map.75 = (f32[192,256]{1,0:T(8,128)S(1)}, f32[200,256]{1,0:T(8,128)S(1)}, f32[200,256]{1,0:T(8,128)S(1)}, f32[200,256]{1,0:T(8,128)S(1)}, f32[2,784,256]{2,1,0:T(8,128)S(1)}) custom-call(f32[1,2]{1,0:T(1,128)S(1)} %copy-done.1, f32[1,2]{1,0:T(1,128)S(1)} %copy-done.2, ...), custom_call_target="tpu_custom_call", output_to_operand_aliasing={{4}: (5, {})} | custom-call | flops 1610612736 | bytes 3145728 | tf_op jit(solution)/shard_map/pallas_call | solution.py:27
  35.0 2.6 %collective-permute-start.19 = (f16[200,256]{1,0:T(8,128)(2,1)S(1)}, f16[200,256]{1,0:T(8,128)(2,1)S(1)}, u32[]{:S(2)}, u32[]{:S(2)}) collective-permute-start(f16[200,256]{1,0:T(8,128)(2,1)S(1)} %convert_element_type.137), channel_id=1, source_target_pairs={{0,1},{1,0},{2,3},{3,2},{4,5},{5,4},{6,7},{7,6},{8,9},{9,8},{10,11... | collective-permute-start | bytes 307208 | tf_op jit(solution)/shard_map/ppermute | solution.py:334
  37.6 0.1 collective-permute-start.20
  37.7 1.5 %collective-permute-start.21 = (f16[200,256]{1,0:T(8,128)(2,1)S(1)}, f16[200,256]{1,0:T(8,128)(2,1)S(1)}, u32[]{:S(2)}, u32[]{:S(2)}) collective-permute-start(f16[200,256]{1,0:T(8,128)(2,1)S(1)} %convert_element_type.141), channel_id=1, source_target_pairs={{0,3},{1,2},{2,1},{3,0},{4,7},{5,6},{6,5},{7,4},{8,11},{9,10},{10,... | collective-permute-start | bytes 307208 | tf_op jit(solution)/shard_map/ppermute | solution.py:334
  39.3 8.6 %collective-permute-done.6 = f16[200,256]{1,0:T(8,128)(2,1)S(1)} collective-permute-done((f16[200,256]{1,0:T(8,128)(2,1)S(1)}, f16[200,256]{1,0:T(8,128)(2,1)S(1)}, u32[]{:S(2)}, u32[]{:S(2)}) %collective-permute-start.6) | collective-permute-done | bytes 102432 | tf_op jit(solution)/shard_map/ppermute | solution.py:334
  47.9 0.1 shard_map.69.own_ref
  48.2 3.4 %collective-permute-start.9 = (bf16[192,256]{1,0:T(8,128)(2,1)S(1)}, bf16[192,256]{1,0:T(8,128)(2,1)S(1)}, u32[]{:S(2)}, u32[]{:S(2)}) collective-permute-start(bf16[192,256]{1,0:T(8,128)(2,1)S(1)} %shard_map.69.own_ref), channel_id=1, source_target_pairs={{0,3},{1,2},{2,1},{3,0},{4,7},{5,6},{6,5},{7,4},{8,11},{9,10},{10,... | collective-permute-start | bytes 294920 | tf_op jit(solution)/shard_map/ppermute | solution.py:340
  51.6 0.7 collective-permute-done.21
  52.3 0.1 shard_map.76.own_ref
  52.4 0.4 collective-permute-start.22
  52.8 1.5 %collective-permute-start.23 = (bf16[192,256]{1,0:T(8,128)(2,1)S(1)}, bf16[192,256]{1,0:T(8,128)(2,1)S(1)}, u32[]{:S(2)}, u32[]{:S(2)}) collective-permute-start(bf16[192,256]{1,0:T(8,128)(2,1)S(1)} %shard_map.76.own_ref), channel_id=1, source_target_pairs={{0,2},{1,3},{2,0},{3,1},{4,6},{5,7},{6,4},{7,5},{8,10},{9,11},{10,... | collective-permute-start | bytes 294920 | tf_op jit(solution)/shard_map/ppermute | solution.py:340
  54.3 1.6 %collective-permute-start.24 = (bf16[192,256]{1,0:T(8,128)(2,1)S(1)}, bf16[192,256]{1,0:T(8,128)(2,1)S(1)}, u32[]{:S(2)}, u32[]{:S(2)}) collective-permute-start(bf16[192,256]{1,0:T(8,128)(2,1)S(1)} %shard_map.76.own_ref), channel_id=1, source_target_pairs={{0,3},{1,2},{2,1},{3,0},{4,7},{5,6},{6,5},{7,4},{8,11},{9,10},{10,... | collective-permute-start | bytes 294920 | tf_op jit(solution)/shard_map/ppermute | solution.py:340
  56.0 7.3 %collective-permute-done.9.rest_2_ = bf16[192,256]{1,0:T(8,128)(2,1)S(1)} collective-permute-done((bf16[192,256]{1,0:T(8,128)(2,1)S(1)}, bf16[192,256]{1,0:T(8,128)(2,1)S(1)}, u32[]{:S(2)}, u32[]{:S(2)}) %collective-permute-start.9) | collective-permute-done | bytes 98336 | tf_op jit(solution)/shard_map/ppermute | solution.py:340
  63.4 3.0 %collective-permute-start.11 = (bf16[128,256]{1,0:T(8,128)(2,1)S(1)}, bf16[128,256]{1,0:T(8,128)(2,1)S(1)}, u32[]{:S(2)}, u32[]{:S(2)}) collective-permute-start(bf16[128,256]{1,0:T(8,128)(2,1)S(1)} %get-tuple-element.72), channel_id=1, source_target_pairs={{8,4},{4,8},{16,12},{12,16},{24,20},{20,24},{9,5},{5,9},{17,13},{1... | collective-permute-start | bytes 196616 | tf_op jit(solution)/shard_map/ppermute | solution.py:284
  66.5 0.8 collective-permute-start.25
  67.2 1.9 %collective-permute-start.26 = (bf16[128,256]{1,0:T(8,128)(2,1)S(1)}, bf16[128,256]{1,0:T(8,128)(2,1)S(1)}, u32[]{:S(2)}, u32[]{:S(2)}) collective-permute-start(bf16[128,256]{1,0:T(8,128)(2,1)S(1)} %get-tuple-element.94), channel_id=1, source_target_pairs={{8,4},{4,8},{16,12},{12,16},{24,20},{20,24},{9,5},{5,9},{17,13},{1... | collective-permute-start | bytes 196616 | tf_op jit(solution)/shard_map/ppermute | solution.py:284
  69.1 1.7 %shard_map.71 = (bf16[1024,256]{1,0:T(8,128)(2,1)S(1)}, f32[2,784,256]{2,1,0:T(8,128)S(1)}, f32[2,2,128,256]{3,2,1,0:T(8,128)S(1)}, f32[2,520,256]{2,1,0:T(8,128)S(1)}) custom-call(f32[1,2]{1,0:T(1,128)S(1)} %copy-done.1, bf16[1536,1024]{1,0:T(8,128)(2,1)S(1)} %shard_map.65.g_ref, bf16[768,256]{1,0:T(8,128)(2,1)S(1)} %get-tuple-element.70.src_ref, ...), custom_call_target="tpu_custom_call" | custom-call | flops 536870912 | bytes 3145728 | tf_op jit(solution)/shard_map/pallas_call | solution.py:27
  70.8 0.1 convert.17
  70.9 0.1 slice_bitcast_fusion.5
  71.0 3.6 %collective-permute-start.13 = (f16[520,256]{1,0:T(8,128)(2,1)S(1)}, f16[520,256]{1,0:T(8,128)(2,1)S(1)}, u32[]{:S(2)}, u32[]{:S(2)}) collective-permute-start(f16[520,256]{1,0:T(8,128)(2,1)S(1)} %get-tuple-element.108), channel_id=1, source_target_pairs={{8,4},{4,8},{16,12},{12,16},{24,20},{20,24},{9,5},{5,9},{17,13},{1... | collective-permute-start | bytes 798728 | tf_op jit(solution)/shard_map/ppermute | solution.py:284
  74.7 1.5 %collective-permute-start.12 = (f16[520,256]{1,0:T(8,128)(2,1)S(1)}, f16[520,256]{1,0:T(8,128)(2,1)S(1)}, u32[]{:S(2)}, u32[]{:S(2)}) collective-permute-start(f16[520,256]{1,0:T(8,128)(2,1)S(1)} %get-tuple-element.107), channel_id=1, source_target_pairs={{4,0},{0,4},{12,8},{8,12},{20,16},{16,20},{28,24},{24,28},{5,1},{1... | collective-permute-start | bytes 798728 | tf_op jit(solution)/shard_map/ppermute | solution.py:283
  76.2 1.7 %shard_map.78 = (bf16[1024,256]{1,0:T(8,128)(2,1)S(1)}, f32[2,784,256]{2,1,0:T(8,128)S(1)}, f32[2,2,128,256]{3,2,1,0:T(8,128)S(1)}, f32[2,520,256]{2,1,0:T(8,128)S(1)}) custom-call(f32[1,2]{1,0:T(1,128)S(1)} %copy-done.1, bf16[1536,1024]{1,0:T(8,128)(2,1)S(1)} %shard_map.65.g_ref, bf16[768,256]{1,0:T(8,128)(2,1)S(1)} %get-tuple-element.92.src_ref, ...), custom_call_target="tpu_custom_call" | custom-call | flops 536870912 | bytes 3145728 | tf_op jit(solution)/shard_map/pallas_call | solution.py:27
  77.9 0.1 convert.19
  78.0 0.1 slice_bitcast_fusion.1
  78.1 2.1 %collective-permute-start.28 = (f16[520,256]{1,0:T(8,128)(2,1)S(1)}, f16[520,256]{1,0:T(8,128)(2,1)S(1)}, u32[]{:S(2)}, u32[]{:S(2)}) collective-permute-start(f16[520,256]{1,0:T(8,128)(2,1)S(1)} %get-tuple-element.104), channel_id=1, source_target_pairs={{8,4},{4,8},{16,12},{12,16},{24,20},{20,24},{9,5},{5,9},{17,13},{1... | collective-permute-start | bytes 798728 | tf_op jit(solution)/shard_map/ppermute | solution.py:284
  80.2 0.9 collective-permute-start.27
  81.2 2.4 %shard_map.72 = (f32[768,256]{1,0:T(8,128)S(1)}, f32[2,784,256]{2,1,0:T(8,128)S(1)}) custom-call(f32[1,2]{1,0:T(1,128)S(1)} %copy-done.1, f32[1,2]{1,0:T(1,128)S(1)} %copy-done.2, bf16[1536,1024]{1,0:T(8,128)(2,1)S(1)} %shard_map.65.g_ref, bf16[768,256]{1,0:T(8,128)(2,1)S(1)} %get-tuple-element.70.src_ref, ...), custom_call_target="tpu_custom_call", output_to_operand_aliasing={{1}: (5, {})} | custom-call | flops 1207959552 | bytes 3145728 | tf_op jit(solution)/shard_map/pallas_call | solution.py:27
  83.6 0.1 maximum_convert_fusion.1.got_ref
  83.7 1.8 %shard_map.73 = (f32[192,256]{1,0:T(8,128)S(1)}, f32[200,256]{1,0:T(8,128)S(1)}, f32[200,256]{1,0:T(8,128)S(1)}, f32[200,256]{1,0:T(8,128)S(1)}) custom-call(f32[1,2]{1,0:T(1,128)S(1)} %copy-done.2, bf16[1536,1024]{1,0:T(8,128)(2,1)S(1)} %shard_map.65.g_ref, f32[768,256]{1,0:T(8,128)S(1)} %get-tuple-element.75.part_ref, ...), custom_call_target="tpu_custom_call" | custom-call | flops 805306368 | bytes 3145728 | tf_op jit(solution)/shard_map/pallas_call | solution.py:27
  85.6 1.5 %collective-permute-start.15 = (f16[200,256]{1,0:T(8,128)(2,1)S(1)}, f16[200,256]{1,0:T(8,128)(2,1)S(1)}, u32[]{:S(2)}, u32[]{:S(2)}) collective-permute-start(f16[200,256]{1,0:T(8,128)(2,1)S(1)} %convert_element_type.130), channel_id=1, source_target_pairs={{0,2},{1,3},{2,0},{3,1},{4,6},{5,7},{6,4},{7,5},{8,10},{9,11},{10,... | collective-permute-start | bytes 307208 | tf_op jit(solution)/shard_map/ppermute | solution.py:334
  87.1 2.1 %collective-permute-start.16 = (f16[200,256]{1,0:T(8,128)(2,1)S(1)}, f16[200,256]{1,0:T(8,128)(2,1)S(1)}, u32[]{:S(2)}, u32[]{:S(2)}) collective-permute-start(f16[200,256]{1,0:T(8,128)(2,1)S(1)} %convert_element_type.132), channel_id=1, source_target_pairs={{0,3},{1,2},{2,1},{3,0},{4,7},{5,6},{6,5},{7,4},{8,11},{9,10},{10,... | collective-permute-start | bytes 307208 | tf_op jit(solution)/shard_map/ppermute | solution.py:334
  89.2 0.1 maximum_convert_fusion.3.got_ref
  89.3 3.6 %shard_map.79 = (f32[192,256]{1,0:T(8,128)S(1)}, f32[200,256]{1,0:T(8,128)S(1)}, f32[200,256]{1,0:T(8,128)S(1)}, f32[200,256]{1,0:T(8,128)S(1)}, f32[2,784,256]{2,1,0:T(8,128)S(1)}) custom-call(f32[1,2]{1,0:T(1,128)S(1)} %copy-done.1, f32[1,2]{1,0:T(1,128)S(1)} %copy-done.2, ...), custom_call_target="tpu_custom_call", output_to_operand_aliasing={{4}: (5, {})} | custom-call | flops 1610612736 | bytes 3145728 | tf_op jit(solution)/shard_map/pallas_call | solution.py:27
  92.9 1.0 collective-permute-start.29
  93.9 0.6 collective-permute-start.30
  94.6 2.1 %collective-permute-start.31 = (f16[200,256]{1,0:T(8,128)(2,1)S(1)}, f16[200,256]{1,0:T(8,128)(2,1)S(1)}, u32[]{:S(2)}, u32[]{:S(2)}) collective-permute-start(f16[200,256]{1,0:T(8,128)(2,1)S(1)} %convert_element_type.150), channel_id=1, source_target_pairs={{0,3},{1,2},{2,1},{3,0},{4,7},{5,6},{6,5},{7,4},{8,11},{9,10},{10,... | collective-permute-start | bytes 307208 | tf_op jit(solution)/shard_map/ppermute | solution.py:334
  96.7 6.4 %collective-permute-done.16 = f16[200,256]{1,0:T(8,128)(2,1)S(1)} collective-permute-done((f16[200,256]{1,0:T(8,128)(2,1)S(1)}, f16[200,256]{1,0:T(8,128)(2,1)S(1)}, u32[]{:S(2)}, u32[]{:S(2)}) %collective-permute-start.16) | collective-permute-done | bytes 102432 | tf_op jit(solution)/shard_map/ppermute | solution.py:334
  103.2 3.7 %collective-permute-done.31 = f16[200,256]{1,0:T(8,128)(2,1)S(1)} collective-permute-done((f16[200,256]{1,0:T(8,128)(2,1)S(1)}, f16[200,256]{1,0:T(8,128)(2,1)S(1)}, u32[]{:S(2)}, u32[]{:S(2)}) %collective-permute-start.31) | collective-permute-done | bytes 102432 | tf_op jit(solution)/shard_map/ppermute | solution.py:334
  106.9 0.9 shard_map.80
  (65 shorter events, 0.8 us)
Async XLA Ops:
  0.0 1.4 %copy-start = (f32[768,512]{1,0:T(8,128)S(1)}, f32[768,512]{1,0:T(8,128)}, u32[]{:S(2)}) copy-start(f32[768,512]{1,0:T(8,128)} %state_ref.1) | copy-start | bytes 4718596
  1.4 0.7 copy-start.3
  2.1 0.7 copy-start.4
  3.2 8.4 %collective-permute-start = (bf16[128,512]{1,0:T(8,128)(2,1)S(1)}, bf16[128,512]{1,0:T(8,128)(2,1)S(1)}, u32[]{:S(2)}, u32[]{:S(2)}) collective-permute-start(bf16[128,512]{1,0:T(8,128)(2,1)S(1)} %get-tuple-element.57), channel_id=1, source_target_pairs={{4,0},{0,4},{12,8},{8,12},{20,16},{16,20},{28,24},{24,28},{5,1},{1... | collective-permute-start | bytes 393224 | tf_op jit(solution)/shard_map/ppermute | solution.py:283
  3.3 8.4 %collective-permute-start.1 = (bf16[128,512]{1,0:T(8,128)(2,1)S(1)}, bf16[128,512]{1,0:T(8,128)(2,1)S(1)}, u32[]{:S(2)}, u32[]{:S(2)}) collective-permute-start(bf16[128,512]{1,0:T(8,128)(2,1)S(1)} %get-tuple-element.58), channel_id=1, source_target_pairs={{8,4},{4,8},{16,12},{12,16},{24,20},{20,24},{9,5},{5,9},{17,13},{1... | collective-permute-start | bytes 393224 | tf_op jit(solution)/shard_map/ppermute | solution.py:284
  5.8 1.9 %copy-start.5 = (bf16[1,768,2048]{2,1,0:T(8,128)(2,1)S(1)}, bf16[1,768,2048]{2,1,0:T(8,128)(2,1)}, u32[]{:S(2)}) copy-start(bf16[1,768,2048]{2,1,0:T(8,128)(2,1)} %inv_ref.1) | copy-start | bytes 9437188
  7.7 3.9 %copy-start.1 = (f32[1,2]{1,0:T(1,128)S(1)}, f32[1,2]{1,0:T(1,128)}, u32[]{:S(2)}) copy-start(f32[1,2]{1,0:T(1,128)} %shift_ref.15) | copy-start | bytes 28
  13.5 12.1 %collective-permute-start.3 = (f16[520,256]{1,0:T(8,128)(2,1)S(1)}, f16[520,256]{1,0:T(8,128)(2,1)S(1)}, u32[]{:S(2)}, u32[]{:S(2)}) collective-permute-start(f16[520,256]{1,0:T(8,128)(2,1)S(1)} %get-tuple-element.110), channel_id=1, source_target_pairs={{8,4},{4,8},{16,12},{12,16},{24,20},{20,24},{9,5},{5,9},{17,13},{1... | collective-permute-start | bytes 798728 | tf_op jit(solution)/shard_map/ppermute | solution.py:284
  16.6 9.1 %collective-permute-start.2 = (f16[520,256]{1,0:T(8,128)(2,1)S(1)}, f16[520,256]{1,0:T(8,128)(2,1)S(1)}, u32[]{:S(2)}, u32[]{:S(2)}) collective-permute-start(f16[520,256]{1,0:T(8,128)(2,1)S(1)} %get-tuple-element.109), channel_id=1, source_target_pairs={{4,0},{0,4},{12,8},{8,12},{20,16},{16,20},{28,24},{24,28},{5,1},{1... | collective-permute-start | bytes 798728 | tf_op jit(solution)/shard_map/ppermute | solution.py:283
  19.7 3.5 %copy-start.2 = (f32[1,2]{1,0:T(1,128)S(1)}, f32[1,2]{1,0:T(1,128)}, u32[]{:S(2)}) copy-start(f32[1,2]{1,0:T(1,128)} %weight_ref.11) | copy-start | bytes 28
  19.9 11.3 %collective-permute-start.18 = (f16[520,256]{1,0:T(8,128)(2,1)S(1)}, f16[520,256]{1,0:T(8,128)(2,1)S(1)}, u32[]{:S(2)}, u32[]{:S(2)}) collective-permute-start(f16[520,256]{1,0:T(8,128)(2,1)S(1)} %get-tuple-element.106), channel_id=1, source_target_pairs={{8,4},{4,8},{16,12},{12,16},{24,20},{20,24},{9,5},{5,9},{17,13},{1... | collective-permute-start | bytes 798728 | tf_op jit(solution)/shard_map/ppermute | solution.py:284
  22.0 9.2 %collective-permute-start.17 = (f16[520,256]{1,0:T(8,128)(2,1)S(1)}, f16[520,256]{1,0:T(8,128)(2,1)S(1)}, u32[]{:S(2)}, u32[]{:S(2)}) collective-permute-start(f16[520,256]{1,0:T(8,128)(2,1)S(1)} %get-tuple-element.105), channel_id=1, source_target_pairs={{4,0},{0,4},{12,8},{8,12},{20,16},{16,20},{28,24},{24,28},{5,1},{1... | collective-permute-start | bytes 798728 | tf_op jit(solution)/shard_map/ppermute | solution.py:283
  27.6 10.1 %collective-permute-start.4 = (f16[200,256]{1,0:T(8,128)(2,1)S(1)}, f16[200,256]{1,0:T(8,128)(2,1)S(1)}, u32[]{:S(2)}, u32[]{:S(2)}) collective-permute-start(f16[200,256]{1,0:T(8,128)(2,1)S(1)} %convert_element_type.119), channel_id=1, source_target_pairs={{0,1},{1,0},{2,3},{3,2},{4,5},{5,4},{6,7},{7,6},{8,9},{9,8},{10,11... | collective-permute-start | bytes 307208 | tf_op jit(solution)/shard_map/ppermute | solution.py:334
  29.2 10.0 %collective-permute-start.5 = (f16[200,256]{1,0:T(8,128)(2,1)S(1)}, f16[200,256]{1,0:T(8,128)(2,1)S(1)}, u32[]{:S(2)}, u32[]{:S(2)}) collective-permute-start(f16[200,256]{1,0:T(8,128)(2,1)S(1)} %convert_element_type.121), channel_id=1, source_target_pairs={{0,2},{1,3},{2,0},{3,1},{4,6},{5,7},{6,4},{7,5},{8,10},{9,11},{10,... | collective-permute-start | bytes 307208 | tf_op jit(solution)/shard_map/ppermute | solution.py:334
  29.6 18.3 %collective-permute-start.6 = (f16[200,256]{1,0:T(8,128)(2,1)S(1)}, f16[200,256]{1,0:T(8,128)(2,1)S(1)}, u32[]{:S(2)}, u32[]{:S(2)}) collective-permute-start(f16[200,256]{1,0:T(8,128)(2,1)S(1)} %convert_element_type.123), channel_id=1, source_target_pairs={{0,3},{1,2},{2,1},{3,0},{4,7},{5,6},{6,5},{7,4},{8,11},{9,10},{10,... | collective-permute-start | bytes 307208 | tf_op jit(solution)/shard_map/ppermute | solution.py:334
  35.0 13.2 %collective-permute-start.19 = (f16[200,256]{1,0:T(8,128)(2,1)S(1)}, f16[200,256]{1,0:T(8,128)(2,1)S(1)}, u32[]{:S(2)}, u32[]{:S(2)}) collective-permute-start(f16[200,256]{1,0:T(8,128)(2,1)S(1)} %convert_element_type.137), channel_id=1, source_target_pairs={{0,1},{1,0},{2,3},{3,2},{4,5},{5,4},{6,7},{7,6},{8,9},{9,8},{10,11... | collective-permute-start | bytes 307208 | tf_op jit(solution)/shard_map/ppermute | solution.py:334
  37.6 14.0 %collective-permute-start.20 = (f16[200,256]{1,0:T(8,128)(2,1)S(1)}, f16[200,256]{1,0:T(8,128)(2,1)S(1)}, u32[]{:S(2)}, u32[]{:S(2)}) collective-permute-start(f16[200,256]{1,0:T(8,128)(2,1)S(1)} %convert_element_type.139), channel_id=1, source_target_pairs={{0,2},{1,3},{2,0},{3,1},{4,6},{5,7},{6,4},{7,5},{8,10},{9,11},{10,... | collective-permute-start | bytes 307208 | tf_op jit(solution)/shard_map/ppermute | solution.py:334
  37.7 14.6 %collective-permute-start.21 = (f16[200,256]{1,0:T(8,128)(2,1)S(1)}, f16[200,256]{1,0:T(8,128)(2,1)S(1)}, u32[]{:S(2)}, u32[]{:S(2)}) collective-permute-start(f16[200,256]{1,0:T(8,128)(2,1)S(1)} %convert_element_type.141), channel_id=1, source_target_pairs={{0,3},{1,2},{2,1},{3,0},{4,7},{5,6},{6,5},{7,4},{8,11},{9,10},{10,... | collective-permute-start | bytes 307208 | tf_op jit(solution)/shard_map/ppermute | solution.py:334
  48.0 6.3 %collective-permute-start.7 = (bf16[192,256]{1,0:T(8,128)(2,1)S(1)}, bf16[192,256]{1,0:T(8,128)(2,1)S(1)}, u32[]{:S(2)}, u32[]{:S(2)}) collective-permute-start(bf16[192,256]{1,0:T(8,128)(2,1)S(1)} %shard_map.69.own_ref), channel_id=1, source_target_pairs={{0,1},{1,0},{2,3},{3,2},{4,5},{5,4},{6,7},{7,6},{8,9},{9,8},{10,11... | collective-permute-start | bytes 294920 | tf_op jit(solution)/shard_map/ppermute | solution.py:340
  48.1 7.9 %collective-permute-start.8 = (bf16[192,256]{1,0:T(8,128)(2,1)S(1)}, bf16[192,256]{1,0:T(8,128)(2,1)S(1)}, u32[]{:S(2)}, u32[]{:S(2)}) collective-permute-start(bf16[192,256]{1,0:T(8,128)(2,1)S(1)} %shard_map.69.own_ref), channel_id=1, source_target_pairs={{0,2},{1,3},{2,0},{3,1},{4,6},{5,7},{6,4},{7,5},{8,10},{9,11},{10,... | collective-permute-start | bytes 294920 | tf_op jit(solution)/shard_map/ppermute | solution.py:340
  48.2 15.1 %collective-permute-start.9 = (bf16[192,256]{1,0:T(8,128)(2,1)S(1)}, bf16[192,256]{1,0:T(8,128)(2,1)S(1)}, u32[]{:S(2)}, u32[]{:S(2)}) collective-permute-start(bf16[192,256]{1,0:T(8,128)(2,1)S(1)} %shard_map.69.own_ref), channel_id=1, source_target_pairs={{0,3},{1,2},{2,1},{3,0},{4,7},{5,6},{6,5},{7,4},{8,11},{9,10},{10,... | collective-permute-start | bytes 294920 | tf_op jit(solution)/shard_map/ppermute | solution.py:340
  52.4 14.0 %collective-permute-start.22 = (bf16[192,256]{1,0:T(8,128)(2,1)S(1)}, bf16[192,256]{1,0:T(8,128)(2,1)S(1)}, u32[]{:S(2)}, u32[]{:S(2)}) collective-permute-start(bf16[192,256]{1,0:T(8,128)(2,1)S(1)} %shard_map.76.own_ref), channel_id=1, source_target_pairs={{0,1},{1,0},{2,3},{3,2},{4,5},{5,4},{6,7},{7,6},{8,9},{9,8},{10,11... | collective-permute-start | bytes 294920 | tf_op jit(solution)/shard_map/ppermute | solution.py:340
  52.8 13.6 %collective-permute-start.23 = (bf16[192,256]{1,0:T(8,128)(2,1)S(1)}, bf16[192,256]{1,0:T(8,128)(2,1)S(1)}, u32[]{:S(2)}, u32[]{:S(2)}) collective-permute-start(bf16[192,256]{1,0:T(8,128)(2,1)S(1)} %shard_map.76.own_ref), channel_id=1, source_target_pairs={{0,2},{1,3},{2,0},{3,1},{4,6},{5,7},{6,4},{7,5},{8,10},{9,11},{10,... | collective-permute-start | bytes 294920 | tf_op jit(solution)/shard_map/ppermute | solution.py:340
  54.3 12.1 %collective-permute-start.24 = (bf16[192,256]{1,0:T(8,128)(2,1)S(1)}, bf16[192,256]{1,0:T(8,128)(2,1)S(1)}, u32[]{:S(2)}, u32[]{:S(2)}) collective-permute-start(bf16[192,256]{1,0:T(8,128)(2,1)S(1)} %shard_map.76.own_ref), channel_id=1, source_target_pairs={{0,3},{1,2},{2,1},{3,0},{4,7},{5,6},{6,5},{7,4},{8,11},{9,10},{10,... | collective-permute-start | bytes 294920 | tf_op jit(solution)/shard_map/ppermute | solution.py:340
  63.3 5.8 %collective-permute-start.10 = (bf16[128,256]{1,0:T(8,128)(2,1)S(1)}, bf16[128,256]{1,0:T(8,128)(2,1)S(1)}, u32[]{:S(2)}, u32[]{:S(2)}) collective-permute-start(bf16[128,256]{1,0:T(8,128)(2,1)S(1)} %get-tuple-element.71), channel_id=1, source_target_pairs={{4,0},{0,4},{12,8},{8,12},{20,16},{16,20},{28,24},{24,28},{5,1},{1... | collective-permute-start | bytes 196616 | tf_op jit(solution)/shard_map/ppermute | solution.py:283
  63.4 5.8 %collective-permute-start.11 = (bf16[128,256]{1,0:T(8,128)(2,1)S(1)}, bf16[128,256]{1,0:T(8,128)(2,1)S(1)}, u32[]{:S(2)}, u32[]{:S(2)}) collective-permute-start(bf16[128,256]{1,0:T(8,128)(2,1)S(1)} %get-tuple-element.72), channel_id=1, source_target_pairs={{8,4},{4,8},{16,12},{12,16},{24,20},{20,24},{9,5},{5,9},{17,13},{1... | collective-permute-start | bytes 196616 | tf_op jit(solution)/shard_map/ppermute | solution.py:284
  66.5 9.7 %collective-permute-start.25 = (bf16[128,256]{1,0:T(8,128)(2,1)S(1)}, bf16[128,256]{1,0:T(8,128)(2,1)S(1)}, u32[]{:S(2)}, u32[]{:S(2)}) collective-permute-start(bf16[128,256]{1,0:T(8,128)(2,1)S(1)} %get-tuple-element.93), channel_id=1, source_target_pairs={{4,0},{0,4},{12,8},{8,12},{20,16},{16,20},{28,24},{24,28},{5,1},{1... | collective-permute-start | bytes 196616 | tf_op jit(solution)/shard_map/ppermute | solution.py:283
  67.2 9.0 %collective-permute-start.26 = (bf16[128,256]{1,0:T(8,128)(2,1)S(1)}, bf16[128,256]{1,0:T(8,128)(2,1)S(1)}, u32[]{:S(2)}, u32[]{:S(2)}) collective-permute-start(bf16[128,256]{1,0:T(8,128)(2,1)S(1)} %get-tuple-element.94), channel_id=1, source_target_pairs={{8,4},{4,8},{16,12},{12,16},{24,20},{20,24},{9,5},{5,9},{17,13},{1... | collective-permute-start | bytes 196616 | tf_op jit(solution)/shard_map/ppermute | solution.py:284
  71.0 12.5 %collective-permute-start.13 = (f16[520,256]{1,0:T(8,128)(2,1)S(1)}, f16[520,256]{1,0:T(8,128)(2,1)S(1)}, u32[]{:S(2)}, u32[]{:S(2)}) collective-permute-start(f16[520,256]{1,0:T(8,128)(2,1)S(1)} %get-tuple-element.108), channel_id=1, source_target_pairs={{8,4},{4,8},{16,12},{12,16},{24,20},{20,24},{9,5},{5,9},{17,13},{1... | collective-permute-start | bytes 798728 | tf_op jit(solution)/shard_map/ppermute | solution.py:284
  74.7 8.9 %collective-permute-start.12 = (f16[520,256]{1,0:T(8,128)(2,1)S(1)}, f16[520,256]{1,0:T(8,128)(2,1)S(1)}, u32[]{:S(2)}, u32[]{:S(2)}) collective-permute-start(f16[520,256]{1,0:T(8,128)(2,1)S(1)} %get-tuple-element.107), channel_id=1, source_target_pairs={{4,0},{0,4},{12,8},{8,12},{20,16},{16,20},{28,24},{24,28},{5,1},{1... | collective-permute-start | bytes 798728 | tf_op jit(solution)/shard_map/ppermute | solution.py:283
  78.1 11.1 %collective-permute-start.28 = (f16[520,256]{1,0:T(8,128)(2,1)S(1)}, f16[520,256]{1,0:T(8,128)(2,1)S(1)}, u32[]{:S(2)}, u32[]{:S(2)}) collective-permute-start(f16[520,256]{1,0:T(8,128)(2,1)S(1)} %get-tuple-element.104), channel_id=1, source_target_pairs={{8,4},{4,8},{16,12},{12,16},{24,20},{20,24},{9,5},{5,9},{17,13},{1... | collective-permute-start | bytes 798728 | tf_op jit(solution)/shard_map/ppermute | solution.py:284
  80.2 9.0 %collective-permute-start.27 = (f16[520,256]{1,0:T(8,128)(2,1)S(1)}, f16[520,256]{1,0:T(8,128)(2,1)S(1)}, u32[]{:S(2)}, u32[]{:S(2)}) collective-permute-start(f16[520,256]{1,0:T(8,128)(2,1)S(1)} %get-tuple-element.103), channel_id=1, source_target_pairs={{4,0},{0,4},{12,8},{8,12},{20,16},{16,20},{28,24},{24,28},{5,1},{1... | collective-permute-start | bytes 798728 | tf_op jit(solution)/shard_map/ppermute | solution.py:283
  85.5 9.1 %collective-permute-start.14 = (f16[200,256]{1,0:T(8,128)(2,1)S(1)}, f16[200,256]{1,0:T(8,128)(2,1)S(1)}, u32[]{:S(2)}, u32[]{:S(2)}) collective-permute-start(f16[200,256]{1,0:T(8,128)(2,1)S(1)} %convert_element_type.128), channel_id=1, source_target_pairs={{0,1},{1,0},{2,3},{3,2},{4,5},{5,4},{6,7},{7,6},{8,9},{9,8},{10,11... | collective-permute-start | bytes 307208 | tf_op jit(solution)/shard_map/ppermute | solution.py:334
  85.6 11.1 %collective-permute-start.15 = (f16[200,256]{1,0:T(8,128)(2,1)S(1)}, f16[200,256]{1,0:T(8,128)(2,1)S(1)}, u32[]{:S(2)}, u32[]{:S(2)}) collective-permute-start(f16[200,256]{1,0:T(8,128)(2,1)S(1)} %convert_element_type.130), channel_id=1, source_target_pairs={{0,2},{1,3},{2,0},{3,1},{4,6},{5,7},{6,4},{7,5},{8,10},{9,11},{10,... | collective-permute-start | bytes 307208 | tf_op jit(solution)/shard_map/ppermute | solution.py:334
  87.1 16.0 %collective-permute-start.16 = (f16[200,256]{1,0:T(8,128)(2,1)S(1)}, f16[200,256]{1,0:T(8,128)(2,1)S(1)}, u32[]{:S(2)}, u32[]{:S(2)}) collective-permute-start(f16[200,256]{1,0:T(8,128)(2,1)S(1)} %convert_element_type.132), channel_id=1, source_target_pairs={{0,3},{1,2},{2,1},{3,0},{4,7},{5,6},{6,5},{7,4},{8,11},{9,10},{10,... | collective-permute-start | bytes 307208 | tf_op jit(solution)/shard_map/ppermute | solution.py:334
  92.9 10.2 %collective-permute-start.29 = (f16[200,256]{1,0:T(8,128)(2,1)S(1)}, f16[200,256]{1,0:T(8,128)(2,1)S(1)}, u32[]{:S(2)}, u32[]{:S(2)}) collective-permute-start(f16[200,256]{1,0:T(8,128)(2,1)S(1)} %convert_element_type.146), channel_id=1, source_target_pairs={{0,1},{1,0},{2,3},{3,2},{4,5},{5,4},{6,7},{7,6},{8,9},{9,8},{10,11... | collective-permute-start | bytes 307208 | tf_op jit(solution)/shard_map/ppermute | solution.py:334
  93.9 9.3 %collective-permute-start.30 = (f16[200,256]{1,0:T(8,128)(2,1)S(1)}, f16[200,256]{1,0:T(8,128)(2,1)S(1)}, u32[]{:S(2)}, u32[]{:S(2)}) collective-permute-start(f16[200,256]{1,0:T(8,128)(2,1)S(1)} %convert_element_type.148), channel_id=1, source_target_pairs={{0,2},{1,3},{2,0},{3,1},{4,6},{5,7},{6,4},{7,5},{8,10},{9,11},{10,... | collective-permute-start | bytes 307208 | tf_op jit(solution)/shard_map/ppermute | solution.py:334
  94.6 12.4 %collective-permute-start.31 = (f16[200,256]{1,0:T(8,128)(2,1)S(1)}, f16[200,256]{1,0:T(8,128)(2,1)S(1)}, u32[]{:S(2)}, u32[]{:S(2)}) collective-permute-start(f16[200,256]{1,0:T(8,128)(2,1)S(1)} %convert_element_type.150), channel_id=1, source_target_pairs={{0,3},{1,2},{2,1},{3,0},{4,7},{5,6},{6,5},{7,4},{8,11},{9,10},{10,... | collective-permute-start | bytes 307208 | tf_op jit(solution)/shard_map/ppermute | solution.py:334

commit v6 on v5

--- a/solution.py
+++ b/solution.py
@@ -19,8 +19,8 @@
 SMEM = pl.BlockSpec(memory_space=pltpu.SMEM)
 
 
-def split_at(chunk):
-    return chunk == 0
+def split_at(chunk, step):
+    return chunk == 0 or step == 0
 
 
 def call(kernel, outs, ins, scratch=(), flops=0, moved=0, alias=()):
@@ -90,12 +90,32 @@
         lane += ref.shape[1]
 
 
-def setup_kernel(row_ref, inv_ref, g_ref):
-    rows, width = inv_ref.shape[1], inv_ref.shape[2] // 2
+def places(row_ref):
+    width = row_ref.shape[1]
     ids = lax.broadcasted_iota(jnp.int32, (width, width), 1)
-    place = (column(row_ref[...], width).astype(jnp.int32) == ids).astype(BF16)
-    g_ref[:rows] = dot(inv_ref[0, :, :width], place).astype(BF16)
-    g_ref[rows:] = dot(inv_ref[0, :, width:], place).astype(BF16)
+    return (column(row_ref[...], width).astype(jnp.int32) == ids).astype(BF16)
+
+
+def setup_kernel(row_ref, inv_ref, outer_ref):
+    rows, width = inv_ref.shape[1], row_ref.shape[1]
+    span, place = outer_ref.shape[0] // 4, places(row_ref)
+    for half in range(2):
+        part = inv_ref.at[0, :, half * width:(half + 1) * width]
+        for side, lo in ((0, 0), (1, rows - span)):
+            at = (2 * half + side) * span
+            outer_ref[at:at + span] = dot(part[lo:lo + span], place).astype(BF16)
+
+
+def inner_kernel(row_ref, inv_ref, outer_ref, g_ref):
+    rows, width = inv_ref.shape[1], row_ref.shape[1]
+    span, place = outer_ref.shape[0] // 4, places(row_ref)
+    for half in range(2):
+        part = inv_ref.at[0, :, half * width:(half + 1) * width]
+        for side, lo in ((0, 0), (1, rows - span)):
+            at = (2 * half + side) * span
+            g_ref[half * rows + lo:half * rows + lo + span] = outer_ref[at:at + span]
+        if rows > 2 * span:
+            g_ref[half * rows + span:(half + 1) * rows - span] = dot(part[span:rows - span], place).astype(BF16)
 
 
 def stencil(x_ref, half, lo, count, rim, far_up, far_down):
@@ -132,7 +152,8 @@
     x_ref[:, 8 + rows:] = jnp.zeros((2, 8, n), F32)
     for lo in (0, rows - span):
         for half in range(2):
-            x_ref[half, 8 + lo:8 + lo + span] = dot(g_ref[half * rows + lo:half * rows + lo + span], ext_ref[...])
+            at = half * rows + lo if g_ref.shape[0] == 2 * rows else (2 * half + (lo > 0)) * span
+            x_ref[half, 8 + lo:8 + lo + span] = dot(g_ref[at:at + span], ext_ref[...])
     for side, lo in ((0, 0), (1, rows - rim)):
         for k in range(0, rim, step):
             out = residual(x_ref, lo + k, step, rim, side == 1, side == 0, src_ref, sigma_ref, a, b)
@@ -291,17 +312,21 @@
         [(VMEM, conductivity), (VMEM, order_list), (VMEM, state)], moved=8 * rows * columns,
     )
     first_halo = exchange(one, two)
+    (g_outer,) = call(
+        setup_kernel, [((8 * rim, order), BF16)], [(VMEM, order_row), (VMEM, inverse)],
+        flops=16 * rim * order * order, moved=6 * rows * order,
+    )
     (g,) = call(
-        setup_kernel, [((2 * rows, order), BF16)], [(VMEM, order_row), (VMEM, inverse)],
+        inner_kernel, [((2 * rows, order), BF16)], [(VMEM, order_row), (VMEM, inverse), (VMEM, g_outer)],
         flops=4 * rows * order * order, moved=6 * rows * order,
     )
 
-    def sweep(source, got, lane, split):
+    def sweep(source, got, lane, tag, split):
         n = source.shape[1]
         ext, x, r, msgs = call(
             functools.partial(edge_kernel, rim, lane),
             [((order, n), BF16), ((2, rows + 16, n), F32), ((2, 2, rim, n), F32), ((2, 4 * rim + TAIL, n), F32)],
-            [(SMEM, pole_shift), (VMEM, g), (VMEM, source), (VMEM, got[0]), (VMEM, got[1]), (VMEM, sigma)],
+            [(SMEM, pole_shift), (VMEM, g_outer if tag == "00" else g), (VMEM, source), (VMEM, got[0]), (VMEM, got[1]), (VMEM, sigma)],
             flops=16 * rim * order * n, moved=4 * rows * order,
         )
         got = exchange(msgs[0].astype(F16), msgs[1].astype(F16))
@@ -348,7 +373,8 @@
     for chunk, n in enumerate(widths):
         source, halo = sources[chunk], first_halo
         for step in range(STEPS):
-            terms = moved(sweep(source, halo, 0 if step else lane, split_at(chunk)))
+            tag = f"{chunk}{step}"
+            terms = moved(sweep(source, halo, 0 if step else lane, tag, split_at(chunk, step)))
             if step + 1 < STEPS:
                 (total,) = call(
                     sum_kernel, [((share, n), BF16)], [(VMEM, x) for x in [sigma_share] + terms],

time: 110 us -> 110 us (level)
  the two profiles are of different devices: /device:TPU:18 before, /device:TPU:3 now
where the time goes in v6:
time: 110 us
  starting transfers between devices  50.9 us (46%)
  Pallas kernels  29.2 us (27%)
  waiting for transfers between devices  23.2 us (21%)
  local copies, waits for them, and re-layouts  5.12 us (5%)
    pallas_call x19, Pallas kernels, call(): pl.pallas_call(kernel, out_shape=[jax.ShapeDtypeStruct(s, d) for s, d in...  29.2 us
    ppermute x7, starting transfers between devices, exchange(): two = lax.ppermute(two, 'sub', pairs2)  22.2 us
    ppermute x12, waiting for transfers between devices, moved(): lax.ppermute(block.astype(F16), 'pole', hop_pairs(hop + 1, poles))  17.5 us
    ppermute x12, starting transfers between devices, moved(): lax.ppermute(block.astype(F16), 'pole', hop_pairs(hop + 1, poles))  15.9 us
    ppermute x6, starting transfers between devices, gathered(): got.append(lax.ppermute(own, 'pole', hop_pairs(hop + 1, poles)))  10.7 us
    ppermute x6, waiting for transfers between devices, gathered(): got.append(lax.ppermute(own, 'pole', hop_pairs(hop + 1, poles)))  5.71 us
    unnamed x12, local copies, waits for them, and re-layouts  4.68 us
  transfers between devices with their start and end apart: 32, of which 7 were waited for; matrix products, arithmetic and copies ran while one was open for 1% of the time, Pallas kernels for 22%

profile of v6, /device:TPU:3, one launch (start us, length us, event | category | flops | bytes accessed | tf_op | source)
XLA Modules:
  0.0 110.1 jit_solution(16651918303420258409)
XLA Ops:
  0.0 1.4 %copy-done = f32[768,512]{1,0:T(8,128)S(1)} copy-done((f32[768,512]{1,0:T(8,128)S(1)}, f32[768,512]{1,0:T(8,128)}, u32[]{:S(2)}) %copy-start) | copy-done | bytes 1572888
  1.4 0.7 copy-done.3
  2.1 0.7 copy-done.4
  2.8 0.4 shard_map.64
  3.2 0.7 collective-permute-start
  3.9 3.0 %collective-permute-start.1 = (bf16[128,512]{1,0:T(8,128)(2,1)S(1)}, bf16[128,512]{1,0:T(8,128)(2,1)S(1)}, u32[]{:S(2)}, u32[]{:S(2)}) collective-permute-start(bf16[128,512]{1,0:T(8,128)(2,1)S(1)} %get-tuple-element.60), channel_id=1, source_target_pairs={{8,4},{4,8},{16,12},{12,16},{24,20},{20,24},{9,5},{5,9},{17,13},{1... | collective-permute-start | bytes 393224 | tf_op jit(solution)/shard_map/ppermute | solution.py:305
  7.0 1.9 %copy-done.5 = bf16[1,768,2048]{2,1,0:T(8,128)(2,1)S(1)} copy-done((bf16[1,768,2048]{2,1,0:T(8,128)(2,1)S(1)}, bf16[1,768,2048]{2,1,0:T(8,128)(2,1)}, u32[]{:S(2)}) %copy-start.5) | copy-done | bytes 3145752
  8.9 2.8 %shard_map.65.outer_ref.g_ref = bf16[1024,1024]{1,0:T(8,128)(2,1)S(1)} custom-call(f32[1,1024]{1,0:T(1,128)S(1)} %get-tuple-element.56.row_ref, bf16[1,768,2048]{2,1,0:T(8,128)(2,1)S(1)} %copy-done.5), custom_call_target="tpu_custom_call" | custom-call | flops 2147483648 | bytes 4718592 | tf_op jit(solution)/shard_map/pallas_call | solution.py:27
  11.7 2.0 %shard_map.66.g_ref = bf16[1536,1024]{1,0:T(8,128)(2,1)S(1)} custom-call(f32[1,1024]{1,0:T(1,128)S(1)} %get-tuple-element.56.row_ref, bf16[1,768,2048]{2,1,0:T(8,128)(2,1)S(1)} %copy-done.5, bf16[1024,1024]{1,0:T(8,128)(2,1)S(1)} %shard_map.65.outer_ref.g_ref), custom_call_target="tpu_custom_call" | custom-call | flops 3221225472 | bytes 4718592 | tf_op jit(solution)/shard_map/pallas_call | solution.py:27
  13.8 1.7 %shard_map.67 = (bf16[1024,256]{1,0:T(8,128)(2,1)S(1)}, f32[2,784,256]{2,1,0:T(8,128)S(1)}, f32[2,2,128,256]{3,2,1,0:T(8,128)S(1)}, f32[2,520,256]{2,1,0:T(8,128)S(1)}) custom-call(f32[1,2]{1,0:T(1,128)S(1)} %copy-done.1, bf16[1024,1024]{1,0:T(8,128)(2,1)S(1)} %shard_map.65.outer_ref.g_ref, f32[768,256]{1,0:T(8,128)S(1)} %get-tuple-element.58.src_ref, ...), custom_call_target="tpu_custom_call" | custom-call | flops 536870912 | bytes 3145728 | tf_op jit(solution)/shard_map/pallas_call | solution.py:27
  15.5 0.1 convert.16
  15.6 1.7 %shard_map.75 = (bf16[1024,256]{1,0:T(8,128)(2,1)S(1)}, f32[2,784,256]{2,1,0:T(8,128)S(1)}, f32[2,2,128,256]{3,2,1,0:T(8,128)S(1)}, f32[2,520,256]{2,1,0:T(8,128)S(1)}) custom-call(f32[1,2]{1,0:T(1,128)S(1)} %copy-done.1, bf16[1536,1024]{1,0:T(8,128)(2,1)S(1)} %shard_map.66.g_ref, f32[768,256]{1,0:T(8,128)S(1)} %get-tuple-element.85.src_ref, ...), custom_call_target="tpu_custom_call" | custom-call | flops 536870912 | bytes 3145728 | tf_op jit(solution)/shard_map/pallas_call | solution.py:27
  17.2 0.1 convert.18
  17.3 0.1 slice_bitcast_fusion.3
  17.5 3.5 %collective-permute-start.18 = (f16[520,256]{1,0:T(8,128)(2,1)S(1)}, f16[520,256]{1,0:T(8,128)(2,1)S(1)}, u32[]{:S(2)}, u32[]{:S(2)}) collective-permute-start(f16[520,256]{1,0:T(8,128)(2,1)S(1)} %get-tuple-element.110), channel_id=1, source_target_pairs={{8,4},{4,8},{16,12},{12,16},{24,20},{20,24},{9,5},{5,9},{17,13},{1... | collective-permute-start | bytes 798728 | tf_op jit(solution)/shard_map/ppermute | solution.py:305
  21.0 0.1 slice_bitcast_fusion.7
  21.2 3.2 %collective-permute-start.3 = (f16[520,256]{1,0:T(8,128)(2,1)S(1)}, f16[520,256]{1,0:T(8,128)(2,1)S(1)}, u32[]{:S(2)}, u32[]{:S(2)}) collective-permute-start(f16[520,256]{1,0:T(8,128)(2,1)S(1)} %get-tuple-element.114), channel_id=1, source_target_pairs={{8,4},{4,8},{16,12},{12,16},{24,20},{20,24},{9,5},{5,9},{17,13},{1... | collective-permute-start | bytes 798728 | tf_op jit(solution)/shard_map/ppermute | solution.py:305
  24.4 2.4 %shard_map.68 = (f32[768,256]{1,0:T(8,128)S(1)}, f32[2,784,256]{2,1,0:T(8,128)S(1)}) custom-call(f32[1,2]{1,0:T(1,128)S(1)} %copy-done.1, f32[1,2]{1,0:T(1,128)S(1)} %copy-done.2, bf16[1536,1024]{1,0:T(8,128)(2,1)S(1)} %shard_map.66.g_ref, f32[768,256]{1,0:T(8,128)S(1)} %get-tuple-element.58.src_ref, ...), custom_call_target="tpu_custom_call", output_to_operand_aliasing={{1}: (5, {})} | custom-call | flops 1207959552 | bytes 3145728 | tf_op jit(solution)/shard_map/pallas_call | solution.py:27
  26.8 2.4 %shard_map.76 = (f32[768,256]{1,0:T(8,128)S(1)}, f32[2,784,256]{2,1,0:T(8,128)S(1)}) custom-call(f32[1,2]{1,0:T(1,128)S(1)} %copy-done.1, f32[1,2]{1,0:T(1,128)S(1)} %copy-done.2, bf16[1536,1024]{1,0:T(8,128)(2,1)S(1)} %shard_map.66.g_ref, f32[768,256]{1,0:T(8,128)S(1)} %get-tuple-element.85.src_ref, ...), custom_call_target="tpu_custom_call", output_to_operand_aliasing={{1}: (5, {})} | custom-call | flops 1207959552 | bytes 3145728 | tf_op jit(solution)/shard_map/pallas_call | solution.py:27
  29.2 0.1 maximum_convert_fusion.2.got_ref
  29.3 1.8 %shard_map.77 = (f32[192,256]{1,0:T(8,128)S(1)}, f32[200,256]{1,0:T(8,128)S(1)}, f32[200,256]{1,0:T(8,128)S(1)}, f32[200,256]{1,0:T(8,128)S(1)}) custom-call(f32[1,2]{1,0:T(1,128)S(1)} %copy-done.2, bf16[1536,1024]{1,0:T(8,128)(2,1)S(1)} %shard_map.66.g_ref, f32[768,256]{1,0:T(8,128)S(1)} %get-tuple-element.88.part_ref, ...), custom_call_target="tpu_custom_call" | custom-call | flops 805306368 | bytes 3145728 | tf_op jit(solution)/shard_map/pallas_call | solution.py:27
  31.2 3.4 %collective-permute-start.21 = (f16[200,256]{1,0:T(8,128)(2,1)S(1)}, f16[200,256]{1,0:T(8,128)(2,1)S(1)}, u32[]{:S(2)}, u32[]{:S(2)}) collective-permute-start(f16[200,256]{1,0:T(8,128)(2,1)S(1)} %convert_element_type.141), channel_id=1, source_target_pairs={{0,3},{1,2},{2,1},{3,0},{4,7},{5,6},{6,5},{7,4},{8,11},{9,10},{10,... | collective-permute-start | bytes 307208 | tf_op jit(solution)/shard_map/ppermute | solution.py:359
  34.6 0.4 collective-permute-start.19
  34.9 0.1 maximum_convert_fusion.got_ref
  35.0 1.8 %shard_map.69 = (f32[192,256]{1,0:T(8,128)S(1)}, f32[200,256]{1,0:T(8,128)S(1)}, f32[200,256]{1,0:T(8,128)S(1)}, f32[200,256]{1,0:T(8,128)S(1)}) custom-call(f32[1,2]{1,0:T(1,128)S(1)} %copy-done.2, bf16[1536,1024]{1,0:T(8,128)(2,1)S(1)} %shard_map.66.g_ref, f32[768,256]{1,0:T(8,128)S(1)} %get-tuple-element.64.part_ref, ...), custom_call_target="tpu_custom_call" | custom-call | flops 805306368 | bytes 3145728 | tf_op jit(solution)/shard_map/pallas_call | solution.py:27
  36.8 3.3 %collective-permute-start.6 = (f16[200,256]{1,0:T(8,128)(2,1)S(1)}, f16[200,256]{1,0:T(8,128)(2,1)S(1)}, u32[]{:S(2)}, u32[]{:S(2)}) collective-permute-start(f16[200,256]{1,0:T(8,128)(2,1)S(1)} %convert_element_type.123), channel_id=1, source_target_pairs={{0,3},{1,2},{2,1},{3,0},{4,7},{5,6},{6,5},{7,4},{8,11},{9,10},{10,... | collective-permute-start | bytes 307208 | tf_op jit(solution)/shard_map/ppermute | solution.py:359
  40.1 0.1 collective-permute-start.5
  40.2 1.5 %collective-permute-start.4 = (f16[200,256]{1,0:T(8,128)(2,1)S(1)}, f16[200,256]{1,0:T(8,128)(2,1)S(1)}, u32[]{:S(2)}, u32[]{:S(2)}) collective-permute-start(f16[200,256]{1,0:T(8,128)(2,1)S(1)} %convert_element_type.119), channel_id=1, source_target_pairs={{0,1},{1,0},{2,3},{3,2},{4,5},{5,4},{6,7},{7,6},{8,9},{9,8},{10,11... | collective-permute-start | bytes 307208 | tf_op jit(solution)/shard_map/ppermute | solution.py:359
  41.8 6.3 %collective-permute-done.20 = f16[200,256]{1,0:T(8,128)(2,1)S(1)} collective-permute-done((f16[200,256]{1,0:T(8,128)(2,1)S(1)}, f16[200,256]{1,0:T(8,128)(2,1)S(1)}, u32[]{:S(2)}, u32[]{:S(2)}) %collective-permute-start.20) | collective-permute-done | bytes 102432 | tf_op jit(solution)/shard_map/ppermute | solution.py:359
  48.1 0.1 shard_map.78.own_ref
  48.2 2.3 %collective-permute-start.24 = (bf16[192,256]{1,0:T(8,128)(2,1)S(1)}, bf16[192,256]{1,0:T(8,128)(2,1)S(1)}, u32[]{:S(2)}, u32[]{:S(2)}) collective-permute-start(bf16[192,256]{1,0:T(8,128)(2,1)S(1)} %shard_map.78.own_ref), channel_id=1, source_target_pairs={{0,3},{1,2},{2,1},{3,0},{4,7},{5,6},{6,5},{7,4},{8,11},{9,10},{10,... | collective-permute-start | bytes 294920 | tf_op jit(solution)/shard_map/ppermute | solution.py:365
  50.5 1.3 %collective-permute-start.22 = (bf16[192,256]{1,0:T(8,128)(2,1)S(1)}, bf16[192,256]{1,0:T(8,128)(2,1)S(1)}, u32[]{:S(2)}, u32[]{:S(2)}) collective-permute-start(bf16[192,256]{1,0:T(8,128)(2,1)S(1)} %shard_map.78.own_ref), channel_id=1, source_target_pairs={{0,1},{1,0},{2,3},{3,2},{4,5},{5,4},{6,7},{7,6},{8,9},{9,8},{10,11... | collective-permute-start | bytes 294920 | tf_op jit(solution)/shard_map/ppermute | solution.py:365
  51.8 0.6 collective-permute-done.5
  52.5 0.1 shard_map.70.own_ref
  52.6 2.3 %collective-permute-start.9 = (bf16[192,256]{1,0:T(8,128)(2,1)S(1)}, bf16[192,256]{1,0:T(8,128)(2,1)S(1)}, u32[]{:S(2)}, u32[]{:S(2)}) collective-permute-start(bf16[192,256]{1,0:T(8,128)(2,1)S(1)} %shard_map.70.own_ref), channel_id=1, source_target_pairs={{0,3},{1,2},{2,1},{3,0},{4,7},{5,6},{6,5},{7,4},{8,11},{9,10},{10,... | collective-permute-start | bytes 294920 | tf_op jit(solution)/shard_map/ppermute | solution.py:365
  54.9 4.8 %collective-permute-start.7 = (bf16[192,256]{1,0:T(8,128)(2,1)S(1)}, bf16[192,256]{1,0:T(8,128)(2,1)S(1)}, u32[]{:S(2)}, u32[]{:S(2)}) collective-permute-start(bf16[192,256]{1,0:T(8,128)(2,1)S(1)} %shard_map.70.own_ref), channel_id=1, source_target_pairs={{0,1},{1,0},{2,3},{3,2},{4,5},{5,4},{6,7},{7,6},{8,9},{9,8},{10,11... | collective-permute-start | bytes 294920 | tf_op jit(solution)/shard_map/ppermute | solution.py:365
  59.7 5.5 %collective-permute-done.23.rest_1_ = bf16[192,256]{1,0:T(8,128)(2,1)S(1)} collective-permute-done((bf16[192,256]{1,0:T(8,128)(2,1)S(1)}, bf16[192,256]{1,0:T(8,128)(2,1)S(1)}, u32[]{:S(2)}, u32[]{:S(2)}) %collective-permute-start.23) | collective-permute-done | bytes 98336 | tf_op jit(solution)/shard_map/ppermute | solution.py:365
  65.2 0.6 collective-permute-start.25
  65.8 3.4 %collective-permute-start.26 = (bf16[128,256]{1,0:T(8,128)(2,1)S(1)}, bf16[128,256]{1,0:T(8,128)(2,1)S(1)}, u32[]{:S(2)}, u32[]{:S(2)}) collective-permute-start(bf16[128,256]{1,0:T(8,128)(2,1)S(1)} %get-tuple-element.98), channel_id=1, source_target_pairs={{8,4},{4,8},{16,12},{12,16},{24,20},{20,24},{9,5},{5,9},{17,13},{1... | collective-permute-start | bytes 196616 | tf_op jit(solution)/shard_map/ppermute | solution.py:305
  69.2 0.2 collective-permute-done.8.rest_1_
  69.4 0.5 collective-permute-start.10
  69.9 2.5 %collective-permute-start.11 = (bf16[128,256]{1,0:T(8,128)(2,1)S(1)}, bf16[128,256]{1,0:T(8,128)(2,1)S(1)}, u32[]{:S(2)}, u32[]{:S(2)}) collective-permute-start(bf16[128,256]{1,0:T(8,128)(2,1)S(1)} %get-tuple-element.74), channel_id=1, source_target_pairs={{8,4},{4,8},{16,12},{12,16},{24,20},{20,24},{9,5},{5,9},{17,13},{1... | collective-permute-start | bytes 196616 | tf_op jit(solution)/shard_map/ppermute | solution.py:305
  72.4 1.7 %shard_map.80 = (bf16[1024,256]{1,0:T(8,128)(2,1)S(1)}, f32[2,784,256]{2,1,0:T(8,128)S(1)}, f32[2,2,128,256]{3,2,1,0:T(8,128)S(1)}, f32[2,520,256]{2,1,0:T(8,128)S(1)}) custom-call(f32[1,2]{1,0:T(1,128)S(1)} %copy-done.1, bf16[1536,1024]{1,0:T(8,128)(2,1)S(1)} %shard_map.66.g_ref, bf16[768,256]{1,0:T(8,128)(2,1)S(1)} %get-tuple-element.96.src_ref, ...), custom_call_target="tpu_custom_call" | custom-call | flops 536870912 | bytes 3145728 | tf_op jit(solution)/shard_map/pallas_call | solution.py:27
  74.1 0.1 convert.19
  74.2 0.1 slice_bitcast_fusion.1
  74.3 0.1 collective-permute-start.27
  74.4 4.0 %collective-permute-start.28 = (f16[520,256]{1,0:T(8,128)(2,1)S(1)}, f16[520,256]{1,0:T(8,128)(2,1)S(1)}, u32[]{:S(2)}, u32[]{:S(2)}) collective-permute-start(f16[520,256]{1,0:T(8,128)(2,1)S(1)} %get-tuple-element.108), channel_id=1, source_target_pairs={{8,4},{4,8},{16,12},{12,16},{24,20},{20,24},{9,5},{5,9},{17,13},{1... | collective-permute-start | bytes 798728 | tf_op jit(solution)/shard_map/ppermute | solution.py:305
  78.4 1.7 %shard_map.72 = (bf16[1024,256]{1,0:T(8,128)(2,1)S(1)}, f32[2,784,256]{2,1,0:T(8,128)S(1)}, f32[2,2,128,256]{3,2,1,0:T(8,128)S(1)}, f32[2,520,256]{2,1,0:T(8,128)S(1)}) custom-call(f32[1,2]{1,0:T(1,128)S(1)} %copy-done.1, bf16[1536,1024]{1,0:T(8,128)(2,1)S(1)} %shard_map.66.g_ref, bf16[768,256]{1,0:T(8,128)(2,1)S(1)} %get-tuple-element.72.src_ref, ...), custom_call_target="tpu_custom_call" | custom-call | flops 536870912 | bytes 3145728 | tf_op jit(solution)/shard_map/pallas_call | solution.py:27
  80.1 0.1 convert.17
  80.2 0.1 slice_bitcast_fusion.5
  80.4 2.7 %collective-permute-start.13 = (f16[520,256]{1,0:T(8,128)(2,1)S(1)}, f16[520,256]{1,0:T(8,128)(2,1)S(1)}, u32[]{:S(2)}, u32[]{:S(2)}) collective-permute-start(f16[520,256]{1,0:T(8,128)(2,1)S(1)} %get-tuple-element.112), channel_id=1, source_target_pairs={{8,4},{4,8},{16,12},{12,16},{24,20},{20,24},{9,5},{5,9},{17,13},{1... | collective-permute-start | bytes 798728 | tf_op jit(solution)/shard_map/ppermute | solution.py:305
  83.1 2.4 %shard_map.73 = (f32[768,256]{1,0:T(8,128)S(1)}, f32[2,784,256]{2,1,0:T(8,128)S(1)}) custom-call(f32[1,2]{1,0:T(1,128)S(1)} %copy-done.1, f32[1,2]{1,0:T(1,128)S(1)} %copy-done.2, bf16[1536,1024]{1,0:T(8,128)(2,1)S(1)} %shard_map.66.g_ref, bf16[768,256]{1,0:T(8,128)(2,1)S(1)} %get-tuple-element.72.src_ref, ...), custom_call_target="tpu_custom_call", output_to_operand_aliasing={{1}: (5, {})} | custom-call | flops 1207959552 | bytes 3145728 | tf_op jit(solution)/shard_map/pallas_call | solution.py:27
  85.5 0.1 maximum_convert_fusion.3.got_ref
  85.6 3.6 %shard_map.81 = (f32[192,256]{1,0:T(8,128)S(1)}, f32[200,256]{1,0:T(8,128)S(1)}, f32[200,256]{1,0:T(8,128)S(1)}, f32[200,256]{1,0:T(8,128)S(1)}, f32[2,784,256]{2,1,0:T(8,128)S(1)}) custom-call(f32[1,2]{1,0:T(1,128)S(1)} %copy-done.1, f32[1,2]{1,0:T(1,128)S(1)} %copy-done.2, ...), custom_call_target="tpu_custom_call", output_to_operand_aliasing={{4}: (5, {})} | custom-call | flops 1610612736 | bytes 3145728 | tf_op jit(solution)/shard_map/pallas_call | solution.py:27
  89.3 2.3 %collective-permute-start.31 = (f16[200,256]{1,0:T(8,128)(2,1)S(1)}, f16[200,256]{1,0:T(8,128)(2,1)S(1)}, u32[]{:S(2)}, u32[]{:S(2)}) collective-permute-start(f16[200,256]{1,0:T(8,128)(2,1)S(1)} %convert_element_type.150), channel_id=1, source_target_pairs={{0,3},{1,2},{2,1},{3,0},{4,7},{5,6},{6,5},{7,4},{8,11},{9,10},{10,... | collective-permute-start | bytes 307208 | tf_op jit(solution)/shard_map/ppermute | solution.py:359
  91.6 1.3 %collective-permute-start.29 = (f16[200,256]{1,0:T(8,128)(2,1)S(1)}, f16[200,256]{1,0:T(8,128)(2,1)S(1)}, u32[]{:S(2)}, u32[]{:S(2)}) collective-permute-start(f16[200,256]{1,0:T(8,128)(2,1)S(1)} %convert_element_type.146), channel_id=1, source_target_pairs={{0,1},{1,0},{2,3},{3,2},{4,5},{5,4},{6,7},{7,6},{8,9},{9,8},{10,11... | collective-permute-start | bytes 307208 | tf_op jit(solution)/shard_map/ppermute | solution.py:359
  92.9 0.1 maximum_convert_fusion.1.got_ref
  93.0 1.8 %shard_map.74 = (f32[192,256]{1,0:T(8,128)S(1)}, f32[200,256]{1,0:T(8,128)S(1)}, f32[200,256]{1,0:T(8,128)S(1)}, f32[200,256]{1,0:T(8,128)S(1)}) custom-call(f32[1,2]{1,0:T(1,128)S(1)} %copy-done.2, bf16[1536,1024]{1,0:T(8,128)(2,1)S(1)} %shard_map.66.g_ref, f32[768,256]{1,0:T(8,128)S(1)} %get-tuple-element.77.part_ref, ...), custom_call_target="tpu_custom_call" | custom-call | flops 805306368 | bytes 3145728 | tf_op jit(solution)/shard_map/pallas_call | solution.py:27
  94.8 2.3 %collective-permute-start.16 = (f16[200,256]{1,0:T(8,128)(2,1)S(1)}, f16[200,256]{1,0:T(8,128)(2,1)S(1)}, u32[]{:S(2)}, u32[]{:S(2)}) collective-permute-start(f16[200,256]{1,0:T(8,128)(2,1)S(1)} %convert_element_type.132), channel_id=1, source_target_pairs={{0,3},{1,2},{2,1},{3,0},{4,7},{5,6},{6,5},{7,4},{8,11},{9,10},{10,... | collective-permute-start | bytes 307208 | tf_op jit(solution)/shard_map/ppermute | solution.py:359
  97.2 1.3 %collective-permute-start.14 = (f16[200,256]{1,0:T(8,128)(2,1)S(1)}, f16[200,256]{1,0:T(8,128)(2,1)S(1)}, u32[]{:S(2)}, u32[]{:S(2)}) collective-permute-start(f16[200,256]{1,0:T(8,128)(2,1)S(1)} %convert_element_type.128), channel_id=1, source_target_pairs={{0,1},{1,0},{2,3},{3,2},{4,5},{5,4},{6,7},{7,6},{8,9},{9,8},{10,11... | collective-permute-start | bytes 307208 | tf_op jit(solution)/shard_map/ppermute | solution.py:359
  98.5 2.1 %collective-permute-done.30 = f16[200,256]{1,0:T(8,128)(2,1)S(1)} collective-permute-done((f16[200,256]{1,0:T(8,128)(2,1)S(1)}, f16[200,256]{1,0:T(8,128)(2,1)S(1)}, u32[]{:S(2)}, u32[]{:S(2)}) %collective-permute-start.30) | collective-permute-done | bytes 102432 | tf_op jit(solution)/shard_map/ppermute | solution.py:359
  100.7 1.7 %collective-permute-done.16 = f16[200,256]{1,0:T(8,128)(2,1)S(1)} collective-permute-done((f16[200,256]{1,0:T(8,128)(2,1)S(1)}, f16[200,256]{1,0:T(8,128)(2,1)S(1)}, u32[]{:S(2)}, u32[]{:S(2)}) %collective-permute-start.16) | collective-permute-done | bytes 102432 | tf_op jit(solution)/shard_map/ppermute | solution.py:359
  102.4 6.8 %collective-permute-done.15 = f16[200,256]{1,0:T(8,128)(2,1)S(1)} collective-permute-done((f16[200,256]{1,0:T(8,128)(2,1)S(1)}, f16[200,256]{1,0:T(8,128)(2,1)S(1)}, u32[]{:S(2)}, u32[]{:S(2)}) %collective-permute-start.15) | collective-permute-done | bytes 102432 | tf_op jit(solution)/shard_map/ppermute | solution.py:359
  109.2 0.9 shard_map.82
  (67 shorter events, 0.8 us)
Async XLA Ops:
  0.0 1.4 %copy-start = (f32[768,512]{1,0:T(8,128)S(1)}, f32[768,512]{1,0:T(8,128)}, u32[]{:S(2)}) copy-start(f32[768,512]{1,0:T(8,128)} %state_ref.1) | copy-start | bytes 4718596
  1.4 0.7 copy-start.3
  2.1 0.7 copy-start.4
  3.2 10.6 %collective-permute-start = (bf16[128,512]{1,0:T(8,128)(2,1)S(1)}, bf16[128,512]{1,0:T(8,128)(2,1)S(1)}, u32[]{:S(2)}, u32[]{:S(2)}) collective-permute-start(bf16[128,512]{1,0:T(8,128)(2,1)S(1)} %get-tuple-element.59), channel_id=1, source_target_pairs={{4,0},{0,4},{12,8},{8,12},{20,16},{16,20},{28,24},{24,28},{5,1},{1... | collective-permute-start | bytes 393224 | tf_op jit(solution)/shard_map/ppermute | solution.py:304
  3.9 9.8 %collective-permute-start.1 = (bf16[128,512]{1,0:T(8,128)(2,1)S(1)}, bf16[128,512]{1,0:T(8,128)(2,1)S(1)}, u32[]{:S(2)}, u32[]{:S(2)}) collective-permute-start(bf16[128,512]{1,0:T(8,128)(2,1)S(1)} %get-tuple-element.60), channel_id=1, source_target_pairs={{8,4},{4,8},{16,12},{12,16},{24,20},{20,24},{9,5},{5,9},{17,13},{1... | collective-permute-start | bytes 393224 | tf_op jit(solution)/shard_map/ppermute | solution.py:305
  7.0 1.9 %copy-start.5 = (bf16[1,768,2048]{2,1,0:T(8,128)(2,1)S(1)}, bf16[1,768,2048]{2,1,0:T(8,128)(2,1)}, u32[]{:S(2)}) copy-start(bf16[1,768,2048]{2,1,0:T(8,128)(2,1)} %inv_ref.3) | copy-start | bytes 9437188
  11.7 2.1 %copy-start.1 = (f32[1,2]{1,0:T(1,128)S(1)}, f32[1,2]{1,0:T(1,128)}, u32[]{:S(2)}) copy-start(f32[1,2]{1,0:T(1,128)} %shift_ref.15) | copy-start | bytes 28
  17.2 7.2 %copy-start.2 = (f32[1,2]{1,0:T(1,128)S(1)}, f32[1,2]{1,0:T(1,128)}, u32[]{:S(2)}) copy-start(f32[1,2]{1,0:T(1,128)} %weight_ref.13) | copy-start | bytes 28
  17.5 11.7 %collective-permute-start.17 = (f16[520,256]{1,0:T(8,128)(2,1)S(1)}, f16[520,256]{1,0:T(8,128)(2,1)S(1)}, u32[]{:S(2)}, u32[]{:S(2)}) collective-permute-start(f16[520,256]{1,0:T(8,128)(2,1)S(1)} %get-tuple-element.109), channel_id=1, source_target_pairs={{4,0},{0,4},{12,8},{8,12},{20,16},{16,20},{28,24},{24,28},{5,1},{1... | collective-permute-start | bytes 798728 | tf_op jit(solution)/shard_map/ppermute | solution.py:304
  17.5 11.7 %collective-permute-start.18 = (f16[520,256]{1,0:T(8,128)(2,1)S(1)}, f16[520,256]{1,0:T(8,128)(2,1)S(1)}, u32[]{:S(2)}, u32[]{:S(2)}) collective-permute-start(f16[520,256]{1,0:T(8,128)(2,1)S(1)} %get-tuple-element.110), channel_id=1, source_target_pairs={{8,4},{4,8},{16,12},{12,16},{24,20},{20,24},{9,5},{5,9},{17,13},{1... | collective-permute-start | bytes 798728 | tf_op jit(solution)/shard_map/ppermute | solution.py:305
  21.2 13.8 %collective-permute-start.2 = (f16[520,256]{1,0:T(8,128)(2,1)S(1)}, f16[520,256]{1,0:T(8,128)(2,1)S(1)}, u32[]{:S(2)}, u32[]{:S(2)}) collective-permute-start(f16[520,256]{1,0:T(8,128)(2,1)S(1)} %get-tuple-element.113), channel_id=1, source_target_pairs={{4,0},{0,4},{12,8},{8,12},{20,16},{16,20},{28,24},{24,28},{5,1},{1... | collective-permute-start | bytes 798728 | tf_op jit(solution)/shard_map/ppermute | solution.py:304
  21.2 13.7 %collective-permute-start.3 = (f16[520,256]{1,0:T(8,128)(2,1)S(1)}, f16[520,256]{1,0:T(8,128)(2,1)S(1)}, u32[]{:S(2)}, u32[]{:S(2)}) collective-permute-start(f16[520,256]{1,0:T(8,128)(2,1)S(1)} %get-tuple-element.114), channel_id=1, source_target_pairs={{8,4},{4,8},{16,12},{12,16},{24,20},{20,24},{9,5},{5,9},{17,13},{1... | collective-permute-start | bytes 798728 | tf_op jit(solution)/shard_map/ppermute | solution.py:305
  31.2 9.1 %collective-permute-start.21 = (f16[200,256]{1,0:T(8,128)(2,1)S(1)}, f16[200,256]{1,0:T(8,128)(2,1)S(1)}, u32[]{:S(2)}, u32[]{:S(2)}) collective-permute-start(f16[200,256]{1,0:T(8,128)(2,1)S(1)} %convert_element_type.141), channel_id=1, source_target_pairs={{0,3},{1,2},{2,1},{3,0},{4,7},{5,6},{6,5},{7,4},{8,11},{9,10},{10,... | collective-permute-start | bytes 307208 | tf_op jit(solution)/shard_map/ppermute | solution.py:359
  34.6 13.5 %collective-permute-start.20 = (f16[200,256]{1,0:T(8,128)(2,1)S(1)}, f16[200,256]{1,0:T(8,128)(2,1)S(1)}, u32[]{:S(2)}, u32[]{:S(2)}) collective-permute-start(f16[200,256]{1,0:T(8,128)(2,1)S(1)} %convert_element_type.139), channel_id=1, source_target_pairs={{0,2},{1,3},{2,0},{3,1},{4,6},{5,7},{6,4},{7,5},{8,10},{9,11},{10,... | collective-permute-start | bytes 307208 | tf_op jit(solution)/shard_map/ppermute | solution.py:359
  34.6 13.5 %collective-permute-start.19 = (f16[200,256]{1,0:T(8,128)(2,1)S(1)}, f16[200,256]{1,0:T(8,128)(2,1)S(1)}, u32[]{:S(2)}, u32[]{:S(2)}) collective-permute-start(f16[200,256]{1,0:T(8,128)(2,1)S(1)} %convert_element_type.137), channel_id=1, source_target_pairs={{0,1},{1,0},{2,3},{3,2},{4,5},{5,4},{6,7},{7,6},{8,9},{9,8},{10,11... | collective-permute-start | bytes 307208 | tf_op jit(solution)/shard_map/ppermute | solution.py:359
  36.8 13.7 %collective-permute-start.6 = (f16[200,256]{1,0:T(8,128)(2,1)S(1)}, f16[200,256]{1,0:T(8,128)(2,1)S(1)}, u32[]{:S(2)}, u32[]{:S(2)}) collective-permute-start(f16[200,256]{1,0:T(8,128)(2,1)S(1)} %convert_element_type.123), channel_id=1, source_target_pairs={{0,3},{1,2},{2,1},{3,0},{4,7},{5,6},{6,5},{7,4},{8,11},{9,10},{10,... | collective-permute-start | bytes 307208 | tf_op jit(solution)/shard_map/ppermute | solution.py:359
  40.1 12.3 %collective-permute-start.5 = (f16[200,256]{1,0:T(8,128)(2,1)S(1)}, f16[200,256]{1,0:T(8,128)(2,1)S(1)}, u32[]{:S(2)}, u32[]{:S(2)}) collective-permute-start(f16[200,256]{1,0:T(8,128)(2,1)S(1)} %convert_element_type.121), channel_id=1, source_target_pairs={{0,2},{1,3},{2,0},{3,1},{4,6},{5,7},{6,4},{7,5},{8,10},{9,11},{10,... | collective-permute-start | bytes 307208 | tf_op jit(solution)/shard_map/ppermute | solution.py:359
  40.2 12.3 %collective-permute-start.4 = (f16[200,256]{1,0:T(8,128)(2,1)S(1)}, f16[200,256]{1,0:T(8,128)(2,1)S(1)}, u32[]{:S(2)}, u32[]{:S(2)}) collective-permute-start(f16[200,256]{1,0:T(8,128)(2,1)S(1)} %convert_element_type.119), channel_id=1, source_target_pairs={{0,1},{1,0},{2,3},{3,2},{4,5},{5,4},{6,7},{7,6},{8,9},{9,8},{10,11... | collective-permute-start | bytes 307208 | tf_op jit(solution)/shard_map/ppermute | solution.py:359
  48.2 6.7 %collective-permute-start.24 = (bf16[192,256]{1,0:T(8,128)(2,1)S(1)}, bf16[192,256]{1,0:T(8,128)(2,1)S(1)}, u32[]{:S(2)}, u32[]{:S(2)}) collective-permute-start(bf16[192,256]{1,0:T(8,128)(2,1)S(1)} %shard_map.78.own_ref), channel_id=1, source_target_pairs={{0,3},{1,2},{2,1},{3,0},{4,7},{5,6},{6,5},{7,4},{8,11},{9,10},{10,... | collective-permute-start | bytes 294920 | tf_op jit(solution)/shard_map/ppermute | solution.py:365
  50.5 14.7 %collective-permute-start.23 = (bf16[192,256]{1,0:T(8,128)(2,1)S(1)}, bf16[192,256]{1,0:T(8,128)(2,1)S(1)}, u32[]{:S(2)}, u32[]{:S(2)}) collective-permute-start(bf16[192,256]{1,0:T(8,128)(2,1)S(1)} %shard_map.78.own_ref), channel_id=1, source_target_pairs={{0,2},{1,3},{2,0},{3,1},{4,6},{5,7},{6,4},{7,5},{8,10},{9,11},{10,... | collective-permute-start | bytes 294920 | tf_op jit(solution)/shard_map/ppermute | solution.py:365
  50.5 14.7 %collective-permute-start.22 = (bf16[192,256]{1,0:T(8,128)(2,1)S(1)}, bf16[192,256]{1,0:T(8,128)(2,1)S(1)}, u32[]{:S(2)}, u32[]{:S(2)}) collective-permute-start(bf16[192,256]{1,0:T(8,128)(2,1)S(1)} %shard_map.78.own_ref), channel_id=1, source_target_pairs={{0,1},{1,0},{2,3},{3,2},{4,5},{5,4},{6,7},{7,6},{8,9},{9,8},{10,11... | collective-permute-start | bytes 294920 | tf_op jit(solution)/shard_map/ppermute | solution.py:365
  52.6 16.6 %collective-permute-start.9 = (bf16[192,256]{1,0:T(8,128)(2,1)S(1)}, bf16[192,256]{1,0:T(8,128)(2,1)S(1)}, u32[]{:S(2)}, u32[]{:S(2)}) collective-permute-start(bf16[192,256]{1,0:T(8,128)(2,1)S(1)} %shard_map.70.own_ref), channel_id=1, source_target_pairs={{0,3},{1,2},{2,1},{3,0},{4,7},{5,6},{6,5},{7,4},{8,11},{9,10},{10,... | collective-permute-start | bytes 294920 | tf_op jit(solution)/shard_map/ppermute | solution.py:365
  54.9 14.5 %collective-permute-start.8 = (bf16[192,256]{1,0:T(8,128)(2,1)S(1)}, bf16[192,256]{1,0:T(8,128)(2,1)S(1)}, u32[]{:S(2)}, u32[]{:S(2)}) collective-permute-start(bf16[192,256]{1,0:T(8,128)(2,1)S(1)} %shard_map.70.own_ref), channel_id=1, source_target_pairs={{0,2},{1,3},{2,0},{3,1},{4,6},{5,7},{6,4},{7,5},{8,10},{9,11},{10,... | collective-permute-start | bytes 294920 | tf_op jit(solution)/shard_map/ppermute | solution.py:365
  54.9 14.5 %collective-permute-start.7 = (bf16[192,256]{1,0:T(8,128)(2,1)S(1)}, bf16[192,256]{1,0:T(8,128)(2,1)S(1)}, u32[]{:S(2)}, u32[]{:S(2)}) collective-permute-start(bf16[192,256]{1,0:T(8,128)(2,1)S(1)} %shard_map.70.own_ref), channel_id=1, source_target_pairs={{0,1},{1,0},{2,3},{3,2},{4,5},{5,4},{6,7},{7,6},{8,9},{9,8},{10,11... | collective-permute-start | bytes 294920 | tf_op jit(solution)/shard_map/ppermute | solution.py:365
  65.2 7.2 %collective-permute-start.25 = (bf16[128,256]{1,0:T(8,128)(2,1)S(1)}, bf16[128,256]{1,0:T(8,128)(2,1)S(1)}, u32[]{:S(2)}, u32[]{:S(2)}) collective-permute-start(bf16[128,256]{1,0:T(8,128)(2,1)S(1)} %get-tuple-element.97), channel_id=1, source_target_pairs={{4,0},{0,4},{12,8},{8,12},{20,16},{16,20},{28,24},{24,28},{5,1},{1... | collective-permute-start | bytes 196616 | tf_op jit(solution)/shard_map/ppermute | solution.py:304
  65.8 6.6 %collective-permute-start.26 = (bf16[128,256]{1,0:T(8,128)(2,1)S(1)}, bf16[128,256]{1,0:T(8,128)(2,1)S(1)}, u32[]{:S(2)}, u32[]{:S(2)}) collective-permute-start(bf16[128,256]{1,0:T(8,128)(2,1)S(1)} %get-tuple-element.98), channel_id=1, source_target_pairs={{8,4},{4,8},{16,12},{12,16},{24,20},{20,24},{9,5},{5,9},{17,13},{1... | collective-permute-start | bytes 196616 | tf_op jit(solution)/shard_map/ppermute | solution.py:305
  69.4 9.0 %collective-permute-start.10 = (bf16[128,256]{1,0:T(8,128)(2,1)S(1)}, bf16[128,256]{1,0:T(8,128)(2,1)S(1)}, u32[]{:S(2)}, u32[]{:S(2)}) collective-permute-start(bf16[128,256]{1,0:T(8,128)(2,1)S(1)} %get-tuple-element.73), channel_id=1, source_target_pairs={{4,0},{0,4},{12,8},{8,12},{20,16},{16,20},{28,24},{24,28},{5,1},{1... | collective-permute-start | bytes 196616 | tf_op jit(solution)/shard_map/ppermute | solution.py:304
  69.9 8.5 %collective-permute-start.11 = (bf16[128,256]{1,0:T(8,128)(2,1)S(1)}, bf16[128,256]{1,0:T(8,128)(2,1)S(1)}, u32[]{:S(2)}, u32[]{:S(2)}) collective-permute-start(bf16[128,256]{1,0:T(8,128)(2,1)S(1)} %get-tuple-element.74), channel_id=1, source_target_pairs={{8,4},{4,8},{16,12},{12,16},{24,20},{20,24},{9,5},{5,9},{17,13},{1... | collective-permute-start | bytes 196616 | tf_op jit(solution)/shard_map/ppermute | solution.py:305
  74.3 11.2 %collective-permute-start.27 = (f16[520,256]{1,0:T(8,128)(2,1)S(1)}, f16[520,256]{1,0:T(8,128)(2,1)S(1)}, u32[]{:S(2)}, u32[]{:S(2)}) collective-permute-start(f16[520,256]{1,0:T(8,128)(2,1)S(1)} %get-tuple-element.107), channel_id=1, source_target_pairs={{4,0},{0,4},{12,8},{8,12},{20,16},{16,20},{28,24},{24,28},{5,1},{1... | collective-permute-start | bytes 798728 | tf_op jit(solution)/shard_map/ppermute | solution.py:304
  74.4 11.1 %collective-permute-start.28 = (f16[520,256]{1,0:T(8,128)(2,1)S(1)}, f16[520,256]{1,0:T(8,128)(2,1)S(1)}, u32[]{:S(2)}, u32[]{:S(2)}) collective-permute-start(f16[520,256]{1,0:T(8,128)(2,1)S(1)} %get-tuple-element.108), channel_id=1, source_target_pairs={{8,4},{4,8},{16,12},{12,16},{24,20},{20,24},{9,5},{5,9},{17,13},{1... | collective-permute-start | bytes 798728 | tf_op jit(solution)/shard_map/ppermute | solution.py:305
  80.3 12.6 %collective-permute-start.12 = (f16[520,256]{1,0:T(8,128)(2,1)S(1)}, f16[520,256]{1,0:T(8,128)(2,1)S(1)}, u32[]{:S(2)}, u32[]{:S(2)}) collective-permute-start(f16[520,256]{1,0:T(8,128)(2,1)S(1)} %get-tuple-element.111), channel_id=1, source_target_pairs={{4,0},{0,4},{12,8},{8,12},{20,16},{16,20},{28,24},{24,28},{5,1},{1... | collective-permute-start | bytes 798728 | tf_op jit(solution)/shard_map/ppermute | solution.py:304
  80.4 12.5 %collective-permute-start.13 = (f16[520,256]{1,0:T(8,128)(2,1)S(1)}, f16[520,256]{1,0:T(8,128)(2,1)S(1)}, u32[]{:S(2)}, u32[]{:S(2)}) collective-permute-start(f16[520,256]{1,0:T(8,128)(2,1)S(1)} %get-tuple-element.112), channel_id=1, source_target_pairs={{8,4},{4,8},{16,12},{12,16},{24,20},{20,24},{9,5},{5,9},{17,13},{1... | collective-permute-start | bytes 798728 | tf_op jit(solution)/shard_map/ppermute | solution.py:305
  89.3 7.9 %collective-permute-start.31 = (f16[200,256]{1,0:T(8,128)(2,1)S(1)}, f16[200,256]{1,0:T(8,128)(2,1)S(1)}, u32[]{:S(2)}, u32[]{:S(2)}) collective-permute-start(f16[200,256]{1,0:T(8,128)(2,1)S(1)} %convert_element_type.150), channel_id=1, source_target_pairs={{0,3},{1,2},{2,1},{3,0},{4,7},{5,6},{6,5},{7,4},{8,11},{9,10},{10,... | collective-permute-start | bytes 307208 | tf_op jit(solution)/shard_map/ppermute | solution.py:359
  91.6 9.1 %collective-permute-start.30 = (f16[200,256]{1,0:T(8,128)(2,1)S(1)}, f16[200,256]{1,0:T(8,128)(2,1)S(1)}, u32[]{:S(2)}, u32[]{:S(2)}) collective-permute-start(f16[200,256]{1,0:T(8,128)(2,1)S(1)} %convert_element_type.148), channel_id=1, source_target_pairs={{0,2},{1,3},{2,0},{3,1},{4,6},{5,7},{6,4},{7,5},{8,10},{9,11},{10,... | collective-permute-start | bytes 307208 | tf_op jit(solution)/shard_map/ppermute | solution.py:359
  91.6 9.1 %collective-permute-start.29 = (f16[200,256]{1,0:T(8,128)(2,1)S(1)}, f16[200,256]{1,0:T(8,128)(2,1)S(1)}, u32[]{:S(2)}, u32[]{:S(2)}) collective-permute-start(f16[200,256]{1,0:T(8,128)(2,1)S(1)} %convert_element_type.146), channel_id=1, source_target_pairs={{0,1},{1,0},{2,3},{3,2},{4,5},{5,4},{6,7},{7,6},{8,9},{9,8},{10,11... | collective-permute-start | bytes 307208 | tf_op jit(solution)/shard_map/ppermute | solution.py:359
  94.8 7.5 %collective-permute-start.16 = (f16[200,256]{1,0:T(8,128)(2,1)S(1)}, f16[200,256]{1,0:T(8,128)(2,1)S(1)}, u32[]{:S(2)}, u32[]{:S(2)}) collective-permute-start(f16[200,256]{1,0:T(8,128)(2,1)S(1)} %convert_element_type.132), channel_id=1, source_target_pairs={{0,3},{1,2},{2,1},{3,0},{4,7},{5,6},{6,5},{7,4},{8,11},{9,10},{10,... | collective-permute-start | bytes 307208 | tf_op jit(solution)/shard_map/ppermute | solution.py:359
  97.1 12.0 %collective-permute-start.15 = (f16[200,256]{1,0:T(8,128)(2,1)S(1)}, f16[200,256]{1,0:T(8,128)(2,1)S(1)}, u32[]{:S(2)}, u32[]{:S(2)}) collective-permute-start(f16[200,256]{1,0:T(8,128)(2,1)S(1)} %convert_element_type.130), channel_id=1, source_target_pairs={{0,2},{1,3},{2,0},{3,1},{4,6},{5,7},{6,4},{7,5},{8,10},{9,11},{10,... | collective-permute-start | bytes 307208 | tf_op jit(solution)/shard_map/ppermute | solution.py:359
  97.2 12.0 %collective-permute-start.14 = (f16[200,256]{1,0:T(8,128)(2,1)S(1)}, f16[200,256]{1,0:T(8,128)(2,1)S(1)}, u32[]{:S(2)}, u32[]{:S(2)}) collective-permute-start(f16[200,256]{1,0:T(8,128)(2,1)S(1)} %convert_element_type.128), channel_id=1, source_target_pairs={{0,1},{1,0},{2,3},{3,2},{4,5},{5,4},{6,7},{7,6},{8,9},{9,8},{10,11... | collective-permute-start | bytes 307208 | tf_op jit(solution)/shard_map/ppermute | solution.py:359

commit v7 on v6

--- a/solution.py
+++ b/solution.py
@@ -74,17 +74,17 @@
     return jnp.transpose(jnp.broadcast_to(row, (8, count)))[:, :1]
 
 
-def start_kernel(rim, sigma_ref, order_ref, state_ref, msg1_ref, msg2_ref, wide_ref, share_ref, row_ref, *chunks):
+def start_kernel(rim, packed_ref, state_ref, msg1_ref, msg2_ref, wide_ref, share_ref, row_ref, *chunks):
     rows, share, lane = state_ref.shape[0], share_ref.shape[0], 0
     parity = lax.rem(lax.axis_index("sub"), 2)
-    sigma = column(sigma_ref[...].reshape(1, rows), rows)
+    sigma = column(packed_ref[:, :rows], rows)
     low = (state_ref[:rim] * sigma[:rim]).astype(BF16)
     high = (state_ref[rows - rim:] * sigma[rows - rim:]).astype(BF16)
     msg1_ref[...] = pick(parity, high, low)
     msg2_ref[...] = pick(parity, low, high)
     wide_ref[...] = jnp.broadcast_to(sigma, wide_ref.shape)
     share_ref[...] = wide_ref[rows_of(lax.axis_index("pole"), share)]
-    row_ref[...] = order_ref[...].astype(F32)
+    row_ref[...] = packed_ref[:, rows:]
     for ref in chunks:
         ref[...] = state_ref[:, lane:lane + ref.shape[1]] * sigma
         lane += ref.shape[1]
@@ -305,11 +305,12 @@
         two = lax.ppermute(two, "sub", pairs2)
         return one, two
 
+    packed = jnp.concatenate([conductivity, order_list[0].astype(F32)])[None]
     one, two, sigma, sigma_share, order_row, *sources = call(
         functools.partial(start_kernel, rim),
         [((rim, columns), BF16), ((rim, columns), BF16), ((rows, widest), F32), ((share, widest), F32), ((1, order), F32)]
         + [((rows, n), F32) for n in widths],
-        [(VMEM, conductivity), (VMEM, order_list), (VMEM, state)], moved=8 * rows * columns,
+        [(VMEM, packed), (VMEM, state)], moved=8 * rows * columns,
     )
     first_halo = exchange(one, two)
     (g_outer,) = call(

time: 110 us -> 110 us (level)
  other arithmetic: 1.05 us -> 2.43 us
  local copies, waits for them, and re-layouts: 5.12 us -> 3.75 us
    unnamed x12 -> x8, local copies, waits for them, and re-layouts: 4.68 us -> 3.3 us
where the time goes in v7:
time: 110 us
  starting transfers between devices  50.9 us (46%)
  Pallas kernels  29.2 us (27%)
  waiting for transfers between devices  23.2 us (21%)
  local copies, waits for them, and re-layouts  3.75 us (3%)
  other arithmetic  2.43 us (2%)
    pallas_call x19, Pallas kernels, call(): pl.pallas_call(kernel, out_shape=[jax.ShapeDtypeStruct(s, d) for s, d in...  29.2 us
    ppermute x7, starting transfers between devices, exchange(): two = lax.ppermute(two, 'sub', pairs2)  22.2 us
    ppermute x12, waiting for transfers between devices, moved(): lax.ppermute(block.astype(F16), 'pole', hop_pairs(hop + 1, poles))  17.5 us
    ppermute x12, starting transfers between devices, moved(): lax.ppermute(block.astype(F16), 'pole', hop_pairs(hop + 1, poles))  15.9 us
    ppermute x6, starting transfers between devices, gathered(): got.append(lax.ppermute(own, 'pole', hop_pairs(hop + 1, poles)))  10.7 us
    ppermute x6, waiting for transfers between devices, gathered(): got.append(lax.ppermute(own, 'pole', hop_pairs(hop + 1, poles)))  5.72 us
    unnamed x8, local copies, waits for them, and re-layouts  3.3 us
  transfers between devices with their start and end apart: 32, of which 7 were waited for; matrix products, arithmetic and copies ran while one was open for 1% of the time, Pallas kernels for 22%

profile of v7, /device:TPU:3, one launch (start us, length us, event | category | flops | bytes accessed | tf_op | source)
XLA Modules:
  0.0 110.1 jit_solution(3746562295873110990)
XLA Ops:
  0.0 0.7 convert_element_type.122
  0.7 0.7 pad_maximum_fusion
  1.4 1.4 %copy-done = f32[768,512]{1,0:T(8,128)S(1)} copy-done((f32[768,512]{1,0:T(8,128)S(1)}, f32[768,512]{1,0:T(8,128)}, u32[]{:S(2)}) %copy-start) | copy-done | bytes 1572888
  2.8 0.4 shard_map.64
  3.2 0.7 collective-permute-start
  4.0 3.0 %collective-permute-start.1 = (bf16[128,512]{1,0:T(8,128)(2,1)S(1)}, bf16[128,512]{1,0:T(8,128)(2,1)S(1)}, u32[]{:S(2)}, u32[]{:S(2)}) collective-permute-start(bf16[128,512]{1,0:T(8,128)(2,1)S(1)} %get-tuple-element.60), channel_id=1, source_target_pairs={{8,4},{4,8},{16,12},{12,16},{24,20},{20,24},{9,5},{5,9},{17,13},{1... | collective-permute-start | bytes 393224 | tf_op jit(solution)/shard_map/ppermute | solution.py:305
  7.0 1.9 %copy-done.3 = bf16[1,768,2048]{2,1,0:T(8,128)(2,1)S(1)} copy-done((bf16[1,768,2048]{2,1,0:T(8,128)(2,1)S(1)}, bf16[1,768,2048]{2,1,0:T(8,128)(2,1)}, u32[]{:S(2)}) %copy-start.3) | copy-done | bytes 3145752
  8.9 2.8 %shard_map.65.outer_ref.g_ref = bf16[1024,1024]{1,0:T(8,128)(2,1)S(1)} custom-call(f32[1,1024]{1,0:T(1,128)S(1)} %get-tuple-element.56.row_ref, bf16[1,768,2048]{2,1,0:T(8,128)(2,1)S(1)} %copy-done.3), custom_call_target="tpu_custom_call" | custom-call | flops 2147483648 | bytes 4718592 | tf_op jit(solution)/shard_map/pallas_call | solution.py:27
  11.7 2.0 %shard_map.66.g_ref = bf16[1536,1024]{1,0:T(8,128)(2,1)S(1)} custom-call(f32[1,1024]{1,0:T(1,128)S(1)} %get-tuple-element.56.row_ref, bf16[1,768,2048]{2,1,0:T(8,128)(2,1)S(1)} %copy-done.3, bf16[1024,1024]{1,0:T(8,128)(2,1)S(1)} %shard_map.65.outer_ref.g_ref), custom_call_target="tpu_custom_call" | custom-call | flops 3221225472 | bytes 4718592 | tf_op jit(solution)/shard_map/pallas_call | solution.py:27
  13.8 1.7 %shard_map.67 = (bf16[1024,256]{1,0:T(8,128)(2,1)S(1)}, f32[2,784,256]{2,1,0:T(8,128)S(1)}, f32[2,2,128,256]{3,2,1,0:T(8,128)S(1)}, f32[2,520,256]{2,1,0:T(8,128)S(1)}) custom-call(f32[1,2]{1,0:T(1,128)S(1)} %copy-done.1, bf16[1024,1024]{1,0:T(8,128)(2,1)S(1)} %shard_map.65.outer_ref.g_ref, f32[768,256]{1,0:T(8,128)S(1)} %get-tuple-element.58.src_ref, ...), custom_call_target="tpu_custom_call" | custom-call | flops 536870912 | bytes 3145728 | tf_op jit(solution)/shard_map/pallas_call | solution.py:27
  15.5 0.1 convert.16
  15.6 1.7 %shard_map.75 = (bf16[1024,256]{1,0:T(8,128)(2,1)S(1)}, f32[2,784,256]{2,1,0:T(8,128)S(1)}, f32[2,2,128,256]{3,2,1,0:T(8,128)S(1)}, f32[2,520,256]{2,1,0:T(8,128)S(1)}) custom-call(f32[1,2]{1,0:T(1,128)S(1)} %copy-done.1, bf16[1536,1024]{1,0:T(8,128)(2,1)S(1)} %shard_map.66.g_ref, f32[768,256]{1,0:T(8,128)S(1)} %get-tuple-element.85.src_ref, ...), custom_call_target="tpu_custom_call" | custom-call | flops 536870912 | bytes 3145728 | tf_op jit(solution)/shard_map/pallas_call | solution.py:27
  17.3 0.1 convert.18
  17.4 0.1 slice_bitcast_fusion.3
  17.5 0.1 collective-permute-start.17
  17.6 3.5 %collective-permute-start.18 = (f16[520,256]{1,0:T(8,128)(2,1)S(1)}, f16[520,256]{1,0:T(8,128)(2,1)S(1)}, u32[]{:S(2)}, u32[]{:S(2)}) collective-permute-start(f16[520,256]{1,0:T(8,128)(2,1)S(1)} %get-tuple-element.110), channel_id=1, source_target_pairs={{8,4},{4,8},{16,12},{12,16},{24,20},{20,24},{9,5},{5,9},{17,13},{1... | collective-permute-start | bytes 798728 | tf_op jit(solution)/shard_map/ppermute | solution.py:305
  21.1 0.1 slice_bitcast_fusion.7
  21.3 3.2 %collective-permute-start.3 = (f16[520,256]{1,0:T(8,128)(2,1)S(1)}, f16[520,256]{1,0:T(8,128)(2,1)S(1)}, u32[]{:S(2)}, u32[]{:S(2)}) collective-permute-start(f16[520,256]{1,0:T(8,128)(2,1)S(1)} %get-tuple-element.114), channel_id=1, source_target_pairs={{8,4},{4,8},{16,12},{12,16},{24,20},{20,24},{9,5},{5,9},{17,13},{1... | collective-permute-start | bytes 798728 | tf_op jit(solution)/shard_map/ppermute | solution.py:305
  24.4 2.4 %shard_map.68 = (f32[768,256]{1,0:T(8,128)S(1)}, f32[2,784,256]{2,1,0:T(8,128)S(1)}) custom-call(f32[1,2]{1,0:T(1,128)S(1)} %copy-done.1, f32[1,2]{1,0:T(1,128)S(1)} %copy-done.2, bf16[1536,1024]{1,0:T(8,128)(2,1)S(1)} %shard_map.66.g_ref, f32[768,256]{1,0:T(8,128)S(1)} %get-tuple-element.58.src_ref, ...), custom_call_target="tpu_custom_call", output_to_operand_aliasing={{1}: (5, {})} | custom-call | flops 1207959552 | bytes 3145728 | tf_op jit(solution)/shard_map/pallas_call | solution.py:27
  26.8 2.4 %shard_map.76 = (f32[768,256]{1,0:T(8,128)S(1)}, f32[2,784,256]{2,1,0:T(8,128)S(1)}) custom-call(f32[1,2]{1,0:T(1,128)S(1)} %copy-done.1, f32[1,2]{1,0:T(1,128)S(1)} %copy-done.2, bf16[1536,1024]{1,0:T(8,128)(2,1)S(1)} %shard_map.66.g_ref, f32[768,256]{1,0:T(8,128)S(1)} %get-tuple-element.85.src_ref, ...), custom_call_target="tpu_custom_call", output_to_operand_aliasing={{1}: (5, {})} | custom-call | flops 1207959552 | bytes 3145728 | tf_op jit(solution)/shard_map/pallas_call | solution.py:27
  29.2 0.1 maximum_convert_fusion.2.got_ref
  29.3 1.8 %shard_map.77 = (f32[192,256]{1,0:T(8,128)S(1)}, f32[200,256]{1,0:T(8,128)S(1)}, f32[200,256]{1,0:T(8,128)S(1)}, f32[200,256]{1,0:T(8,128)S(1)}) custom-call(f32[1,2]{1,0:T(1,128)S(1)} %copy-done.2, bf16[1536,1024]{1,0:T(8,128)(2,1)S(1)} %shard_map.66.g_ref, f32[768,256]{1,0:T(8,128)S(1)} %get-tuple-element.88.part_ref, ...), custom_call_target="tpu_custom_call" | custom-call | flops 805306368 | bytes 3145728 | tf_op jit(solution)/shard_map/pallas_call | solution.py:27
  31.2 3.4 %collective-permute-start.21 = (f16[200,256]{1,0:T(8,128)(2,1)S(1)}, f16[200,256]{1,0:T(8,128)(2,1)S(1)}, u32[]{:S(2)}, u32[]{:S(2)}) collective-permute-start(f16[200,256]{1,0:T(8,128)(2,1)S(1)} %convert_element_type.149), channel_id=1, source_target_pairs={{0,3},{1,2},{2,1},{3,0},{4,7},{5,6},{6,5},{7,4},{8,11},{9,10},{10,... | collective-permute-start | bytes 307208 | tf_op jit(solution)/shard_map/ppermute | solution.py:360
  34.6 0.4 collective-permute-start.19
  34.9 0.1 maximum_convert_fusion.got_ref
  35.0 1.8 %shard_map.69 = (f32[192,256]{1,0:T(8,128)S(1)}, f32[200,256]{1,0:T(8,128)S(1)}, f32[200,256]{1,0:T(8,128)S(1)}, f32[200,256]{1,0:T(8,128)S(1)}) custom-call(f32[1,2]{1,0:T(1,128)S(1)} %copy-done.2, bf16[1536,1024]{1,0:T(8,128)(2,1)S(1)} %shard_map.66.g_ref, f32[768,256]{1,0:T(8,128)S(1)} %get-tuple-element.64.part_ref, ...), custom_call_target="tpu_custom_call" | custom-call | flops 805306368 | bytes 3145728 | tf_op jit(solution)/shard_map/pallas_call | solution.py:27
  36.8 3.3 %collective-permute-start.6 = (f16[200,256]{1,0:T(8,128)(2,1)S(1)}, f16[200,256]{1,0:T(8,128)(2,1)S(1)}, u32[]{:S(2)}, u32[]{:S(2)}) collective-permute-start(f16[200,256]{1,0:T(8,128)(2,1)S(1)} %convert_element_type.131), channel_id=1, source_target_pairs={{0,3},{1,2},{2,1},{3,0},{4,7},{5,6},{6,5},{7,4},{8,11},{9,10},{10,... | collective-permute-start | bytes 307208 | tf_op jit(solution)/shard_map/ppermute | solution.py:360
  40.1 0.1 collective-permute-start.5
  40.2 1.5 %collective-permute-start.4 = (f16[200,256]{1,0:T(8,128)(2,1)S(1)}, f16[200,256]{1,0:T(8,128)(2,1)S(1)}, u32[]{:S(2)}, u32[]{:S(2)}) collective-permute-start(f16[200,256]{1,0:T(8,128)(2,1)S(1)} %convert_element_type.127), channel_id=1, source_target_pairs={{0,1},{1,0},{2,3},{3,2},{4,5},{5,4},{6,7},{7,6},{8,9},{9,8},{10,11... | collective-permute-start | bytes 307208 | tf_op jit(solution)/shard_map/ppermute | solution.py:360
  41.8 6.3 %collective-permute-done.20 = f16[200,256]{1,0:T(8,128)(2,1)S(1)} collective-permute-done((f16[200,256]{1,0:T(8,128)(2,1)S(1)}, f16[200,256]{1,0:T(8,128)(2,1)S(1)}, u32[]{:S(2)}, u32[]{:S(2)}) %collective-permute-start.20) | collective-permute-done | bytes 102432 | tf_op jit(solution)/shard_map/ppermute | solution.py:360
  48.1 0.1 shard_map.78.own_ref
  48.2 2.3 %collective-permute-start.24 = (bf16[192,256]{1,0:T(8,128)(2,1)S(1)}, bf16[192,256]{1,0:T(8,128)(2,1)S(1)}, u32[]{:S(2)}, u32[]{:S(2)}) collective-permute-start(bf16[192,256]{1,0:T(8,128)(2,1)S(1)} %shard_map.78.own_ref), channel_id=1, source_target_pairs={{0,3},{1,2},{2,1},{3,0},{4,7},{5,6},{6,5},{7,4},{8,11},{9,10},{10,... | collective-permute-start | bytes 294920 | tf_op jit(solution)/shard_map/ppermute | solution.py:366
  50.5 1.3 %collective-permute-start.22 = (bf16[192,256]{1,0:T(8,128)(2,1)S(1)}, bf16[192,256]{1,0:T(8,128)(2,1)S(1)}, u32[]{:S(2)}, u32[]{:S(2)}) collective-permute-start(bf16[192,256]{1,0:T(8,128)(2,1)S(1)} %shard_map.78.own_ref), channel_id=1, source_target_pairs={{0,1},{1,0},{2,3},{3,2},{4,5},{5,4},{6,7},{7,6},{8,9},{9,8},{10,11... | collective-permute-start | bytes 294920 | tf_op jit(solution)/shard_map/ppermute | solution.py:366
  51.9 0.6 collective-permute-done.5
  52.5 0.1 shard_map.70.own_ref
  52.6 2.3 %collective-permute-start.9 = (bf16[192,256]{1,0:T(8,128)(2,1)S(1)}, bf16[192,256]{1,0:T(8,128)(2,1)S(1)}, u32[]{:S(2)}, u32[]{:S(2)}) collective-permute-start(bf16[192,256]{1,0:T(8,128)(2,1)S(1)} %shard_map.70.own_ref), channel_id=1, source_target_pairs={{0,3},{1,2},{2,1},{3,0},{4,7},{5,6},{6,5},{7,4},{8,11},{9,10},{10,... | collective-permute-start | bytes 294920 | tf_op jit(solution)/shard_map/ppermute | solution.py:366
  54.9 4.7 %collective-permute-start.7 = (bf16[192,256]{1,0:T(8,128)(2,1)S(1)}, bf16[192,256]{1,0:T(8,128)(2,1)S(1)}, u32[]{:S(2)}, u32[]{:S(2)}) collective-permute-start(bf16[192,256]{1,0:T(8,128)(2,1)S(1)} %shard_map.70.own_ref), channel_id=1, source_target_pairs={{0,1},{1,0},{2,3},{3,2},{4,5},{5,4},{6,7},{7,6},{8,9},{9,8},{10,11... | collective-permute-start | bytes 294920 | tf_op jit(solution)/shard_map/ppermute | solution.py:366
  59.7 5.5 %collective-permute-done.23.rest_1_ = bf16[192,256]{1,0:T(8,128)(2,1)S(1)} collective-permute-done((bf16[192,256]{1,0:T(8,128)(2,1)S(1)}, bf16[192,256]{1,0:T(8,128)(2,1)S(1)}, u32[]{:S(2)}, u32[]{:S(2)}) %collective-permute-start.23) | collective-permute-done | bytes 98336 | tf_op jit(solution)/shard_map/ppermute | solution.py:366
  65.2 0.6 collective-permute-start.25
  65.8 3.4 %collective-permute-start.26 = (bf16[128,256]{1,0:T(8,128)(2,1)S(1)}, bf16[128,256]{1,0:T(8,128)(2,1)S(1)}, u32[]{:S(2)}, u32[]{:S(2)}) collective-permute-start(bf16[128,256]{1,0:T(8,128)(2,1)S(1)} %get-tuple-element.98), channel_id=1, source_target_pairs={{8,4},{4,8},{16,12},{12,16},{24,20},{20,24},{9,5},{5,9},{17,13},{1... | collective-permute-start | bytes 196616 | tf_op jit(solution)/shard_map/ppermute | solution.py:305
  69.2 0.2 collective-permute-done.8.rest_1_
  69.4 0.5 collective-permute-start.10
  70.0 2.5 %collective-permute-start.11 = (bf16[128,256]{1,0:T(8,128)(2,1)S(1)}, bf16[128,256]{1,0:T(8,128)(2,1)S(1)}, u32[]{:S(2)}, u32[]{:S(2)}) collective-permute-start(bf16[128,256]{1,0:T(8,128)(2,1)S(1)} %get-tuple-element.74), channel_id=1, source_target_pairs={{8,4},{4,8},{16,12},{12,16},{24,20},{20,24},{9,5},{5,9},{17,13},{1... | collective-permute-start | bytes 196616 | tf_op jit(solution)/shard_map/ppermute | solution.py:305
  72.4 1.7 %shard_map.80 = (bf16[1024,256]{1,0:T(8,128)(2,1)S(1)}, f32[2,784,256]{2,1,0:T(8,128)S(1)}, f32[2,2,128,256]{3,2,1,0:T(8,128)S(1)}, f32[2,520,256]{2,1,0:T(8,128)S(1)}) custom-call(f32[1,2]{1,0:T(1,128)S(1)} %copy-done.1, bf16[1536,1024]{1,0:T(8,128)(2,1)S(1)} %shard_map.66.g_ref, bf16[768,256]{1,0:T(8,128)(2,1)S(1)} %get-tuple-element.96.src_ref, ...), custom_call_target="tpu_custom_call" | custom-call | flops 536870912 | bytes 3145728 | tf_op jit(solution)/shard_map/pallas_call | solution.py:27
  74.1 0.1 convert.19
  74.2 0.1 slice_bitcast_fusion.1
  74.4 4.0 %collective-permute-start.28 = (f16[520,256]{1,0:T(8,128)(2,1)S(1)}, f16[520,256]{1,0:T(8,128)(2,1)S(1)}, u32[]{:S(2)}, u32[]{:S(2)}) collective-permute-start(f16[520,256]{1,0:T(8,128)(2,1)S(1)} %get-tuple-element.108), channel_id=1, source_target_pairs={{8,4},{4,8},{16,12},{12,16},{24,20},{20,24},{9,5},{5,9},{17,13},{1... | collective-permute-start | bytes 798728 | tf_op jit(solution)/shard_map/ppermute | solution.py:305
  78.4 1.7 %shard_map.72 = (bf16[1024,256]{1,0:T(8,128)(2,1)S(1)}, f32[2,784,256]{2,1,0:T(8,128)S(1)}, f32[2,2,128,256]{3,2,1,0:T(8,128)S(1)}, f32[2,520,256]{2,1,0:T(8,128)S(1)}) custom-call(f32[1,2]{1,0:T(1,128)S(1)} %copy-done.1, bf16[1536,1024]{1,0:T(8,128)(2,1)S(1)} %shard_map.66.g_ref, bf16[768,256]{1,0:T(8,128)(2,1)S(1)} %get-tuple-element.72.src_ref, ...), custom_call_target="tpu_custom_call" | custom-call | flops 536870912 | bytes 3145728 | tf_op jit(solution)/shard_map/pallas_call | solution.py:27
  80.1 0.1 convert.17
  80.2 0.1 slice_bitcast_fusion.5
  80.4 2.7 %collective-permute-start.13 = (f16[520,256]{1,0:T(8,128)(2,1)S(1)}, f16[520,256]{1,0:T(8,128)(2,1)S(1)}, u32[]{:S(2)}, u32[]{:S(2)}) collective-permute-start(f16[520,256]{1,0:T(8,128)(2,1)S(1)} %get-tuple-element.112), channel_id=1, source_target_pairs={{8,4},{4,8},{16,12},{12,16},{24,20},{20,24},{9,5},{5,9},{17,13},{1... | collective-permute-start | bytes 798728 | tf_op jit(solution)/shard_map/ppermute | solution.py:305
  83.1 2.4 %shard_map.73 = (f32[768,256]{1,0:T(8,128)S(1)}, f32[2,784,256]{2,1,0:T(8,128)S(1)}) custom-call(f32[1,2]{1,0:T(1,128)S(1)} %copy-done.1, f32[1,2]{1,0:T(1,128)S(1)} %copy-done.2, bf16[1536,1024]{1,0:T(8,128)(2,1)S(1)} %shard_map.66.g_ref, bf16[768,256]{1,0:T(8,128)(2,1)S(1)} %get-tuple-element.72.src_ref, ...), custom_call_target="tpu_custom_call", output_to_operand_aliasing={{1}: (5, {})} | custom-call | flops 1207959552 | bytes 3145728 | tf_op jit(solution)/shard_map/pallas_call | solution.py:27
  85.5 0.1 maximum_convert_fusion.3.got_ref
  85.6 3.6 %shard_map.81 = (f32[192,256]{1,0:T(8,128)S(1)}, f32[200,256]{1,0:T(8,128)S(1)}, f32[200,256]{1,0:T(8,128)S(1)}, f32[200,256]{1,0:T(8,128)S(1)}, f32[2,784,256]{2,1,0:T(8,128)S(1)}) custom-call(f32[1,2]{1,0:T(1,128)S(1)} %copy-done.1, f32[1,2]{1,0:T(1,128)S(1)} %copy-done.2, ...), custom_call_target="tpu_custom_call", output_to_operand_aliasing={{4}: (5, {})} | custom-call | flops 1610612736 | bytes 3145728 | tf_op jit(solution)/shard_map/pallas_call | solution.py:27
  89.3 2.3 %collective-permute-start.31 = (f16[200,256]{1,0:T(8,128)(2,1)S(1)}, f16[200,256]{1,0:T(8,128)(2,1)S(1)}, u32[]{:S(2)}, u32[]{:S(2)}) collective-permute-start(f16[200,256]{1,0:T(8,128)(2,1)S(1)} %convert_element_type.158), channel_id=1, source_target_pairs={{0,3},{1,2},{2,1},{3,0},{4,7},{5,6},{6,5},{7,4},{8,11},{9,10},{10,... | collective-permute-start | bytes 307208 | tf_op jit(solution)/shard_map/ppermute | solution.py:360
  91.6 1.3 %collective-permute-start.29 = (f16[200,256]{1,0:T(8,128)(2,1)S(1)}, f16[200,256]{1,0:T(8,128)(2,1)S(1)}, u32[]{:S(2)}, u32[]{:S(2)}) collective-permute-start(f16[200,256]{1,0:T(8,128)(2,1)S(1)} %convert_element_type.154), channel_id=1, source_target_pairs={{0,1},{1,0},{2,3},{3,2},{4,5},{5,4},{6,7},{7,6},{8,9},{9,8},{10,11... | collective-permute-start | bytes 307208 | tf_op jit(solution)/shard_map/ppermute | solution.py:360
  92.9 0.1 maximum_convert_fusion.1.got_ref
  93.0 1.8 %shard_map.74 = (f32[192,256]{1,0:T(8,128)S(1)}, f32[200,256]{1,0:T(8,128)S(1)}, f32[200,256]{1,0:T(8,128)S(1)}, f32[200,256]{1,0:T(8,128)S(1)}) custom-call(f32[1,2]{1,0:T(1,128)S(1)} %copy-done.2, bf16[1536,1024]{1,0:T(8,128)(2,1)S(1)} %shard_map.66.g_ref, f32[768,256]{1,0:T(8,128)S(1)} %get-tuple-element.77.part_ref, ...), custom_call_target="tpu_custom_call" | custom-call | flops 805306368 | bytes 3145728 | tf_op jit(solution)/shard_map/pallas_call | solution.py:27
  94.8 2.3 %collective-permute-start.16 = (f16[200,256]{1,0:T(8,128)(2,1)S(1)}, f16[200,256]{1,0:T(8,128)(2,1)S(1)}, u32[]{:S(2)}, u32[]{:S(2)}) collective-permute-start(f16[200,256]{1,0:T(8,128)(2,1)S(1)} %convert_element_type.140), channel_id=1, source_target_pairs={{0,3},{1,2},{2,1},{3,0},{4,7},{5,6},{6,5},{7,4},{8,11},{9,10},{10,... | collective-permute-start | bytes 307208 | tf_op jit(solution)/shard_map/ppermute | solution.py:360
  97.3 1.3 %collective-permute-start.14 = (f16[200,256]{1,0:T(8,128)(2,1)S(1)}, f16[200,256]{1,0:T(8,128)(2,1)S(1)}, u32[]{:S(2)}, u32[]{:S(2)}) collective-permute-start(f16[200,256]{1,0:T(8,128)(2,1)S(1)} %convert_element_type.136), channel_id=1, source_target_pairs={{0,1},{1,0},{2,3},{3,2},{4,5},{5,4},{6,7},{7,6},{8,9},{9,8},{10,11... | collective-permute-start | bytes 307208 | tf_op jit(solution)/shard_map/ppermute | solution.py:360
  98.6 2.1 %collective-permute-done.30 = f16[200,256]{1,0:T(8,128)(2,1)S(1)} collective-permute-done((f16[200,256]{1,0:T(8,128)(2,1)S(1)}, f16[200,256]{1,0:T(8,128)(2,1)S(1)}, u32[]{:S(2)}, u32[]{:S(2)}) %collective-permute-start.30) | collective-permute-done | bytes 102432 | tf_op jit(solution)/shard_map/ppermute | solution.py:360
  100.7 1.6 %collective-permute-done.16 = f16[200,256]{1,0:T(8,128)(2,1)S(1)} collective-permute-done((f16[200,256]{1,0:T(8,128)(2,1)S(1)}, f16[200,256]{1,0:T(8,128)(2,1)S(1)}, u32[]{:S(2)}, u32[]{:S(2)}) %collective-permute-start.16) | collective-permute-done | bytes 102432 | tf_op jit(solution)/shard_map/ppermute | solution.py:360
  102.4 6.8 %collective-permute-done.15 = f16[200,256]{1,0:T(8,128)(2,1)S(1)} collective-permute-done((f16[200,256]{1,0:T(8,128)(2,1)S(1)}, f16[200,256]{1,0:T(8,128)(2,1)S(1)}, u32[]{:S(2)}, u32[]{:S(2)}) %collective-permute-start.15) | collective-permute-done | bytes 102432 | tf_op jit(solution)/shard_map/ppermute | solution.py:360
  109.2 0.9 shard_map.82
  (66 shorter events, 0.8 us)
Async XLA Ops:
  1.4 1.4 %copy-start = (f32[768,512]{1,0:T(8,128)S(1)}, f32[768,512]{1,0:T(8,128)}, u32[]{:S(2)}) copy-start(f32[768,512]{1,0:T(8,128)} %state_ref.1) | copy-start | bytes 4718596
  3.2 10.6 %collective-permute-start = (bf16[128,512]{1,0:T(8,128)(2,1)S(1)}, bf16[128,512]{1,0:T(8,128)(2,1)S(1)}, u32[]{:S(2)}, u32[]{:S(2)}) collective-permute-start(bf16[128,512]{1,0:T(8,128)(2,1)S(1)} %get-tuple-element.59), channel_id=1, source_target_pairs={{4,0},{0,4},{12,8},{8,12},{20,16},{16,20},{28,24},{24,28},{5,1},{1... | collective-permute-start | bytes 393224 | tf_op jit(solution)/shard_map/ppermute | solution.py:304
  4.0 9.8 %collective-permute-start.1 = (bf16[128,512]{1,0:T(8,128)(2,1)S(1)}, bf16[128,512]{1,0:T(8,128)(2,1)S(1)}, u32[]{:S(2)}, u32[]{:S(2)}) collective-permute-start(bf16[128,512]{1,0:T(8,128)(2,1)S(1)} %get-tuple-element.60), channel_id=1, source_target_pairs={{8,4},{4,8},{16,12},{12,16},{24,20},{20,24},{9,5},{5,9},{17,13},{1... | collective-permute-start | bytes 393224 | tf_op jit(solution)/shard_map/ppermute | solution.py:305
  7.0 1.9 %copy-start.3 = (bf16[1,768,2048]{2,1,0:T(8,128)(2,1)S(1)}, bf16[1,768,2048]{2,1,0:T(8,128)(2,1)}, u32[]{:S(2)}) copy-start(bf16[1,768,2048]{2,1,0:T(8,128)(2,1)} %inv_ref.3) | copy-start | bytes 9437188
  11.7 2.1 %copy-start.1 = (f32[1,2]{1,0:T(1,128)S(1)}, f32[1,2]{1,0:T(1,128)}, u32[]{:S(2)}) copy-start(f32[1,2]{1,0:T(1,128)} %shift_ref.15) | copy-start | bytes 28
  17.3 7.2 %copy-start.2 = (f32[1,2]{1,0:T(1,128)S(1)}, f32[1,2]{1,0:T(1,128)}, u32[]{:S(2)}) copy-start(f32[1,2]{1,0:T(1,128)} %weight_ref.13) | copy-start | bytes 28
  17.5 11.7 %collective-permute-start.17 = (f16[520,256]{1,0:T(8,128)(2,1)S(1)}, f16[520,256]{1,0:T(8,128)(2,1)S(1)}, u32[]{:S(2)}, u32[]{:S(2)}) collective-permute-start(f16[520,256]{1,0:T(8,128)(2,1)S(1)} %get-tuple-element.109), channel_id=1, source_target_pairs={{4,0},{0,4},{12,8},{8,12},{20,16},{16,20},{28,24},{24,28},{5,1},{1... | collective-permute-start | bytes 798728 | tf_op jit(solution)/shard_map/ppermute | solution.py:304
  17.6 11.7 %collective-permute-start.18 = (f16[520,256]{1,0:T(8,128)(2,1)S(1)}, f16[520,256]{1,0:T(8,128)(2,1)S(1)}, u32[]{:S(2)}, u32[]{:S(2)}) collective-permute-start(f16[520,256]{1,0:T(8,128)(2,1)S(1)} %get-tuple-element.110), channel_id=1, source_target_pairs={{8,4},{4,8},{16,12},{12,16},{24,20},{20,24},{9,5},{5,9},{17,13},{1... | collective-permute-start | bytes 798728 | tf_op jit(solution)/shard_map/ppermute | solution.py:305
  21.2 13.8 %collective-permute-start.2 = (f16[520,256]{1,0:T(8,128)(2,1)S(1)}, f16[520,256]{1,0:T(8,128)(2,1)S(1)}, u32[]{:S(2)}, u32[]{:S(2)}) collective-permute-start(f16[520,256]{1,0:T(8,128)(2,1)S(1)} %get-tuple-element.113), channel_id=1, source_target_pairs={{4,0},{0,4},{12,8},{8,12},{20,16},{16,20},{28,24},{24,28},{5,1},{1... | collective-permute-start | bytes 798728 | tf_op jit(solution)/shard_map/ppermute | solution.py:304
  21.3 13.7 %collective-permute-start.3 = (f16[520,256]{1,0:T(8,128)(2,1)S(1)}, f16[520,256]{1,0:T(8,128)(2,1)S(1)}, u32[]{:S(2)}, u32[]{:S(2)}) collective-permute-start(f16[520,256]{1,0:T(8,128)(2,1)S(1)} %get-tuple-element.114), channel_id=1, source_target_pairs={{8,4},{4,8},{16,12},{12,16},{24,20},{20,24},{9,5},{5,9},{17,13},{1... | collective-permute-start | bytes 798728 | tf_op jit(solution)/shard_map/ppermute | solution.py:305
  31.2 9.0 %collective-permute-start.21 = (f16[200,256]{1,0:T(8,128)(2,1)S(1)}, f16[200,256]{1,0:T(8,128)(2,1)S(1)}, u32[]{:S(2)}, u32[]{:S(2)}) collective-permute-start(f16[200,256]{1,0:T(8,128)(2,1)S(1)} %convert_element_type.149), channel_id=1, source_target_pairs={{0,3},{1,2},{2,1},{3,0},{4,7},{5,6},{6,5},{7,4},{8,11},{9,10},{10,... | collective-permute-start | bytes 307208 | tf_op jit(solution)/shard_map/ppermute | solution.py:360
  34.6 13.5 %collective-permute-start.20 = (f16[200,256]{1,0:T(8,128)(2,1)S(1)}, f16[200,256]{1,0:T(8,128)(2,1)S(1)}, u32[]{:S(2)}, u32[]{:S(2)}) collective-permute-start(f16[200,256]{1,0:T(8,128)(2,1)S(1)} %convert_element_type.147), channel_id=1, source_target_pairs={{0,2},{1,3},{2,0},{3,1},{4,6},{5,7},{6,4},{7,5},{8,10},{9,11},{10,... | collective-permute-start | bytes 307208 | tf_op jit(solution)/shard_map/ppermute | solution.py:360
  34.6 13.5 %collective-permute-start.19 = (f16[200,256]{1,0:T(8,128)(2,1)S(1)}, f16[200,256]{1,0:T(8,128)(2,1)S(1)}, u32[]{:S(2)}, u32[]{:S(2)}) collective-permute-start(f16[200,256]{1,0:T(8,128)(2,1)S(1)} %convert_element_type.145), channel_id=1, source_target_pairs={{0,1},{1,0},{2,3},{3,2},{4,5},{5,4},{6,7},{7,6},{8,9},{9,8},{10,11... | collective-permute-start | bytes 307208 | tf_op jit(solution)/shard_map/ppermute | solution.py:360
  36.8 13.7 %collective-permute-start.6 = (f16[200,256]{1,0:T(8,128)(2,1)S(1)}, f16[200,256]{1,0:T(8,128)(2,1)S(1)}, u32[]{:S(2)}, u32[]{:S(2)}) collective-permute-start(f16[200,256]{1,0:T(8,128)(2,1)S(1)} %convert_element_type.131), channel_id=1, source_target_pairs={{0,3},{1,2},{2,1},{3,0},{4,7},{5,6},{6,5},{7,4},{8,11},{9,10},{10,... | collective-permute-start | bytes 307208 | tf_op jit(solution)/shard_map/ppermute | solution.py:360
  40.1 12.3 %collective-permute-start.5 = (f16[200,256]{1,0:T(8,128)(2,1)S(1)}, f16[200,256]{1,0:T(8,128)(2,1)S(1)}, u32[]{:S(2)}, u32[]{:S(2)}) collective-permute-start(f16[200,256]{1,0:T(8,128)(2,1)S(1)} %convert_element_type.129), channel_id=1, source_target_pairs={{0,2},{1,3},{2,0},{3,1},{4,6},{5,7},{6,4},{7,5},{8,10},{9,11},{10,... | collective-permute-start | bytes 307208 | tf_op jit(solution)/shard_map/ppermute | solution.py:360
  40.2 12.3 %collective-permute-start.4 = (f16[200,256]{1,0:T(8,128)(2,1)S(1)}, f16[200,256]{1,0:T(8,128)(2,1)S(1)}, u32[]{:S(2)}, u32[]{:S(2)}) collective-permute-start(f16[200,256]{1,0:T(8,128)(2,1)S(1)} %convert_element_type.127), channel_id=1, source_target_pairs={{0,1},{1,0},{2,3},{3,2},{4,5},{5,4},{6,7},{7,6},{8,9},{9,8},{10,11... | collective-permute-start | bytes 307208 | tf_op jit(solution)/shard_map/ppermute | solution.py:360
  48.2 6.7 %collective-permute-start.24 = (bf16[192,256]{1,0:T(8,128)(2,1)S(1)}, bf16[192,256]{1,0:T(8,128)(2,1)S(1)}, u32[]{:S(2)}, u32[]{:S(2)}) collective-permute-start(bf16[192,256]{1,0:T(8,128)(2,1)S(1)} %shard_map.78.own_ref), channel_id=1, source_target_pairs={{0,3},{1,2},{2,1},{3,0},{4,7},{5,6},{6,5},{7,4},{8,11},{9,10},{10,... | collective-permute-start | bytes 294920 | tf_op jit(solution)/shard_map/ppermute | solution.py:366
  50.5 14.6 %collective-permute-start.23 = (bf16[192,256]{1,0:T(8,128)(2,1)S(1)}, bf16[192,256]{1,0:T(8,128)(2,1)S(1)}, u32[]{:S(2)}, u32[]{:S(2)}) collective-permute-start(bf16[192,256]{1,0:T(8,128)(2,1)S(1)} %shard_map.78.own_ref), channel_id=1, source_target_pairs={{0,2},{1,3},{2,0},{3,1},{4,6},{5,7},{6,4},{7,5},{8,10},{9,11},{10,... | collective-permute-start | bytes 294920 | tf_op jit(solution)/shard_map/ppermute | solution.py:366
  50.5 14.6 %collective-permute-start.22 = (bf16[192,256]{1,0:T(8,128)(2,1)S(1)}, bf16[192,256]{1,0:T(8,128)(2,1)S(1)}, u32[]{:S(2)}, u32[]{:S(2)}) collective-permute-start(bf16[192,256]{1,0:T(8,128)(2,1)S(1)} %shard_map.78.own_ref), channel_id=1, source_target_pairs={{0,1},{1,0},{2,3},{3,2},{4,5},{5,4},{6,7},{7,6},{8,9},{9,8},{10,11... | collective-permute-start | bytes 294920 | tf_op jit(solution)/shard_map/ppermute | solution.py:366
  52.6 16.5 %collective-permute-start.9 = (bf16[192,256]{1,0:T(8,128)(2,1)S(1)}, bf16[192,256]{1,0:T(8,128)(2,1)S(1)}, u32[]{:S(2)}, u32[]{:S(2)}) collective-permute-start(bf16[192,256]{1,0:T(8,128)(2,1)S(1)} %shard_map.70.own_ref), channel_id=1, source_target_pairs={{0,3},{1,2},{2,1},{3,0},{4,7},{5,6},{6,5},{7,4},{8,11},{9,10},{10,... | collective-permute-start | bytes 294920 | tf_op jit(solution)/shard_map/ppermute | solution.py:366
  54.9 14.5 %collective-permute-start.8 = (bf16[192,256]{1,0:T(8,128)(2,1)S(1)}, bf16[192,256]{1,0:T(8,128)(2,1)S(1)}, u32[]{:S(2)}, u32[]{:S(2)}) collective-permute-start(bf16[192,256]{1,0:T(8,128)(2,1)S(1)} %shard_map.70.own_ref), channel_id=1, source_target_pairs={{0,2},{1,3},{2,0},{3,1},{4,6},{5,7},{6,4},{7,5},{8,10},{9,11},{10,... | collective-permute-start | bytes 294920 | tf_op jit(solution)/shard_map/ppermute | solution.py:366
  54.9 14.5 %collective-permute-start.7 = (bf16[192,256]{1,0:T(8,128)(2,1)S(1)}, bf16[192,256]{1,0:T(8,128)(2,1)S(1)}, u32[]{:S(2)}, u32[]{:S(2)}) collective-permute-start(bf16[192,256]{1,0:T(8,128)(2,1)S(1)} %shard_map.70.own_ref), channel_id=1, source_target_pairs={{0,1},{1,0},{2,3},{3,2},{4,5},{5,4},{6,7},{7,6},{8,9},{9,8},{10,11... | collective-permute-start | bytes 294920 | tf_op jit(solution)/shard_map/ppermute | solution.py:366
  65.2 7.2 %collective-permute-start.25 = (bf16[128,256]{1,0:T(8,128)(2,1)S(1)}, bf16[128,256]{1,0:T(8,128)(2,1)S(1)}, u32[]{:S(2)}, u32[]{:S(2)}) collective-permute-start(bf16[128,256]{1,0:T(8,128)(2,1)S(1)} %get-tuple-element.97), channel_id=1, source_target_pairs={{4,0},{0,4},{12,8},{8,12},{20,16},{16,20},{28,24},{24,28},{5,1},{1... | collective-permute-start | bytes 196616 | tf_op jit(solution)/shard_map/ppermute | solution.py:304
  65.8 6.6 %collective-permute-start.26 = (bf16[128,256]{1,0:T(8,128)(2,1)S(1)}, bf16[128,256]{1,0:T(8,128)(2,1)S(1)}, u32[]{:S(2)}, u32[]{:S(2)}) collective-permute-start(bf16[128,256]{1,0:T(8,128)(2,1)S(1)} %get-tuple-element.98), channel_id=1, source_target_pairs={{8,4},{4,8},{16,12},{12,16},{24,20},{20,24},{9,5},{5,9},{17,13},{1... | collective-permute-start | bytes 196616 | tf_op jit(solution)/shard_map/ppermute | solution.py:305
  69.4 9.0 %collective-permute-start.10 = (bf16[128,256]{1,0:T(8,128)(2,1)S(1)}, bf16[128,256]{1,0:T(8,128)(2,1)S(1)}, u32[]{:S(2)}, u32[]{:S(2)}) collective-permute-start(bf16[128,256]{1,0:T(8,128)(2,1)S(1)} %get-tuple-element.73), channel_id=1, source_target_pairs={{4,0},{0,4},{12,8},{8,12},{20,16},{16,20},{28,24},{24,28},{5,1},{1... | collective-permute-start | bytes 196616 | tf_op jit(solution)/shard_map/ppermute | solution.py:304
  70.0 8.5 %collective-permute-start.11 = (bf16[128,256]{1,0:T(8,128)(2,1)S(1)}, bf16[128,256]{1,0:T(8,128)(2,1)S(1)}, u32[]{:S(2)}, u32[]{:S(2)}) collective-permute-start(bf16[128,256]{1,0:T(8,128)(2,1)S(1)} %get-tuple-element.74), channel_id=1, source_target_pairs={{8,4},{4,8},{16,12},{12,16},{24,20},{20,24},{9,5},{5,9},{17,13},{1... | collective-permute-start | bytes 196616 | tf_op jit(solution)/shard_map/ppermute | solution.py:305
  74.3 11.2 %collective-permute-start.27 = (f16[520,256]{1,0:T(8,128)(2,1)S(1)}, f16[520,256]{1,0:T(8,128)(2,1)S(1)}, u32[]{:S(2)}, u32[]{:S(2)}) collective-permute-start(f16[520,256]{1,0:T(8,128)(2,1)S(1)} %get-tuple-element.107), channel_id=1, source_target_pairs={{4,0},{0,4},{12,8},{8,12},{20,16},{16,20},{28,24},{24,28},{5,1},{1... | collective-permute-start | bytes 798728 | tf_op jit(solution)/shard_map/ppermute | solution.py:304
  74.4 11.1 %collective-permute-start.28 = (f16[520,256]{1,0:T(8,128)(2,1)S(1)}, f16[520,256]{1,0:T(8,128)(2,1)S(1)}, u32[]{:S(2)}, u32[]{:S(2)}) collective-permute-start(f16[520,256]{1,0:T(8,128)(2,1)S(1)} %get-tuple-element.108), channel_id=1, source_target_pairs={{8,4},{4,8},{16,12},{12,16},{24,20},{20,24},{9,5},{5,9},{17,13},{1... | collective-permute-start | bytes 798728 | tf_op jit(solution)/shard_map/ppermute | solution.py:305
  80.3 12.6 %collective-permute-start.12 = (f16[520,256]{1,0:T(8,128)(2,1)S(1)}, f16[520,256]{1,0:T(8,128)(2,1)S(1)}, u32[]{:S(2)}, u32[]{:S(2)}) collective-permute-start(f16[520,256]{1,0:T(8,128)(2,1)S(1)} %get-tuple-element.111), channel_id=1, source_target_pairs={{4,0},{0,4},{12,8},{8,12},{20,16},{16,20},{28,24},{24,28},{5,1},{1... | collective-permute-start | bytes 798728 | tf_op jit(solution)/shard_map/ppermute | solution.py:304
  80.4 12.5 %collective-permute-start.13 = (f16[520,256]{1,0:T(8,128)(2,1)S(1)}, f16[520,256]{1,0:T(8,128)(2,1)S(1)}, u32[]{:S(2)}, u32[]{:S(2)}) collective-permute-start(f16[520,256]{1,0:T(8,128)(2,1)S(1)} %get-tuple-element.112), channel_id=1, source_target_pairs={{8,4},{4,8},{16,12},{12,16},{24,20},{20,24},{9,5},{5,9},{17,13},{1... | collective-permute-start | bytes 798728 | tf_op jit(solution)/shard_map/ppermute | solution.py:305
  89.3 7.9 %collective-permute-start.31 = (f16[200,256]{1,0:T(8,128)(2,1)S(1)}, f16[200,256]{1,0:T(8,128)(2,1)S(1)}, u32[]{:S(2)}, u32[]{:S(2)}) collective-permute-start(f16[200,256]{1,0:T(8,128)(2,1)S(1)} %convert_element_type.158), channel_id=1, source_target_pairs={{0,3},{1,2},{2,1},{3,0},{4,7},{5,6},{6,5},{7,4},{8,11},{9,10},{10,... | collective-permute-start | bytes 307208 | tf_op jit(solution)/shard_map/ppermute | solution.py:360
  91.6 9.1 %collective-permute-start.30 = (f16[200,256]{1,0:T(8,128)(2,1)S(1)}, f16[200,256]{1,0:T(8,128)(2,1)S(1)}, u32[]{:S(2)}, u32[]{:S(2)}) collective-permute-start(f16[200,256]{1,0:T(8,128)(2,1)S(1)} %convert_element_type.156), channel_id=1, source_target_pairs={{0,2},{1,3},{2,0},{3,1},{4,6},{5,7},{6,4},{7,5},{8,10},{9,11},{10,... | collective-permute-start | bytes 307208 | tf_op jit(solution)/shard_map/ppermute | solution.py:360
  91.6 9.1 %collective-permute-start.29 = (f16[200,256]{1,0:T(8,128)(2,1)S(1)}, f16[200,256]{1,0:T(8,128)(2,1)S(1)}, u32[]{:S(2)}, u32[]{:S(2)}) collective-permute-start(f16[200,256]{1,0:T(8,128)(2,1)S(1)} %convert_element_type.154), channel_id=1, source_target_pairs={{0,1},{1,0},{2,3},{3,2},{4,5},{5,4},{6,7},{7,6},{8,9},{9,8},{10,11... | collective-permute-start | bytes 307208 | tf_op jit(solution)/shard_map/ppermute | solution.py:360
  94.8 7.5 %collective-permute-start.16 = (f16[200,256]{1,0:T(8,128)(2,1)S(1)}, f16[200,256]{1,0:T(8,128)(2,1)S(1)}, u32[]{:S(2)}, u32[]{:S(2)}) collective-permute-start(f16[200,256]{1,0:T(8,128)(2,1)S(1)} %convert_element_type.140), channel_id=1, source_target_pairs={{0,3},{1,2},{2,1},{3,0},{4,7},{5,6},{6,5},{7,4},{8,11},{9,10},{10,... | collective-permute-start | bytes 307208 | tf_op jit(solution)/shard_map/ppermute | solution.py:360
  97.2 12.0 %collective-permute-start.15 = (f16[200,256]{1,0:T(8,128)(2,1)S(1)}, f16[200,256]{1,0:T(8,128)(2,1)S(1)}, u32[]{:S(2)}, u32[]{:S(2)}) collective-permute-start(f16[200,256]{1,0:T(8,128)(2,1)S(1)} %convert_element_type.138), channel_id=1, source_target_pairs={{0,2},{1,3},{2,0},{3,1},{4,6},{5,7},{6,4},{7,5},{8,10},{9,11},{10,... | collective-permute-start | bytes 307208 | tf_op jit(solution)/shard_map/ppermute | solution.py:360
  97.3 12.0 %collective-permute-start.14 = (f16[200,256]{1,0:T(8,128)(2,1)S(1)}, f16[200,256]{1,0:T(8,128)(2,1)S(1)}, u32[]{:S(2)}, u32[]{:S(2)}) collective-permute-start(f16[200,256]{1,0:T(8,128)(2,1)S(1)} %convert_element_type.136), channel_id=1, source_target_pairs={{0,1},{1,0},{2,3},{3,2},{4,5},{5,4},{6,7},{7,6},{8,9},{9,8},{10,11... | collective-permute-start | bytes 307208 | tf_op jit(solution)/shard_map/ppermute | solution.py:360
